TPU v7x, 32 devices: a whole 2x2x4 slice. The times are simulated.
32 devices in a mesh: groups: 2 (over y), wide: 4 (over z), narrow: 2 (over x), pair: 2 (over core).
Axes of the slice: x: 2, y: 2, z: 4, core: 2. Of those that a mesh axis runs over, the one named last changes fastest.
Arguments:
- volume: bfloat16 [48, 16, 64, 128], P(('groups', 'wide'), 'narrow', 'pair'), parts along dimension 0, may hold values from -6 to 6
- w_encode: bfloat16 [3, 3, 3, 128, 128], replicated, may hold values from -0.109375 to 0.109375
- b_encode: float32 [128], replicated, may hold values from -3 to 3
- w_down: bfloat16 [2, 2, 2, 128, 256], replicated, may hold values from -0.1875 to 0.1875
- b_down: float32 [256], replicated, may hold values from -3 to 3
- w_bottom: bfloat16 [3, 3, 3, 256, 256], replicated, may hold values from -0.078125 to 0.078125
- b_bottom: float32 [256], replicated, may hold values from -3 to 3
- w_up: bfloat16 [2, 2, 2, 256, 128], replicated, may hold values from -0.375 to 0.375
- b_up: float32 [128], replicated, may hold values from -3 to 3
- w_decode: bfloat16 [3, 3, 3, 256, 128], replicated, may hold values from -0.078125 to 0.078125
- b_decode: float32 [128], replicated, may hold values from -3 to 3
Outputs:
- decoded: bfloat16 [48, 16, 64, 128], P(('groups', 'wide'), 'narrow', 'pair'), parts along dimension 0
There are 2 independent parts, one for each index of `groups`. A program takes and returns all parts, laid end to end along the dimension named above; an argument that names none is the same for every part. Nothing has to cross between parts.
All inputs are finite; a program needn't handle non-finite values.
Results may differ from a plain program's by a relative error of at most 0.008.
Values may be sent and summed in bfloat16 or wider, within the bound.
No kernel may reach another device: no remote copies, remote signals or barrier semaphores. Data moves between devices by JAX's collectives and lax.ppermute only.
A program may use at most 64 MiB of HBM per device.

v0:
```python
import jax
import jax.numpy as jnp
from jax import lax
from jax.sharding import PartitionSpec as P

leak_slope = 0.01


def padded_2(block, sides, width):
    for axis, dim in sides:
        count = lax.axis_size(axis)
        forward = [(i, i + 1) for i in range(count - 1)]
        backward = [(target, source) for source, target in forward]
        low = lax.ppermute(
            lax.slice_in_dim(block, block.shape[dim] - width, None, axis=dim), axis, forward
        )
        high = lax.ppermute(lax.slice_in_dim(block, 0, width, axis=dim), axis, backward)
        block = jnp.concatenate([low, block, high], axis=dim)
    return block


def leaky_relu(values):
    return jnp.maximum(values, leak_slope * values)


def conv_taps(padded, weight, first_cells, second_cells, third_cells):
    channels = padded.shape[-1]
    outputs = weight.shape[-1]
    summed = jnp.zeros((first_cells * second_cells * third_cells, outputs), jnp.float32)
    for offset_a in range(3):
        window_rows = jnp.concatenate(
            [
                padded[
                    offset_a : offset_a + first_cells,
                    offset_b : offset_b + second_cells,
                    offset_c : offset_c + third_cells,
                ]
                for offset_b in range(3)
                for offset_c in range(3)
            ],
            axis=-1,
        )
        summed = summed + jnp.dot(
            window_rows.reshape(-1, 9 * channels),
            weight[offset_a].reshape(9 * channels, outputs),
            preferred_element_type=jnp.float32,
        )
    return summed


def body(
    volume, w_encode, b_encode, w_down, b_down, w_bottom, b_bottom, w_up, b_up, w_decode, b_decode
):
    depth_cells, height_cells, width_cells, skip_width = volume.shape
    deep_width = w_down.shape[4]
    half_depth, half_height, half_width = (depth_cells // 2, height_cells // 2, width_cells // 2)
    framed_input = padded_2(volume, (("wide", 0), ("narrow", 1), ("pair", 2)), 1)
    encoded = leaky_relu(
        conv_taps(framed_input, w_encode, depth_cells, height_cells, width_cells) + b_encode
    )
    encoded = encoded.astype(jnp.bfloat16).reshape(
        depth_cells, height_cells, width_cells, skip_width
    )
    blocks = encoded.reshape(half_depth, 2, half_height, 2, half_width, 2, skip_width)
    blocks = blocks.transpose(0, 2, 4, 1, 3, 5, 6).reshape(
        half_depth * half_height * half_width, 8 * skip_width
    )
    coarse = jnp.dot(
        blocks, w_down.reshape(8 * skip_width, deep_width), preferred_element_type=jnp.float32
    )
    coarse = (
        leaky_relu(coarse + b_down)
        .astype(jnp.bfloat16)
        .reshape(half_depth, half_height, half_width, deep_width)
    )
    coarse_padded = padded_2(coarse, (("wide", 0), ("narrow", 1), ("pair", 2)), 1)
    summed = conv_taps(coarse_padded, w_bottom, half_depth, half_height, half_width)
    bottom = (
        leaky_relu(summed + b_bottom)
        .astype(jnp.bfloat16)
        .reshape(half_depth, half_height, half_width, deep_width)
    )
    up_matrix = jnp.transpose(w_up, (3, 0, 1, 2, 4)).reshape(deep_width, 8 * skip_width)
    lifted = jnp.dot(bottom.reshape(-1, deep_width), up_matrix, preferred_element_type=jnp.float32)
    lifted = lifted + jnp.tile(b_up, 8)
    raised = lifted.astype(jnp.bfloat16).reshape(
        half_depth, half_height, half_width, 2, 2, 2, skip_width
    )
    raised = raised.transpose(0, 3, 1, 4, 2, 5, 6).reshape(
        depth_cells, height_cells, width_cells, skip_width
    )
    joined = padded_2(
        jnp.concatenate([raised, encoded], axis=-1), (("wide", 0), ("narrow", 1), ("pair", 2)), 1
    )
    decoded = leaky_relu(
        conv_taps(joined, w_decode, depth_cells, height_cells, width_cells) + b_decode
    )
    return decoded.astype(jnp.bfloat16).reshape(depth_cells, height_cells, width_cells, skip_width)


def solution(mesh):
    return jax.shard_map(
        body,
        mesh=mesh,
        in_specs=(
            P(("groups", "wide"), "narrow", "pair", None),
            P(),
            P(),
            P(),
            P(),
            P(),
            P(),
            P(),
            P(),
            P(),
            P(),
        ),
        out_specs=P(("groups", "wide"), "narrow", "pair", None),
        check_vma=False,
    )
```

profile of v0, /device:TPU:0, one launch (start us, length us, event | category | flops | bytes accessed | tf_op | source)
XLA Modules:
  0.0 97.7 jit_solution(7281089214132819046)
XLA Ops:
  0.0 0.9 fusion.29
  0.9 5.0 %collective-permute-start = (bf16[1,8,32,128]{3,2,1,0:T(8,128)(2,1)S(1)}, bf16[1,8,32,128]{3,2,1,0:T(8,128)(2,1)S(1)}, u32[]{:S(2)}, u32[]{:S(2)}) collective-permute-start(bf16[1,8,32,128]{3,2,1,0:T(8,128)(2,1)S(1)} %get-tuple-element.84), channel_id=1, source_target_pairs={{0,4},{4,8},{8,12},{1,5},{5,9},{9,13},{2,6},{6,10},{10,14},{3,7},{... | collective-permute-start | bytes 196616 | tf_op jit(solution)/shard_map/ppermute | solution.py:14
  5.9 1.3 %collective-permute-start.1 = (bf16[1,8,32,128]{3,2,1,0:T(8,128)(2,1)S(1)}, bf16[1,8,32,128]{3,2,1,0:T(8,128)(2,1)S(1)}, u32[]{:S(2)}, u32[]{:S(2)}) collective-permute-start(bf16[1,8,32,128]{3,2,1,0:T(8,128)(2,1)S(1)} %get-tuple-element.83), channel_id=1, source_target_pairs={{4,0},{8,4},{12,8},{5,1},{9,5},{13,9},{6,2},{10,6},{14,10},{7,3},{... | collective-permute-start | bytes 196616 | tf_op jit(solution)/shard_map/ppermute | solution.py:17
  7.2 0.6 collective-permute-done
  7.8 1.1 %constant_dynamic-update-slice_fusion.1 = bf16[8,8,32,128]{3,2,1,0:T(8,128)(2,1)S(1)} fusion(bf16[8,8,32,128]{3,2,1,0:T(8,128)(2,1)S(1)} %constant_dynamic-update-slice_fusion.2, bf16[6,8,32,128]{3,2,1,0:T(8,128)(2,1)} %param.11), kind=kLoop, calls=%fused_computation.96 | loop fusion | bytes 786432
  8.9 3.2 %collective-permute-done.1 = bf16[1,8,32,128]{3,2,1,0:T(8,128)(2,1)S(1)} collective-permute-done((bf16[1,8,32,128]{3,2,1,0:T(8,128)(2,1)S(1)}, bf16[1,8,32,128]{3,2,1,0:T(8,128)(2,1)S(1)}, u32[]{:S(2)}, u32[]{:S(2)}) %collective-permute-start.1) | collective-permute-done | bytes 65568 | tf_op jit(solution)/shard_map/ppermute | solution.py:17
  12.1 1.3 %collective-permute-start.3 = (bf16[8,1,32,128]{3,2,1,0:T(8,128)(2,1)S(1)}, bf16[8,1,32,128]{3,2,1,0:T(8,128)(2,1)S(1)}, u32[]{:S(2)}, u32[]{:S(2)}) collective-permute-start(bf16[8,1,32,128]{3,2,1,0:T(8,128)(2,1)S(1)} %get-tuple-element.79), channel_id=1, source_target_pairs={{2,0},{3,1},{6,4},{7,5},{10,8},{11,9},{14,12},{15,13},{18,16},{19,... | collective-permute-start | bytes 196616 | tf_op jit(solution)/shard_map/ppermute | solution.py:17
  13.4 4.5 %collective-permute-start.2 = (bf16[8,1,32,128]{3,2,1,0:T(8,128)(2,1)S(1)}, bf16[8,1,32,128]{3,2,1,0:T(8,128)(2,1)S(1)}, u32[]{:S(2)}, u32[]{:S(2)}) collective-permute-start(bf16[8,1,32,128]{3,2,1,0:T(8,128)(2,1)S(1)} %get-tuple-element.78), channel_id=1, source_target_pairs={{0,2},{1,3},{4,6},{5,7},{8,10},{9,11},{12,14},{13,15},{16,18},{17,... | collective-permute-start | bytes 196616 | tf_op jit(solution)/shard_map/ppermute | solution.py:14
  18.3 1.6 %collective-permute-done.2 = bf16[8,1,32,128]{3,2,1,0:T(8,128)(2,1)S(1)} collective-permute-done((bf16[8,1,32,128]{3,2,1,0:T(8,128)(2,1)S(1)}, bf16[8,1,32,128]{3,2,1,0:T(8,128)(2,1)S(1)}, u32[]{:S(2)}, u32[]{:S(2)}) %collective-permute-start.2) | collective-permute-done | bytes 65568 | tf_op jit(solution)/shard_map/ppermute | solution.py:14
  19.9 1.3 %collective-permute-start.5 = (bf16[8,10,1,128]{3,2,1,0:T(2,128)(2,1)S(1)}, bf16[8,10,1,128]{3,2,1,0:T(2,128)(2,1)S(1)}, u32[]{:S(2)}, u32[]{:S(2)}) collective-permute-start(bf16[8,10,1,128]{3,2,1,0:T(2,128)(2,1)S(1)} %get-tuple-element.70), channel_id=1, source_target_pairs={{1,0},{3,2},{5,4},{7,6},{9,8},{11,10},{13,12},{15,14},{17,16},{19,... | collective-permute-start | bytes 61448 | tf_op jit(solution)/shard_map/ppermute | solution.py:17
  21.2 3.0 %collective-permute-start.4 = (bf16[8,10,1,128]{3,2,1,0:T(2,128)(2,1)S(1)}, bf16[8,10,1,128]{3,2,1,0:T(2,128)(2,1)S(1)}, u32[]{:S(2)}, u32[]{:S(2)}) collective-permute-start(bf16[8,10,1,128]{3,2,1,0:T(2,128)(2,1)S(1)} %get-tuple-element.71), channel_id=1, source_target_pairs={{0,1},{2,3},{4,5},{6,7},{8,9},{10,11},{12,13},{14,15},{16,17},{18,... | collective-permute-start | bytes 61448 | tf_op jit(solution)/shard_map/ppermute | solution.py:14
  24.3 1.2 %fusion.27 = (bf16[1,3,3,128,128]{4,3,2,1,0:T(8,128)(2,1)S(1)}, bf16[1,3,3,128,128]{4,3,2,1,0:T(8,128)(2,1)S(1)}, bf16[1,3,3,128,128]{4,3,2,1,0:T(8,128)(2,1)S(1)}) fusion(bf16[3,3,3,128,128]{4,3,2,1,0:T(8,128)(2,1)} %param.12), kind=kLoop, calls=%fused_computation.167 | loop fusion | bytes 1769472 | tf_op jit(solution)/shard_map/slice | solution.py:45
  25.5 0.6 pad_maximum_fusion.2
  26.3 0.4 fusion.18
  26.7 0.5 slice_dynamic-update-slice_fusion.20
  28.1 0.5 slice_dynamic-update-slice_fusion.18
  29.4 0.5 slice_dynamic-update-slice_fusion.16
  29.8 1.1 %fusion.31 = f32[1536,128]{1,0:T(8,128)S(1)} fusion(bf16[1536,1152]{1,0:T(8,128)(2,1)S(1)} %bitcast.89, bf16[1152,128]{1,0:T(8,128)(2,1)S(1)} %bitcast.110), kind=kOutput, calls=%fused_computation.171 | convolution fusion | flops 452984832 | bytes 4620288 | tf_op jit(solution)/shard_map/dot_general | solution.py:43
  31.0 1.1 %convolution_add_fusion.1 = f32[1536,128]{1,0:T(8,128)S(1)} fusion(f32[1536,128]{1,0:T(8,128)S(1)} %fusion.31, bf16[1536,1152]{1,0:T(8,128)(2,1)S(1)} %bitcast.88, bf16[1152,128]{1,0:T(8,128)(2,1)S(1)} %bitcast.109), kind=kOutput, calls=%fused_computation.2 | convolution fusion | flops 453181440 | bytes 5406720 | tf_op jit(solution)/shard_map/dot_general | solution.py:43
  32.1 1.1 %fusion.4 = bf16[1536,128]{1,0:T(8,128)(2,1)S(1)} fusion(f32[1536,128]{1,0:T(8,128)S(1)} %convolution_add_fusion.1, bf16[1536,1152]{1,0:T(8,128)(2,1)S(1)} %bitcast.126, bf16[1152,128]{1,0:T(8,128)(2,1)S(1)} %bitcast.123, f32[128]{0:T(128)S(1)} %copy-done.8), kind=kOutput, calls=%fused_computation.13 | convolution fusion | flops 453967872 | bytes 5014016 | tf_op jit(solution)/shard_map/dot_general | solution.py:43
  34.1 1.3 %collective-permute-start.7 = (bf16[1,4,16,256]{3,2,1,0:T(8,128)(2,1)S(1)}, bf16[1,4,16,256]{3,2,1,0:T(8,128)(2,1)S(1)}, u32[]{:S(2)}, u32[]{:S(2)}) collective-permute-start(bf16[1,4,16,256]{3,2,1,0:T(8,128)(2,1)S(1)} %bitcast.128), channel_id=1, source_target_pairs={{4,0},{8,4},{12,8},{5,1},{9,5},{13,9},{6,2},{10,6},{14,10},{7,3},{... | collective-permute-start | bytes 98312 | tf_op jit(solution)/shard_map/ppermute | solution.py:17
  35.4 4.5 %collective-permute-start.6 = (bf16[1,4,16,256]{3,2,1,0:T(8,128)(2,1)S(1)}, bf16[1,4,16,256]{3,2,1,0:T(8,128)(2,1)S(1)}, u32[]{:S(2)}, u32[]{:S(2)}) collective-permute-start(bf16[1,4,16,256]{3,2,1,0:T(8,128)(2,1)S(1)} %bitcast.127), channel_id=1, source_target_pairs={{0,4},{4,8},{8,12},{1,5},{5,9},{9,13},{2,6},{6,10},{10,14},{3,7},{... | collective-permute-start | bytes 98312 | tf_op jit(solution)/shard_map/ppermute | solution.py:14
  40.0 3.4 %fusion.25 = (bf16[1,3,3,256,256]{4,3,2,1,0:T(8,128)(2,1)}, bf16[1,3,3,256,256]{4,3,2,1,0:T(8,128)(2,1)S(1)}, bf16[1,3,3,256,256]{4,3,2,1,0:T(8,128)(2,1)S(1)}) fusion(bf16[3,3,3,256,256]{4,3,2,1,0:T(8,128)(2,1)} %param.16), kind=kLoop, calls=%fused_computation.165 | loop fusion | bytes 7077888 | tf_op jit(solution)/shard_map/slice | solution.py:45
  43.4 1.3 %collective-permute-start.9 = (bf16[5,1,16,256]{3,2,1,0:T(8,128)(2,1)S(1)}, bf16[5,1,16,256]{3,2,1,0:T(8,128)(2,1)S(1)}, u32[]{:S(2)}, u32[]{:S(2)}) collective-permute-start(bf16[5,1,16,256]{3,2,1,0:T(8,128)(2,1)S(1)} %get-tuple-element.116), channel_id=1, source_target_pairs={{2,0},{3,1},{6,4},{7,5},{10,8},{11,9},{14,12},{15,13},{18,16},{19,... | collective-permute-start | bytes 122888 | tf_op jit(solution)/shard_map/ppermute | solution.py:17
  44.7 4.5 %collective-permute-start.8 = (bf16[5,1,16,256]{3,2,1,0:T(8,128)(2,1)S(1)}, bf16[5,1,16,256]{3,2,1,0:T(8,128)(2,1)S(1)}, u32[]{:S(2)}, u32[]{:S(2)}) collective-permute-start(bf16[5,1,16,256]{3,2,1,0:T(8,128)(2,1)S(1)} %get-tuple-element.115), channel_id=1, source_target_pairs={{0,2},{1,3},{4,6},{5,7},{8,10},{9,11},{12,14},{13,15},{16,18},{17,... | collective-permute-start | bytes 122888 | tf_op jit(solution)/shard_map/ppermute | solution.py:14
  49.3 2.0 %copy.14 = bf16[2,2,2,256,128]{3,4,2,1,0:T(8,128)(2,1)} copy(bf16[2,2,2,256,128]{4,3,2,1,0:T(8,128)(2,1)} %param.18) | data formatting | bytes 1048576 | tf_op args[7]
  51.4 1.3 %collective-permute-start.11 = (bf16[5,6,1,256]{3,2,1,0:T(2,128)(2,1)S(1)}, bf16[5,6,1,256]{3,2,1,0:T(2,128)(2,1)S(1)}, u32[]{:S(2)}, u32[]{:S(2)}) collective-permute-start(bf16[5,6,1,256]{3,2,1,0:T(2,128)(2,1)S(1)} %get-tuple-element.105), channel_id=1, source_target_pairs={{1,0},{3,2},{5,4},{7,6},{9,8},{11,10},{13,12},{15,14},{17,16},{19,... | collective-permute-start | bytes 46088 | tf_op jit(solution)/shard_map/ppermute | solution.py:17
  52.7 3.0 %collective-permute-start.10 = (bf16[5,6,1,256]{3,2,1,0:T(2,128)(2,1)S(1)}, bf16[5,6,1,256]{3,2,1,0:T(2,128)(2,1)S(1)}, u32[]{:S(2)}, u32[]{:S(2)}) collective-permute-start(bf16[5,6,1,256]{3,2,1,0:T(2,128)(2,1)S(1)} %get-tuple-element.106), channel_id=1, source_target_pairs={{0,1},{2,3},{4,5},{6,7},{8,9},{10,11},{12,13},{14,15},{16,17},{18,... | collective-permute-start | bytes 46088 | tf_op jit(solution)/shard_map/ppermute | solution.py:14
  55.8 0.8 collective-permute-done.10
  58.5 2.4 %fusion.2 = bf16[192,1024]{1,0:T(8,128)(2,1)S(1)} fusion(bf16[256,1024]{0,1:T(8,128)(2,1)S(1)} %bitcast.107, f32[1024]{0:T(1024)S(1)} %broadcast_bitcast_fusion, f32[192,256]{1,0:T(8,128)S(1)} %convolution_add_fusion.7, bf16[192,2304]{1,0:T(8,128)(2,1)} %bitcast.111, bf16[2304,256]{1,0:T(8,128)(2,1)} %bitcast.97, f32[256]{0:T(256)S(1)} %copy-done.6), kind=kOutput, calls=%fused_computation.9 | convolution fusion | flops 327794688 | bytes 3183616 | tf_op jit(solution)/shard_map/dot_general | solution.py:84
  61.6 1.3 %collective-permute-start.13 = (bf16[1,8,32,256]{3,2,1,0:T(8,128)(2,1)S(1)}, bf16[1,8,32,256]{3,2,1,0:T(8,128)(2,1)S(1)}, u32[]{:S(2)}, u32[]{:S(2)}) collective-permute-start(bf16[1,8,32,256]{3,2,1,0:T(8,128)(2,1)S(1)} %get-tuple-element.67), channel_id=1, source_target_pairs={{4,0},{8,4},{12,8},{5,1},{9,5},{13,9},{6,2},{10,6},{14,10},{7,3},{... | collective-permute-start | bytes 393224 | tf_op jit(solution)/shard_map/ppermute | solution.py:17
  62.9 4.6 %collective-permute-start.12 = (bf16[1,8,32,256]{3,2,1,0:T(8,128)(2,1)S(1)}, bf16[1,8,32,256]{3,2,1,0:T(8,128)(2,1)S(1)}, u32[]{:S(2)}, u32[]{:S(2)}) collective-permute-start(bf16[1,8,32,256]{3,2,1,0:T(8,128)(2,1)S(1)} %get-tuple-element.66), channel_id=1, source_target_pairs={{0,4},{4,8},{8,12},{1,5},{5,9},{9,13},{2,6},{6,10},{10,14},{3,7},{... | collective-permute-start | bytes 393224 | tf_op jit(solution)/shard_map/ppermute | solution.py:14
  67.5 1.8 %collective-permute-done.13 = bf16[1,8,32,256]{3,2,1,0:T(8,128)(2,1)S(1)} collective-permute-done((bf16[1,8,32,256]{3,2,1,0:T(8,128)(2,1)S(1)}, bf16[1,8,32,256]{3,2,1,0:T(8,128)(2,1)S(1)}, u32[]{:S(2)}, u32[]{:S(2)}) %collective-permute-start.13) | collective-permute-done | bytes 131104 | tf_op jit(solution)/shard_map/ppermute | solution.py:17
  69.3 1.2 %collective-permute-done.12 = bf16[1,8,32,256]{3,2,1,0:T(8,128)(2,1)S(1)} collective-permute-done((bf16[1,8,32,256]{3,2,1,0:T(8,128)(2,1)S(1)}, bf16[1,8,32,256]{3,2,1,0:T(8,128)(2,1)S(1)}, u32[]{:S(2)}, u32[]{:S(2)}) %collective-permute-start.12) | collective-permute-done | bytes 131104 | tf_op jit(solution)/shard_map/ppermute | solution.py:14
  70.5 1.3 %collective-permute-start.15 = (bf16[8,1,32,256]{3,2,1,0:T(8,128)(2,1)S(1)}, bf16[8,1,32,256]{3,2,1,0:T(8,128)(2,1)S(1)}, u32[]{:S(2)}, u32[]{:S(2)}) collective-permute-start(bf16[8,1,32,256]{3,2,1,0:T(8,128)(2,1)S(1)} %get-tuple-element.42), channel_id=1, source_target_pairs={{2,0},{3,1},{6,4},{7,5},{10,8},{11,9},{14,12},{15,13},{18,16},{19,... | collective-permute-start | bytes 393224 | tf_op jit(solution)/shard_map/ppermute | solution.py:17
  71.8 4.7 %collective-permute-start.14 = (bf16[8,1,32,256]{3,2,1,0:T(8,128)(2,1)S(1)}, bf16[8,1,32,256]{3,2,1,0:T(8,128)(2,1)S(1)}, u32[]{:S(2)}, u32[]{:S(2)}) collective-permute-start(bf16[8,1,32,256]{3,2,1,0:T(8,128)(2,1)S(1)} %get-tuple-element.41), channel_id=1, source_target_pairs={{0,2},{1,3},{4,6},{5,7},{8,10},{9,11},{12,14},{13,15},{16,18},{17,... | collective-permute-start | bytes 393224 | tf_op jit(solution)/shard_map/ppermute | solution.py:14
  76.5 1.6 %fusion.26 = (bf16[1,3,3,256,128]{4,3,2,1,0:T(8,128)(2,1)S(1)}, bf16[1,3,3,256,128]{4,3,2,1,0:T(8,128)(2,1)S(1)}, bf16[1,3,3,256,128]{4,3,2,1,0:T(8,128)(2,1)S(1)}) fusion(bf16[3,3,3,256,128]{4,3,2,1,0:T(8,128)(2,1)} %param.20), kind=kLoop, calls=%fused_computation.166 | loop fusion | bytes 3538944 | tf_op jit(solution)/shard_map/slice | solution.py:45
  78.1 0.7 collective-permute-done.14
  79.0 1.3 %collective-permute-start.17 = (bf16[8,10,1,256]{3,2,1,0:T(2,128)(2,1)S(1)}, bf16[8,10,1,256]{3,2,1,0:T(2,128)(2,1)S(1)}, u32[]{:S(2)}, u32[]{:S(2)}) collective-permute-start(bf16[8,10,1,256]{3,2,1,0:T(2,128)(2,1)S(1)} %get-tuple-element.31), channel_id=1, source_target_pairs={{1,0},{3,2},{5,4},{7,6},{9,8},{11,10},{13,12},{15,14},{17,16},{19,... | collective-permute-start | bytes 122888 | tf_op jit(solution)/shard_map/ppermute | solution.py:17
  80.3 3.0 %collective-permute-start.16 = (bf16[8,10,1,256]{3,2,1,0:T(2,128)(2,1)S(1)}, bf16[8,10,1,256]{3,2,1,0:T(2,128)(2,1)S(1)}, u32[]{:S(2)}, u32[]{:S(2)}) collective-permute-start(bf16[8,10,1,256]{3,2,1,0:T(2,128)(2,1)S(1)} %get-tuple-element.32), channel_id=1, source_target_pairs={{0,1},{2,3},{4,5},{6,7},{8,9},{10,11},{12,13},{14,15},{16,17},{18,... | collective-permute-start | bytes 122888 | tf_op jit(solution)/shard_map/ppermute | solution.py:14
  83.8 0.5 collective-permute-done.16
  84.3 2.5 %pad_maximum_fusion = (bf16[8,10,33,256]{3,2,1,0:T(8,128)(2,1)S(1)}, bf16[8,10,33,256]{3,2,1,0:T(8,128)(2,1)S(1)}) fusion(bf16[8,10,1,256]{3,2,1,0:T(2,128)(2,1)S(1)} %collective-permute-done.17, bf16[8,1,32,256]{3,2,1,0:T(8,128)(2,1)S(1)} %collective-permute-done.15, bf16[1,8,32,256]{3,2,1,0:T(8,128)(2,1)S(1)} %collective-permute-done.13, ...), kind=kLoop, calls=%fused_computation.7 | loop fusion | flops 18923520 | bytes 4096000 | tf_op jit(solution)/shard_map/concatenate | solution.py:18
  87.2 0.5 slice_dynamic-update-slice_fusion.5
  88.1 0.5 slice_dynamic-update-slice_fusion.3
  89.3 0.8 slice_dynamic-update-slice_fusion
  90.5 2.0 %fusion.33 = f32[1536,128]{1,0:T(8,128)S(1)} fusion(bf16[1536,2304]{1,0:T(8,128)(2,1)S(1)} %bitcast.125, bf16[2304,128]{1,0:T(8,128)(2,1)S(1)} %bitcast.114), kind=kOutput, calls=%fused_computation.173 | convolution fusion | flops 905969664 | bytes 8454144 | tf_op jit(solution)/shard_map/dot_general | solution.py:43
  92.8 2.1 %convolution_add_fusion.3 = f32[1536,128]{1,0:T(8,128)S(1)} fusion(f32[1536,128]{1,0:T(8,128)S(1)} %fusion.33, bf16[1536,2304]{1,0:T(8,128)(2,1)S(1)} %constant_dynamic-update-slice_fusion.31, bf16[2304,128]{1,0:T(8,128)(2,1)S(1)} %bitcast.106), kind=kOutput, calls=%fused_computation.4 | convolution fusion | flops 906166272 | bytes 9240576 | tf_op jit(solution)/shard_map/dot_general | solution.py:43
  94.9 2.8 %fusion.3 = bf16[1536,128]{1,0:T(8,128)(2,1)} fusion(f32[1536,128]{1,0:T(8,128)S(1)} %convolution_add_fusion.3, bf16[1536,2304]{1,0:T(8,128)(2,1)S(1)} %bitcast.124, bf16[2304,128]{1,0:T(8,128)(2,1)S(1)} %bitcast.113, f32[128]{0:T(128)S(1)} %copy-done.9), kind=kOutput, calls=%fused_computation.11 | convolution fusion | flops 906952704 | bytes 8847872 | tf_op jit(solution)/shard_map/dot_general | solution.py:43
  (90 shorter events, 8.4 us)
Async XLA Ops:
  0.0 33.8 %copy-start = (bf16[2,2,2,128,256]{4,3,2,1,0:T(8,128)(2,1)S(1)}, bf16[2,2,2,128,256]{4,3,2,1,0:T(8,128)(2,1)}, u32[]{:S(2)}) copy-start(bf16[2,2,2,128,256]{4,3,2,1,0:T(8,128)(2,1)} %param.14) | copy-start | bytes 1572868
  0.9 6.9 %collective-permute-start = (bf16[1,8,32,128]{3,2,1,0:T(8,128)(2,1)S(1)}, bf16[1,8,32,128]{3,2,1,0:T(8,128)(2,1)S(1)}, u32[]{:S(2)}, u32[]{:S(2)}) collective-permute-start(bf16[1,8,32,128]{3,2,1,0:T(8,128)(2,1)S(1)} %get-tuple-element.84), channel_id=1, source_target_pairs={{0,4},{4,8},{8,12},{1,5},{5,9},{9,13},{2,6},{6,10},{10,14},{3,7},{... | collective-permute-start | bytes 196616 | tf_op jit(solution)/shard_map/ppermute | solution.py:14
  5.9 6.2 %collective-permute-start.1 = (bf16[1,8,32,128]{3,2,1,0:T(8,128)(2,1)S(1)}, bf16[1,8,32,128]{3,2,1,0:T(8,128)(2,1)S(1)}, u32[]{:S(2)}, u32[]{:S(2)}) collective-permute-start(bf16[1,8,32,128]{3,2,1,0:T(8,128)(2,1)S(1)} %get-tuple-element.83), channel_id=1, source_target_pairs={{4,0},{8,4},{12,8},{5,1},{9,5},{13,9},{6,2},{10,6},{14,10},{7,3},{... | collective-permute-start | bytes 196616 | tf_op jit(solution)/shard_map/ppermute | solution.py:17
  12.1 6.2 %collective-permute-start.3 = (bf16[8,1,32,128]{3,2,1,0:T(8,128)(2,1)S(1)}, bf16[8,1,32,128]{3,2,1,0:T(8,128)(2,1)S(1)}, u32[]{:S(2)}, u32[]{:S(2)}) collective-permute-start(bf16[8,1,32,128]{3,2,1,0:T(8,128)(2,1)S(1)} %get-tuple-element.79), channel_id=1, source_target_pairs={{2,0},{3,1},{6,4},{7,5},{10,8},{11,9},{14,12},{15,13},{18,16},{19,... | collective-permute-start | bytes 196616 | tf_op jit(solution)/shard_map/ppermute | solution.py:17
  13.4 6.4 %collective-permute-start.2 = (bf16[8,1,32,128]{3,2,1,0:T(8,128)(2,1)S(1)}, bf16[8,1,32,128]{3,2,1,0:T(8,128)(2,1)S(1)}, u32[]{:S(2)}, u32[]{:S(2)}) collective-permute-start(bf16[8,1,32,128]{3,2,1,0:T(8,128)(2,1)S(1)} %get-tuple-element.78), channel_id=1, source_target_pairs={{0,2},{1,3},{4,6},{5,7},{8,10},{9,11},{12,14},{13,15},{16,18},{17,... | collective-permute-start | bytes 196616 | tf_op jit(solution)/shard_map/ppermute | solution.py:14
  19.9 5.6 %collective-permute-start.5 = (bf16[8,10,1,128]{3,2,1,0:T(2,128)(2,1)S(1)}, bf16[8,10,1,128]{3,2,1,0:T(2,128)(2,1)S(1)}, u32[]{:S(2)}, u32[]{:S(2)}) collective-permute-start(bf16[8,10,1,128]{3,2,1,0:T(2,128)(2,1)S(1)} %get-tuple-element.70), channel_id=1, source_target_pairs={{1,0},{3,2},{5,4},{7,6},{9,8},{11,10},{13,12},{15,14},{17,16},{19,... | collective-permute-start | bytes 61448 | tf_op jit(solution)/shard_map/ppermute | solution.py:17
  21.2 4.3 %collective-permute-start.4 = (bf16[8,10,1,128]{3,2,1,0:T(2,128)(2,1)S(1)}, bf16[8,10,1,128]{3,2,1,0:T(2,128)(2,1)S(1)}, u32[]{:S(2)}, u32[]{:S(2)}) collective-permute-start(bf16[8,10,1,128]{3,2,1,0:T(2,128)(2,1)S(1)} %get-tuple-element.71), channel_id=1, source_target_pairs={{0,1},{2,3},{4,5},{6,7},{8,9},{10,11},{12,13},{14,15},{16,17},{18,... | collective-permute-start | bytes 61448 | tf_op jit(solution)/shard_map/ppermute | solution.py:14
  26.3 1.3 %copy-start.2 = (bf16[6,8,32,128]{3,2,1,0:T(8,128)(2,1)S(1)}, bf16[6,8,32,128]{3,2,1,0:T(8,128)(2,1)}, u32[]{:S(2)}) copy-start(bf16[6,8,32,128]{3,2,1,0:T(8,128)(2,1)} %param.11) | copy-start | bytes 1179652
  30.9 1.1 %copy-start.8 = (f32[128]{0:T(128)S(1)}, f32[128]{0:T(128)}, u32[]{:S(2)}) copy-start(f32[128]{0:T(128)} %param.13) | copy-start | bytes 1540
  32.1 1.7 %copy-start.5 = (f32[256]{0:T(256)S(1)}, f32[256]{0:T(256)}, u32[]{:S(2)}) copy-start(f32[256]{0:T(256)} %param.15) | copy-start | bytes 3076
  34.1 9.2 %collective-permute-start.7 = (bf16[1,4,16,256]{3,2,1,0:T(8,128)(2,1)S(1)}, bf16[1,4,16,256]{3,2,1,0:T(8,128)(2,1)S(1)}, u32[]{:S(2)}, u32[]{:S(2)}) collective-permute-start(bf16[1,4,16,256]{3,2,1,0:T(8,128)(2,1)S(1)} %bitcast.128), channel_id=1, source_target_pairs={{4,0},{8,4},{12,8},{5,1},{9,5},{13,9},{6,2},{10,6},{14,10},{7,3},{... | collective-permute-start | bytes 98312 | tf_op jit(solution)/shard_map/ppermute | solution.py:17
  35.4 13.8 %copy-start.7 = (f32[128]{0:T(128)S(1)}, f32[128]{0:T(128)}, u32[]{:S(2)}) copy-start(f32[128]{0:T(128)} %param.19) | copy-start | bytes 1540
  35.4 7.9 %collective-permute-start.6 = (bf16[1,4,16,256]{3,2,1,0:T(8,128)(2,1)S(1)}, bf16[1,4,16,256]{3,2,1,0:T(8,128)(2,1)S(1)}, u32[]{:S(2)}, u32[]{:S(2)}) collective-permute-start(bf16[1,4,16,256]{3,2,1,0:T(8,128)(2,1)S(1)} %bitcast.127), channel_id=1, source_target_pairs={{0,4},{4,8},{8,12},{1,5},{5,9},{9,13},{2,6},{6,10},{10,14},{3,7},{... | collective-permute-start | bytes 98312 | tf_op jit(solution)/shard_map/ppermute | solution.py:14
  43.4 7.9 %collective-permute-start.9 = (bf16[5,1,16,256]{3,2,1,0:T(8,128)(2,1)S(1)}, bf16[5,1,16,256]{3,2,1,0:T(8,128)(2,1)S(1)}, u32[]{:S(2)}, u32[]{:S(2)}) collective-permute-start(bf16[5,1,16,256]{3,2,1,0:T(8,128)(2,1)S(1)} %get-tuple-element.116), channel_id=1, source_target_pairs={{2,0},{3,1},{6,4},{7,5},{10,8},{11,9},{14,12},{15,13},{18,16},{19,... | collective-permute-start | bytes 122888 | tf_op jit(solution)/shard_map/ppermute | solution.py:17
  44.7 6.6 %collective-permute-start.8 = (bf16[5,1,16,256]{3,2,1,0:T(8,128)(2,1)S(1)}, bf16[5,1,16,256]{3,2,1,0:T(8,128)(2,1)S(1)}, u32[]{:S(2)}, u32[]{:S(2)}) collective-permute-start(bf16[5,1,16,256]{3,2,1,0:T(8,128)(2,1)S(1)} %get-tuple-element.115), channel_id=1, source_target_pairs={{0,2},{1,3},{4,6},{5,7},{8,10},{9,11},{12,14},{13,15},{16,18},{17,... | collective-permute-start | bytes 122888 | tf_op jit(solution)/shard_map/ppermute | solution.py:14
  51.4 4.4 %collective-permute-start.11 = (bf16[5,6,1,256]{3,2,1,0:T(2,128)(2,1)S(1)}, bf16[5,6,1,256]{3,2,1,0:T(2,128)(2,1)S(1)}, u32[]{:S(2)}, u32[]{:S(2)}) collective-permute-start(bf16[5,6,1,256]{3,2,1,0:T(2,128)(2,1)S(1)} %get-tuple-element.105), channel_id=1, source_target_pairs={{1,0},{3,2},{5,4},{7,6},{9,8},{11,10},{13,12},{15,14},{17,16},{19,... | collective-permute-start | bytes 46088 | tf_op jit(solution)/shard_map/ppermute | solution.py:17
  52.7 3.9 %collective-permute-start.10 = (bf16[5,6,1,256]{3,2,1,0:T(2,128)(2,1)S(1)}, bf16[5,6,1,256]{3,2,1,0:T(2,128)(2,1)S(1)}, u32[]{:S(2)}, u32[]{:S(2)}) collective-permute-start(bf16[5,6,1,256]{3,2,1,0:T(2,128)(2,1)S(1)} %get-tuple-element.106), channel_id=1, source_target_pairs={{0,1},{2,3},{4,5},{6,7},{8,9},{10,11},{12,13},{14,15},{16,17},{18,... | collective-permute-start | bytes 46088 | tf_op jit(solution)/shard_map/ppermute | solution.py:14
  57.1 1.1 %copy-start.6 = (f32[256]{0:T(256)S(1)}, f32[256]{0:T(256)}, u32[]{:S(2)}) copy-start(f32[256]{0:T(256)} %param.17) | copy-start | bytes 3076
  57.2 1.0 %copy-start.4 = (bf16[3,4,16,2304]{3,2,1,0:T(8,128)(2,1)}, bf16[3,4,16,2304]{3,2,1,0:T(8,128)(2,1)S(1)}, u32[]{:S(2)}) copy-start(bf16[3,4,16,2304]{3,2,1,0:T(8,128)(2,1)S(1)} %get-tuple-element.85) | copy-start | bytes 2654212
  57.2 1.4 %copy-start.3 = (bf16[2,2,2,256,128]{3,4,2,1,0:T(8,128)(2,1)S(1)}, bf16[2,2,2,256,128]{3,4,2,1,0:T(8,128)(2,1)}, u32[]{:S(2)}) copy-start(bf16[2,2,2,256,128]{3,4,2,1,0:T(8,128)(2,1)} %copy.14) | copy-start | bytes 1572868
  61.6 7.6 %collective-permute-start.13 = (bf16[1,8,32,256]{3,2,1,0:T(8,128)(2,1)S(1)}, bf16[1,8,32,256]{3,2,1,0:T(8,128)(2,1)S(1)}, u32[]{:S(2)}, u32[]{:S(2)}) collective-permute-start(bf16[1,8,32,256]{3,2,1,0:T(8,128)(2,1)S(1)} %get-tuple-element.67), channel_id=1, source_target_pairs={{4,0},{8,4},{12,8},{5,1},{9,5},{13,9},{6,2},{10,6},{14,10},{7,3},{... | collective-permute-start | bytes 393224 | tf_op jit(solution)/shard_map/ppermute | solution.py:17
  62.9 7.5 %collective-permute-start.12 = (bf16[1,8,32,256]{3,2,1,0:T(8,128)(2,1)S(1)}, bf16[1,8,32,256]{3,2,1,0:T(8,128)(2,1)S(1)}, u32[]{:S(2)}, u32[]{:S(2)}) collective-permute-start(bf16[1,8,32,256]{3,2,1,0:T(8,128)(2,1)S(1)} %get-tuple-element.66), channel_id=1, source_target_pairs={{0,4},{4,8},{8,12},{1,5},{5,9},{9,13},{2,6},{6,10},{10,14},{3,7},{... | collective-permute-start | bytes 393224 | tf_op jit(solution)/shard_map/ppermute | solution.py:14
  70.5 7.6 %collective-permute-start.15 = (bf16[8,1,32,256]{3,2,1,0:T(8,128)(2,1)S(1)}, bf16[8,1,32,256]{3,2,1,0:T(8,128)(2,1)S(1)}, u32[]{:S(2)}, u32[]{:S(2)}) collective-permute-start(bf16[8,1,32,256]{3,2,1,0:T(8,128)(2,1)S(1)} %get-tuple-element.42), channel_id=1, source_target_pairs={{2,0},{3,1},{6,4},{7,5},{10,8},{11,9},{14,12},{15,13},{18,16},{19,... | collective-permute-start | bytes 393224 | tf_op jit(solution)/shard_map/ppermute | solution.py:17
  71.8 7.1 %collective-permute-start.14 = (bf16[8,1,32,256]{3,2,1,0:T(8,128)(2,1)S(1)}, bf16[8,1,32,256]{3,2,1,0:T(8,128)(2,1)S(1)}, u32[]{:S(2)}, u32[]{:S(2)}) collective-permute-start(bf16[8,1,32,256]{3,2,1,0:T(8,128)(2,1)S(1)} %get-tuple-element.41), channel_id=1, source_target_pairs={{0,2},{1,3},{4,6},{5,7},{8,10},{9,11},{12,14},{13,15},{16,18},{17,... | collective-permute-start | bytes 393224 | tf_op jit(solution)/shard_map/ppermute | solution.py:14
  79.0 4.7 %collective-permute-start.17 = (bf16[8,10,1,256]{3,2,1,0:T(2,128)(2,1)S(1)}, bf16[8,10,1,256]{3,2,1,0:T(2,128)(2,1)S(1)}, u32[]{:S(2)}, u32[]{:S(2)}) collective-permute-start(bf16[8,10,1,256]{3,2,1,0:T(2,128)(2,1)S(1)} %get-tuple-element.31), channel_id=1, source_target_pairs={{1,0},{3,2},{5,4},{7,6},{9,8},{11,10},{13,12},{15,14},{17,16},{19,... | collective-permute-start | bytes 122888 | tf_op jit(solution)/shard_map/ppermute | solution.py:17
  80.3 3.9 %collective-permute-start.16 = (bf16[8,10,1,256]{3,2,1,0:T(2,128)(2,1)S(1)}, bf16[8,10,1,256]{3,2,1,0:T(2,128)(2,1)S(1)}, u32[]{:S(2)}, u32[]{:S(2)}) collective-permute-start(bf16[8,10,1,256]{3,2,1,0:T(2,128)(2,1)S(1)} %get-tuple-element.32), channel_id=1, source_target_pairs={{0,1},{2,3},{4,5},{6,7},{8,9},{10,11},{12,13},{14,15},{16,17},{18,... | collective-permute-start | bytes 122888 | tf_op jit(solution)/shard_map/ppermute | solution.py:14
  92.7 2.1 %copy-start.9 = (f32[128]{0:T(128)S(1)}, f32[128]{0:T(128)}, u32[]{:S(2)}) copy-start(f32[128]{0:T(128)} %param.21) | copy-start | bytes 1540
  94.9 2.8 %copy-start.1 = (bf16[2,2,2,128,256]{4,3,2,1,0:T(8,128)(2,1)S(1)}, bf16[2,2,2,128,256]{4,3,2,1,0:T(8,128)(2,1)}, u32[]{:S(2)}) copy-start(bf16[2,2,2,128,256]{4,3,2,1,0:T(8,128)(2,1)} %param.14) | copy-start | bytes 1572868
where the time goes:
time: 99.3 us; the launch traced here: 97.7 us
  starting transfers between devices  48.6 us (49%)
  local copies, waits for them, and re-layouts  18.3 us (18%)
  matrix products  13.7 us (14%)
  waiting for transfers between devices  10.7 us (11%)
  other arithmetic  5.5 us (6%)
    ppermute x9, starting transfers between devices, padded_2(): lax.ppermute(lax.slice_in_dim(block, block.shape[dim] - width, None, axis...  37 us
    ppermute x9, starting transfers between devices, padded_2(): lax.ppermute(lax.slice_in_dim(block, 0, width, axis=dim), axis, backward)  11.6 us
    dot_general x8, matrix products, conv_taps(): jnp.dot(window_rows.reshape(-1, 9 * channels), weight[offset_a].reshape(9...  11.1 us
    unnamed x59, local copies, waits for them, and re-layouts  8.52 us
    slice x3, local copies, waits for them, and re-layouts, conv_taps(): weight[offset_a].reshape(9 * channels, outputs)  6.15 us
    ppermute x9, waiting for transfers between devices, padded_2(): lax.ppermute(lax.slice_in_dim(block, block.shape[dim] - width, None, axis...  5.35 us
    ppermute x9, waiting for transfers between devices, padded_2(): lax.ppermute(lax.slice_in_dim(block, 0, width, axis=dim), axis, backward)  5.31 us
    concatenate x8, other arithmetic, padded_2(): block = jnp.concatenate([low, block, high], axis=dim)  3.95 us
  transfers between devices with their start and end apart: 18, of which 9 were waited for; matrix products, arithmetic and copies ran while one was open for 10% of the time, Pallas kernels for 0%

commit v1 on v0

v1 whole, which is shorter than its diff:
```python
import functools

import jax
import jax.numpy as jnp
from jax import lax
from jax.experimental import pallas as pl
from jax.experimental.pallas import tpu as pltpu
from jax.sharding import PartitionSpec as P

leak_slope = 0.01
f32 = jnp.float32
bf16 = jnp.bfloat16


def leaky_relu(values):
    return jnp.maximum(values, leak_slope * values)


def line_exchange(axis, to_low, to_high):
    count = lax.axis_size(axis)
    if count == 2:
        sent = jnp.where(lax.axis_index(axis) == 0, to_high, to_low)
        got = lax.ppermute(sent, axis, [(0, 1), (1, 0)])
        return got, got
    up = [(i, i + 1) for i in range(count - 1)]
    down = [(b, a) for a, b in up]
    return lax.ppermute(to_high, axis, up), lax.ppermute(to_low, axis, down)


def snake_pairs(groups, count, step):
    order = [
        group * count + (place if group % 2 == 0 else count - 1 - place)
        for group in range(groups)
        for place in range(count)
    ]
    total = len(order)
    return [(order[i], order[(i + step) % total]) for i in range(total)]


def wide_exchange(to_low, to_high):
    groups, count = lax.axis_size("groups"), lax.axis_size("wide")
    even = lax.axis_index("groups") % 2 == 0
    axes = ("groups", "wide")
    forward = lax.ppermute(
        jnp.where(even, to_high, to_low), axes, snake_pairs(groups, count, 1)
    )
    backward = lax.ppermute(
        jnp.where(even, to_low, to_high), axes, snake_pairs(groups, count, -1)
    )
    return forward, backward


def call(kernel, outs, scratch=()):
    return pl.pallas_call(
        kernel,
        out_shape=[jax.ShapeDtypeStruct(shape, bf16) for shape in outs],
        scratch_shapes=list(scratch),
    )


def edges(axis):
    place = lax.axis_index(axis)
    return place == 0, place == lax.axis_size(axis) - 1


def fill_frame(ext, own, rows_low, rows_high, planes_ahead, planes_behind, deep, tall):
    depth, height = own.shape[0], own.shape[1]
    ext[deep : deep + depth, tall : tall + height] = own[...]
    ext[deep : deep + depth, :tall] = rows_low
    ext[deep : deep + depth, tall + height :] = rows_high
    even = lax.axis_index("groups") % 2 == 0

    @pl.when(even)
    def _():
        ext[:deep] = planes_ahead
        ext[deep + depth :] = planes_behind

    @pl.when(jnp.logical_not(even))
    def _():
        ext[:deep] = planes_behind
        ext[deep + depth :] = planes_ahead

    first, last = edges("narrow")

    @pl.when(first)
    def _():
        ext[:, :tall] = jnp.zeros((ext.shape[0], tall) + ext.shape[2:], bf16)

    @pl.when(last)
    def _():
        ext[:, tall + height :] = jnp.zeros((ext.shape[0], tall) + ext.shape[2:], bf16)

    first, last = edges("wide")

    @pl.when(first)
    def _():
        ext[:deep] = jnp.zeros((deep,) + ext.shape[1:], bf16)

    @pl.when(last)
    def _():
        ext[deep + depth :] = jnp.zeros((deep,) + ext.shape[1:], bf16)


def write_columns(columns, plane, low, high, lanes):
    if columns.shape[0] == 1:
        at_low = lax.axis_index("pair") == 0
        columns[0, plane, :, lanes] = jnp.where(at_low, high, low)
    else:
        columns[0, plane, :, lanes] = low
        columns[1, plane, :, lanes] = high


def column_values(block, half):
    lanes = block.shape[-1]
    wide = block.astype(f32)
    if half:
        return wide[:, 0, : lanes // 2].astype(bf16), wide[:, -1, lanes // 2 :].astype(bf16)
    return wide[:, 0, :].astype(bf16), wide[:, -1, :].astype(bf16)


def shifted(values, column, step):
    columns = values.shape[1]
    spot = lax.broadcasted_iota(jnp.int32, values.shape, 1)
    if step > 0:
        return jnp.where(spot == 0, column[:, None, :], pltpu.roll(values, 1, 1))
    return jnp.where(
        spot == columns - 1, column[:, None, :], pltpu.roll(values, columns - 1, 1)
    )


def pair_columns(left, right, plane, lanes):
    first, last = edges("pair")
    low = left[plane, :, lanes].astype(f32)
    high = right[plane, :, lanes].astype(f32)
    return (
        jnp.where(first, jnp.zeros_like(low), low),
        jnp.where(last, jnp.zeros_like(high), high),
    )


def spread_pairs(taps, base, block, low, high):
    lanes = block.shape[-1] // 2
    wide = block.astype(f32)
    taps[:, :, base : base + lanes] = shifted(wide[:, :, lanes:], low, 1).astype(bf16)
    taps[:, :, base + lanes : base + 3 * lanes] = block
    taps[:, :, base + 3 * lanes : base + 4 * lanes] = shifted(
        wide[:, :, :lanes], high, -1
    ).astype(bf16)


def spread_weights(packed, tap, base, taken):
    rows, outs = taken[0].shape
    blank = jnp.zeros((rows, outs), bf16)
    for cell in range(4):
        at = base + cell * rows
        packed[tap, at : at + rows, :outs] = taken[cell] if cell < 3 else blank
        packed[tap, at : at + rows, outs:] = taken[cell - 1] if cell > 0 else blank


def conv_rows(taps, packed, depth, height):
    lanes = taps.shape[-1]
    summed = None
    for a in range(3):
        for b in range(3):
            rows = taps[a : a + depth, b : b + height].reshape(-1, lanes)
            part = jnp.dot(rows, packed[3 * a + b], preferred_element_type=f32)
            summed = part if summed is None else summed + part
    return summed


def frame_kernel(own, low, high, ahead, behind, ext, columns):
    fill_frame(ext, own, low[...], high[...], ahead[...], behind[...], 1, 1)
    for plane in range(ext.shape[0]):
        left, right = column_values(ext[plane], True)
        write_columns(columns, plane, left, right, slice(None))


def encode_kernel(ext, left, right, weight, bias, down, down_bias, encoded, coarse, taps, packed):
    lanes = ext.shape[-1]
    for plane in range(ext.shape[0]):
        low, high = pair_columns(left, right, plane, slice(None))
        spread_pairs(taps.at[plane], 0, ext[plane], low, high)
    for tap in range(9):
        spread_weights(packed, tap, 0, [weight[tap, c] for c in range(3)])
    deep, _, tall, _, columns, _ = encoded.shape
    summed = conv_rows(taps, packed, 2 * deep, 2 * tall)
    summed = leaky_relu(summed + jnp.tile(bias[...], (1, 2))).astype(bf16)
    encoded[...] = summed.reshape(encoded.shape)
    lifted = None
    for a in range(2):
        for b in range(2):
            part = jnp.dot(
                encoded[:, a, :, b].reshape(-1, lanes), down[2 * a + b], preferred_element_type=f32
            )
            lifted = part if lifted is None else lifted + part
    coarse[...] = leaky_relu(lifted + down_bias[...]).astype(bf16).reshape(coarse.shape)


def frame_two_kernel(
    coarse, encoded, low, high, ahead, behind, coarse_ext, encoded_ext, columns
):
    depth, height = coarse.shape[:2]
    flat = 2 * depth
    tail = low.shape[1:]
    split = 2 * coarse_ext.shape[1]

    def planes(ref):
        return (
            ref[:split].reshape((2,) + coarse_ext.shape[1:]),
            ref[split:].reshape((1,) + encoded_ext.shape[1:]),
        )

    def rows(ref):
        return (
            ref[:flat].reshape((depth, 2) + tail),
            ref[flat:].reshape((2 * depth, 1) + tail),
        )

    low_c, low_e = rows(low)
    high_c, high_e = rows(high)
    ahead_c, ahead_e = planes(ahead)
    behind_c, behind_e = planes(behind)
    fill_frame(coarse_ext, coarse, low_c, high_c, ahead_c, behind_c, 2, 2)
    fill_frame(encoded_ext, encoded, low_e, high_e, ahead_e, behind_e, 1, 1)
    for plane in range(coarse_ext.shape[0]):
        left, right = column_values(coarse_ext[plane], False)
        write_columns(columns, plane, left, right, slice(None))


def bottom_kernel(
    coarse_ext, left, right, weight, bias, up, up_bias, encoded_ext, raised, columns, taps
):
    lanes = coarse_ext.shape[-1]
    for plane in range(coarse_ext.shape[0]):
        low, high = pair_columns(left, right, plane, slice(None))
        block = coarse_ext[plane]
        wide = block.astype(f32)
        taps[plane, :, :, :lanes] = shifted(wide, low, 1).astype(bf16)
        taps[plane, :, :, lanes : 2 * lanes] = block
        taps[plane, :, :, 2 * lanes :] = shifted(wide, high, -1).astype(bf16)
    deep, _, tall, _, count, _ = raised.shape
    summed = conv_rows(taps, weight, deep, tall)
    bottom = leaky_relu(summed + bias[...]).astype(bf16)
    both = jnp.tile(up_bias[...], (1, 2))
    for a in range(2):
        for b in range(2):
            matrix = jnp.concatenate([up[2 * a + b, 0], up[2 * a + b, 1]], axis=-1)
            lifted = jnp.dot(bottom, matrix, preferred_element_type=f32) + both
            raised[:, a, :, b] = lifted.astype(bf16).reshape(deep, tall, count, lanes)
    blank_plane = jnp.zeros(raised.shape[1:], bf16)
    blank_row = jnp.zeros((deep, 2, 2, count, lanes), bf16)
    first, last = edges("narrow")

    @pl.when(first)
    def _():
        raised[:, :, 0] = blank_row

    @pl.when(last)
    def _():
        raised[:, :, tall - 1] = blank_row

    first, last = edges("wide")

    @pl.when(first)
    def _():
        raised[0] = blank_plane

    @pl.when(last)
    def _():
        raised[deep - 1] = blank_plane

    planes, height = encoded_ext.shape[:2]
    half = lanes // 2
    for plane in range(planes):
        z, a = (plane + 1) // 2, (plane + 1) % 2
        whole = raised[z, a].reshape(2 * tall, count, lanes)[1 : 1 + height]
        low, high = column_values(whole, True)
        write_columns(columns, plane, low, high, slice(0, half))
        low, high = column_values(encoded_ext[plane], True)
        write_columns(columns, plane, low, high, slice(half, lanes))


def decode_kernel(raised, encoded_ext, left, right, weight, bias, decoded, taps, packed):
    planes, height, columns, lanes = encoded_ext.shape
    half = lanes // 2
    for plane in range(planes):
        low, high = pair_columns(left, right, plane, slice(0, half))
        spread_pairs(taps.at[plane], 0, raised[plane + 1, 1 : 1 + height], low, high)
        low, high = pair_columns(left, right, plane, slice(half, lanes))
        spread_pairs(taps.at[plane], 2 * lanes, encoded_ext[plane], low, high)
    for tap in range(9):
        spread_weights(packed, tap, 0, [weight[tap, c, :half] for c in range(3)])
        spread_weights(packed, tap, 2 * lanes, [weight[tap, c, half:] for c in range(3)])
    depth, rows = decoded.shape[:2]
    summed = conv_rows(taps, packed, depth, rows)
    summed = leaky_relu(summed + jnp.tile(bias[...], (1, 2)))
    decoded[...] = summed.astype(bf16).reshape(decoded.shape)


def rows_of(block, low, high, tall):
    return line_exchange("narrow", block[:, :tall], block[:, block.shape[1] - tall :])


def frame_planes(block, low, high, deep):
    depth = block.shape[0]
    return tuple(
        jnp.concatenate([low[at], block[at], high[at]], axis=1)
        for at in (slice(0, deep), slice(depth - deep, depth))
    )


def pair_exchange(columns):
    return line_exchange("pair", columns[0], columns[-1])


def body(
    volume, w_encode, b_encode, w_down, b_down, w_bottom, b_bottom, w_up, b_up, w_decode, b_decode
):
    depth, height, width, skip = volume.shape
    deep_width = w_down.shape[4]
    half_depth, half_height, pairs = depth // 2, height // 2, width // 2
    lanes = 2 * skip
    sides = 1 if lax.axis_size("pair") == 2 else 2

    packed = volume.reshape(depth, height, pairs, lanes)
    low, high = line_exchange("narrow", packed[:, :1], packed[:, -1:])
    ahead, behind = wide_exchange(*frame_planes(packed, low, high, 1))
    framed, columns = call(
        frame_kernel,
        [(depth + 2, height + 2, pairs, lanes), (sides, depth + 2, height + 2, skip)],
    )(packed, low, high, ahead, behind)
    left, right = pair_exchange(columns)

    encoded, coarse = call(
        encode_kernel,
        [
            (half_depth, 2, half_height, 2, pairs, lanes),
            (half_depth, half_height, pairs, deep_width),
        ],
        [
            pltpu.VMEM((depth + 2, height + 2, pairs, 2 * lanes), bf16),
            pltpu.VMEM((9, 2 * lanes, lanes), bf16),
        ],
    )(
        framed,
        left,
        right,
        w_encode.reshape(9, 3, skip, skip),
        b_encode.reshape(1, skip),
        w_down.reshape(4, lanes, deep_width),
        b_down.reshape(1, deep_width),
    )
    encoded = encoded.reshape(depth, height, pairs, lanes)

    def rows(start_c, start_e):
        c = lax.slice_in_dim(coarse, start_c, start_c + 2, axis=1)
        e = lax.slice_in_dim(encoded, start_e, start_e + 1, axis=1)
        return jnp.concatenate(
            [c.reshape(-1, pairs, deep_width), e.reshape(-1, pairs, lanes)], axis=0
        )

    low, high = line_exchange(
        "narrow", rows(0, 0), rows(half_height - 2, height - 1)
    )
    split = 2 * half_depth

    def parts(got):
        return (
            got[:split].reshape(half_depth, 2, pairs, deep_width),
            got[split:].reshape(depth, 1, pairs, lanes),
        )

    (low_c, low_e), (high_c, high_e) = parts(low), parts(high)
    sent = [
        jnp.concatenate(
            [c.reshape(-1, pairs, deep_width), e.reshape(-1, pairs, lanes)], axis=0
        )
        for c, e in zip(
            frame_planes(coarse, low_c, high_c, 2), frame_planes(encoded, low_e, high_e, 1)
        )
    ]
    ahead, behind = wide_exchange(*sent)
    coarse_ext, encoded_ext, columns = call(
        frame_two_kernel,
        [
            (half_depth + 4, half_height + 4, pairs, deep_width),
            (depth + 2, height + 2, pairs, lanes),
            (sides, half_depth + 4, half_height + 4, deep_width),
        ],
    )(coarse, encoded, low, high, ahead, behind)
    left, right = pair_exchange(columns)

    raised, columns = call(
        bottom_kernel,
        [
            (half_depth + 2, 2, half_height + 2, 2, pairs, lanes),
            (sides, depth + 2, height + 2, lanes),
        ],
        [pltpu.VMEM((half_depth + 4, half_height + 4, pairs, 3 * deep_width), bf16)],
    )(
        coarse_ext,
        left,
        right,
        w_bottom.reshape(9, 3 * deep_width, deep_width),
        b_bottom.reshape(1, deep_width),
        w_up.reshape(4, 2, deep_width, skip),
        b_up.reshape(1, skip),
        encoded_ext,
    )
    left, right = pair_exchange(columns)

    (decoded,) = call(
        decode_kernel,
        [(depth, height, pairs, lanes)],
        [
            pltpu.VMEM((depth + 2, height + 2, pairs, 4 * lanes), bf16),
            pltpu.VMEM((9, 4 * lanes, lanes), bf16),
        ],
    )(
        raised.reshape(depth + 4, height + 4, pairs, lanes),
        encoded_ext,
        left,
        right,
        w_decode.reshape(9, 3, lanes, skip),
        b_decode.reshape(1, skip),
    )
    return decoded.reshape(depth, height, width, skip)


def solution(mesh):
    return jax.shard_map(
        body,
        mesh=mesh,
        in_specs=(
            P(("groups", "wide"), "narrow", "pair", None),
            P(),
            P(),
            P(),
            P(),
            P(),
            P(),
            P(),
            P(),
            P(),
            P(),
        ),
        out_specs=P(("groups", "wide"), "narrow", "pair", None),
        check_vma=False,
    )
```

time: 99.3 us -> 60.8 us (0.61); the launches traced: 97.7 us -> 60.3 us
  starting transfers between devices: 48.6 us -> 9.05 us
  Pallas kernels: 0 us -> 22.4 us
  matrix products: 13.7 us -> 0 us
  local copies, waits for them, and re-layouts: 18.3 us -> 9.9 us
  waiting for transfers between devices: 10.7 us -> 18.6 us
  other arithmetic: 5.5 us -> 0.16 us
    ppermute x18 -> x9, starting transfers between devices: 48.6 us -> 9.05 us  [the longest x5 4.75 us: line_exchange(): got = lax.ppermute(sent, axis, [(0, 1), (1, 0)])]
    pallas_call x0 -> x5, Pallas kernels: none -> 22.4 us  [the longest x1 7.05 us: body(): call(decode_kernel, [(depth, height, pairs, lanes)], [pltpu.VMEM((depth +...]
    dot_general x10 -> x0, matrix products: 13.7 us -> none  [the longest x8 11.1 us: conv_taps(): jnp.dot(window_rows.reshape(-1, 9 * channels), weight[offset_a].reshape(9...]
    ppermute x18 -> x9, waiting for transfers between devices: 10.7 us -> 18.6 us  [the longest x5 8.59 us: line_exchange(): got = lax.ppermute(sent, axis, [(0, 1), (1, 0)])]
    unnamed x59 -> x20, local copies, waits for them, and re-layouts: 8.52 us -> 3.16 us
    slice x6 -> x7, local copies, waits for them, and re-layouts: 7.11 us -> 2.65 us  [the longest x3 1.81 us: frame_planes(): block[at]]
    concatenate x8 -> x1, other arithmetic: 3.95 us -> 0.03 us  [frame_planes(): jnp.concatenate([low[at], block[at], high[at]], axis=1)]
    reshape x3, local copies, waits for them, and re-layouts: 0.94 us -> 3.01 us  [the longest x1 1.87 us: body(): return decoded.reshape(depth, height, width, skip)]
  transfers between devices with their start and end apart: 18 -> 9, of which waited for: 9 -> 9; matrix products, arithmetic and copies ran while one was open for 10% -> 2% of each run, Pallas kernels for 0% -> 0%
where the time goes in v1:
time: 60.8 us; the launch traced here: 60.3 us
  Pallas kernels  22.4 us (37%)
  waiting for transfers between devices  18.6 us (31%)
  local copies, waits for them, and re-layouts  9.9 us (16%)
  starting transfers between devices  9.05 us (15%)
    ppermute x5, waiting for transfers between devices, line_exchange(): got = lax.ppermute(sent, axis, [(0, 1), (1, 0)])  8.59 us
    pallas_call x1, Pallas kernels, body(): call(decode_kernel, [(depth, height, pairs, lanes)], [pltpu.VMEM((depth +...  7.05 us
    ppermute x2, waiting for transfers between devices, wide_exchange(): lax.ppermute(jnp.where(even, to_low, to_high), axes, snake_pairs(groups,...  6.79 us
    pallas_call x1, Pallas kernels, body(): call(bottom_kernel, [(half_depth + 2, 2, half_height + 2, 2, pairs, lanes...  6.2 us
    ppermute x5, starting transfers between devices, line_exchange(): got = lax.ppermute(sent, axis, [(0, 1), (1, 0)])  4.75 us
    pallas_call x1, Pallas kernels, body(): call(encode_kernel, [(half_depth, 2, half_height, 2, pairs, lanes), (half...  4.71 us
    ppermute x2, starting transfers between devices, wide_exchange(): lax.ppermute(jnp.where(even, to_low, to_high), axes, snake_pairs(groups,...  3.73 us
    ppermute x2, waiting for transfers between devices, wide_exchange(): lax.ppermute(jnp.where(even, to_high, to_low), axes, snake_pairs(groups,...  3.26 us
  transfers between devices with their start and end apart: 9, of which 9 were waited for; matrix products, arithmetic and copies ran while one was open for 2% of the time, Pallas kernels for 0%

profile of v1, /device:TPU:0, one launch (start us, length us, event | category | flops | bytes accessed | tf_op | source)
XLA Modules:
  0.0 60.3 jit_solution(4943985538054638215)
XLA Ops:
  0.0 1.1 %reshape.244.own = bf16[6,8,16,256]{3,2,1,0:T(8,128)(2,1)S(1)} reshape(bf16[6,8,32,128]{3,2,1,0:T(8,128)(2,1)} %param.11) | data formatting | bytes 786432 | tf_op jit(solution)/shard_map/reshape | solution.py:325
  1.1 0.0 copy-start
  1.2 3.0 %collective-permute-start = (bf16[6,1,16,256]{3,2,1,0:T(8,128)(2,1)S(1)}, bf16[6,1,16,256]{3,2,1,0:T(8,128)(2,1)S(1)}, u32[]{:S(2)}, u32[]{:S(2)}) collective-permute-start(bf16[6,1,16,256]{3,2,1,0:T(8,128)(2,1)S(1)} %slice_select_fusion), channel_id=1, source_target_pairs={{0,2},{2,0},{1,3},{3,1},{4,6},{6,4},{5,7},{7,5},{8,10},{10,8},{9,1... | collective-permute-start | bytes 147464 | tf_op jit(solution)/shard_map/ppermute | solution.py:23
  4.2 0.9 %fusion.1 = (bf16[1,8,32,128]{3,2,1,0:T(8,128)(2,1)S(1)}, bf16[1,8,32,128]{3,2,1,0:T(8,128)(2,1)S(1)}) fusion(bf16[6,8,32,128]{3,2,1,0:T(8,128)(2,1)} %param.11), kind=kLoop, calls=%fused_computation.20 | loop fusion | bytes 262144 | tf_op jit(solution)/shard_map/slice | solution.py:307
  5.2 1.1 %collective-permute-done.low.high = bf16[6,1,16,256]{3,2,1,0:T(8,128)(2,1)S(1)} collective-permute-done((bf16[6,1,16,256]{3,2,1,0:T(8,128)(2,1)S(1)}, bf16[6,1,16,256]{3,2,1,0:T(8,128)(2,1)S(1)}, u32[]{:S(2)}, u32[]{:S(2)}) %collective-permute-start) | collective-permute-done | bytes 49184 | tf_op jit(solution)/shard_map/ppermute | solution.py:23
  6.3 0.0 copy-start.2
  6.3 2.1 %collective-permute-start.2 = (bf16[1,10,16,256]{3,2,1,0:T(8,128)(2,1)S(1)}, bf16[1,10,16,256]{3,2,1,0:T(8,128)(2,1)S(1)}, u32[]{:S(2)}, u32[]{:S(2)}) collective-permute-start(bf16[1,10,16,256]{3,2,1,0:T(8,128)(2,1)S(1)} %get-tuple-element.31), channel_id=1, source_target_pairs={{0,16},{4,0},{8,4},{12,8},{28,12},{24,28},{20,24},{16,20},{1,17},{... | collective-permute-start | bytes 245768 | tf_op jit(solution)/shard_map/ppermute | solution.py:47
  8.4 0.1 collective-permute-start.1
  8.5 2.4 %collective-permute-done.2.behind = bf16[1,10,16,256]{3,2,1,0:T(8,128)(2,1)S(1)} collective-permute-done((bf16[1,10,16,256]{3,2,1,0:T(8,128)(2,1)S(1)}, bf16[1,10,16,256]{3,2,1,0:T(8,128)(2,1)S(1)}, u32[]{:S(2)}, u32[]{:S(2)}) %collective-permute-start.2) | collective-permute-done | bytes 81952 | tf_op jit(solution)/shard_map/ppermute | solution.py:47
  10.9 0.0 copy-start.8
  10.9 2.0 %collective-permute-done.1.ahead = bf16[1,10,16,256]{3,2,1,0:T(8,128)(2,1)S(1)} collective-permute-done((bf16[1,10,16,256]{3,2,1,0:T(8,128)(2,1)S(1)}, bf16[1,10,16,256]{3,2,1,0:T(8,128)(2,1)S(1)}, u32[]{:S(2)}, u32[]{:S(2)}) %collective-permute-start.1) | collective-permute-done | bytes 81952 | tf_op jit(solution)/shard_map/ppermute | solution.py:44
  12.8 0.0 copy-done
  12.8 0.0 copy-done.2
  12.9 0.0 copy-done.8
  12.9 0.0 copy-start.9
  12.9 0.6 %copy-done.9 = bf16[1,10,16,256]{3,2,1,0:T(8,128)(2,1)} copy-done((bf16[1,10,16,256]{3,2,1,0:T(8,128)(2,1)}, bf16[1,10,16,256]{3,2,1,0:T(8,128)(2,1)S(1)}, u32[]{:S(2)}) %copy-start.9) | copy-done | bytes 81944
  13.5 2.0 %shard_map.109 = (bf16[8,10,16,256]{3,2,1,0:T(8,128)(2,1)}, bf16[1,8,10,128]{3,2,1,0:T(8,128)(2,1)}) custom-call(bf16[6,8,16,256]{3,2,1,0:T(8,128)(2,1)} %copy-done, bf16[6,1,16,256]{3,2,1,0:T(8,128)(2,1)} %copy-done.2, bf16[6,1,16,256]{3,2,1,0:T(8,128)(2,1)} %copy-done.2, bf16[1,10,16,256]{3,2,1,0:T(8,128)(2,1)} %copy-done.9, bf16[1,10,16,256]{3,2,1,0:T(8,128)(2,1)} %copy-done.8), custom_call_target="tpu_custom_call" | custom-call | tf_op jit(solution)/shard_map/pallas_call | solution.py:328
  15.5 0.0 collective-permute-start.3
  15.5 1.4 %collective-permute-done.3.left.right = bf16[8,10,128]{2,1,0:T(8,128)(2,1)S(1)} collective-permute-done((bf16[8,10,128]{2,1,0:T(8,128)(2,1)}, bf16[8,10,128]{2,1,0:T(8,128)(2,1)S(1)}, u32[]{:S(2)}, u32[]{:S(2)}) %collective-permute-start.3) | collective-permute-done | bytes 20512 | tf_op jit(solution)/shard_map/ppermute | solution.py:23
  16.9 0.0 copy-start.6
  16.9 0.6 copy-done.6
  17.5 4.7 %shard_map.110 = (bf16[3,2,4,2,16,256]{5,4,3,2,1,0:T(8,128)(2,1)}, bf16[3,4,16,256]{3,2,1,0:T(8,128)(2,1)}) custom-call(bf16[8,10,16,256]{3,2,1,0:T(8,128)(2,1)} %get-tuple-element.14.ext, bf16[8,10,128]{2,1,0:T(8,128)(2,1)} %copy-done.6, bf16[8,10,128]{2,1,0:T(8,128)(2,1)} %copy-done.6, bf16[9,3,128,128]{3,2,1,0:T(8,128)(2,1)} %bitcast.52, ...), custom_call_target="tpu_custom_call" | custom-call | tf_op jit(solution)/shard_map/pallas_call | solution.py:334
  22.3 0.8 %fusion.4 = (bf16[3,2,16,256]{3,2,1,0:T(8,128)(2,1)S(1)}, bf16[3,2,16,256]{3,2,1,0:T(8,128)(2,1)S(1)}) fusion(bf16[3,4,16,256]{3,2,1,0:T(8,128)(2,1)} %get-tuple-element.16.coarse), kind=kLoop, calls=%fused_computation.23 | loop fusion | bytes 196608 | tf_op jit(solution)/shard_map/slice | solution.py:356
  23.1 0.9 %fusion.2 = (bf16[2,4,16,256]{3,2,1,0:T(8,128)(2,1)S(1)}, bf16[2,4,16,256]{3,2,1,0:T(8,128)(2,1)S(1)}) fusion(bf16[3,4,16,256]{3,2,1,0:T(8,128)(2,1)} %get-tuple-element.16.coarse), kind=kLoop, calls=%fused_computation.21 | loop fusion | bytes 262144 | tf_op jit(solution)/shard_map/slice | solution.py:307
  24.0 1.0 %copy.12 = bf16[3,2,4,2,16,256]{5,4,1,0,3,2:T(8,128)(2,1)S(1)} copy(bf16[3,2,4,2,16,256]{5,4,3,2,1,0:T(8,128)(2,1)} %get-tuple-element.17) | data formatting | bytes 786432 | tf_op jit(solution)/shard_map/pallas_call | solution.py:334
  25.1 1.6 %collective-permute-start.4 = (bf16[12,16,256]{2,1,0:T(8,128)(2,1)S(1)}, bf16[12,16,256]{2,1,0:T(8,128)(2,1)S(1)}, u32[]{:S(2)}, u32[]{:S(2)}) collective-permute-start(bf16[12,16,256]{2,1,0:T(8,128)(2,1)S(1)} %maximum_select_fusion), channel_id=1, source_target_pairs={{0,2},{2,0},{1,3},{3,1},{4,6},{6,4},{5,7},{7,5},{8,10},{10,8},{9,1... | collective-permute-start | bytes 294920 | tf_op jit(solution)/shard_map/ppermute | solution.py:23
  26.7 3.4 %collective-permute-done.4.low.high = bf16[12,16,256]{2,1,0:T(8,128)(2,1)S(1)} collective-permute-done((bf16[12,16,256]{2,1,0:T(8,128)(2,1)S(1)}, bf16[12,16,256]{2,1,0:T(8,128)(2,1)S(1)}, u32[]{:S(2)}, u32[]{:S(2)}) %collective-permute-start.4) | collective-permute-done | bytes 98336 | tf_op jit(solution)/shard_map/ppermute | solution.py:23
  30.0 0.0 copy-start.1
  30.2 1.6 %collective-permute-start.6 = (bf16[26,16,256]{2,1,0:T(8,128)(2,1)S(1)}, bf16[26,16,256]{2,1,0:T(8,128)(2,1)S(1)}, u32[]{:S(2)}, u32[]{:S(2)}) collective-permute-start(bf16[26,16,256]{2,1,0:T(8,128)(2,1)S(1)} %get-tuple-element.23), channel_id=1, source_target_pairs={{0,16},{4,0},{8,4},{12,8},{28,12},{24,28},{20,24},{16,20},{1,17},{... | collective-permute-start | bytes 638984 | tf_op jit(solution)/shard_map/ppermute | solution.py:47
  31.8 0.5 collective-permute-start.5
  32.2 4.4 %collective-permute-done.6.behind = bf16[26,16,256]{2,1,0:T(8,128)(2,1)S(1)} collective-permute-done((bf16[26,16,256]{2,1,0:T(8,128)(2,1)S(1)}, bf16[26,16,256]{2,1,0:T(8,128)(2,1)S(1)}, u32[]{:S(2)}, u32[]{:S(2)}) %collective-permute-start.6) | collective-permute-done | bytes 213024 | tf_op jit(solution)/shard_map/ppermute | solution.py:47
  36.7 0.0 copy-start.4
  36.7 1.3 %collective-permute-done.5.ahead = bf16[26,16,256]{2,1,0:T(8,128)(2,1)S(1)} collective-permute-done((bf16[26,16,256]{2,1,0:T(8,128)(2,1)S(1)}, bf16[26,16,256]{2,1,0:T(8,128)(2,1)S(1)}, u32[]{:S(2)}, u32[]{:S(2)}) %collective-permute-start.5) | collective-permute-done | bytes 213024 | tf_op jit(solution)/shard_map/ppermute | solution.py:44
  38.0 0.0 copy-start.5
  38.0 0.0 copy-done.1
  38.0 0.0 copy-done.4
  38.0 0.7 %copy-done.5 = bf16[26,16,256]{2,1,0:T(8,128)(2,1)} copy-done((bf16[26,16,256]{2,1,0:T(8,128)(2,1)}, bf16[26,16,256]{2,1,0:T(8,128)(2,1)S(1)}, u32[]{:S(2)}) %copy-start.5) | copy-done | bytes 213016
  38.7 2.4 %shard_map.111 = (bf16[7,8,16,256]{3,2,1,0:T(8,128)(2,1)}, bf16[8,10,16,256]{3,2,1,0:T(8,128)(2,1)}, bf16[1,7,8,256]{3,2,1,0:T(8,128)(2,1)}) custom-call(bf16[3,4,16,256]{3,2,1,0:T(8,128)(2,1)} %get-tuple-element.16.coarse, bf16[6,8,16,256]{3,2,1,0:T(8,128)(2,1)} %bitcast.48, bf16[12,16,256]{2,1,0:T(8,128)(2,1)} %copy-done.1, ...), custom_call_target="tpu_custom_call" | custom-call | tf_op jit(solution)/shard_map/pallas_call | solution.py:383
  41.1 0.0 collective-permute-start.7
  41.1 1.4 %collective-permute-done.7.left.right = bf16[7,8,256]{2,1,0:T(8,128)(2,1)S(1)} collective-permute-done((bf16[7,8,256]{2,1,0:T(8,128)(2,1)}, bf16[7,8,256]{2,1,0:T(8,128)(2,1)S(1)}, u32[]{:S(2)}, u32[]{:S(2)}) %collective-permute-start.7) | collective-permute-done | bytes 28704 | tf_op jit(solution)/shard_map/ppermute | solution.py:23
  42.5 0.0 copy-start.7
  42.5 0.6 copy-done.7
  43.1 6.2 %shard_map.112 = (bf16[5,2,6,2,16,256]{5,4,3,2,1,0:T(8,128)(2,1)}, bf16[1,8,10,256]{3,2,1,0:T(8,128)(2,1)}) custom-call(bf16[7,8,16,256]{3,2,1,0:T(8,128)(2,1)} %get-tuple-element.18.coarse_ext, bf16[7,8,256]{2,1,0:T(8,128)(2,1)} %copy-done.7, bf16[7,8,256]{2,1,0:T(8,128)(2,1)} %copy-done.7, bf16[9,768,256]{2,1,0:T(8,128)(2,1)} %bitcast.46, ...), custom_call_target="tpu_custom_call" | custom-call | tf_op jit(solution)/shard_map/pallas_call | solution.py:393
  49.3 0.2 collective-permute-start.8
  49.5 1.3 %collective-permute-done.8.left.right = bf16[8,10,256]{2,1,0:T(8,128)(2,1)S(1)} collective-permute-done((bf16[8,10,256]{2,1,0:T(8,128)(2,1)}, bf16[8,10,256]{2,1,0:T(8,128)(2,1)S(1)}, u32[]{:S(2)}, u32[]{:S(2)}) %collective-permute-start.8) | collective-permute-done | bytes 40992 | tf_op jit(solution)/shard_map/ppermute | solution.py:23
  50.8 0.6 %copy-done.3 = bf16[8,10,256]{2,1,0:T(8,128)(2,1)} copy-done((bf16[8,10,256]{2,1,0:T(8,128)(2,1)}, bf16[8,10,256]{2,1,0:T(8,128)(2,1)S(1)}, u32[]{:S(2)}) %copy-start.3) | copy-done | bytes 40984
  51.4 7.0 %shard_map.113 = bf16[6,8,16,256]{3,2,1,0:T(8,128)(2,1)} custom-call(bf16[10,12,16,256]{3,2,1,0:T(8,128)(2,1)} %bitcast.51, bf16[8,10,16,256]{3,2,1,0:T(8,128)(2,1)} %get-tuple-element.20.encoded_ext, bf16[8,10,256]{2,1,0:T(8,128)(2,1)} %copy-done.3, bf16[8,10,256]{2,1,0:T(8,128)(2,1)} %copy-done.3, bf16[9,3,256,128]{3,2,1,0:T(8,128)(2,1)} %bitcast.47, ...), custom_call_target="tpu_custom_call" | custom-call | tf_op jit(solution)/shard_map/pallas_call | solution.py:412
  58.4 1.9 %reshape.265 = bf16[6,8,32,128]{3,2,1,0:T(8,128)(2,1)} reshape(bf16[6,8,16,256]{3,2,1,0:T(8,128)(2,1)} %shard_map.113) | data formatting | bytes 786432 | tf_op jit(solution)/shard_map/reshape | solution.py:427
  (15 shorter events, 0.2 us)
Async XLA Ops:
  1.1 11.7 %copy-start = (bf16[6,8,16,256]{3,2,1,0:T(8,128)(2,1)}, bf16[6,8,16,256]{3,2,1,0:T(8,128)(2,1)S(1)}, u32[]{:S(2)}) copy-start(bf16[6,8,16,256]{3,2,1,0:T(8,128)(2,1)S(1)} %reshape.244.own) | copy-start | bytes 1179652
  1.2 5.1 %collective-permute-start = (bf16[6,1,16,256]{3,2,1,0:T(8,128)(2,1)S(1)}, bf16[6,1,16,256]{3,2,1,0:T(8,128)(2,1)S(1)}, u32[]{:S(2)}, u32[]{:S(2)}) collective-permute-start(bf16[6,1,16,256]{3,2,1,0:T(8,128)(2,1)S(1)} %slice_select_fusion), channel_id=1, source_target_pairs={{0,2},{2,0},{1,3},{3,1},{4,6},{6,4},{5,7},{7,5},{8,10},{10,8},{9,1... | collective-permute-start | bytes 147464 | tf_op jit(solution)/shard_map/ppermute | solution.py:23
  6.3 6.6 %copy-start.2 = (bf16[6,1,16,256]{3,2,1,0:T(8,128)(2,1)}, bf16[6,1,16,256]{3,2,1,0:T(8,128)(2,1)S(1)}, u32[]{:S(2)}) copy-start(bf16[6,1,16,256]{3,2,1,0:T(8,128)(2,1)S(1)} %collective-permute-done.low.high) | copy-start | bytes 147460
  6.3 4.6 %collective-permute-start.2 = (bf16[1,10,16,256]{3,2,1,0:T(8,128)(2,1)S(1)}, bf16[1,10,16,256]{3,2,1,0:T(8,128)(2,1)S(1)}, u32[]{:S(2)}, u32[]{:S(2)}) collective-permute-start(bf16[1,10,16,256]{3,2,1,0:T(8,128)(2,1)S(1)} %get-tuple-element.31), channel_id=1, source_target_pairs={{0,16},{4,0},{8,4},{12,8},{28,12},{24,28},{20,24},{16,20},{1,17},{... | collective-permute-start | bytes 245768 | tf_op jit(solution)/shard_map/ppermute | solution.py:47
  8.4 4.4 %collective-permute-start.1 = (bf16[1,10,16,256]{3,2,1,0:T(8,128)(2,1)S(1)}, bf16[1,10,16,256]{3,2,1,0:T(8,128)(2,1)S(1)}, u32[]{:S(2)}, u32[]{:S(2)}) collective-permute-start(bf16[1,10,16,256]{3,2,1,0:T(8,128)(2,1)S(1)} %get-tuple-element.32), channel_id=1, source_target_pairs={{0,4},{4,8},{8,12},{12,28},{28,24},{24,20},{20,16},{16,0},{1,5},{5... | collective-permute-start | bytes 245768 | tf_op jit(solution)/shard_map/ppermute | solution.py:44
  10.9 2.0 %copy-start.8 = (bf16[1,10,16,256]{3,2,1,0:T(8,128)(2,1)}, bf16[1,10,16,256]{3,2,1,0:T(8,128)(2,1)S(1)}, u32[]{:S(2)}) copy-start(bf16[1,10,16,256]{3,2,1,0:T(8,128)(2,1)S(1)} %collective-permute-done.2.behind) | copy-start | bytes 245764
  12.9 0.6 %copy-start.9 = (bf16[1,10,16,256]{3,2,1,0:T(8,128)(2,1)}, bf16[1,10,16,256]{3,2,1,0:T(8,128)(2,1)S(1)}, u32[]{:S(2)}) copy-start(bf16[1,10,16,256]{3,2,1,0:T(8,128)(2,1)S(1)} %collective-permute-done.1.ahead) | copy-start | bytes 245764
  15.5 1.4 %collective-permute-start.3 = (bf16[8,10,128]{2,1,0:T(8,128)(2,1)}, bf16[8,10,128]{2,1,0:T(8,128)(2,1)S(1)}, u32[]{:S(2)}, u32[]{:S(2)}) collective-permute-start(bf16[8,10,128]{2,1,0:T(8,128)(2,1)} %bitcast.67), channel_id=1, source_target_pairs={{0,1},{1,0},{2,3},{3,2},{4,5},{5,4},{6,7},{7,6},{8,9},{9,8},{10,11... | collective-permute-start | bytes 61448 | tf_op jit(solution)/shard_map/ppermute | solution.py:23
  16.9 0.6 copy-start.6
  25.1 4.9 %collective-permute-start.4 = (bf16[12,16,256]{2,1,0:T(8,128)(2,1)S(1)}, bf16[12,16,256]{2,1,0:T(8,128)(2,1)S(1)}, u32[]{:S(2)}, u32[]{:S(2)}) collective-permute-start(bf16[12,16,256]{2,1,0:T(8,128)(2,1)S(1)} %maximum_select_fusion), channel_id=1, source_target_pairs={{0,2},{2,0},{1,3},{3,1},{4,6},{6,4},{5,7},{7,5},{8,10},{10,8},{9,1... | collective-permute-start | bytes 294920 | tf_op jit(solution)/shard_map/ppermute | solution.py:23
  30.0 8.0 %copy-start.1 = (bf16[12,16,256]{2,1,0:T(8,128)(2,1)}, bf16[12,16,256]{2,1,0:T(8,128)(2,1)S(1)}, u32[]{:S(2)}) copy-start(bf16[12,16,256]{2,1,0:T(8,128)(2,1)S(1)} %collective-permute-done.4.low.high) | copy-start | bytes 294916
  30.2 6.5 %collective-permute-start.6 = (bf16[26,16,256]{2,1,0:T(8,128)(2,1)S(1)}, bf16[26,16,256]{2,1,0:T(8,128)(2,1)S(1)}, u32[]{:S(2)}, u32[]{:S(2)}) collective-permute-start(bf16[26,16,256]{2,1,0:T(8,128)(2,1)S(1)} %get-tuple-element.23), channel_id=1, source_target_pairs={{0,16},{4,0},{8,4},{12,8},{28,12},{24,28},{20,24},{16,20},{1,17},{... | collective-permute-start | bytes 638984 | tf_op jit(solution)/shard_map/ppermute | solution.py:47
  31.8 6.2 %collective-permute-start.5 = (bf16[26,16,256]{2,1,0:T(8,128)(2,1)S(1)}, bf16[26,16,256]{2,1,0:T(8,128)(2,1)S(1)}, u32[]{:S(2)}, u32[]{:S(2)}) collective-permute-start(bf16[26,16,256]{2,1,0:T(8,128)(2,1)S(1)} %get-tuple-element.24), channel_id=1, source_target_pairs={{0,4},{4,8},{8,12},{12,28},{28,24},{24,20},{20,16},{16,0},{1,5},{5... | collective-permute-start | bytes 638984 | tf_op jit(solution)/shard_map/ppermute | solution.py:44
  36.7 1.3 %copy-start.4 = (bf16[26,16,256]{2,1,0:T(8,128)(2,1)}, bf16[26,16,256]{2,1,0:T(8,128)(2,1)S(1)}, u32[]{:S(2)}) copy-start(bf16[26,16,256]{2,1,0:T(8,128)(2,1)S(1)} %collective-permute-done.6.behind) | copy-start | bytes 638980
  38.0 0.7 %copy-start.5 = (bf16[26,16,256]{2,1,0:T(8,128)(2,1)}, bf16[26,16,256]{2,1,0:T(8,128)(2,1)S(1)}, u32[]{:S(2)}) copy-start(bf16[26,16,256]{2,1,0:T(8,128)(2,1)S(1)} %collective-permute-done.5.ahead) | copy-start | bytes 638980
  41.1 1.4 %collective-permute-start.7 = (bf16[7,8,256]{2,1,0:T(8,128)(2,1)}, bf16[7,8,256]{2,1,0:T(8,128)(2,1)S(1)}, u32[]{:S(2)}, u32[]{:S(2)}) collective-permute-start(bf16[7,8,256]{2,1,0:T(8,128)(2,1)} %bitcast.68), channel_id=1, source_target_pairs={{0,1},{1,0},{2,3},{3,2},{4,5},{5,4},{6,7},{7,6},{8,9},{9,8},{10,11... | collective-permute-start | bytes 86024 | tf_op jit(solution)/shard_map/ppermute | solution.py:23
  42.5 0.6 copy-start.7
  49.3 1.5 %collective-permute-start.8 = (bf16[8,10,256]{2,1,0:T(8,128)(2,1)}, bf16[8,10,256]{2,1,0:T(8,128)(2,1)S(1)}, u32[]{:S(2)}, u32[]{:S(2)}) collective-permute-start(bf16[8,10,256]{2,1,0:T(8,128)(2,1)} %bitcast.66), channel_id=1, source_target_pairs={{0,1},{1,0},{2,3},{3,2},{4,5},{5,4},{6,7},{7,6},{8,9},{9,8},{10,11... | collective-permute-start | bytes 122888 | tf_op jit(solution)/shard_map/ppermute | solution.py:23
  50.8 0.6 %copy-start.3 = (bf16[8,10,256]{2,1,0:T(8,128)(2,1)}, bf16[8,10,256]{2,1,0:T(8,128)(2,1)S(1)}, u32[]{:S(2)}) copy-start(bf16[8,10,256]{2,1,0:T(8,128)(2,1)S(1)} %collective-permute-done.8.left.right) | copy-start | bytes 122884

commit v2 on v1

--- a/solution.py
+++ b/solution.py
@@ -16,15 +16,18 @@
     return jnp.maximum(values, leak_slope * values)
 
 
-def line_exchange(axis, to_low, to_high):
+def sides_of(axis):
+    return 1 if lax.axis_size(axis) == 2 else 2
+
+
+def line_exchange(axis, sent):
     count = lax.axis_size(axis)
     if count == 2:
-        sent = jnp.where(lax.axis_index(axis) == 0, to_high, to_low)
-        got = lax.ppermute(sent, axis, [(0, 1), (1, 0)])
+        got = lax.ppermute(sent[0], axis, [(0, 1), (1, 0)])
         return got, got
     up = [(i, i + 1) for i in range(count - 1)]
     down = [(b, a) for a, b in up]
-    return lax.ppermute(to_high, axis, up), lax.ppermute(to_low, axis, down)
+    return lax.ppermute(sent[1], axis, up), lax.ppermute(sent[0], axis, down)
 
 
 def snake_pairs(groups, count, step):
@@ -37,24 +40,21 @@
     return [(order[i], order[(i + step) % total]) for i in range(total)]
 
 
-def wide_exchange(to_low, to_high):
+def wide_exchange(ahead, behind):
     groups, count = lax.axis_size("groups"), lax.axis_size("wide")
-    even = lax.axis_index("groups") % 2 == 0
     axes = ("groups", "wide")
-    forward = lax.ppermute(
-        jnp.where(even, to_high, to_low), axes, snake_pairs(groups, count, 1)
-    )
-    backward = lax.ppermute(
-        jnp.where(even, to_low, to_high), axes, snake_pairs(groups, count, -1)
-    )
-    return forward, backward
-
-
-def call(kernel, outs, scratch=()):
+    return (
+        lax.ppermute(ahead, axes, snake_pairs(groups, count, 1)),
+        lax.ppermute(behind, axes, snake_pairs(groups, count, -1)),
+    )
+
+
+def call(kernel, outs, scratch=(), megabytes=24):
     return pl.pallas_call(
         kernel,
         out_shape=[jax.ShapeDtypeStruct(shape, bf16) for shape in outs],
         scratch_shapes=list(scratch),
+        compiler_params=pltpu.CompilerParams(vmem_limit_bytes=megabytes << 20),
     )
 
 
@@ -168,32 +168,131 @@
     return summed
 
 
+def choose_side(axis, sent, put):
+    if sent.shape[0] == 1:
+        at_low = lax.axis_index(axis) == 0
+
+        @pl.when(at_low)
+        def _():
+            put(0, True)
+
+        @pl.when(jnp.logical_not(at_low))
+        def _():
+            put(0, False)
+
+    else:
+        put(0, False)
+        put(1, True)
+
+
+def pack_pairs(out, cells, spread):
+    pairs, lanes = out.shape[1], cells.shape[-1]
+    spread[...] = cells.astype(f32)
+    for odd in range(2):
+        half = spread[:, pl.ds(odd, pairs, stride=2), :]
+        out[:, :, odd * lanes : (odd + 1) * lanes] = half.astype(bf16)
+
+
+def edge_row_kernel(volume, edge_rows, spread):
+    height = volume.shape[1]
+
+    def put(slot, high):
+        pack_pairs(edge_rows.at[slot], volume[:, height - 1 if high else 0], spread)
+
+    choose_side("narrow", edge_rows, put)
+
+
+def pack_kernel(volume, packed, spread):
+    for plane in range(volume.shape[0]):
+        pack_pairs(packed.at[plane], volume[plane], spread.at[plane])
+
+
+def put_planes(ahead, behind, put):
+    even = lax.axis_index("groups") % 2 == 0
+
+    @pl.when(even)
+    def _():
+        put(ahead, True)
+        put(behind, False)
+
+    @pl.when(jnp.logical_not(even))
+    def _():
+        put(ahead, False)
+        put(behind, True)
+
+
+def edge_plane_kernel(own, low, high, ahead, behind):
+    depth, height = own.shape[:2]
+
+    def put(ref, top):
+        plane = depth - 1 if top else 0
+        ref[0, :1] = low[plane][None]
+        ref[0, 1 : 1 + height] = own[plane]
+        ref[0, 1 + height :] = high[plane][None]
+
+    put_planes(ahead, behind, put)
+
+
+def edge_plane_two_kernel(coarse, encoded, low, high, ahead, behind):
+    deep, tall = coarse.shape[:2]
+    depth, height = encoded.shape[:2]
+    step = tall + 4
+    split = 2 * step
+
+    def put(ref, top):
+        for layer in range(2):
+            plane = deep - 2 + layer if top else layer
+            at = layer * step
+            ref[at : at + 2] = low[2 * plane : 2 * plane + 2]
+            ref[at + 2 : at + 2 + tall] = coarse[plane]
+            ref[at + 2 + tall : at + step] = high[2 * plane : 2 * plane + 2]
+        plane = depth - 1 if top else 0
+        ref[split] = low[2 * deep + plane]
+        ref[split + 1 : split + 1 + height] = encoded[plane]
+        ref[split + 1 + height] = high[2 * deep + plane]
+
+    put_planes(ahead, behind, put)
+
+
 def frame_kernel(own, low, high, ahead, behind, ext, columns):
-    fill_frame(ext, own, low[...], high[...], ahead[...], behind[...], 1, 1)
+    fill_frame(ext, own, low[...][:, None], high[...][:, None], ahead[...], behind[...], 1, 1)
     for plane in range(ext.shape[0]):
         left, right = column_values(ext[plane], True)
         write_columns(columns, plane, left, right, slice(None))
 
 
-def encode_kernel(ext, left, right, weight, bias, down, down_bias, encoded, coarse, taps, packed):
+def encode_kernel(
+    ext, left, right, weight, bias, down, down_bias, encoded, coarse, edge_rows, taps, packed
+):
     lanes = ext.shape[-1]
     for plane in range(ext.shape[0]):
         low, high = pair_columns(left, right, plane, slice(None))
         spread_pairs(taps.at[plane], 0, ext[plane], low, high)
     for tap in range(9):
         spread_weights(packed, tap, 0, [weight[tap, c] for c in range(3)])
-    deep, _, tall, _, columns, _ = encoded.shape
-    summed = conv_rows(taps, packed, 2 * deep, 2 * tall)
-    summed = leaky_relu(summed + jnp.tile(bias[...], (1, 2))).astype(bf16)
-    encoded[...] = summed.reshape(encoded.shape)
+    depth, height, columns, _ = encoded.shape
+    deep, tall, _, deep_lanes = coarse.shape
+    summed = conv_rows(taps, packed, depth, height)
+    fine = leaky_relu(summed + jnp.tile(bias[...], (1, 2))).astype(bf16)
+    fine = fine.reshape(deep, 2, tall, 2, columns, lanes)
+    encoded[...] = fine.reshape(encoded.shape)
     lifted = None
     for a in range(2):
         for b in range(2):
             part = jnp.dot(
-                encoded[:, a, :, b].reshape(-1, lanes), down[2 * a + b], preferred_element_type=f32
+                fine[:, a, :, b].reshape(-1, lanes), down[2 * a + b], preferred_element_type=f32
             )
             lifted = part if lifted is None else lifted + part
     coarse[...] = leaky_relu(lifted + down_bias[...]).astype(bf16).reshape(coarse.shape)
+
+    def put(slot, high):
+        first = tall - 2 if high else 0
+        edge_rows[slot, : 2 * deep] = coarse[:, first : first + 2].reshape(
+            2 * deep, columns, deep_lanes
+        )
+        edge_rows[slot, 2 * deep :] = encoded[:, height - 1 if high else 0]
+
+    choose_side("narrow", edge_rows, put)
 
 
 def frame_two_kernel(
@@ -280,7 +379,9 @@
         write_columns(columns, plane, low, high, slice(half, lanes))
 
 
-def decode_kernel(raised, encoded_ext, left, right, weight, bias, decoded, taps, packed):
+def decode_kernel(
+    raised, encoded_ext, left, right, weight, bias, decoded, taps, packed, spread
+):
     planes, height, columns, lanes = encoded_ext.shape
     half = lanes // 2
     for plane in range(planes):
@@ -291,26 +392,13 @@
     for tap in range(9):
         spread_weights(packed, tap, 0, [weight[tap, c, :half] for c in range(3)])
         spread_weights(packed, tap, 2 * lanes, [weight[tap, c, half:] for c in range(3)])
-    depth, rows = decoded.shape[:2]
+    depth, rows, _, outs = decoded.shape
     summed = conv_rows(taps, packed, depth, rows)
     summed = leaky_relu(summed + jnp.tile(bias[...], (1, 2)))
-    decoded[...] = summed.astype(bf16).reshape(decoded.shape)
-
-
-def rows_of(block, low, high, tall):
-    return line_exchange("narrow", block[:, :tall], block[:, block.shape[1] - tall :])
-
-
-def frame_planes(block, low, high, deep):
-    depth = block.shape[0]
-    return tuple(
-        jnp.concatenate([low[at], block[at], high[at]], axis=1)
-        for at in (slice(0, deep), slice(depth - deep, depth))
-    )
-
-
-def pair_exchange(columns):
-    return line_exchange("pair", columns[0], columns[-1])
+    for odd in range(2):
+        half = summed[:, odd * outs : (odd + 1) * outs].reshape(depth, rows, columns, outs)
+        spread[:, :, pl.ds(odd, columns, stride=2), :] = half
+    decoded[...] = spread[...].astype(bf16)
 
 
 def body(
@@ -320,22 +408,37 @@
     deep_width = w_down.shape[4]
     half_depth, half_height, pairs = depth // 2, height // 2, width // 2
     lanes = 2 * skip
-    sides = 1 if lax.axis_size("pair") == 2 else 2
-
-    packed = volume.reshape(depth, height, pairs, lanes)
-    low, high = line_exchange("narrow", packed[:, :1], packed[:, -1:])
-    ahead, behind = wide_exchange(*frame_planes(packed, low, high, 1))
+    sides, row_sides = sides_of("pair"), sides_of("narrow")
+
+    (edge_rows,) = call(
+        edge_row_kernel,
+        [(row_sides, depth, pairs, lanes)],
+        [pltpu.VMEM((depth, width, skip), f32)],
+        8,
+    )(volume)
+    low, high = line_exchange("narrow", edge_rows)
+    (packed,) = call(
+        pack_kernel,
+        [(depth, height, pairs, lanes)],
+        [pltpu.VMEM((depth, height, width, skip), f32)],
+        8,
+    )(volume)
+    ahead, behind = call(edge_plane_kernel, [(1, height + 2, pairs, lanes)] * 2, (), 8)(
+        packed, low, high
+    )
+    ahead, behind = wide_exchange(ahead, behind)
     framed, columns = call(
         frame_kernel,
         [(depth + 2, height + 2, pairs, lanes), (sides, depth + 2, height + 2, skip)],
     )(packed, low, high, ahead, behind)
-    left, right = pair_exchange(columns)
-
-    encoded, coarse = call(
+    left, right = line_exchange("pair", columns)
+
+    encoded, coarse, edge_rows = call(
         encode_kernel,
         [
-            (half_depth, 2, half_height, 2, pairs, lanes),
+            (depth, height, pairs, lanes),
             (half_depth, half_height, pairs, deep_width),
+            (row_sides, 2 * half_depth + depth, pairs, lanes),
         ],
         [
             pltpu.VMEM((depth + 2, height + 2, pairs, 2 * lanes), bf16),
@@ -350,36 +453,10 @@
         w_down.reshape(4, lanes, deep_width),
         b_down.reshape(1, deep_width),
     )
-    encoded = encoded.reshape(depth, height, pairs, lanes)
-
-    def rows(start_c, start_e):
-        c = lax.slice_in_dim(coarse, start_c, start_c + 2, axis=1)
-        e = lax.slice_in_dim(encoded, start_e, start_e + 1, axis=1)
-        return jnp.concatenate(
-            [c.reshape(-1, pairs, deep_width), e.reshape(-1, pairs, lanes)], axis=0
-        )
-
-    low, high = line_exchange(
-        "narrow", rows(0, 0), rows(half_height - 2, height - 1)
-    )
-    split = 2 * half_depth
-
-    def parts(got):
-        return (
-            got[:split].reshape(half_depth, 2, pairs, deep_width),
-            got[split:].reshape(depth, 1, pairs, lanes),
-        )
-
-    (low_c, low_e), (high_c, high_e) = parts(low), parts(high)
-    sent = [
-        jnp.concatenate(
-            [c.reshape(-1, pairs, deep_width), e.reshape(-1, pairs, lanes)], axis=0
-        )
-        for c, e in zip(
-            frame_planes(coarse, low_c, high_c, 2), frame_planes(encoded, low_e, high_e, 1)
-        )
-    ]
-    ahead, behind = wide_exchange(*sent)
+    low, high = line_exchange("narrow", edge_rows)
+    message = (2 * (half_height + 4) + height + 2, pairs, lanes)
+    ahead, behind = call(edge_plane_two_kernel, [message] * 2, (), 8)(coarse, encoded, low, high)
+    ahead, behind = wide_exchange(ahead, behind)
     coarse_ext, encoded_ext, columns = call(
         frame_two_kernel,
         [
@@ -388,7 +465,7 @@
             (sides, half_depth + 4, half_height + 4, deep_width),
         ],
     )(coarse, encoded, low, high, ahead, behind)
-    left, right = pair_exchange(columns)
+    left, right = line_exchange("pair", columns)
 
     raised, columns = call(
         bottom_kernel,
@@ -407,14 +484,15 @@
         b_up.reshape(1, skip),
         encoded_ext,
     )
-    left, right = pair_exchange(columns)
+    left, right = line_exchange("pair", columns)
 
     (decoded,) = call(
         decode_kernel,
-        [(depth, height, pairs, lanes)],
+        [(depth, height, width, skip)],
         [
             pltpu.VMEM((depth + 2, height + 2, pairs, 4 * lanes), bf16),
             pltpu.VMEM((9, 4 * lanes, lanes), bf16),
+            pltpu.VMEM((depth, height, width, skip), f32),
         ],
     )(
         raised.reshape(depth + 4, height + 4, pairs, lanes),
@@ -424,7 +502,7 @@
         w_decode.reshape(9, 3, lanes, skip),
         b_decode.reshape(1, skip),
     )
-    return decoded.reshape(depth, height, width, skip)
+    return decoded
 
 
 def solution(mesh):

time: 60.8 us -> 44.4 us (0.73)
  Pallas kernels: 22.4 us -> 11.2 us
  local copies, waits for them, and re-layouts: 9.9 us -> 4.71 us
    pallas_call x2 -> x6, Pallas kernels: 11.8 us -> 7.93 us  [the longest x1 5.19 us: body(): call(decode_kernel, [(depth, height, width, skip)], [pltpu.VMEM((depth +...]
    pallas_call x1, Pallas kernels: 6.2 us -> 2.87 us  [body(): call(bottom_kernel, [(half_depth + 2, 2, half_height + 2, 2, pairs, lanes...]
    reshape x3 -> x0, local copies, waits for them, and re-layouts: 3.01 us -> none  [the longest x1 1.87 us: body(): return decoded.reshape(depth, height, width, skip)]
    slice x7 -> x0, local copies, waits for them, and re-layouts: 2.65 us -> none  [the longest x3 1.81 us: frame_planes(): block[at]]
    pallas_call x1, Pallas kernels: 2.41 us -> 0.28 us  [body(): call(frame_two_kernel, [(half_depth + 4, half_height + 4, pairs, deep_wid...]
    pallas_call x1, Pallas kernels: 2.03 us -> 0.15 us  [body(): call(frame_kernel, [(depth + 2, height + 2, pairs, lanes), (sides, depth...]
    unnamed x20 -> x22, local copies, waits for them, and re-layouts: 3.16 us -> 4.71 us
    pallas_call x1 -> x0, local copies, waits for them, and re-layouts: 1.03 us -> none  [body(): call(encode_kernel, [(half_depth, 2, half_height, 2, pairs, lanes), (half...]
  transfers between devices with their start and end apart: 9 -> 9, of which waited for: 9 -> 9; matrix products, arithmetic and copies ran while one was open for 2% -> 0% of each run, Pallas kernels for 0% -> 0%
where the time goes in v2:
time: 44.4 us; the launch traced here: 44.2 us
  waiting for transfers between devices  19 us (43%)
  Pallas kernels  11.2 us (25%)
  starting transfers between devices  9.18 us (21%)
  local copies, waits for them, and re-layouts  4.71 us (11%)
    ppermute x5, waiting for transfers between devices, line_exchange(): got = lax.ppermute(sent[0], axis, [(0, 1), (1, 0)])  8.79 us
    ppermute x2, waiting for transfers between devices, wide_exchange(): lax.ppermute(ahead, axes, snake_pairs(groups, count, 1))  6.79 us
    pallas_call x1, Pallas kernels, body(): call(decode_kernel, [(depth, height, width, skip)], [pltpu.VMEM((depth +...  5.19 us
    ppermute x5, starting transfers between devices, line_exchange(): got = lax.ppermute(sent[0], axis, [(0, 1), (1, 0)])  4.94 us
    unnamed x22, local copies, waits for them, and re-layouts  4.71 us
    ppermute x2, starting transfers between devices, wide_exchange(): lax.ppermute(ahead, axes, snake_pairs(groups, count, 1))  3.79 us
    ppermute x2, waiting for transfers between devices, wide_exchange(): lax.ppermute(behind, axes, snake_pairs(groups, count, -1))  3.38 us
    pallas_call x1, Pallas kernels, body(): call(bottom_kernel, [(half_depth + 2, 2, half_height + 2, 2, pairs, lanes...  2.87 us
  transfers between devices with their start and end apart: 9, of which 9 were waited for; matrix products, arithmetic and copies ran while one was open for 0% of the time, Pallas kernels for 0%

profile of v2, /device:TPU:0, one launch (start us, length us, event | category | flops | bytes accessed | tf_op | source)
XLA Modules:
  0.0 44.2 jit_solution(2331042197177563594)
XLA Ops:
  0.0 0.0 copy-start
  0.0 0.0 copy-start.2
  0.0 1.1 %copy-done.2 = bf16[6,8,32,128]{3,2,1,0:T(8,128)(2,1)S(1)} copy-done((bf16[6,8,32,128]{3,2,1,0:T(8,128)(2,1)S(1)}, bf16[6,8,32,128]{3,2,1,0:T(8,128)(2,1)}, u32[]{:S(2)}) %copy-start.2) | copy-done | bytes 393240
  1.2 3.0 %collective-permute-start = (bf16[6,16,256]{2,1,0:T(8,128)(2,1)S(1)}, bf16[6,16,256]{2,1,0:T(8,128)(2,1)S(1)}, u32[]{:S(2)}, u32[]{:S(2)}) collective-permute-start(bf16[6,16,256]{2,1,0:T(8,128)(2,1)S(1)} %bitcast.22), channel_id=1, source_target_pairs={{0,2},{2,0},{1,3},{3,1},{4,6},{6,4},{5,7},{7,5},{8,10},{10,8},{9,1... | collective-permute-start | bytes 147464 | tf_op jit(solution)/shard_map/ppermute | solution.py:26
  4.2 0.1 shard_map.109.own
  4.3 1.9 %collective-permute-done.low.high = bf16[6,16,256]{2,1,0:T(8,128)(2,1)S(1)} collective-permute-done((bf16[6,16,256]{2,1,0:T(8,128)(2,1)S(1)}, bf16[6,16,256]{2,1,0:T(8,128)(2,1)S(1)}, u32[]{:S(2)}, u32[]{:S(2)}) %collective-permute-start) | collective-permute-done | bytes 49184 | tf_op jit(solution)/shard_map/ppermute | solution.py:26
  6.3 2.2 %collective-permute-start.1 = (bf16[1,10,16,256]{3,2,1,0:T(8,128)(2,1)S(1)}, bf16[1,10,16,256]{3,2,1,0:T(8,128)(2,1)S(1)}, u32[]{:S(2)}, u32[]{:S(2)}) collective-permute-start(bf16[1,10,16,256]{3,2,1,0:T(8,128)(2,1)S(1)} %get-tuple-element.19), channel_id=1, source_target_pairs={{0,4},{4,8},{8,12},{12,28},{28,24},{24,20},{20,16},{16,0},{1,5},{5... | collective-permute-start | bytes 245768 | tf_op jit(solution)/shard_map/ppermute | solution.py:47
  8.5 0.0 collective-permute-start.2
  8.5 2.4 %collective-permute-done.1.ahead = bf16[1,10,16,256]{3,2,1,0:T(8,128)(2,1)S(1)} collective-permute-done((bf16[1,10,16,256]{3,2,1,0:T(8,128)(2,1)S(1)}, bf16[1,10,16,256]{3,2,1,0:T(8,128)(2,1)S(1)}, u32[]{:S(2)}, u32[]{:S(2)}) %collective-permute-start.1) | collective-permute-done | bytes 81952 | tf_op jit(solution)/shard_map/ppermute | solution.py:47
  10.8 2.1 %collective-permute-done.2.behind = bf16[1,10,16,256]{3,2,1,0:T(8,128)(2,1)S(1)} collective-permute-done((bf16[1,10,16,256]{3,2,1,0:T(8,128)(2,1)S(1)}, bf16[1,10,16,256]{3,2,1,0:T(8,128)(2,1)S(1)}, u32[]{:S(2)}, u32[]{:S(2)}) %collective-permute-start.2) | collective-permute-done | bytes 81952 | tf_op jit(solution)/shard_map/ppermute | solution.py:48
  12.9 0.1 shard_map.112
  13.1 0.1 collective-permute-start.3
  13.1 1.2 %collective-permute-done.3.left.right = bf16[8,10,128]{2,1,0:T(8,128)(2,1)S(1)} collective-permute-done((bf16[8,10,128]{2,1,0:T(8,128)(2,1)S(1)}, bf16[8,10,128]{2,1,0:T(8,128)(2,1)S(1)}, u32[]{:S(2)}, u32[]{:S(2)}) %collective-permute-start.3) | collective-permute-done | bytes 20512 | tf_op jit(solution)/shard_map/ppermute | solution.py:26
  14.3 0.0 copy-start.3
  14.3 1.2 %copy-done.3 = bf16[3,3,3,128,128]{4,3,2,1,0:T(8,128)(2,1)S(1)} copy-done((bf16[3,3,3,128,128]{4,3,2,1,0:T(8,128)(2,1)S(1)}, bf16[3,3,3,128,128]{4,3,2,1,0:T(8,128)(2,1)}, u32[]{:S(2)}) %copy-start.3) | copy-done | bytes 884760
  15.5 0.0 copy-start.5
  15.5 1.0 %copy-done.5 = bf16[2,2,2,128,256]{4,3,2,1,0:T(8,128)(2,1)S(1)} copy-done((bf16[2,2,2,128,256]{4,3,2,1,0:T(8,128)(2,1)S(1)}, bf16[2,2,2,128,256]{4,3,2,1,0:T(8,128)(2,1)}, u32[]{:S(2)}) %copy-start.5) | copy-done | bytes 524312
  16.5 0.0 copy-start.6
  16.5 0.7 %copy-done.6 = f32[256]{0:T(256)S(1)} copy-done((f32[256]{0:T(256)S(1)}, f32[256]{0:T(256)}, u32[]{:S(2)}) %copy-start.6) | copy-done | bytes 1048
  17.2 0.0 copy-start.8
  17.2 0.7 %copy-done.8 = f32[128]{0:T(128)S(1)} copy-done((f32[128]{0:T(128)S(1)}, f32[128]{0:T(128)}, u32[]{:S(2)}) %copy-start.8) | copy-done | bytes 536
  17.9 0.0 copy-start.4
  17.9 0.0 copy-start.7
  17.9 0.0 copy-start.9
  17.9 2.5 %shard_map.113 = (bf16[6,8,16,256]{3,2,1,0:T(8,128)(2,1)S(1)}, bf16[3,4,16,256]{3,2,1,0:T(8,128)(2,1)S(1)}, bf16[1,12,16,256]{3,2,1,0:T(8,128)(2,1)S(1)}) custom-call(bf16[8,10,16,256]{3,2,1,0:T(8,128)(2,1)S(1)} %get-tuple-element.21.ext, bf16[8,10,128]{2,1,0:T(8,128)(2,1)S(1)} %collective-permute-done.3.left.right, ...), custom_call_target="tpu_custom_call" | custom-call | tf_op jit(solution)/shard_map/pallas_call | solution.py:436
  20.4 0.0 copy-start.1
  20.4 0.0 copy-start.10
  20.5 1.6 %collective-permute-start.4 = (bf16[12,16,256]{2,1,0:T(8,128)(2,1)S(1)}, bf16[12,16,256]{2,1,0:T(8,128)(2,1)S(1)}, u32[]{:S(2)}, u32[]{:S(2)}) collective-permute-start(bf16[12,16,256]{2,1,0:T(8,128)(2,1)S(1)} %bitcast.28), channel_id=1, source_target_pairs={{0,2},{2,0},{1,3},{3,1},{4,6},{6,4},{5,7},{7,5},{8,10},{10,8},{9,1... | collective-permute-start | bytes 294920 | tf_op jit(solution)/shard_map/ppermute | solution.py:26
  22.0 3.4 %collective-permute-done.4.low.high = bf16[12,16,256]{2,1,0:T(8,128)(2,1)S(1)} collective-permute-done((bf16[12,16,256]{2,1,0:T(8,128)(2,1)S(1)}, bf16[12,16,256]{2,1,0:T(8,128)(2,1)S(1)}, u32[]{:S(2)}, u32[]{:S(2)}) %collective-permute-start.4) | collective-permute-done | bytes 98336 | tf_op jit(solution)/shard_map/ppermute | solution.py:26
  25.4 1.6 %collective-permute-start.5 = (bf16[26,16,256]{2,1,0:T(8,128)(2,1)S(1)}, bf16[26,16,256]{2,1,0:T(8,128)(2,1)S(1)}, u32[]{:S(2)}, u32[]{:S(2)}) collective-permute-start(bf16[26,16,256]{2,1,0:T(8,128)(2,1)S(1)} %get-tuple-element.26), channel_id=1, source_target_pairs={{0,4},{4,8},{8,12},{12,28},{28,24},{24,20},{20,16},{16,0},{1,5},{5... | collective-permute-start | bytes 638984 | tf_op jit(solution)/shard_map/ppermute | solution.py:47
  27.0 0.5 %collective-permute-start.6 = (bf16[26,16,256]{2,1,0:T(8,128)(2,1)S(1)}, bf16[26,16,256]{2,1,0:T(8,128)(2,1)S(1)}, u32[]{:S(2)}, u32[]{:S(2)}) collective-permute-start(bf16[26,16,256]{2,1,0:T(8,128)(2,1)S(1)} %get-tuple-element.27), channel_id=1, source_target_pairs={{0,16},{4,0},{8,4},{12,8},{28,12},{24,28},{20,24},{16,20},{1,17},{... | collective-permute-start | bytes 638984 | tf_op jit(solution)/shard_map/ppermute | solution.py:48
  27.5 4.4 %collective-permute-done.5.ahead = bf16[26,16,256]{2,1,0:T(8,128)(2,1)S(1)} collective-permute-done((bf16[26,16,256]{2,1,0:T(8,128)(2,1)S(1)}, bf16[26,16,256]{2,1,0:T(8,128)(2,1)S(1)}, u32[]{:S(2)}, u32[]{:S(2)}) %collective-permute-start.5) | collective-permute-done | bytes 213024 | tf_op jit(solution)/shard_map/ppermute | solution.py:47
  31.9 1.3 %collective-permute-done.6.behind = bf16[26,16,256]{2,1,0:T(8,128)(2,1)S(1)} collective-permute-done((bf16[26,16,256]{2,1,0:T(8,128)(2,1)S(1)}, bf16[26,16,256]{2,1,0:T(8,128)(2,1)S(1)}, u32[]{:S(2)}, u32[]{:S(2)}) %collective-permute-start.6) | collective-permute-done | bytes 213024 | tf_op jit(solution)/shard_map/ppermute | solution.py:48
  33.2 0.3 shard_map.115
  33.5 0.1 collective-permute-start.7
  33.6 1.2 %collective-permute-done.7.left.right = bf16[7,8,256]{2,1,0:T(8,128)(2,1)S(1)} collective-permute-done((bf16[7,8,256]{2,1,0:T(8,128)(2,1)S(1)}, bf16[7,8,256]{2,1,0:T(8,128)(2,1)S(1)}, u32[]{:S(2)}, u32[]{:S(2)}) %collective-permute-start.7) | collective-permute-done | bytes 28704 | tf_op jit(solution)/shard_map/ppermute | solution.py:26
  34.8 0.0 copy-done
  34.8 0.0 copy-done.4
  34.8 0.0 copy-done.7
  34.8 0.0 copy-done.9
  34.8 2.9 %shard_map.116 = (bf16[5,2,6,2,16,256]{5,4,3,2,1,0:T(8,128)(2,1)S(1)}, bf16[1,8,10,256]{3,2,1,0:T(8,128)(2,1)S(1)}) custom-call(bf16[7,8,16,256]{3,2,1,0:T(8,128)(2,1)S(1)} %get-tuple-element.28.coarse_ext, bf16[7,8,256]{2,1,0:T(8,128)(2,1)S(1)} %collective-permute-done.7.left.right, bf16[7,8,256]{2,1,0:T(8,128)(2,1)S(1)} %collective-permute-done.7.left.right, ...), custom_call_target="tpu_custom_call" | custom-call | tf_op jit(solution)/shard_map/pallas_call | solution.py:470
  37.7 0.2 collective-permute-start.8
  37.9 1.1 %collective-permute-done.8.left.right = bf16[8,10,256]{2,1,0:T(8,128)(2,1)S(1)} collective-permute-done((bf16[8,10,256]{2,1,0:T(8,128)(2,1)S(1)}, bf16[8,10,256]{2,1,0:T(8,128)(2,1)S(1)}, u32[]{:S(2)}, u32[]{:S(2)}) %collective-permute-start.8) | collective-permute-done | bytes 40992 | tf_op jit(solution)/shard_map/ppermute | solution.py:26
  39.0 0.0 copy-done.1
  39.0 0.0 copy-done.10
  39.0 5.2 %shard_map.117 = bf16[6,8,32,128]{3,2,1,0:T(8,128)(2,1)} custom-call(bf16[10,12,16,256]{3,2,1,0:T(8,128)(2,1)S(1)} %bitcast.18, bf16[8,10,16,256]{3,2,1,0:T(8,128)(2,1)S(1)} %get-tuple-element.30.encoded_ext, bf16[8,10,256]{2,1,0:T(8,128)(2,1)S(1)} %collective-permute-done.8.left.right, bf16[8,10,256]{2,1,0:T(8,128)(2,1)S(1)} %collective-permute-done.8.left.right, ...), custom_call_target="tpu_custom_call" | custom-call | tf_op jit(solution)/shard_map/pallas_call | solution.py:489
  (3 shorter events, 0.1 us)
Async XLA Ops:
  0.0 34.8 %copy-start = (bf16[3,3,3,256,256]{4,3,2,1,0:T(8,128)(2,1)S(1)}, bf16[3,3,3,256,256]{4,3,2,1,0:T(8,128)(2,1)}, u32[]{:S(2)}) copy-start(bf16[3,3,3,256,256]{4,3,2,1,0:T(8,128)(2,1)} %param.16) | copy-start | bytes 10616836
  0.0 1.1 %copy-start.2 = (bf16[6,8,32,128]{3,2,1,0:T(8,128)(2,1)S(1)}, bf16[6,8,32,128]{3,2,1,0:T(8,128)(2,1)}, u32[]{:S(2)}) copy-start(bf16[6,8,32,128]{3,2,1,0:T(8,128)(2,1)} %volume.3) | copy-start | bytes 1179652
  1.2 5.1 %collective-permute-start = (bf16[6,16,256]{2,1,0:T(8,128)(2,1)S(1)}, bf16[6,16,256]{2,1,0:T(8,128)(2,1)S(1)}, u32[]{:S(2)}, u32[]{:S(2)}) collective-permute-start(bf16[6,16,256]{2,1,0:T(8,128)(2,1)S(1)} %bitcast.22), channel_id=1, source_target_pairs={{0,2},{2,0},{1,3},{3,1},{4,6},{6,4},{5,7},{7,5},{8,10},{10,8},{9,1... | collective-permute-start | bytes 147464 | tf_op jit(solution)/shard_map/ppermute | solution.py:26
  6.3 4.5 %collective-permute-start.1 = (bf16[1,10,16,256]{3,2,1,0:T(8,128)(2,1)S(1)}, bf16[1,10,16,256]{3,2,1,0:T(8,128)(2,1)S(1)}, u32[]{:S(2)}, u32[]{:S(2)}) collective-permute-start(bf16[1,10,16,256]{3,2,1,0:T(8,128)(2,1)S(1)} %get-tuple-element.19), channel_id=1, source_target_pairs={{0,4},{4,8},{8,12},{12,28},{28,24},{24,20},{20,16},{16,0},{1,5},{5... | collective-permute-start | bytes 245768 | tf_op jit(solution)/shard_map/ppermute | solution.py:47
  8.5 4.4 %collective-permute-start.2 = (bf16[1,10,16,256]{3,2,1,0:T(8,128)(2,1)S(1)}, bf16[1,10,16,256]{3,2,1,0:T(8,128)(2,1)S(1)}, u32[]{:S(2)}, u32[]{:S(2)}) collective-permute-start(bf16[1,10,16,256]{3,2,1,0:T(8,128)(2,1)S(1)} %get-tuple-element.20), channel_id=1, source_target_pairs={{0,16},{4,0},{8,4},{12,8},{28,12},{24,28},{20,24},{16,20},{1,17},{... | collective-permute-start | bytes 245768 | tf_op jit(solution)/shard_map/ppermute | solution.py:48
  13.1 1.3 %collective-permute-start.3 = (bf16[8,10,128]{2,1,0:T(8,128)(2,1)S(1)}, bf16[8,10,128]{2,1,0:T(8,128)(2,1)S(1)}, u32[]{:S(2)}, u32[]{:S(2)}) collective-permute-start(bf16[8,10,128]{2,1,0:T(8,128)(2,1)S(1)} %bitcast.30), channel_id=1, source_target_pairs={{0,1},{1,0},{2,3},{3,2},{4,5},{5,4},{6,7},{7,6},{8,9},{9,8},{10,11... | collective-permute-start | bytes 61448 | tf_op jit(solution)/shard_map/ppermute | solution.py:26
  14.3 1.2 %copy-start.3 = (bf16[3,3,3,128,128]{4,3,2,1,0:T(8,128)(2,1)S(1)}, bf16[3,3,3,128,128]{4,3,2,1,0:T(8,128)(2,1)}, u32[]{:S(2)}) copy-start(bf16[3,3,3,128,128]{4,3,2,1,0:T(8,128)(2,1)} %param.12) | copy-start | bytes 2654212
  15.5 1.0 %copy-start.5 = (bf16[2,2,2,128,256]{4,3,2,1,0:T(8,128)(2,1)S(1)}, bf16[2,2,2,128,256]{4,3,2,1,0:T(8,128)(2,1)}, u32[]{:S(2)}) copy-start(bf16[2,2,2,128,256]{4,3,2,1,0:T(8,128)(2,1)} %param.14) | copy-start | bytes 1572868
  16.5 0.7 %copy-start.6 = (f32[256]{0:T(256)S(1)}, f32[256]{0:T(256)}, u32[]{:S(2)}) copy-start(f32[256]{0:T(256)} %param.15) | copy-start | bytes 3076
  17.2 0.7 %copy-start.8 = (f32[128]{0:T(128)S(1)}, f32[128]{0:T(128)}, u32[]{:S(2)}) copy-start(f32[128]{0:T(128)} %param.13) | copy-start | bytes 1540
  17.9 16.9 %copy-start.4 = (bf16[2,2,2,256,128]{4,3,2,1,0:T(8,128)(2,1)S(1)}, bf16[2,2,2,256,128]{4,3,2,1,0:T(8,128)(2,1)}, u32[]{:S(2)}) copy-start(bf16[2,2,2,256,128]{4,3,2,1,0:T(8,128)(2,1)} %param.18) | copy-start | bytes 1572868
  17.9 16.9 %copy-start.7 = (f32[256]{0:T(256)S(1)}, f32[256]{0:T(256)}, u32[]{:S(2)}) copy-start(f32[256]{0:T(256)} %param.17) | copy-start | bytes 3076
  17.9 16.9 %copy-start.9 = (f32[128]{0:T(128)S(1)}, f32[128]{0:T(128)}, u32[]{:S(2)}) copy-start(f32[128]{0:T(128)} %param.19) | copy-start | bytes 1540
  20.4 18.6 %copy-start.1 = (bf16[3,3,3,256,128]{4,3,2,1,0:T(8,128)(2,1)S(1)}, bf16[3,3,3,256,128]{4,3,2,1,0:T(8,128)(2,1)}, u32[]{:S(2)}) copy-start(bf16[3,3,3,256,128]{4,3,2,1,0:T(8,128)(2,1)} %param.20) | copy-start | bytes 5308420
  20.4 18.6 %copy-start.10 = (f32[128]{0:T(128)S(1)}, f32[128]{0:T(128)}, u32[]{:S(2)}) copy-start(f32[128]{0:T(128)} %param.21) | copy-start | bytes 1540
  20.5 4.9 %collective-permute-start.4 = (bf16[12,16,256]{2,1,0:T(8,128)(2,1)S(1)}, bf16[12,16,256]{2,1,0:T(8,128)(2,1)S(1)}, u32[]{:S(2)}, u32[]{:S(2)}) collective-permute-start(bf16[12,16,256]{2,1,0:T(8,128)(2,1)S(1)} %bitcast.28), channel_id=1, source_target_pairs={{0,2},{2,0},{1,3},{3,1},{4,6},{6,4},{5,7},{7,5},{8,10},{10,8},{9,1... | collective-permute-start | bytes 294920 | tf_op jit(solution)/shard_map/ppermute | solution.py:26
  25.4 6.5 %collective-permute-start.5 = (bf16[26,16,256]{2,1,0:T(8,128)(2,1)S(1)}, bf16[26,16,256]{2,1,0:T(8,128)(2,1)S(1)}, u32[]{:S(2)}, u32[]{:S(2)}) collective-permute-start(bf16[26,16,256]{2,1,0:T(8,128)(2,1)S(1)} %get-tuple-element.26), channel_id=1, source_target_pairs={{0,4},{4,8},{8,12},{12,28},{28,24},{24,20},{20,16},{16,0},{1,5},{5... | collective-permute-start | bytes 638984 | tf_op jit(solution)/shard_map/ppermute | solution.py:47
  27.0 6.2 %collective-permute-start.6 = (bf16[26,16,256]{2,1,0:T(8,128)(2,1)S(1)}, bf16[26,16,256]{2,1,0:T(8,128)(2,1)S(1)}, u32[]{:S(2)}, u32[]{:S(2)}) collective-permute-start(bf16[26,16,256]{2,1,0:T(8,128)(2,1)S(1)} %get-tuple-element.27), channel_id=1, source_target_pairs={{0,16},{4,0},{8,4},{12,8},{28,12},{24,28},{20,24},{16,20},{1,17},{... | collective-permute-start | bytes 638984 | tf_op jit(solution)/shard_map/ppermute | solution.py:48
  33.5 1.3 %collective-permute-start.7 = (bf16[7,8,256]{2,1,0:T(8,128)(2,1)S(1)}, bf16[7,8,256]{2,1,0:T(8,128)(2,1)S(1)}, u32[]{:S(2)}, u32[]{:S(2)}) collective-permute-start(bf16[7,8,256]{2,1,0:T(8,128)(2,1)S(1)} %bitcast.31), channel_id=1, source_target_pairs={{0,1},{1,0},{2,3},{3,2},{4,5},{5,4},{6,7},{7,6},{8,9},{9,8},{10,11... | collective-permute-start | bytes 86024 | tf_op jit(solution)/shard_map/ppermute | solution.py:26
  37.7 1.3 %collective-permute-start.8 = (bf16[8,10,256]{2,1,0:T(8,128)(2,1)S(1)}, bf16[8,10,256]{2,1,0:T(8,128)(2,1)S(1)}, u32[]{:S(2)}, u32[]{:S(2)}) collective-permute-start(bf16[8,10,256]{2,1,0:T(8,128)(2,1)S(1)} %bitcast.29), channel_id=1, source_target_pairs={{0,1},{1,0},{2,3},{3,2},{4,5},{5,4},{6,7},{7,6},{8,9},{9,8},{10,11... | collective-permute-start | bytes 122888 | tf_op jit(solution)/shard_map/ppermute | solution.py:26

commit v3 on v2

--- a/solution.py
+++ b/solution.py
@@ -54,6 +54,7 @@
         kernel,
         out_shape=[jax.ShapeDtypeStruct(shape, bf16) for shape in outs],
         scratch_shapes=list(scratch),
+        cost_estimate=pl.CostEstimate(flops=4 * 10**9, transcendentals=0, bytes_accessed=10**6),
         compiler_params=pltpu.CompilerParams(vmem_limit_bytes=megabytes << 20),
     )
 

time: 44.4 us -> 40.7 us (0.917)
  local copies, waits for them, and re-layouts: 4.71 us -> 1.04 us
    unnamed x22, local copies, waits for them, and re-layouts: 4.71 us -> 1.04 us
where the time goes in v3:
time: 40.7 us; the launch traced here: 40.6 us
  waiting for transfers between devices  18.9 us (46%)
  Pallas kernels  11.2 us (28%)
  starting transfers between devices  9.29 us (23%)
  local copies, waits for them, and re-layouts  1.04 us (3%)
    ppermute x5, waiting for transfers between devices, line_exchange(): got = lax.ppermute(sent[0], axis, [(0, 1), (1, 0)])  8.78 us
    ppermute x2, waiting for transfers between devices, wide_exchange(): lax.ppermute(ahead, axes, snake_pairs(groups, count, 1))  6.65 us
    pallas_call x1, Pallas kernels, body(): call(decode_kernel, [(depth, height, width, skip)], [pltpu.VMEM((depth +...  5.16 us
    ppermute x5, starting transfers between devices, line_exchange(): got = lax.ppermute(sent[0], axis, [(0, 1), (1, 0)])  4.94 us
    ppermute x2, starting transfers between devices, wide_exchange(): lax.ppermute(ahead, axes, snake_pairs(groups, count, 1))  3.79 us
    ppermute x2, waiting for transfers between devices, wide_exchange(): lax.ppermute(behind, axes, snake_pairs(groups, count, -1))  3.51 us
    pallas_call x1, Pallas kernels, body(): call(bottom_kernel, [(half_depth + 2, 2, half_height + 2, 2, pairs, lanes...  2.86 us
    pallas_call x1, Pallas kernels, body(): call(encode_kernel, [(depth, height, pairs, lanes), (half_depth, half_hei...  2.56 us
  transfers between devices with their start and end apart: 9, of which 9 were waited for; matrix products, arithmetic and copies ran while one was open for 0% of the time, Pallas kernels for 0%

profile of v3, /device:TPU:0, one launch (start us, length us, event | category | flops | bytes accessed | tf_op | source)
XLA Modules:
  0.0 40.6 jit_solution(11508035512978743601)
XLA Ops:
  0.0 0.0 copy-start.5
  0.0 1.0 %copy-done.5 = bf16[6,8,32,128]{3,2,1,0:T(8,128)(2,1)S(1)} copy-done((bf16[6,8,32,128]{3,2,1,0:T(8,128)(2,1)S(1)}, bf16[6,8,32,128]{3,2,1,0:T(8,128)(2,1)}, u32[]{:S(2)}) %copy-start.5) | copy-done | bytes 393240
  1.0 3.0 %collective-permute-start = (bf16[6,16,256]{2,1,0:T(8,128)(2,1)S(1)}, bf16[6,16,256]{2,1,0:T(8,128)(2,1)S(1)}, u32[]{:S(2)}, u32[]{:S(2)}) collective-permute-start(bf16[6,16,256]{2,1,0:T(8,128)(2,1)S(1)} %bitcast.23), channel_id=1, source_target_pairs={{0,2},{2,0},{1,3},{3,1},{4,6},{6,4},{5,7},{7,5},{8,10},{10,8},{9,1... | collective-permute-start | bytes 147464 | tf_op jit(solution)/shard_map/ppermute | solution.py:26
  4.1 0.1 shard_map.109.own
  4.2 1.9 %collective-permute-done.low.high = bf16[6,16,256]{2,1,0:T(8,128)(2,1)S(1)} collective-permute-done((bf16[6,16,256]{2,1,0:T(8,128)(2,1)S(1)}, bf16[6,16,256]{2,1,0:T(8,128)(2,1)S(1)}, u32[]{:S(2)}, u32[]{:S(2)}) %collective-permute-start) | collective-permute-done | bytes 49184 | tf_op jit(solution)/shard_map/ppermute | solution.py:26
  6.1 2.2 %collective-permute-start.1 = (bf16[1,10,16,256]{3,2,1,0:T(8,128)(2,1)S(1)}, bf16[1,10,16,256]{3,2,1,0:T(8,128)(2,1)S(1)}, u32[]{:S(2)}, u32[]{:S(2)}) collective-permute-start(bf16[1,10,16,256]{3,2,1,0:T(8,128)(2,1)S(1)} %get-tuple-element.19), channel_id=1, source_target_pairs={{0,4},{4,8},{8,12},{12,28},{28,24},{24,20},{20,16},{16,0},{1,5},{5... | collective-permute-start | bytes 245768 | tf_op jit(solution)/shard_map/ppermute | solution.py:47
  8.3 0.0 copy-start.2
  8.3 0.0 copy-start.3
  8.3 0.0 copy-start.6
  8.3 0.0 copy-start.8
  8.3 0.1 collective-permute-start.2
  8.4 2.3 %collective-permute-done.1.ahead = bf16[1,10,16,256]{3,2,1,0:T(8,128)(2,1)S(1)} collective-permute-done((bf16[1,10,16,256]{3,2,1,0:T(8,128)(2,1)S(1)}, bf16[1,10,16,256]{3,2,1,0:T(8,128)(2,1)S(1)}, u32[]{:S(2)}, u32[]{:S(2)}) %collective-permute-start.1) | collective-permute-done | bytes 81952 | tf_op jit(solution)/shard_map/ppermute | solution.py:47
  10.7 2.1 %collective-permute-done.2.behind = bf16[1,10,16,256]{3,2,1,0:T(8,128)(2,1)S(1)} collective-permute-done((bf16[1,10,16,256]{3,2,1,0:T(8,128)(2,1)S(1)}, bf16[1,10,16,256]{3,2,1,0:T(8,128)(2,1)S(1)}, u32[]{:S(2)}, u32[]{:S(2)}) %collective-permute-start.2) | collective-permute-done | bytes 81952 | tf_op jit(solution)/shard_map/ppermute | solution.py:48
  12.8 0.1 shard_map.112
  13.0 0.1 collective-permute-start.3
  13.0 1.2 %collective-permute-done.3.left.right = bf16[8,10,128]{2,1,0:T(8,128)(2,1)S(1)} collective-permute-done((bf16[8,10,128]{2,1,0:T(8,128)(2,1)S(1)}, bf16[8,10,128]{2,1,0:T(8,128)(2,1)S(1)}, u32[]{:S(2)}, u32[]{:S(2)}) %collective-permute-start.3) | collective-permute-done | bytes 20512 | tf_op jit(solution)/shard_map/ppermute | solution.py:26
  14.2 0.0 copy-done.2
  14.2 0.0 copy-done.3
  14.2 0.0 copy-done.6
  14.3 0.0 copy-done.8
  14.3 2.6 %shard_map.113 = (bf16[6,8,16,256]{3,2,1,0:T(8,128)(2,1)S(1)}, bf16[3,4,16,256]{3,2,1,0:T(8,128)(2,1)S(1)}, bf16[1,12,16,256]{3,2,1,0:T(8,128)(2,1)S(1)}) custom-call(bf16[8,10,16,256]{3,2,1,0:T(8,128)(2,1)S(1)} %get-tuple-element.21.ext, bf16[8,10,128]{2,1,0:T(8,128)(2,1)S(1)} %collective-permute-done.3.left.right, ...), custom_call_target="tpu_custom_call" | custom-call | flops 4000000000 | bytes 1000000 | tf_op jit(solution)/shard_map/pallas_call | solution.py:437
  16.8 1.6 %collective-permute-start.4 = (bf16[12,16,256]{2,1,0:T(8,128)(2,1)S(1)}, bf16[12,16,256]{2,1,0:T(8,128)(2,1)S(1)}, u32[]{:S(2)}, u32[]{:S(2)}) collective-permute-start(bf16[12,16,256]{2,1,0:T(8,128)(2,1)S(1)} %bitcast.21), channel_id=1, source_target_pairs={{0,2},{2,0},{1,3},{3,1},{4,6},{6,4},{5,7},{7,5},{8,10},{10,8},{9,1... | collective-permute-start | bytes 294920 | tf_op jit(solution)/shard_map/ppermute | solution.py:26
  18.4 3.4 %collective-permute-done.4.low.high = bf16[12,16,256]{2,1,0:T(8,128)(2,1)S(1)} collective-permute-done((bf16[12,16,256]{2,1,0:T(8,128)(2,1)S(1)}, bf16[12,16,256]{2,1,0:T(8,128)(2,1)S(1)}, u32[]{:S(2)}, u32[]{:S(2)}) %collective-permute-start.4) | collective-permute-done | bytes 98336 | tf_op jit(solution)/shard_map/ppermute | solution.py:26
  21.8 1.6 %collective-permute-start.5 = (bf16[26,16,256]{2,1,0:T(8,128)(2,1)S(1)}, bf16[26,16,256]{2,1,0:T(8,128)(2,1)S(1)}, u32[]{:S(2)}, u32[]{:S(2)}) collective-permute-start(bf16[26,16,256]{2,1,0:T(8,128)(2,1)S(1)} %get-tuple-element.26), channel_id=1, source_target_pairs={{0,4},{4,8},{8,12},{12,28},{28,24},{24,20},{20,16},{16,0},{1,5},{5... | collective-permute-start | bytes 638984 | tf_op jit(solution)/shard_map/ppermute | solution.py:47
  23.4 0.0 copy-start
  23.4 0.0 copy-start.4
  23.4 0.0 copy-start.7
  23.4 0.0 copy-start.9
  23.4 0.5 %collective-permute-start.6 = (bf16[26,16,256]{2,1,0:T(8,128)(2,1)S(1)}, bf16[26,16,256]{2,1,0:T(8,128)(2,1)S(1)}, u32[]{:S(2)}, u32[]{:S(2)}) collective-permute-start(bf16[26,16,256]{2,1,0:T(8,128)(2,1)S(1)} %get-tuple-element.27), channel_id=1, source_target_pairs={{0,16},{4,0},{8,4},{12,8},{28,12},{24,28},{20,24},{16,20},{1,17},{... | collective-permute-start | bytes 638984 | tf_op jit(solution)/shard_map/ppermute | solution.py:48
  23.9 4.4 %collective-permute-done.5.ahead = bf16[26,16,256]{2,1,0:T(8,128)(2,1)S(1)} collective-permute-done((bf16[26,16,256]{2,1,0:T(8,128)(2,1)S(1)}, bf16[26,16,256]{2,1,0:T(8,128)(2,1)S(1)}, u32[]{:S(2)}, u32[]{:S(2)}) %collective-permute-start.5) | collective-permute-done | bytes 213024 | tf_op jit(solution)/shard_map/ppermute | solution.py:47
  28.3 1.4 %collective-permute-done.6.behind = bf16[26,16,256]{2,1,0:T(8,128)(2,1)S(1)} collective-permute-done((bf16[26,16,256]{2,1,0:T(8,128)(2,1)S(1)}, bf16[26,16,256]{2,1,0:T(8,128)(2,1)S(1)}, u32[]{:S(2)}, u32[]{:S(2)}) %collective-permute-start.6) | collective-permute-done | bytes 213024 | tf_op jit(solution)/shard_map/ppermute | solution.py:48
  29.7 0.3 shard_map.115
  29.9 0.1 collective-permute-start.7
  30.0 1.2 %collective-permute-done.7.left.right = bf16[7,8,256]{2,1,0:T(8,128)(2,1)S(1)} collective-permute-done((bf16[7,8,256]{2,1,0:T(8,128)(2,1)S(1)}, bf16[7,8,256]{2,1,0:T(8,128)(2,1)S(1)}, u32[]{:S(2)}, u32[]{:S(2)}) %collective-permute-start.7) | collective-permute-done | bytes 28704 | tf_op jit(solution)/shard_map/ppermute | solution.py:26
  31.2 0.0 copy-done
  31.2 0.0 copy-done.4
  31.2 0.0 copy-done.7
  31.2 0.0 copy-done.9
  31.2 0.0 copy-start.1
  31.2 0.0 copy-start.10
  31.3 2.9 %shard_map.116 = (bf16[5,2,6,2,16,256]{5,4,3,2,1,0:T(8,128)(2,1)S(1)}, bf16[1,8,10,256]{3,2,1,0:T(8,128)(2,1)S(1)}) custom-call(bf16[7,8,16,256]{3,2,1,0:T(8,128)(2,1)S(1)} %get-tuple-element.28.coarse_ext, bf16[7,8,256]{2,1,0:T(8,128)(2,1)S(1)} %collective-permute-done.7.left.right, bf16[7,8,256]{2,1,0:T(8,128)(2,1)S(1)} %collective-permute-done.7.left.right, ...), custom_call_target="tpu_custom_call" | custom-call | flops 4000000000 | bytes 1000000 | tf_op jit(solution)/shard_map/pallas_call | solution.py:471
  34.1 0.2 collective-permute-start.8
  34.3 1.1 %collective-permute-done.8.left.right = bf16[8,10,256]{2,1,0:T(8,128)(2,1)S(1)} collective-permute-done((bf16[8,10,256]{2,1,0:T(8,128)(2,1)S(1)}, bf16[8,10,256]{2,1,0:T(8,128)(2,1)S(1)}, u32[]{:S(2)}, u32[]{:S(2)}) %collective-permute-start.8) | collective-permute-done | bytes 40992 | tf_op jit(solution)/shard_map/ppermute | solution.py:26
  35.4 0.0 copy-done.1
  35.4 0.0 copy-done.10
  35.4 5.2 %shard_map.117 = bf16[6,8,32,128]{3,2,1,0:T(8,128)(2,1)} custom-call(bf16[10,12,16,256]{3,2,1,0:T(8,128)(2,1)S(1)} %bitcast.31, bf16[8,10,16,256]{3,2,1,0:T(8,128)(2,1)S(1)} %get-tuple-element.30.encoded_ext, bf16[8,10,256]{2,1,0:T(8,128)(2,1)S(1)} %collective-permute-done.8.left.right, bf16[8,10,256]{2,1,0:T(8,128)(2,1)S(1)} %collective-permute-done.8.left.right, ...), custom_call_target="tpu_custom_call" | custom-call | flops 4000000000 | bytes 1000000 | tf_op jit(solution)/shard_map/pallas_call | solution.py:490
  (3 shorter events, 0.1 us)
Async XLA Ops:
  0.0 1.0 %copy-start.5 = (bf16[6,8,32,128]{3,2,1,0:T(8,128)(2,1)S(1)}, bf16[6,8,32,128]{3,2,1,0:T(8,128)(2,1)}, u32[]{:S(2)}) copy-start(bf16[6,8,32,128]{3,2,1,0:T(8,128)(2,1)} %volume.3) | copy-start | bytes 1179652
  1.0 5.1 %collective-permute-start = (bf16[6,16,256]{2,1,0:T(8,128)(2,1)S(1)}, bf16[6,16,256]{2,1,0:T(8,128)(2,1)S(1)}, u32[]{:S(2)}, u32[]{:S(2)}) collective-permute-start(bf16[6,16,256]{2,1,0:T(8,128)(2,1)S(1)} %bitcast.23), channel_id=1, source_target_pairs={{0,2},{2,0},{1,3},{3,1},{4,6},{6,4},{5,7},{7,5},{8,10},{10,8},{9,1... | collective-permute-start | bytes 147464 | tf_op jit(solution)/shard_map/ppermute | solution.py:26
  6.1 4.5 %collective-permute-start.1 = (bf16[1,10,16,256]{3,2,1,0:T(8,128)(2,1)S(1)}, bf16[1,10,16,256]{3,2,1,0:T(8,128)(2,1)S(1)}, u32[]{:S(2)}, u32[]{:S(2)}) collective-permute-start(bf16[1,10,16,256]{3,2,1,0:T(8,128)(2,1)S(1)} %get-tuple-element.19), channel_id=1, source_target_pairs={{0,4},{4,8},{8,12},{12,28},{28,24},{24,20},{20,16},{16,0},{1,5},{5... | collective-permute-start | bytes 245768 | tf_op jit(solution)/shard_map/ppermute | solution.py:47
  8.3 5.9 %copy-start.2 = (bf16[3,3,3,128,128]{4,3,2,1,0:T(8,128)(2,1)S(1)}, bf16[3,3,3,128,128]{4,3,2,1,0:T(8,128)(2,1)}, u32[]{:S(2)}) copy-start(bf16[3,3,3,128,128]{4,3,2,1,0:T(8,128)(2,1)} %param.12) | copy-start | bytes 2654212
  8.3 5.9 %copy-start.3 = (bf16[2,2,2,128,256]{4,3,2,1,0:T(8,128)(2,1)S(1)}, bf16[2,2,2,128,256]{4,3,2,1,0:T(8,128)(2,1)}, u32[]{:S(2)}) copy-start(bf16[2,2,2,128,256]{4,3,2,1,0:T(8,128)(2,1)} %param.14) | copy-start | bytes 1572868
  8.3 5.9 %copy-start.6 = (f32[256]{0:T(256)S(1)}, f32[256]{0:T(256)}, u32[]{:S(2)}) copy-start(f32[256]{0:T(256)} %param.15) | copy-start | bytes 3076
  8.3 5.9 %copy-start.8 = (f32[128]{0:T(128)S(1)}, f32[128]{0:T(128)}, u32[]{:S(2)}) copy-start(f32[128]{0:T(128)} %param.13) | copy-start | bytes 1540
  8.3 4.5 %collective-permute-start.2 = (bf16[1,10,16,256]{3,2,1,0:T(8,128)(2,1)S(1)}, bf16[1,10,16,256]{3,2,1,0:T(8,128)(2,1)S(1)}, u32[]{:S(2)}, u32[]{:S(2)}) collective-permute-start(bf16[1,10,16,256]{3,2,1,0:T(8,128)(2,1)S(1)} %get-tuple-element.20), channel_id=1, source_target_pairs={{0,16},{4,0},{8,4},{12,8},{28,12},{24,28},{20,24},{16,20},{1,17},{... | collective-permute-start | bytes 245768 | tf_op jit(solution)/shard_map/ppermute | solution.py:48
  13.0 1.3 %collective-permute-start.3 = (bf16[8,10,128]{2,1,0:T(8,128)(2,1)S(1)}, bf16[8,10,128]{2,1,0:T(8,128)(2,1)S(1)}, u32[]{:S(2)}, u32[]{:S(2)}) collective-permute-start(bf16[8,10,128]{2,1,0:T(8,128)(2,1)S(1)} %bitcast.24), channel_id=1, source_target_pairs={{0,1},{1,0},{2,3},{3,2},{4,5},{5,4},{6,7},{7,6},{8,9},{9,8},{10,11... | collective-permute-start | bytes 61448 | tf_op jit(solution)/shard_map/ppermute | solution.py:26
  16.8 4.9 %collective-permute-start.4 = (bf16[12,16,256]{2,1,0:T(8,128)(2,1)S(1)}, bf16[12,16,256]{2,1,0:T(8,128)(2,1)S(1)}, u32[]{:S(2)}, u32[]{:S(2)}) collective-permute-start(bf16[12,16,256]{2,1,0:T(8,128)(2,1)S(1)} %bitcast.21), channel_id=1, source_target_pairs={{0,2},{2,0},{1,3},{3,1},{4,6},{6,4},{5,7},{7,5},{8,10},{10,8},{9,1... | collective-permute-start | bytes 294920 | tf_op jit(solution)/shard_map/ppermute | solution.py:26
  21.8 6.5 %collective-permute-start.5 = (bf16[26,16,256]{2,1,0:T(8,128)(2,1)S(1)}, bf16[26,16,256]{2,1,0:T(8,128)(2,1)S(1)}, u32[]{:S(2)}, u32[]{:S(2)}) collective-permute-start(bf16[26,16,256]{2,1,0:T(8,128)(2,1)S(1)} %get-tuple-element.26), channel_id=1, source_target_pairs={{0,4},{4,8},{8,12},{12,28},{28,24},{24,20},{20,16},{16,0},{1,5},{5... | collective-permute-start | bytes 638984 | tf_op jit(solution)/shard_map/ppermute | solution.py:47
  23.4 7.8 %copy-start = (bf16[3,3,3,256,256]{4,3,2,1,0:T(8,128)(2,1)S(1)}, bf16[3,3,3,256,256]{4,3,2,1,0:T(8,128)(2,1)}, u32[]{:S(2)}) copy-start(bf16[3,3,3,256,256]{4,3,2,1,0:T(8,128)(2,1)} %param.16) | copy-start | bytes 10616836
  23.4 7.8 %copy-start.4 = (bf16[2,2,2,256,128]{4,3,2,1,0:T(8,128)(2,1)S(1)}, bf16[2,2,2,256,128]{4,3,2,1,0:T(8,128)(2,1)}, u32[]{:S(2)}) copy-start(bf16[2,2,2,256,128]{4,3,2,1,0:T(8,128)(2,1)} %param.18) | copy-start | bytes 1572868
  23.4 7.8 %copy-start.7 = (f32[256]{0:T(256)S(1)}, f32[256]{0:T(256)}, u32[]{:S(2)}) copy-start(f32[256]{0:T(256)} %param.17) | copy-start | bytes 3076
  23.4 7.8 %copy-start.9 = (f32[128]{0:T(128)S(1)}, f32[128]{0:T(128)}, u32[]{:S(2)}) copy-start(f32[128]{0:T(128)} %param.19) | copy-start | bytes 1540
  23.4 6.2 %collective-permute-start.6 = (bf16[26,16,256]{2,1,0:T(8,128)(2,1)S(1)}, bf16[26,16,256]{2,1,0:T(8,128)(2,1)S(1)}, u32[]{:S(2)}, u32[]{:S(2)}) collective-permute-start(bf16[26,16,256]{2,1,0:T(8,128)(2,1)S(1)} %get-tuple-element.27), channel_id=1, source_target_pairs={{0,16},{4,0},{8,4},{12,8},{28,12},{24,28},{20,24},{16,20},{1,17},{... | collective-permute-start | bytes 638984 | tf_op jit(solution)/shard_map/ppermute | solution.py:48
  29.9 1.3 %collective-permute-start.7 = (bf16[7,8,256]{2,1,0:T(8,128)(2,1)S(1)}, bf16[7,8,256]{2,1,0:T(8,128)(2,1)S(1)}, u32[]{:S(2)}, u32[]{:S(2)}) collective-permute-start(bf16[7,8,256]{2,1,0:T(8,128)(2,1)S(1)} %bitcast.25), channel_id=1, source_target_pairs={{0,1},{1,0},{2,3},{3,2},{4,5},{5,4},{6,7},{7,6},{8,9},{9,8},{10,11... | collective-permute-start | bytes 86024 | tf_op jit(solution)/shard_map/ppermute | solution.py:26
  31.2 4.2 %copy-start.1 = (bf16[3,3,3,256,128]{4,3,2,1,0:T(8,128)(2,1)S(1)}, bf16[3,3,3,256,128]{4,3,2,1,0:T(8,128)(2,1)}, u32[]{:S(2)}) copy-start(bf16[3,3,3,256,128]{4,3,2,1,0:T(8,128)(2,1)} %param.20) | copy-start | bytes 5308420
  31.2 4.2 %copy-start.10 = (f32[128]{0:T(128)S(1)}, f32[128]{0:T(128)}, u32[]{:S(2)}) copy-start(f32[128]{0:T(128)} %param.21) | copy-start | bytes 1540
  34.1 1.3 %collective-permute-start.8 = (bf16[8,10,256]{2,1,0:T(8,128)(2,1)S(1)}, bf16[8,10,256]{2,1,0:T(8,128)(2,1)S(1)}, u32[]{:S(2)}, u32[]{:S(2)}) collective-permute-start(bf16[8,10,256]{2,1,0:T(8,128)(2,1)S(1)} %bitcast.22), channel_id=1, source_target_pairs={{0,1},{1,0},{2,3},{3,2},{4,5},{5,4},{6,7},{7,6},{8,9},{9,8},{10,11... | collective-permute-start | bytes 122888 | tf_op jit(solution)/shard_map/ppermute | solution.py:26

commit v4 on v3

v4 whole, which is shorter than its diff:
```python
import functools

import jax
import jax.numpy as jnp
from jax import lax
from jax.experimental import pallas as pl
from jax.experimental.pallas import tpu as pltpu
from jax.sharding import PartitionSpec as P

leak_slope = 0.01
f32 = jnp.float32
bf16 = jnp.bfloat16


def leaky_relu(values):
    return jnp.maximum(values, leak_slope * values)


def sides_of(axis):
    return 1 if lax.axis_size(axis) == 2 else 2


def line_exchange(axis, sent):
    count = lax.axis_size(axis)
    if count == 2:
        got = lax.ppermute(sent[0], axis, [(0, 1), (1, 0)])
        return got, got
    up = [(i, i + 1) for i in range(count - 1)]
    down = [(b, a) for a, b in up]
    return lax.ppermute(sent[1], axis, up), lax.ppermute(sent[0], axis, down)


def snake_pairs(groups, count, step):
    order = [
        group * count + (place if group % 2 == 0 else count - 1 - place)
        for group in range(groups)
        for place in range(count)
    ]
    total = len(order)
    return [(order[i], order[(i + step) % total]) for i in range(total)]


def ring_exchange(sent):
    groups, count = lax.axis_size("groups"), lax.axis_size("wide")
    pairs = [
        (2 * a + core, 2 * b + core)
        for core, step in ((0, 1), (1, -1))
        for a, b in snake_pairs(groups, count, step)
    ]
    return lax.ppermute(sent, ("groups", "wide", "pair"), pairs)


def corner_exchange(sent):
    groups, count, tall = (lax.axis_size(axis) for axis in ("groups", "wide", "narrow"))
    moves = [(0, 1), (1, 0)] if tall == 2 else [(i, i + 1) for i in range(tall - 1)]

    def move(array, rows):
        pairs = [
            ((a * tall + c) * 2 + core, (b * tall + d) * 2 + core)
            for core, step in ((0, 1), (1, -1))
            for a, b in snake_pairs(groups, count, step)
            for c, d in rows
        ]
        return lax.ppermute(array, ("groups", "wide", "narrow", "pair"), pairs)

    if tall == 2:
        got = move(sent[0], moves)
        return got, got
    return move(sent[1], moves), move(sent[0], [(d, c) for c, d in moves])


def call(kernel, outs, scratch=(), megabytes=24):
    return pl.pallas_call(
        kernel,
        out_shape=[jax.ShapeDtypeStruct(shape, bf16) for shape in outs],
        scratch_shapes=list(scratch),
        cost_estimate=pl.CostEstimate(flops=4 * 10**9, transcendentals=0, bytes_accessed=10**6),
        compiler_params=pltpu.CompilerParams(vmem_limit_bytes=megabytes << 20),
    )


def edges(axis):
    place = lax.axis_index(axis)
    return place == 0, place == lax.axis_size(axis) - 1


def sends_high():
    even = lax.axis_index("groups") % 2 == 0
    return (lax.axis_index("pair") == 0) == even


def either(condition, put):
    @pl.when(condition)
    def _():
        put(True)

    @pl.when(jnp.logical_not(condition))
    def _():
        put(False)


def rows_at(ref, at, *lead):
    count = 1
    for size in lead:
        count *= size
    return ref[at : at + count].reshape(lead + tuple(ref.shape[1:]))


def layout(fields):
    planes, corners, spots = 0, 0, []
    for shape, deep, tall in fields:
        spots.append((planes, corners))
        planes += deep * shape[1]
        corners += deep * tall
    return spots, planes, corners


def fill_planes(ext, base, middle, low, high):
    deep, height = middle.shape[:2]
    tall = low.shape[1]
    ext[base : base + deep, :tall] = low
    ext[base : base + deep, tall : tall + height] = middle
    ext[base : base + deep, tall + height :] = high


def fill_block(ext, own, low, high, at, deep, tall):
    depth = own.shape[0]
    fill_planes(
        ext,
        deep,
        own[...],
        rows_at(low, at, depth, tall),
        rows_at(high, at, depth, tall),
    )


def clear_edges(ext, deep, tall):
    first, last = edges("narrow")
    planes, rows = ext.shape[:2]
    blank_rows = jnp.zeros((planes, tall) + ext.shape[2:], bf16)
    blank_planes = jnp.zeros((deep,) + ext.shape[1:], bf16)

    @pl.when(first)
    def _():
        ext[:, :tall] = blank_rows

    @pl.when(last)
    def _():
        ext[:, rows - tall :] = blank_rows

    first, last = edges("wide")

    @pl.when(first)
    def _():
        ext[:deep] = blank_planes

    @pl.when(last)
    def _():
        ext[planes - deep :] = blank_planes


def fill_frame(ext, own, low, high, planes, corner_low, corner_high, passed, spot, at, deep, tall):
    depth, height = own.shape[:2]
    plane_at, corner_at = spot
    count = corner_low.shape[0] // 2
    split = planes.shape[0] // 2
    fill_block(ext, own, low, high, at, deep, tall)
    near = (
        rows_at(planes, plane_at, deep, height),
        rows_at(corner_low, corner_at, deep, tall),
        rows_at(corner_high, corner_at, deep, tall),
    )
    last = passed.shape[0] - count
    far = (
        rows_at(passed, plane_at, deep, height),
        rows_at(passed, split + corner_at, deep, tall),
        rows_at(passed, last + corner_at, deep, tall),
    )

    either(sends_high(), put_sides(ext, depth, deep, near, far))
    clear_edges(ext, deep, tall)


def put_sides(ext, depth, deep, near, far):
    def put(low_is_near):
        fill_planes(ext, 0, *(near if low_is_near else far))
        fill_planes(ext, deep + depth, *(far if low_is_near else near))

    return put


def fill_columns(columns, got, frame, planes, corner_low, corner_high, spot, height, deep, tall, half):
    plane_at, corner_at = spot
    count, corners = planes.shape[0] // 2, corner_low.shape[0] // 2
    columns[...] = got[...]
    fill_planes(
        frame,
        0,
        rows_at(planes, count + plane_at, deep, height),
        rows_at(corner_low, corners + corner_at, deep, tall),
        rows_at(corner_high, corners + corner_at, deep, tall),
    )
    first, last = edges("narrow")
    blank = jnp.zeros((deep, tall) + frame.shape[2:], bf16)

    @pl.when(first)
    def _():
        frame[:, :tall] = blank

    @pl.when(last)
    def _():
        frame[:, tall + height :] = blank

    at_low = lax.axis_index("pair") == 0
    total = columns.shape[0]
    at_edge = edges("wide")

    def put(low_side):
        edge = at_edge[0] if low_side else at_edge[1]
        for layer in range(deep):
            low, high = column_values(frame[layer], half)
            chosen = jnp.where(at_low, low, high)
            chosen = jnp.where(edge, jnp.zeros_like(chosen), chosen)
            columns[layer if low_side else total - deep + layer] = chosen

    either(sends_high(), put)


def write_columns(columns, plane, low, high, lanes):
    at_low = lax.axis_index("pair") == 0
    columns[plane, :, lanes] = jnp.where(at_low, high, low)


def column_values(block, half):
    lanes = block.shape[-1]
    wide = block.astype(f32)
    if half:
        return wide[:, 0, : lanes // 2].astype(bf16), wide[:, -1, lanes // 2 :].astype(bf16)
    return wide[:, 0, :].astype(bf16), wide[:, -1, :].astype(bf16)


def shifted(values, column, step):
    columns = values.shape[1]
    spot = lax.broadcasted_iota(jnp.int32, values.shape, 1)
    if step > 0:
        return jnp.where(spot == 0, column[:, None, :], pltpu.roll(values, 1, 1))
    return jnp.where(
        spot == columns - 1, column[:, None, :], pltpu.roll(values, columns - 1, 1)
    )


def pair_columns(got, plane, lanes):
    first, last = edges("pair")
    column = got[plane, :, lanes].astype(f32)
    blank = jnp.zeros_like(column)
    return jnp.where(first, blank, column), jnp.where(last, blank, column)


def spread_pairs(taps, base, block, low, high):
    lanes = block.shape[-1] // 2
    wide = block.astype(f32)
    taps[:, :, base : base + lanes] = shifted(wide[:, :, lanes:], low, 1).astype(bf16)
    taps[:, :, base + lanes : base + 3 * lanes] = block
    taps[:, :, base + 3 * lanes : base + 4 * lanes] = shifted(
        wide[:, :, :lanes], high, -1
    ).astype(bf16)


def spread_weights(packed, tap, base, taken):
    rows, outs = taken[0].shape
    blank = jnp.zeros((rows, outs), bf16)
    for cell in range(4):
        at = base + cell * rows
        packed[tap, at : at + rows, :outs] = taken[cell] if cell < 3 else blank
        packed[tap, at : at + rows, outs:] = taken[cell - 1] if cell > 0 else blank


def conv_rows(taps, packed, depth, height):
    lanes = taps.shape[-1]
    summed = None
    for a in range(3):
        for b in range(3):
            rows = taps[a : a + depth, b : b + height].reshape(-1, lanes)
            part = jnp.dot(rows, packed[3 * a + b], preferred_element_type=f32)
            summed = part if summed is None else summed + part
    return summed


def choose_side(axis, sent, put):
    if sent.shape[0] == 1:
        at_low = lax.axis_index(axis) == 0

        @pl.when(at_low)
        def _():
            put(0, True)

        @pl.when(jnp.logical_not(at_low))
        def _():
            put(0, False)

    else:
        put(0, False)
        put(1, True)


def pack_pairs(out, cells, spread):
    pairs, lanes = out.shape[1], cells.shape[-1]
    spread[...] = cells.astype(f32)
    for odd in range(2):
        half = spread[:, pl.ds(odd, pairs, stride=2), :]
        out[:, :, odd * lanes : (odd + 1) * lanes] = half.astype(bf16)


def pack_kernel(volume, packed, spread):
    for plane in range(volume.shape[0]):
        pack_pairs(packed.at[plane], volume[plane], spread.at[plane])


def edge_kernel(sizes, *refs):
    fields, (edge_rows, handed) = refs[: len(sizes)], refs[len(sizes) :]

    def put_rows(slot, high):
        at = 0
        for field, (_, _, tall) in zip(fields, sizes):
            depth, height = field.shape[:2]
            first = height - tall if high else 0
            rows = field[:, first : first + tall]
            edge_rows[slot, at : at + depth * tall] = rows.reshape((depth * tall,) + rows.shape[2:])
            at += depth * tall

    choose_side("narrow", edge_rows, put_rows)
    either(sends_high(), lambda high: put_boundary(handed, fields, sizes, not high))


def put_boundary(out, fields, sizes, high):
    at = 0
    for field, (_, deep, _) in zip(fields, sizes):
        depth, height = field.shape[:2]
        planes = field[depth - deep :] if high else field[:deep]
        out[at : at + deep * height] = planes.reshape((deep * height,) + planes.shape[2:])
        at += deep * height


def plane_kernel(sizes, *refs):
    fields, (handed, planes, corners) = refs[: len(sizes)], refs[len(sizes) :]
    spots, count, few = layout(sizes)
    planes[count:] = handed[...]
    either(sends_high(), lambda high: put_boundary(planes, fields, sizes, high))

    def put(slot, high):
        for (shape, deep, tall), (plane_at, corner_at) in zip(sizes, spots):
            height = shape[1]
            first = height - tall if high else 0
            for part in range(2):
                for layer in range(deep):
                    source = part * count + plane_at + layer * height + first
                    target = part * few + corner_at + layer * tall
                    corners[slot, target : target + tall] = planes[source : source + tall]

    choose_side("narrow", corners, put)


def pass_kernel(sizes, half, *refs):
    own, low, high, planes, corner_low, corner_high, passed, columns, ext = refs
    (shape, deep, tall), (_, count, few) = sizes[0], layout(sizes)
    depth, height = shape[:2]
    passed[:count] = planes[count:]
    passed[count : count + few] = corner_low[few:]
    passed[passed.shape[0] - few :] = corner_high[few:]
    fill_block(ext, own, low, high, 0, deep, tall)
    near = (
        rows_at(planes, 0, deep, height),
        rows_at(corner_low, 0, deep, tall),
        rows_at(corner_high, 0, deep, tall),
    )
    blank = tuple(jnp.zeros_like(part) for part in near)
    either(sends_high(), put_sides(ext, depth, deep, near, blank))
    clear_edges(ext, deep, tall)
    for plane in range(ext.shape[0]):
        left, right = column_values(ext[plane], half)
        write_columns(columns, plane, left, right, slice(None))


def encode_kernel(
    own,
    low,
    high,
    planes,
    corner_low,
    corner_high,
    passed,
    got,
    weight,
    bias,
    down,
    down_bias,
    encoded,
    coarse,
    ext,
    columns_in,
    frame,
    taps,
    packed,
):
    lanes = ext.shape[-1]
    spot = (0, 0)
    fill_frame(ext, own, low, high, planes, corner_low, corner_high, passed, spot, 0, 1, 1)
    fill_columns(
        columns_in, got, frame, planes, corner_low, corner_high, spot, own.shape[1], 1, 1, True
    )
    for plane in range(ext.shape[0]):
        before, after = pair_columns(columns_in, plane, slice(None))
        spread_pairs(taps.at[plane], 0, ext[plane], before, after)
    for tap in range(9):
        spread_weights(packed, tap, 0, [weight[tap, c] for c in range(3)])
    depth, height, columns, _ = encoded.shape
    deep, tall = coarse.shape[:2]
    summed = conv_rows(taps, packed, depth, height)
    fine = leaky_relu(summed + jnp.tile(bias[...], (1, 2))).astype(bf16)
    fine = fine.reshape(deep, 2, tall, 2, columns, lanes)
    encoded[...] = fine.reshape(encoded.shape)
    lifted = None
    for a in range(2):
        for b in range(2):
            part = jnp.dot(
                fine[:, a, :, b].reshape(-1, lanes), down[2 * a + b], preferred_element_type=f32
            )
            lifted = part if lifted is None else lifted + part
    coarse[...] = leaky_relu(lifted + down_bias[...]).astype(bf16).reshape(coarse.shape)


def bottom_kernel(
    sizes,
    coarse,
    encoded,
    low,
    high,
    planes,
    corner_low,
    corner_high,
    passed,
    got,
    weight,
    bias,
    up,
    up_bias,
    raised,
    encoded_ext,
    columns,
    coarse_ext,
    columns_in,
    frame,
    taps,
):
    lanes = coarse_ext.shape[-1]
    spots = layout(sizes)[0]
    at = 0
    for ext, own, spot, (shape, deep, tall) in zip(
        (coarse_ext, encoded_ext), (coarse, encoded), spots, sizes
    ):
        fill_frame(
            ext, own, low, high, planes, corner_low, corner_high, passed, spot, at, deep, tall
        )
        at += shape[0] * tall
    (shape, deep, tall), spot = sizes[0], spots[0]
    fill_columns(
        columns_in, got, frame, planes, corner_low, corner_high, spot, shape[1], deep, tall, False
    )
    for plane in range(coarse_ext.shape[0]):
        before, after = pair_columns(columns_in, plane, slice(None))
        block = coarse_ext[plane]
        wide = block.astype(f32)
        taps[plane, :, :, :lanes] = shifted(wide, before, 1).astype(bf16)
        taps[plane, :, :, lanes : 2 * lanes] = block
        taps[plane, :, :, 2 * lanes :] = shifted(wide, after, -1).astype(bf16)
    deep, _, tall, _, count, _ = raised.shape
    summed = conv_rows(taps, weight, deep, tall)
    bottom = leaky_relu(summed + bias[...]).astype(bf16)
    both = jnp.tile(up_bias[...], (1, 2))
    for a in range(2):
        for b in range(2):
            matrix = jnp.concatenate([up[2 * a + b, 0], up[2 * a + b, 1]], axis=-1)
            lifted = jnp.dot(bottom, matrix, preferred_element_type=f32) + both
            raised[:, a, :, b] = lifted.astype(bf16).reshape(deep, tall, count, lanes)
    blank_plane = jnp.zeros(raised.shape[1:], bf16)
    blank_row = jnp.zeros((deep, 2, 2, count, lanes), bf16)
    first, last = edges("narrow")

    @pl.when(first)
    def _():
        raised[:, :, 0] = blank_row

    @pl.when(last)
    def _():
        raised[:, :, tall - 1] = blank_row

    first, last = edges("wide")

    @pl.when(first)
    def _():
        raised[0] = blank_plane

    @pl.when(last)
    def _():
        raised[deep - 1] = blank_plane

    planes, height = encoded_ext.shape[:2]
    half = lanes // 2
    for plane in range(planes):
        z, a = (plane + 1) // 2, (plane + 1) % 2
        whole = raised[z, a].reshape(2 * tall, count, lanes)[1 : 1 + height]
        low, high = column_values(whole, True)
        write_columns(columns, plane, low, high, slice(0, half))
        low, high = column_values(encoded_ext[plane], True)
        write_columns(columns, plane, low, high, slice(half, lanes))


def decode_kernel(
    raised, encoded_ext, columns_in, weight, bias, decoded, taps, packed, spread
):
    planes, height, columns, lanes = encoded_ext.shape
    half = lanes // 2
    for plane in range(planes):
        low, high = pair_columns(columns_in, plane, slice(0, half))
        spread_pairs(taps.at[plane], 0, raised[plane + 1, 1 : 1 + height], low, high)
        low, high = pair_columns(columns_in, plane, slice(half, lanes))
        spread_pairs(taps.at[plane], 2 * lanes, encoded_ext[plane], low, high)
    for tap in range(9):
        spread_weights(packed, tap, 0, [weight[tap, c, :half] for c in range(3)])
        spread_weights(packed, tap, 2 * lanes, [weight[tap, c, half:] for c in range(3)])
    depth, rows, _, outs = decoded.shape
    summed = conv_rows(taps, packed, depth, rows)
    summed = leaky_relu(summed + jnp.tile(bias[...], (1, 2)))
    for odd in range(2):
        half = summed[:, odd * outs : (odd + 1) * outs].reshape(depth, rows, columns, outs)
        spread[:, :, pl.ds(odd, columns, stride=2), :] = half
    decoded[...] = spread[...].astype(bf16)


def exchange(fields, halos, half):
    sizes = [(field.shape, deep, tall) for field, (deep, tall) in zip(fields, halos)]
    _, planes, corners = layout(sizes)
    cells = fields[0].shape[2:]
    sides = sides_of("narrow")
    swap = [(0, 1), (1, 0)]
    rows = sum(shape[0] * tall for shape, _, tall in sizes)
    edge_rows, handed = call(
        functools.partial(edge_kernel, sizes), [(sides, rows) + cells, (planes,) + cells], (), 8
    )(*fields)
    handed = lax.ppermute(handed, "pair", swap)
    low, high = line_exchange("narrow", edge_rows)
    ring, corner = call(
        functools.partial(plane_kernel, sizes),
        [(2 * planes,) + cells, (sides, 2 * corners) + cells],
        (),
        8,
    )(*fields, handed)
    ring = ring_exchange(ring)
    corner_low, corner_high = corner_exchange(corner)
    received = (low, high, ring, corner_low, corner_high)
    shape, deep, tall = sizes[0]
    framed = (shape[0] + 2 * deep, shape[1] + 2 * tall)
    lanes = cells[1] // 2 if half else cells[1]
    passed, columns = call(
        functools.partial(pass_kernel, sizes, half),
        [(planes + sides * corners,) + cells, framed + (lanes,)],
        [pltpu.VMEM(framed + cells, bf16)],
        8,
    )(fields[0], *received)
    passed = lax.ppermute(passed, "pair", swap)
    columns = lax.ppermute(columns, "pair", swap)
    return sizes, received + (passed, columns)


def body(
    volume, w_encode, b_encode, w_down, b_down, w_bottom, b_bottom, w_up, b_up, w_decode, b_decode
):
    depth, height, width, skip = volume.shape
    deep_width = w_down.shape[4]
    half_depth, half_height, pairs = depth // 2, height // 2, width // 2
    lanes = 2 * skip
    framed = (depth + 2, height + 2)
    coarse_framed = (half_depth + 4, half_height + 4)

    (packed,) = call(
        pack_kernel,
        [(depth, height, pairs, lanes)],
        [pltpu.VMEM((depth, height, width, skip), f32)],
        8,
    )(volume)
    _, received = exchange([packed], [(1, 1)], True)
    encoded, coarse = call(
        encode_kernel,
        [(depth, height, pairs, lanes), (half_depth, half_height, pairs, deep_width)],
        [
            pltpu.VMEM(framed + (pairs, lanes), bf16),
            pltpu.VMEM(framed + (skip,), bf16),
            pltpu.VMEM((1, height + 2, pairs, lanes), bf16),
            pltpu.VMEM(framed + (pairs, 2 * lanes), bf16),
            pltpu.VMEM((9, 2 * lanes, lanes), bf16),
        ],
    )(
        packed,
        *received,
        w_encode.reshape(9, 3, skip, skip),
        b_encode.reshape(1, skip),
        w_down.reshape(4, lanes, deep_width),
        b_down.reshape(1, deep_width),
    )

    sizes, received = exchange([coarse, encoded], [(2, 2), (1, 1)], False)
    raised, encoded_ext, columns = call(
        functools.partial(bottom_kernel, sizes),
        [
            (half_depth + 2, 2, half_height + 2, 2, pairs, lanes),
            framed + (pairs, lanes),
            framed + (lanes,),
        ],
        [
            pltpu.VMEM(coarse_framed + (pairs, deep_width), bf16),
            pltpu.VMEM(coarse_framed + (deep_width,), bf16),
            pltpu.VMEM((2, half_height + 4, pairs, deep_width), bf16),
            pltpu.VMEM(coarse_framed + (pairs, 3 * deep_width), bf16),
        ],
    )(
        coarse,
        encoded,
        *received,
        w_bottom.reshape(9, 3 * deep_width, deep_width),
        b_bottom.reshape(1, deep_width),
        w_up.reshape(4, 2, deep_width, skip),
        b_up.reshape(1, skip),
    )
    columns = lax.ppermute(columns, "pair", [(0, 1), (1, 0)])

    (decoded,) = call(
        decode_kernel,
        [(depth, height, width, skip)],
        [
            pltpu.VMEM(framed + (pairs, 4 * lanes), bf16),
            pltpu.VMEM((9, 4 * lanes, lanes), bf16),
            pltpu.VMEM((depth, height, width, skip), f32),
        ],
    )(
        raised.reshape(depth + 4, height + 4, pairs, lanes),
        encoded_ext,
        columns,
        w_decode.reshape(9, 3, lanes, skip),
        b_decode.reshape(1, skip),
    )
    return decoded


def solution(mesh):
    return jax.shard_map(
        body,
        mesh=mesh,
        in_specs=(
            P(("groups", "wide"), "narrow", "pair", None),
            P(),
            P(),
            P(),
            P(),
            P(),
            P(),
            P(),
            P(),
            P(),
            P(),
        ),
        out_specs=P(("groups", "wide"), "narrow", "pair", None),
        check_vma=False,
    )
```

time: 40.7 us -> 37.5 us (0.921)
  waiting for transfers between devices: 18.9 us -> 11.4 us
  starting transfers between devices: 9.29 us -> 13.2 us
    ppermute x4 -> x11, starting transfers between devices: 4.35 us -> 11.1 us  [the longest x2 4.53 us: ring_exchange(): return lax.ppermute(sent, ('groups', 'wide', 'pair'), pairs)]
    ppermute x5 -> x2, waiting for transfers between devices: 8.78 us -> 3.51 us  [line_exchange(): got = lax.ppermute(sent[0], axis, [(0, 1), (1, 0)])]
    ppermute x5 -> x2, starting transfers between devices: 4.94 us -> 2.02 us  [line_exchange(): got = lax.ppermute(sent[0], axis, [(0, 1), (1, 0)])]
    ppermute x4 -> x11, waiting for transfers between devices: 10.2 us -> 7.94 us  [the longest x2 3.24 us: move(): return lax.ppermute(array, ('groups', 'wide', 'narrow', 'pair'), pairs)]
    pallas_call x7 -> x8, Pallas kernels: 8.5 us -> 8.78 us  [the longest x1 5.22 us: body(): call(decode_kernel, [(depth, height, width, skip)], [pltpu.VMEM(framed +...]
  transfers between devices with their start and end apart: 9 -> 13, of which waited for: 9 -> 9; matrix products, arithmetic and copies ran while one was open for 0% -> 0% of each run, Pallas kernels for 0% -> 0%
where the time goes in v4:
time: 37.5 us; the launch traced here: 37.3 us
  starting transfers between devices  13.2 us (35%)
  Pallas kernels  11.6 us (31%)
  waiting for transfers between devices  11.4 us (30%)
  local copies, waits for them, and re-layouts  1.04 us (3%)
    pallas_call x1, Pallas kernels, body(): call(decode_kernel, [(depth, height, width, skip)], [pltpu.VMEM(framed +...  5.22 us
    ppermute x2, starting transfers between devices, ring_exchange(): return lax.ppermute(sent, ('groups', 'wide', 'pair'), pairs)  4.53 us
    ppermute x2, starting transfers between devices, move(): return lax.ppermute(array, ('groups', 'wide', 'narrow', 'pair'), pairs)  4.16 us
    ppermute x2, waiting for transfers between devices, line_exchange(): got = lax.ppermute(sent[0], axis, [(0, 1), (1, 0)])  3.51 us
    ppermute x2, waiting for transfers between devices, move(): return lax.ppermute(array, ('groups', 'wide', 'narrow', 'pair'), pairs)  3.24 us
    pallas_call x1, Pallas kernels, body(): call(functools.partial(bottom_kernel, sizes), [(half_depth + 2, 2, half_h...  3.06 us
    pallas_call x1, Pallas kernels, body(): call(encode_kernel, [(depth, height, pairs, lanes), (half_depth, half_hei...  2.65 us
    ppermute x2, starting transfers between devices, line_exchange(): got = lax.ppermute(sent[0], axis, [(0, 1), (1, 0)])  2.02 us
  transfers between devices with their start and end apart: 13, of which 9 were waited for; matrix products, arithmetic and copies ran while one was open for 0% of the time, Pallas kernels for 0%

profile of v4, /device:TPU:0, one launch (start us, length us, event | category | flops | bytes accessed | tf_op | source)
XLA Modules:
  0.0 37.3 jit_solution(10593941271233343351)
XLA Ops:
  0.0 0.0 copy-start.5
  0.0 1.0 %copy-done.5 = bf16[6,8,32,128]{3,2,1,0:T(8,128)(2,1)S(1)} copy-done((bf16[6,8,32,128]{3,2,1,0:T(8,128)(2,1)S(1)}, bf16[6,8,32,128]{3,2,1,0:T(8,128)(2,1)}, u32[]{:S(2)}) %copy-start.5) | copy-done | bytes 393240
  1.0 0.1 shard_map.109.refs_0_.own
  1.2 0.6 %collective-permute-start.1 = (bf16[8,16,256]{2,1,0:T(8,128)(2,1)S(1)}, bf16[8,16,256]{2,1,0:T(8,128)(2,1)S(1)}, u32[]{:S(2)}, u32[]{:S(2)}) collective-permute-start(bf16[8,16,256]{2,1,0:T(8,128)(2,1)S(1)} %get-tuple-element.23), channel_id=1, source_target_pairs={{0,1},{1,0},{2,3},{3,2},{4,5},{5,4},{6,7},{7,6},{8,9},{9,8},{10,11... | collective-permute-start | bytes 196616 | tf_op jit(solution)/shard_map/ppermute | solution.py:550
  1.7 0.9 %collective-permute-done.1.refs_1_ = bf16[8,16,256]{2,1,0:T(8,128)(2,1)S(1)} collective-permute-done((bf16[8,16,256]{2,1,0:T(8,128)(2,1)S(1)}, bf16[8,16,256]{2,1,0:T(8,128)(2,1)S(1)}, u32[]{:S(2)}, u32[]{:S(2)}) %collective-permute-start.1) | collective-permute-done | bytes 65568 | tf_op jit(solution)/shard_map/ppermute | solution.py:550
  2.7 3.0 %collective-permute-start.2 = (bf16[16,16,256]{2,1,0:T(8,128)(2,1)S(1)}, bf16[16,16,256]{2,1,0:T(8,128)(2,1)S(1)}, u32[]{:S(2)}, u32[]{:S(2)}) collective-permute-start(bf16[16,16,256]{2,1,0:T(8,128)(2,1)S(1)} %get-tuple-element.24), channel_id=1, source_target_pairs={{0,4},{4,8},{8,12},{12,28},{28,24},{24,20},{20,16},{16,0},{1,17},{... | collective-permute-start | bytes 393224 | tf_op jit(solution)/shard_map/ppermute | solution.py:50
  5.6 1.5 %collective-permute-start = (bf16[6,16,256]{2,1,0:T(8,128)(2,1)S(1)}, bf16[6,16,256]{2,1,0:T(8,128)(2,1)S(1)}, u32[]{:S(2)}, u32[]{:S(2)}) collective-permute-start(bf16[6,16,256]{2,1,0:T(8,128)(2,1)S(1)} %bitcast.22), channel_id=1, source_target_pairs={{0,2},{2,0},{1,3},{3,1},{4,6},{6,4},{5,7},{7,5},{8,10},{10,8},{9,1... | collective-permute-start | bytes 147464 | tf_op jit(solution)/shard_map/ppermute | solution.py:26
  7.1 0.0 copy-start.2
  7.1 0.0 copy-start.3
  7.1 1.6 %collective-permute-start.3 = (bf16[2,16,256]{2,1,0:T(8,128)(2,1)S(1)}, bf16[2,16,256]{2,1,0:T(8,128)(2,1)S(1)}, u32[]{:S(2)}, u32[]{:S(2)}) collective-permute-start(bf16[2,16,256]{2,1,0:T(8,128)(2,1)S(1)} %bitcast.23), channel_id=1, source_target_pairs={{0,6},{2,4},{4,10},{6,8},{8,14},{10,12},{12,30},{14,28},{28,26},{3... | collective-permute-start | bytes 49160 | tf_op jit(solution)/shard_map/ppermute | solution.py:64
  8.7 1.0 %collective-permute-done.refs_1_.refs_2_.low.high = bf16[6,16,256]{2,1,0:T(8,128)(2,1)S(1)} collective-permute-done((bf16[6,16,256]{2,1,0:T(8,128)(2,1)S(1)}, bf16[6,16,256]{2,1,0:T(8,128)(2,1)S(1)}, u32[]{:S(2)}, u32[]{:S(2)}) %collective-permute-start) | collective-permute-done | bytes 49184 | tf_op jit(solution)/shard_map/ppermute | solution.py:26
  9.7 2.2 %collective-permute-done.3.refs_4_.refs_5_.corner_low.corner_high = bf16[2,16,256]{2,1,0:T(8,128)(2,1)S(1)} collective-permute-done((bf16[2,16,256]{2,1,0:T(8,128)(2,1)S(1)}, bf16[2,16,256]{2,1,0:T(8,128)(2,1)S(1)}, u32[]{:S(2)}, u32[]{:S(2)}) %collective-permute-start.3) | collective-permute-done | bytes 16416 | tf_op jit(solution)/shard_map/ppermute | solution.py:64
  11.9 0.0 collective-permute-done.2.refs_3_.planes
  11.9 0.1 shard_map.112
  12.0 0.1 collective-permute-start.4
  12.1 0.5 %collective-permute-start.5 = (bf16[8,10,128]{2,1,0:T(8,128)(2,1)S(1)}, bf16[8,10,128]{2,1,0:T(8,128)(2,1)S(1)}, u32[]{:S(2)}, u32[]{:S(2)}) collective-permute-start(bf16[8,10,128]{2,1,0:T(8,128)(2,1)S(1)} %get-tuple-element.27), channel_id=1, source_target_pairs={{0,1},{1,0},{2,3},{3,2},{4,5},{5,4},{6,7},{7,6},{8,9},{9,8},{10,11... | collective-permute-start | bytes 61448 | tf_op jit(solution)/shard_map/ppermute | solution.py:571
  12.6 0.9 %collective-permute-done.5.got = bf16[8,10,128]{2,1,0:T(8,128)(2,1)S(1)} collective-permute-done((bf16[8,10,128]{2,1,0:T(8,128)(2,1)S(1)}, bf16[8,10,128]{2,1,0:T(8,128)(2,1)S(1)}, u32[]{:S(2)}, u32[]{:S(2)}) %collective-permute-start.5) | collective-permute-done | bytes 20512 | tf_op jit(solution)/shard_map/ppermute | solution.py:571
  13.5 0.0 collective-permute-done.4.passed
  13.5 0.0 copy-done.2
  13.5 0.0 copy-done.3
  13.5 0.0 copy-done.6
  13.5 0.0 copy-done.8
  13.5 2.6 %shard_map.113 = (bf16[6,8,16,256]{3,2,1,0:T(8,128)(2,1)S(1)}, bf16[3,4,16,256]{3,2,1,0:T(8,128)(2,1)S(1)}) custom-call(bf16[6,8,16,256]{3,2,1,0:T(8,128)(2,1)S(1)} %shard_map.109.refs_0_.own, bf16[6,16,256]{2,1,0:T(8,128)(2,1)S(1)} %collective-permute-done.refs_1_.refs_2_.low.high, bf16[6,16,256]{2,1,0:T(8,128)(2,1)S(1)} %collective-permute-done.refs_1_.refs_2_.low.high, ...), custom_call_target="tpu_custom_call" | custom-call | flops 4000000000 | bytes 1000000 | tf_op jit(solution)/shard_map/pallas_call | solution.py:592
  16.2 0.4 %collective-permute-start.7 = (bf16[16,16,256]{2,1,0:T(8,128)(2,1)S(1)}, bf16[16,16,256]{2,1,0:T(8,128)(2,1)S(1)}, u32[]{:S(2)}, u32[]{:S(2)}) collective-permute-start(bf16[16,16,256]{2,1,0:T(8,128)(2,1)S(1)} %get-tuple-element.31), channel_id=1, source_target_pairs={{0,1},{1,0},{2,3},{3,2},{4,5},{5,4},{6,7},{7,6},{8,9},{9,8},{10,11... | collective-permute-start | bytes 393224 | tf_op jit(solution)/shard_map/ppermute | solution.py:550
  16.6 1.0 %collective-permute-done.7.refs_2_ = bf16[16,16,256]{2,1,0:T(8,128)(2,1)S(1)} collective-permute-done((bf16[16,16,256]{2,1,0:T(8,128)(2,1)S(1)}, bf16[16,16,256]{2,1,0:T(8,128)(2,1)S(1)}, u32[]{:S(2)}, u32[]{:S(2)}) %collective-permute-start.7) | collective-permute-done | bytes 131104 | tf_op jit(solution)/shard_map/ppermute | solution.py:550
  17.7 1.6 %collective-permute-start.8 = (bf16[32,16,256]{2,1,0:T(8,128)(2,1)S(1)}, bf16[32,16,256]{2,1,0:T(8,128)(2,1)S(1)}, u32[]{:S(2)}, u32[]{:S(2)}) collective-permute-start(bf16[32,16,256]{2,1,0:T(8,128)(2,1)S(1)} %get-tuple-element.32), channel_id=1, source_target_pairs={{0,4},{4,8},{8,12},{12,28},{28,24},{24,20},{20,16},{16,0},{1,17},{... | collective-permute-start | bytes 786440 | tf_op jit(solution)/shard_map/ppermute | solution.py:50
  19.3 0.5 %collective-permute-start.6 = (bf16[12,16,256]{2,1,0:T(8,128)(2,1)S(1)}, bf16[12,16,256]{2,1,0:T(8,128)(2,1)S(1)}, u32[]{:S(2)}, u32[]{:S(2)}) collective-permute-start(bf16[12,16,256]{2,1,0:T(8,128)(2,1)S(1)} %bitcast.20), channel_id=1, source_target_pairs={{0,2},{2,0},{1,3},{3,1},{4,6},{6,4},{5,7},{7,5},{8,10},{10,8},{9,1... | collective-permute-start | bytes 294920 | tf_op jit(solution)/shard_map/ppermute | solution.py:26
  19.8 2.6 %collective-permute-start.9 = (bf16[10,16,256]{2,1,0:T(8,128)(2,1)S(1)}, bf16[10,16,256]{2,1,0:T(8,128)(2,1)S(1)}, u32[]{:S(2)}, u32[]{:S(2)}) collective-permute-start(bf16[10,16,256]{2,1,0:T(8,128)(2,1)S(1)} %bitcast.21), channel_id=1, source_target_pairs={{0,6},{2,4},{4,10},{6,8},{8,14},{10,12},{12,30},{14,28},{28,26},{3... | collective-permute-start | bytes 245768 | tf_op jit(solution)/shard_map/ppermute | solution.py:64
  22.4 2.5 %collective-permute-done.6.refs_1_.refs_2_.low.high = bf16[12,16,256]{2,1,0:T(8,128)(2,1)S(1)} collective-permute-done((bf16[12,16,256]{2,1,0:T(8,128)(2,1)S(1)}, bf16[12,16,256]{2,1,0:T(8,128)(2,1)S(1)}, u32[]{:S(2)}, u32[]{:S(2)}) %collective-permute-start.6) | collective-permute-done | bytes 98336 | tf_op jit(solution)/shard_map/ppermute | solution.py:26
  24.9 1.1 %collective-permute-done.9.refs_4_.refs_5_.corner_low.corner_high = bf16[10,16,256]{2,1,0:T(8,128)(2,1)S(1)} collective-permute-done((bf16[10,16,256]{2,1,0:T(8,128)(2,1)S(1)}, bf16[10,16,256]{2,1,0:T(8,128)(2,1)S(1)}, u32[]{:S(2)}, u32[]{:S(2)}) %collective-permute-start.9) | collective-permute-done | bytes 81952 | tf_op jit(solution)/shard_map/ppermute | solution.py:64
  25.9 0.0 collective-permute-done.8.refs_3_.planes
  26.0 0.2 shard_map.116
  26.2 0.1 collective-permute-start.10
  26.2 0.5 %collective-permute-start.11 = (bf16[7,8,256]{2,1,0:T(8,128)(2,1)S(1)}, bf16[7,8,256]{2,1,0:T(8,128)(2,1)S(1)}, u32[]{:S(2)}, u32[]{:S(2)}) collective-permute-start(bf16[7,8,256]{2,1,0:T(8,128)(2,1)S(1)} %get-tuple-element.35), channel_id=1, source_target_pairs={{0,1},{1,0},{2,3},{3,2},{4,5},{5,4},{6,7},{7,6},{8,9},{9,8},{10,11... | collective-permute-start | bytes 86024 | tf_op jit(solution)/shard_map/ppermute | solution.py:571
  26.7 0.9 %collective-permute-done.11.got = bf16[7,8,256]{2,1,0:T(8,128)(2,1)S(1)} collective-permute-done((bf16[7,8,256]{2,1,0:T(8,128)(2,1)S(1)}, bf16[7,8,256]{2,1,0:T(8,128)(2,1)S(1)}, u32[]{:S(2)}, u32[]{:S(2)}) %collective-permute-start.11) | collective-permute-done | bytes 28704 | tf_op jit(solution)/shard_map/ppermute | solution.py:571
  27.7 0.0 collective-permute-done.10.passed
  27.7 0.0 copy-done
  27.7 0.0 copy-done.4
  27.7 0.0 copy-done.7
  27.7 0.0 copy-done.9
  27.7 0.0 copy-start.1
  27.7 0.0 copy-start.10
  27.7 3.1 %shard_map.117 = (bf16[5,2,6,2,16,256]{5,4,3,2,1,0:T(8,128)(2,1)S(1)}, bf16[8,10,16,256]{3,2,1,0:T(8,128)(2,1)S(1)}, bf16[8,10,256]{2,1,0:T(8,128)(2,1)S(1)}) custom-call(bf16[3,4,16,256]{3,2,1,0:T(8,128)(2,1)S(1)} %get-tuple-element.28.refs_0_.coarse, bf16[6,8,16,256]{3,2,1,0:T(8,128)(2,1)S(1)} %get-tuple-element.29.refs_1_.encoded, ...), custom_call_target="tpu_custom_call" | custom-call | flops 4000000000 | bytes 1000000 | tf_op jit(solution)/shard_map/pallas_call | solution.py:612
  30.8 0.3 collective-permute-start.12
  31.1 1.0 %collective-permute-done.12.columns_in = bf16[8,10,256]{2,1,0:T(8,128)(2,1)S(1)} collective-permute-done((bf16[8,10,256]{2,1,0:T(8,128)(2,1)S(1)}, bf16[8,10,256]{2,1,0:T(8,128)(2,1)S(1)}, u32[]{:S(2)}, u32[]{:S(2)}) %collective-permute-start.12) | collective-permute-done | bytes 40992 | tf_op jit(solution)/shard_map/ppermute | solution.py:634
  32.1 0.0 copy-done.1
  32.1 0.0 copy-done.10
  32.1 5.2 %shard_map.118 = bf16[6,8,32,128]{3,2,1,0:T(8,128)(2,1)} custom-call(bf16[10,12,16,256]{3,2,1,0:T(8,128)(2,1)S(1)} %bitcast.29, bf16[8,10,16,256]{3,2,1,0:T(8,128)(2,1)S(1)} %get-tuple-element.37.encoded_ext, bf16[8,10,256]{2,1,0:T(8,128)(2,1)S(1)} %collective-permute-done.12.columns_in, bf16[9,3,256,128]{3,2,1,0:T(8,128)(2,1)S(1)} %bitcast.16, ...), custom_call_target="tpu_custom_call" | custom-call | flops 4000000000 | bytes 1000000 | tf_op jit(solution)/shard_map/pallas_call | solution.py:636
  (10 shorter events, 0.2 us)
Async XLA Ops:
  0.0 1.0 %copy-start.5 = (bf16[6,8,32,128]{3,2,1,0:T(8,128)(2,1)S(1)}, bf16[6,8,32,128]{3,2,1,0:T(8,128)(2,1)}, u32[]{:S(2)}) copy-start(bf16[6,8,32,128]{3,2,1,0:T(8,128)(2,1)} %volume.1) | copy-start | bytes 1179652
  1.2 1.5 %collective-permute-start.1 = (bf16[8,16,256]{2,1,0:T(8,128)(2,1)S(1)}, bf16[8,16,256]{2,1,0:T(8,128)(2,1)S(1)}, u32[]{:S(2)}, u32[]{:S(2)}) collective-permute-start(bf16[8,16,256]{2,1,0:T(8,128)(2,1)S(1)} %get-tuple-element.23), channel_id=1, source_target_pairs={{0,1},{1,0},{2,3},{3,2},{4,5},{5,4},{6,7},{7,6},{8,9},{9,8},{10,11... | collective-permute-start | bytes 196616 | tf_op jit(solution)/shard_map/ppermute | solution.py:550
  2.7 9.2 %collective-permute-start.2 = (bf16[16,16,256]{2,1,0:T(8,128)(2,1)S(1)}, bf16[16,16,256]{2,1,0:T(8,128)(2,1)S(1)}, u32[]{:S(2)}, u32[]{:S(2)}) collective-permute-start(bf16[16,16,256]{2,1,0:T(8,128)(2,1)S(1)} %get-tuple-element.24), channel_id=1, source_target_pairs={{0,4},{4,8},{8,12},{12,28},{28,24},{24,20},{20,16},{16,0},{1,17},{... | collective-permute-start | bytes 393224 | tf_op jit(solution)/shard_map/ppermute | solution.py:50
  5.6 4.1 %collective-permute-start = (bf16[6,16,256]{2,1,0:T(8,128)(2,1)S(1)}, bf16[6,16,256]{2,1,0:T(8,128)(2,1)S(1)}, u32[]{:S(2)}, u32[]{:S(2)}) collective-permute-start(bf16[6,16,256]{2,1,0:T(8,128)(2,1)S(1)} %bitcast.22), channel_id=1, source_target_pairs={{0,2},{2,0},{1,3},{3,1},{4,6},{6,4},{5,7},{7,5},{8,10},{10,8},{9,1... | collective-permute-start | bytes 147464 | tf_op jit(solution)/shard_map/ppermute | solution.py:26
  7.1 6.4 %copy-start.2 = (bf16[3,3,3,128,128]{4,3,2,1,0:T(8,128)(2,1)S(1)}, bf16[3,3,3,128,128]{4,3,2,1,0:T(8,128)(2,1)}, u32[]{:S(2)}) copy-start(bf16[3,3,3,128,128]{4,3,2,1,0:T(8,128)(2,1)} %param.12) | copy-start | bytes 2654212
  7.1 6.4 %copy-start.3 = (bf16[2,2,2,128,256]{4,3,2,1,0:T(8,128)(2,1)S(1)}, bf16[2,2,2,128,256]{4,3,2,1,0:T(8,128)(2,1)}, u32[]{:S(2)}) copy-start(bf16[2,2,2,128,256]{4,3,2,1,0:T(8,128)(2,1)} %param.14) | copy-start | bytes 1572868
  7.1 6.4 %copy-start.6 = (f32[256]{0:T(256)S(1)}, f32[256]{0:T(256)}, u32[]{:S(2)}) copy-start(f32[256]{0:T(256)} %param.15) | copy-start | bytes 3076
  7.1 6.4 %copy-start.8 = (f32[128]{0:T(128)S(1)}, f32[128]{0:T(128)}, u32[]{:S(2)}) copy-start(f32[128]{0:T(128)} %param.13) | copy-start | bytes 1540
  7.1 4.8 %collective-permute-start.3 = (bf16[2,16,256]{2,1,0:T(8,128)(2,1)S(1)}, bf16[2,16,256]{2,1,0:T(8,128)(2,1)S(1)}, u32[]{:S(2)}, u32[]{:S(2)}) collective-permute-start(bf16[2,16,256]{2,1,0:T(8,128)(2,1)S(1)} %bitcast.23), channel_id=1, source_target_pairs={{0,6},{2,4},{4,10},{6,8},{8,14},{10,12},{12,30},{14,28},{28,26},{3... | collective-permute-start | bytes 49160 | tf_op jit(solution)/shard_map/ppermute | solution.py:64
  12.0 1.4 %collective-permute-start.4 = (bf16[9,16,256]{2,1,0:T(8,128)(2,1)S(1)}, bf16[9,16,256]{2,1,0:T(8,128)(2,1)S(1)}, u32[]{:S(2)}, u32[]{:S(2)}) collective-permute-start(bf16[9,16,256]{2,1,0:T(8,128)(2,1)S(1)} %get-tuple-element.26), channel_id=1, source_target_pairs={{0,1},{1,0},{2,3},{3,2},{4,5},{5,4},{6,7},{7,6},{8,9},{9,8},{10,11... | collective-permute-start | bytes 221192 | tf_op jit(solution)/shard_map/ppermute | solution.py:570
  12.1 1.4 %collective-permute-start.5 = (bf16[8,10,128]{2,1,0:T(8,128)(2,1)S(1)}, bf16[8,10,128]{2,1,0:T(8,128)(2,1)S(1)}, u32[]{:S(2)}, u32[]{:S(2)}) collective-permute-start(bf16[8,10,128]{2,1,0:T(8,128)(2,1)S(1)} %get-tuple-element.27), channel_id=1, source_target_pairs={{0,1},{1,0},{2,3},{3,2},{4,5},{5,4},{6,7},{7,6},{8,9},{9,8},{10,11... | collective-permute-start | bytes 61448 | tf_op jit(solution)/shard_map/ppermute | solution.py:571
  16.2 1.4 %collective-permute-start.7 = (bf16[16,16,256]{2,1,0:T(8,128)(2,1)S(1)}, bf16[16,16,256]{2,1,0:T(8,128)(2,1)S(1)}, u32[]{:S(2)}, u32[]{:S(2)}) collective-permute-start(bf16[16,16,256]{2,1,0:T(8,128)(2,1)S(1)} %get-tuple-element.31), channel_id=1, source_target_pairs={{0,1},{1,0},{2,3},{3,2},{4,5},{5,4},{6,7},{7,6},{8,9},{9,8},{10,11... | collective-permute-start | bytes 393224 | tf_op jit(solution)/shard_map/ppermute | solution.py:550
  17.7 8.3 %collective-permute-start.8 = (bf16[32,16,256]{2,1,0:T(8,128)(2,1)S(1)}, bf16[32,16,256]{2,1,0:T(8,128)(2,1)S(1)}, u32[]{:S(2)}, u32[]{:S(2)}) collective-permute-start(bf16[32,16,256]{2,1,0:T(8,128)(2,1)S(1)} %get-tuple-element.32), channel_id=1, source_target_pairs={{0,4},{4,8},{8,12},{12,28},{28,24},{24,20},{20,16},{16,0},{1,17},{... | collective-permute-start | bytes 786440 | tf_op jit(solution)/shard_map/ppermute | solution.py:50
  19.3 5.6 %collective-permute-start.6 = (bf16[12,16,256]{2,1,0:T(8,128)(2,1)S(1)}, bf16[12,16,256]{2,1,0:T(8,128)(2,1)S(1)}, u32[]{:S(2)}, u32[]{:S(2)}) collective-permute-start(bf16[12,16,256]{2,1,0:T(8,128)(2,1)S(1)} %bitcast.20), channel_id=1, source_target_pairs={{0,2},{2,0},{1,3},{3,1},{4,6},{6,4},{5,7},{7,5},{8,10},{10,8},{9,1... | collective-permute-start | bytes 294920 | tf_op jit(solution)/shard_map/ppermute | solution.py:26
  19.8 7.9 %copy-start = (bf16[3,3,3,256,256]{4,3,2,1,0:T(8,128)(2,1)S(1)}, bf16[3,3,3,256,256]{4,3,2,1,0:T(8,128)(2,1)}, u32[]{:S(2)}) copy-start(bf16[3,3,3,256,256]{4,3,2,1,0:T(8,128)(2,1)} %param.16) | copy-start | bytes 10616836
  19.8 7.9 %copy-start.4 = (bf16[2,2,2,256,128]{4,3,2,1,0:T(8,128)(2,1)S(1)}, bf16[2,2,2,256,128]{4,3,2,1,0:T(8,128)(2,1)}, u32[]{:S(2)}) copy-start(bf16[2,2,2,256,128]{4,3,2,1,0:T(8,128)(2,1)} %param.18) | copy-start | bytes 1572868
  19.8 7.9 %copy-start.7 = (f32[256]{0:T(256)S(1)}, f32[256]{0:T(256)}, u32[]{:S(2)}) copy-start(f32[256]{0:T(256)} %param.17) | copy-start | bytes 3076
  19.8 7.9 %copy-start.9 = (f32[128]{0:T(128)S(1)}, f32[128]{0:T(128)}, u32[]{:S(2)}) copy-start(f32[128]{0:T(128)} %param.19) | copy-start | bytes 1540
  19.8 6.2 %collective-permute-start.9 = (bf16[10,16,256]{2,1,0:T(8,128)(2,1)S(1)}, bf16[10,16,256]{2,1,0:T(8,128)(2,1)S(1)}, u32[]{:S(2)}, u32[]{:S(2)}) collective-permute-start(bf16[10,16,256]{2,1,0:T(8,128)(2,1)S(1)} %bitcast.21), channel_id=1, source_target_pairs={{0,6},{2,4},{4,10},{6,8},{8,14},{10,12},{12,30},{14,28},{28,26},{3... | collective-permute-start | bytes 245768 | tf_op jit(solution)/shard_map/ppermute | solution.py:64
  26.2 1.5 %collective-permute-start.10 = (bf16[21,16,256]{2,1,0:T(8,128)(2,1)S(1)}, bf16[21,16,256]{2,1,0:T(8,128)(2,1)S(1)}, u32[]{:S(2)}, u32[]{:S(2)}) collective-permute-start(bf16[21,16,256]{2,1,0:T(8,128)(2,1)S(1)} %get-tuple-element.34), channel_id=1, source_target_pairs={{0,1},{1,0},{2,3},{3,2},{4,5},{5,4},{6,7},{7,6},{8,9},{9,8},{10,11... | collective-permute-start | bytes 516104 | tf_op jit(solution)/shard_map/ppermute | solution.py:570
  26.2 1.4 %collective-permute-start.11 = (bf16[7,8,256]{2,1,0:T(8,128)(2,1)S(1)}, bf16[7,8,256]{2,1,0:T(8,128)(2,1)S(1)}, u32[]{:S(2)}, u32[]{:S(2)}) collective-permute-start(bf16[7,8,256]{2,1,0:T(8,128)(2,1)S(1)} %get-tuple-element.35), channel_id=1, source_target_pairs={{0,1},{1,0},{2,3},{3,2},{4,5},{5,4},{6,7},{7,6},{8,9},{9,8},{10,11... | collective-permute-start | bytes 86024 | tf_op jit(solution)/shard_map/ppermute | solution.py:571
  27.7 4.4 %copy-start.1 = (bf16[3,3,3,256,128]{4,3,2,1,0:T(8,128)(2,1)S(1)}, bf16[3,3,3,256,128]{4,3,2,1,0:T(8,128)(2,1)}, u32[]{:S(2)}) copy-start(bf16[3,3,3,256,128]{4,3,2,1,0:T(8,128)(2,1)} %param.20) | copy-start | bytes 5308420
  27.7 4.4 %copy-start.10 = (f32[128]{0:T(128)S(1)}, f32[128]{0:T(128)}, u32[]{:S(2)}) copy-start(f32[128]{0:T(128)} %param.21) | copy-start | bytes 1540
  30.8 1.3 %collective-permute-start.12 = (bf16[8,10,256]{2,1,0:T(8,128)(2,1)S(1)}, bf16[8,10,256]{2,1,0:T(8,128)(2,1)S(1)}, u32[]{:S(2)}, u32[]{:S(2)}) collective-permute-start(bf16[8,10,256]{2,1,0:T(8,128)(2,1)S(1)} %get-tuple-element.38), channel_id=1, source_target_pairs={{0,1},{1,0},{2,3},{3,2},{4,5},{5,4},{6,7},{7,6},{8,9},{9,8},{10,11... | collective-permute-start | bytes 122888 | tf_op jit(solution)/shard_map/ppermute | solution.py:634

commit v5 on v4

--- a/solution.py
+++ b/solution.py
@@ -6,6 +6,7 @@
 from jax.experimental import pallas as pl
 from jax.experimental.pallas import tpu as pltpu
 from jax.sharding import PartitionSpec as P
+
 
 leak_slope = 0.01
 f32 = jnp.float32
@@ -381,6 +382,14 @@
         write_columns(columns, plane, left, right, slice(None))
 
 
+def weight_kernel(weight, packed):
+    outs = weight.shape[-1]
+    for tap in range(9):
+        for block in range(weight.shape[2] // outs):
+            rows = slice(block * outs, (block + 1) * outs)
+            spread_weights(packed, tap, 4 * outs * block, [weight[tap, c, rows] for c in range(3)])
+
+
 def encode_kernel(
     own,
     low,
@@ -390,7 +399,7 @@
     corner_high,
     passed,
     got,
-    weight,
+    packed,
     bias,
     down,
     down_bias,
@@ -400,7 +409,6 @@
     columns_in,
     frame,
     taps,
-    packed,
 ):
     lanes = ext.shape[-1]
     spot = (0, 0)
@@ -411,8 +419,6 @@
     for plane in range(ext.shape[0]):
         before, after = pair_columns(columns_in, plane, slice(None))
         spread_pairs(taps.at[plane], 0, ext[plane], before, after)
-    for tap in range(9):
-        spread_weights(packed, tap, 0, [weight[tap, c] for c in range(3)])
     depth, height, columns, _ = encoded.shape
     deep, tall = coarse.shape[:2]
     summed = conv_rows(taps, packed, depth, height)
@@ -516,7 +522,7 @@
 
 
 def decode_kernel(
-    raised, encoded_ext, columns_in, weight, bias, decoded, taps, packed, spread
+    raised, encoded_ext, columns_in, packed, bias, decoded, taps, spread
 ):
     planes, height, columns, lanes = encoded_ext.shape
     half = lanes // 2
@@ -525,9 +531,6 @@
         spread_pairs(taps.at[plane], 0, raised[plane + 1, 1 : 1 + height], low, high)
         low, high = pair_columns(columns_in, plane, slice(half, lanes))
         spread_pairs(taps.at[plane], 2 * lanes, encoded_ext[plane], low, high)
-    for tap in range(9):
-        spread_weights(packed, tap, 0, [weight[tap, c, :half] for c in range(3)])
-        spread_weights(packed, tap, 2 * lanes, [weight[tap, c, half:] for c in range(3)])
     depth, rows, _, outs = decoded.shape
     summed = conv_rows(taps, packed, depth, rows)
     summed = leaky_relu(summed + jnp.tile(bias[...], (1, 2)))
@@ -537,7 +540,7 @@
     decoded[...] = spread[...].astype(bf16)
 
 
-def exchange(fields, halos, half):
+def exchange(fields, halos, half, weight):
     sizes = [(field.shape, deep, tall) for field, (deep, tall) in zip(fields, halos)]
     _, planes, corners = layout(sizes)
     cells = fields[0].shape[2:]
@@ -557,6 +560,8 @@
     )(*fields, handed)
     ring = ring_exchange(ring)
     corner_low, corner_high = corner_exchange(corner)
+    outs = weight.shape[-1]
+    (weights,) = call(weight_kernel, [(9, 4 * weight.shape[2], 2 * outs)], (), 8)(weight)
     received = (low, high, ring, corner_low, corner_high)
     shape, deep, tall = sizes[0]
     framed = (shape[0] + 2 * deep, shape[1] + 2 * tall)
@@ -569,7 +574,7 @@
     )(fields[0], *received)
     passed = lax.ppermute(passed, "pair", swap)
     columns = lax.ppermute(columns, "pair", swap)
-    return sizes, received + (passed, columns)
+    return sizes, weights, received + (passed, columns)
 
 
 def body(
@@ -588,7 +593,9 @@
         [pltpu.VMEM((depth, height, width, skip), f32)],
         8,
     )(volume)
-    _, received = exchange([packed], [(1, 1)], True)
+    _, encode_weights, received = exchange(
+        [packed], [(1, 1)], True, w_encode.reshape(9, 3, skip, skip)
+    )
     encoded, coarse = call(
         encode_kernel,
         [(depth, height, pairs, lanes), (half_depth, half_height, pairs, deep_width)],
@@ -597,18 +604,19 @@
             pltpu.VMEM(framed + (skip,), bf16),
             pltpu.VMEM((1, height + 2, pairs, lanes), bf16),
             pltpu.VMEM(framed + (pairs, 2 * lanes), bf16),
-            pltpu.VMEM((9, 2 * lanes, lanes), bf16),
         ],
     )(
         packed,
         *received,
-        w_encode.reshape(9, 3, skip, skip),
+        encode_weights,
         b_encode.reshape(1, skip),
         w_down.reshape(4, lanes, deep_width),
         b_down.reshape(1, deep_width),
     )
 
-    sizes, received = exchange([coarse, encoded], [(2, 2), (1, 1)], False)
+    sizes, decode_weights, received = exchange(
+        [coarse, encoded], [(2, 2), (1, 1)], False, w_decode.reshape(9, 3, lanes, skip)
+    )
     raised, encoded_ext, columns = call(
         functools.partial(bottom_kernel, sizes),
         [
@@ -638,14 +646,13 @@
         [(depth, height, width, skip)],
         [
             pltpu.VMEM(framed + (pairs, 4 * lanes), bf16),
-            pltpu.VMEM((9, 4 * lanes, lanes), bf16),
             pltpu.VMEM((depth, height, width, skip), f32),
         ],
     )(
         raised.reshape(depth + 4, height + 4, pairs, lanes),
         encoded_ext,
         columns,
-        w_decode.reshape(9, 3, lanes, skip),
+        decode_weights,
         b_decode.reshape(1, skip),
     )
     return decoded

time: 37.5 us -> 37 us (0.987)
  waiting for transfers between devices: 11.4 us -> 10.7 us
    pallas_call x0 -> x2, Pallas kernels: none -> 0.91 us  [exchange(): call(weight_kernel, [(9, 4 * weight.shape[2], 2 * outs)], (), 8)(weight)]
    ppermute x1, waiting for transfers between devices: 0.99 us -> 0.37 us  [body(): columns = lax.ppermute(columns, 'pair', [(0, 1), (1, 0)])]
    ppermute x2, waiting for transfers between devices: 1.8 us -> 1.31 us  [exchange(): columns = lax.ppermute(columns, 'pair', swap)]
    ppermute x2, starting transfers between devices: 0.99 us -> 0.57 us  [exchange(): columns = lax.ppermute(columns, 'pair', swap)]
    ppermute x2, starting transfers between devices: 0.14 us -> 0.57 us  [exchange(): passed = lax.ppermute(passed, 'pair', swap)]
    pallas_call x1, Pallas kernels: 5.22 us -> 4.83 us  [body(): call(decode_kernel, [(depth, height, width, skip)], [pltpu.VMEM(framed +...]
  transfers between devices with their start and end apart: 13 -> 13, of which waited for: 9 -> 10; matrix products, arithmetic and copies ran while one was open for 0% -> 0% of each run, Pallas kernels for 0% -> 2%
where the time goes in v5:
time: 37 us; the launch traced here: 36.9 us
  starting transfers between devices  13 us (35%)
  Pallas kernels  11.9 us (32%)
  waiting for transfers between devices  10.7 us (29%)
  local copies, waits for them, and re-layouts  1.16 us (3%)
    pallas_call x1, Pallas kernels, body(): call(decode_kernel, [(depth, height, width, skip)], [pltpu.VMEM(framed +...  4.83 us
    ppermute x2, starting transfers between devices, ring_exchange(): return lax.ppermute(sent, ('groups', 'wide', 'pair'), pairs)  4.53 us
    ppermute x2, starting transfers between devices, move(): return lax.ppermute(array, ('groups', 'wide', 'narrow', 'pair'), pairs)  4.11 us
    ppermute x2, waiting for transfers between devices, line_exchange(): got = lax.ppermute(sent[0], axis, [(0, 1), (1, 0)])  3.45 us
    ppermute x2, waiting for transfers between devices, move(): return lax.ppermute(array, ('groups', 'wide', 'narrow', 'pair'), pairs)  3.3 us
    pallas_call x1, Pallas kernels, body(): call(functools.partial(bottom_kernel, sizes), [(half_depth + 2, 2, half_h...  3.06 us
    pallas_call x1, Pallas kernels, body(): call(encode_kernel, [(depth, height, pairs, lanes), (half_depth, half_hei...  2.47 us
    ppermute x2, starting transfers between devices, line_exchange(): got = lax.ppermute(sent[0], axis, [(0, 1), (1, 0)])  2.02 us
  transfers between devices with their start and end apart: 13, of which 10 were waited for; matrix products, arithmetic and copies ran while one was open for 0% of the time, Pallas kernels for 2%

profile of v5, /device:TPU:0, one launch (start us, length us, event | category | flops | bytes accessed | tf_op | source)
XLA Modules:
  0.0 36.9 jit_solution(17110517674383824948)
XLA Ops:
  0.0 0.0 copy-start.5
  0.0 1.0 %copy-done.5 = bf16[6,8,32,128]{3,2,1,0:T(8,128)(2,1)S(1)} copy-done((bf16[6,8,32,128]{3,2,1,0:T(8,128)(2,1)S(1)}, bf16[6,8,32,128]{3,2,1,0:T(8,128)(2,1)}, u32[]{:S(2)}) %copy-start.5) | copy-done | bytes 393240
  1.0 0.1 shard_map.109.refs_0_.own
  1.2 0.6 %collective-permute-start.1 = (bf16[8,16,256]{2,1,0:T(8,128)(2,1)S(1)}, bf16[8,16,256]{2,1,0:T(8,128)(2,1)S(1)}, u32[]{:S(2)}, u32[]{:S(2)}) collective-permute-start(bf16[8,16,256]{2,1,0:T(8,128)(2,1)S(1)} %get-tuple-element.23), channel_id=1, source_target_pairs={{0,1},{1,0},{2,3},{3,2},{4,5},{5,4},{6,7},{7,6},{8,9},{9,8},{10,11... | collective-permute-start | bytes 196616 | tf_op jit(solution)/shard_map/ppermute | solution.py:553
  1.7 0.9 %collective-permute-done.1.refs_1_ = bf16[8,16,256]{2,1,0:T(8,128)(2,1)S(1)} collective-permute-done((bf16[8,16,256]{2,1,0:T(8,128)(2,1)S(1)}, bf16[8,16,256]{2,1,0:T(8,128)(2,1)S(1)}, u32[]{:S(2)}, u32[]{:S(2)}) %collective-permute-start.1) | collective-permute-done | bytes 65568 | tf_op jit(solution)/shard_map/ppermute | solution.py:553
  2.7 3.0 %collective-permute-start.2 = (bf16[16,16,256]{2,1,0:T(8,128)(2,1)S(1)}, bf16[16,16,256]{2,1,0:T(8,128)(2,1)S(1)}, u32[]{:S(2)}, u32[]{:S(2)}) collective-permute-start(bf16[16,16,256]{2,1,0:T(8,128)(2,1)S(1)} %get-tuple-element.24), channel_id=1, source_target_pairs={{0,4},{4,8},{8,12},{12,28},{28,24},{24,20},{20,16},{16,0},{1,17},{... | collective-permute-start | bytes 393224 | tf_op jit(solution)/shard_map/ppermute | solution.py:51
  5.6 1.5 %collective-permute-start = (bf16[6,16,256]{2,1,0:T(8,128)(2,1)S(1)}, bf16[6,16,256]{2,1,0:T(8,128)(2,1)S(1)}, u32[]{:S(2)}, u32[]{:S(2)}) collective-permute-start(bf16[6,16,256]{2,1,0:T(8,128)(2,1)S(1)} %bitcast.22), channel_id=1, source_target_pairs={{0,2},{2,0},{1,3},{3,1},{4,6},{6,4},{5,7},{7,5},{8,10},{10,8},{9,1... | collective-permute-start | bytes 147464 | tf_op jit(solution)/shard_map/ppermute | solution.py:27
  7.1 0.0 copy-start.2
  7.1 1.5 %collective-permute-start.3 = (bf16[2,16,256]{2,1,0:T(8,128)(2,1)S(1)}, bf16[2,16,256]{2,1,0:T(8,128)(2,1)S(1)}, u32[]{:S(2)}, u32[]{:S(2)}) collective-permute-start(bf16[2,16,256]{2,1,0:T(8,128)(2,1)S(1)} %bitcast.23), channel_id=1, source_target_pairs={{0,6},{2,4},{4,10},{6,8},{8,14},{10,12},{12,30},{14,28},{28,26},{3... | collective-permute-start | bytes 49160 | tf_op jit(solution)/shard_map/ppermute | solution.py:65
  8.7 1.0 %collective-permute-done.refs_1_.refs_2_.low.high = bf16[6,16,256]{2,1,0:T(8,128)(2,1)S(1)} collective-permute-done((bf16[6,16,256]{2,1,0:T(8,128)(2,1)S(1)}, bf16[6,16,256]{2,1,0:T(8,128)(2,1)S(1)}, u32[]{:S(2)}, u32[]{:S(2)}) %collective-permute-start) | collective-permute-done | bytes 49184 | tf_op jit(solution)/shard_map/ppermute | solution.py:27
  9.7 2.1 %collective-permute-done.3.refs_4_.refs_5_.corner_low.corner_high = bf16[2,16,256]{2,1,0:T(8,128)(2,1)S(1)} collective-permute-done((bf16[2,16,256]{2,1,0:T(8,128)(2,1)S(1)}, bf16[2,16,256]{2,1,0:T(8,128)(2,1)S(1)}, u32[]{:S(2)}, u32[]{:S(2)}) %collective-permute-start.3) | collective-permute-done | bytes 16416 | tf_op jit(solution)/shard_map/ppermute | solution.py:65
  11.8 0.0 collective-permute-done.2.refs_3_.planes
  11.8 0.1 shard_map.112
  12.0 0.1 collective-permute-start.5
  12.1 0.5 %collective-permute-start.4 = (bf16[9,16,256]{2,1,0:T(8,128)(2,1)S(1)}, bf16[9,16,256]{2,1,0:T(8,128)(2,1)S(1)}, u32[]{:S(2)}, u32[]{:S(2)}) collective-permute-start(bf16[9,16,256]{2,1,0:T(8,128)(2,1)S(1)} %get-tuple-element.26), channel_id=1, source_target_pairs={{0,1},{1,0},{2,3},{3,2},{4,5},{5,4},{6,7},{7,6},{8,9},{9,8},{10,11... | collective-permute-start | bytes 221192 | tf_op jit(solution)/shard_map/ppermute | solution.py:575
  12.6 0.0 copy-done.2
  12.6 0.3 shard_map.113.packed
  12.9 0.4 %collective-permute-done.5.got = bf16[8,10,128]{2,1,0:T(8,128)(2,1)S(1)} collective-permute-done((bf16[8,10,128]{2,1,0:T(8,128)(2,1)S(1)}, bf16[8,10,128]{2,1,0:T(8,128)(2,1)S(1)}, u32[]{:S(2)}, u32[]{:S(2)}) %collective-permute-start.5) | collective-permute-done | bytes 20512 | tf_op jit(solution)/shard_map/ppermute | solution.py:576
  13.3 0.2 collective-permute-done.4.passed
  13.5 0.1 copy-done.3
  13.6 0.0 copy-done.6
  13.6 0.0 copy-done.8
  13.6 2.5 %shard_map.114 = (bf16[6,8,16,256]{3,2,1,0:T(8,128)(2,1)S(1)}, bf16[3,4,16,256]{3,2,1,0:T(8,128)(2,1)S(1)}) custom-call(bf16[6,8,16,256]{3,2,1,0:T(8,128)(2,1)S(1)} %shard_map.109.refs_0_.own, bf16[6,16,256]{2,1,0:T(8,128)(2,1)S(1)} %collective-permute-done.refs_1_.refs_2_.low.high, bf16[6,16,256]{2,1,0:T(8,128)(2,1)S(1)} %collective-permute-done.refs_1_.refs_2_.low.high, ...), custom_call_target="tpu_custom_call" | custom-call | flops 4000000000 | bytes 1000000 | tf_op jit(solution)/shard_map/pallas_call | solution.py:599
  16.1 0.3 collective-permute-start.7
  16.5 1.1 %collective-permute-done.7.refs_2_ = bf16[16,16,256]{2,1,0:T(8,128)(2,1)S(1)} collective-permute-done((bf16[16,16,256]{2,1,0:T(8,128)(2,1)S(1)}, bf16[16,16,256]{2,1,0:T(8,128)(2,1)S(1)}, u32[]{:S(2)}, u32[]{:S(2)}) %collective-permute-start.7) | collective-permute-done | bytes 131104 | tf_op jit(solution)/shard_map/ppermute | solution.py:553
  17.6 1.6 %collective-permute-start.8 = (bf16[32,16,256]{2,1,0:T(8,128)(2,1)S(1)}, bf16[32,16,256]{2,1,0:T(8,128)(2,1)S(1)}, u32[]{:S(2)}, u32[]{:S(2)}) collective-permute-start(bf16[32,16,256]{2,1,0:T(8,128)(2,1)S(1)} %get-tuple-element.32), channel_id=1, source_target_pairs={{0,4},{4,8},{8,12},{12,28},{28,24},{24,20},{20,16},{16,0},{1,17},{... | collective-permute-start | bytes 786440 | tf_op jit(solution)/shard_map/ppermute | solution.py:51
  19.2 0.5 %collective-permute-start.6 = (bf16[12,16,256]{2,1,0:T(8,128)(2,1)S(1)}, bf16[12,16,256]{2,1,0:T(8,128)(2,1)S(1)}, u32[]{:S(2)}, u32[]{:S(2)}) collective-permute-start(bf16[12,16,256]{2,1,0:T(8,128)(2,1)S(1)} %bitcast.20), channel_id=1, source_target_pairs={{0,2},{2,0},{1,3},{3,1},{4,6},{6,4},{5,7},{7,5},{8,10},{10,8},{9,1... | collective-permute-start | bytes 294920 | tf_op jit(solution)/shard_map/ppermute | solution.py:27
  19.7 2.6 %collective-permute-start.9 = (bf16[10,16,256]{2,1,0:T(8,128)(2,1)S(1)}, bf16[10,16,256]{2,1,0:T(8,128)(2,1)S(1)}, u32[]{:S(2)}, u32[]{:S(2)}) collective-permute-start(bf16[10,16,256]{2,1,0:T(8,128)(2,1)S(1)} %bitcast.21), channel_id=1, source_target_pairs={{0,6},{2,4},{4,10},{6,8},{8,14},{10,12},{12,30},{14,28},{28,26},{3... | collective-permute-start | bytes 245768 | tf_op jit(solution)/shard_map/ppermute | solution.py:65
  22.3 2.4 %collective-permute-done.6.refs_1_.refs_2_.low.high = bf16[12,16,256]{2,1,0:T(8,128)(2,1)S(1)} collective-permute-done((bf16[12,16,256]{2,1,0:T(8,128)(2,1)S(1)}, bf16[12,16,256]{2,1,0:T(8,128)(2,1)S(1)}, u32[]{:S(2)}, u32[]{:S(2)}) %collective-permute-start.6) | collective-permute-done | bytes 98336 | tf_op jit(solution)/shard_map/ppermute | solution.py:27
  24.7 1.2 %collective-permute-done.9.refs_4_.refs_5_.corner_low.corner_high = bf16[10,16,256]{2,1,0:T(8,128)(2,1)S(1)} collective-permute-done((bf16[10,16,256]{2,1,0:T(8,128)(2,1)S(1)}, bf16[10,16,256]{2,1,0:T(8,128)(2,1)S(1)}, u32[]{:S(2)}, u32[]{:S(2)}) %collective-permute-start.9) | collective-permute-done | bytes 81952 | tf_op jit(solution)/shard_map/ppermute | solution.py:65
  25.9 0.0 collective-permute-done.8.refs_3_.planes
  25.9 0.2 shard_map.117
  26.1 0.1 collective-permute-start.10
  26.2 0.5 %collective-permute-start.11 = (bf16[7,8,256]{2,1,0:T(8,128)(2,1)S(1)}, bf16[7,8,256]{2,1,0:T(8,128)(2,1)S(1)}, u32[]{:S(2)}, u32[]{:S(2)}) collective-permute-start(bf16[7,8,256]{2,1,0:T(8,128)(2,1)S(1)} %get-tuple-element.35), channel_id=1, source_target_pairs={{0,1},{1,0},{2,3},{3,2},{4,5},{5,4},{6,7},{7,6},{8,9},{9,8},{10,11... | collective-permute-start | bytes 86024 | tf_op jit(solution)/shard_map/ppermute | solution.py:576
  26.7 0.9 %collective-permute-done.11.got = bf16[7,8,256]{2,1,0:T(8,128)(2,1)S(1)} collective-permute-done((bf16[7,8,256]{2,1,0:T(8,128)(2,1)S(1)}, bf16[7,8,256]{2,1,0:T(8,128)(2,1)S(1)}, u32[]{:S(2)}, u32[]{:S(2)}) %collective-permute-start.11) | collective-permute-done | bytes 28704 | tf_op jit(solution)/shard_map/ppermute | solution.py:576
  27.6 0.0 collective-permute-done.10.passed
  27.6 0.0 copy-done
  27.6 0.0 copy-done.4
  27.6 0.0 copy-done.7
  27.6 0.0 copy-done.9
  27.6 0.0 copy-start.1
  27.6 3.1 %shard_map.118 = (bf16[5,2,6,2,16,256]{5,4,3,2,1,0:T(8,128)(2,1)S(1)}, bf16[8,10,16,256]{3,2,1,0:T(8,128)(2,1)S(1)}, bf16[8,10,256]{2,1,0:T(8,128)(2,1)S(1)}) custom-call(bf16[3,4,16,256]{3,2,1,0:T(8,128)(2,1)S(1)} %get-tuple-element.28.refs_0_.coarse, bf16[6,8,16,256]{3,2,1,0:T(8,128)(2,1)S(1)} %get-tuple-element.29.refs_1_.encoded, ...), custom_call_target="tpu_custom_call" | custom-call | flops 4000000000 | bytes 1000000 | tf_op jit(solution)/shard_map/pallas_call | solution.py:620
  30.7 0.3 collective-permute-start.12
  31.0 0.0 copy-done.1
  31.0 0.6 %shard_map.119.packed = bf16[9,1024,256]{2,1,0:T(8,128)(2,1)S(1)} custom-call(bf16[9,3,256,128]{3,2,1,0:T(8,128)(2,1)S(1)} %bitcast.16), custom_call_target="tpu_custom_call" | custom-call | flops 4000000000 | bytes 1000000 | tf_op jit(solution)/shard_map/pallas_call | solution.py:564
  31.7 0.4 %collective-permute-done.12.columns_in = bf16[8,10,256]{2,1,0:T(8,128)(2,1)S(1)} collective-permute-done((bf16[8,10,256]{2,1,0:T(8,128)(2,1)S(1)}, bf16[8,10,256]{2,1,0:T(8,128)(2,1)S(1)}, u32[]{:S(2)}, u32[]{:S(2)}) %collective-permute-start.12) | collective-permute-done | bytes 40992 | tf_op jit(solution)/shard_map/ppermute | solution.py:642
  32.0 0.0 copy-done.10
  32.0 4.8 %shard_map.120 = bf16[6,8,32,128]{3,2,1,0:T(8,128)(2,1)} custom-call(bf16[10,12,16,256]{3,2,1,0:T(8,128)(2,1)S(1)} %bitcast.29, bf16[8,10,16,256]{3,2,1,0:T(8,128)(2,1)S(1)} %get-tuple-element.37.encoded_ext, bf16[8,10,256]{2,1,0:T(8,128)(2,1)S(1)} %collective-permute-done.12.columns_in, bf16[9,1024,256]{2,1,0:T(8,128)(2,1)S(1)} %shard_map.119.packed, ...), custom_call_target="tpu_custom_call" | custom-call | flops 4000000000 | bytes 1000000 | tf_op jit(solution)/shard_map/pallas_call | solution.py:644
  (12 shorter events, 0.2 us)
Async XLA Ops:
  0.0 1.0 %copy-start.5 = (bf16[6,8,32,128]{3,2,1,0:T(8,128)(2,1)S(1)}, bf16[6,8,32,128]{3,2,1,0:T(8,128)(2,1)}, u32[]{:S(2)}) copy-start(bf16[6,8,32,128]{3,2,1,0:T(8,128)(2,1)} %volume.1) | copy-start | bytes 1179652
  1.2 1.5 %collective-permute-start.1 = (bf16[8,16,256]{2,1,0:T(8,128)(2,1)S(1)}, bf16[8,16,256]{2,1,0:T(8,128)(2,1)S(1)}, u32[]{:S(2)}, u32[]{:S(2)}) collective-permute-start(bf16[8,16,256]{2,1,0:T(8,128)(2,1)S(1)} %get-tuple-element.23), channel_id=1, source_target_pairs={{0,1},{1,0},{2,3},{3,2},{4,5},{5,4},{6,7},{7,6},{8,9},{9,8},{10,11... | collective-permute-start | bytes 196616 | tf_op jit(solution)/shard_map/ppermute | solution.py:553
  2.7 9.2 %collective-permute-start.2 = (bf16[16,16,256]{2,1,0:T(8,128)(2,1)S(1)}, bf16[16,16,256]{2,1,0:T(8,128)(2,1)S(1)}, u32[]{:S(2)}, u32[]{:S(2)}) collective-permute-start(bf16[16,16,256]{2,1,0:T(8,128)(2,1)S(1)} %get-tuple-element.24), channel_id=1, source_target_pairs={{0,4},{4,8},{8,12},{12,28},{28,24},{24,20},{20,16},{16,0},{1,17},{... | collective-permute-start | bytes 393224 | tf_op jit(solution)/shard_map/ppermute | solution.py:51
  5.6 4.1 %collective-permute-start = (bf16[6,16,256]{2,1,0:T(8,128)(2,1)S(1)}, bf16[6,16,256]{2,1,0:T(8,128)(2,1)S(1)}, u32[]{:S(2)}, u32[]{:S(2)}) collective-permute-start(bf16[6,16,256]{2,1,0:T(8,128)(2,1)S(1)} %bitcast.22), channel_id=1, source_target_pairs={{0,2},{2,0},{1,3},{3,1},{4,6},{6,4},{5,7},{7,5},{8,10},{10,8},{9,1... | collective-permute-start | bytes 147464 | tf_op jit(solution)/shard_map/ppermute | solution.py:27
  7.1 5.4 %copy-start.2 = (bf16[3,3,3,128,128]{4,3,2,1,0:T(8,128)(2,1)S(1)}, bf16[3,3,3,128,128]{4,3,2,1,0:T(8,128)(2,1)}, u32[]{:S(2)}) copy-start(bf16[3,3,3,128,128]{4,3,2,1,0:T(8,128)(2,1)} %param.12) | copy-start | bytes 2654212
  7.1 4.7 %collective-permute-start.3 = (bf16[2,16,256]{2,1,0:T(8,128)(2,1)S(1)}, bf16[2,16,256]{2,1,0:T(8,128)(2,1)S(1)}, u32[]{:S(2)}, u32[]{:S(2)}) collective-permute-start(bf16[2,16,256]{2,1,0:T(8,128)(2,1)S(1)} %bitcast.23), channel_id=1, source_target_pairs={{0,6},{2,4},{4,10},{6,8},{8,14},{10,12},{12,30},{14,28},{28,26},{3... | collective-permute-start | bytes 49160 | tf_op jit(solution)/shard_map/ppermute | solution.py:65
  12.0 1.3 %collective-permute-start.5 = (bf16[8,10,128]{2,1,0:T(8,128)(2,1)S(1)}, bf16[8,10,128]{2,1,0:T(8,128)(2,1)S(1)}, u32[]{:S(2)}, u32[]{:S(2)}) collective-permute-start(bf16[8,10,128]{2,1,0:T(8,128)(2,1)S(1)} %get-tuple-element.27), channel_id=1, source_target_pairs={{0,1},{1,0},{2,3},{3,2},{4,5},{5,4},{6,7},{7,6},{8,9},{9,8},{10,11... | collective-permute-start | bytes 61448 | tf_op jit(solution)/shard_map/ppermute | solution.py:576
  12.1 1.4 %collective-permute-start.4 = (bf16[9,16,256]{2,1,0:T(8,128)(2,1)S(1)}, bf16[9,16,256]{2,1,0:T(8,128)(2,1)S(1)}, u32[]{:S(2)}, u32[]{:S(2)}) collective-permute-start(bf16[9,16,256]{2,1,0:T(8,128)(2,1)S(1)} %get-tuple-element.26), channel_id=1, source_target_pairs={{0,1},{1,0},{2,3},{3,2},{4,5},{5,4},{6,7},{7,6},{8,9},{9,8},{10,11... | collective-permute-start | bytes 221192 | tf_op jit(solution)/shard_map/ppermute | solution.py:575
  12.6 1.0 %copy-start.3 = (bf16[2,2,2,128,256]{4,3,2,1,0:T(8,128)(2,1)S(1)}, bf16[2,2,2,128,256]{4,3,2,1,0:T(8,128)(2,1)}, u32[]{:S(2)}) copy-start(bf16[2,2,2,128,256]{4,3,2,1,0:T(8,128)(2,1)} %param.14) | copy-start | bytes 1572868
  12.6 1.0 %copy-start.6 = (f32[256]{0:T(256)S(1)}, f32[256]{0:T(256)}, u32[]{:S(2)}) copy-start(f32[256]{0:T(256)} %param.15) | copy-start | bytes 3076
  12.6 1.0 %copy-start.8 = (f32[128]{0:T(128)S(1)}, f32[128]{0:T(128)}, u32[]{:S(2)}) copy-start(f32[128]{0:T(128)} %param.13) | copy-start | bytes 1540
  16.1 1.4 %collective-permute-start.7 = (bf16[16,16,256]{2,1,0:T(8,128)(2,1)S(1)}, bf16[16,16,256]{2,1,0:T(8,128)(2,1)S(1)}, u32[]{:S(2)}, u32[]{:S(2)}) collective-permute-start(bf16[16,16,256]{2,1,0:T(8,128)(2,1)S(1)} %get-tuple-element.31), channel_id=1, source_target_pairs={{0,1},{1,0},{2,3},{3,2},{4,5},{5,4},{6,7},{7,6},{8,9},{9,8},{10,11... | collective-permute-start | bytes 393224 | tf_op jit(solution)/shard_map/ppermute | solution.py:553
  17.6 8.3 %collective-permute-start.8 = (bf16[32,16,256]{2,1,0:T(8,128)(2,1)S(1)}, bf16[32,16,256]{2,1,0:T(8,128)(2,1)S(1)}, u32[]{:S(2)}, u32[]{:S(2)}) collective-permute-start(bf16[32,16,256]{2,1,0:T(8,128)(2,1)S(1)} %get-tuple-element.32), channel_id=1, source_target_pairs={{0,4},{4,8},{8,12},{12,28},{28,24},{24,20},{20,16},{16,0},{1,17},{... | collective-permute-start | bytes 786440 | tf_op jit(solution)/shard_map/ppermute | solution.py:51
  19.2 5.5 %collective-permute-start.6 = (bf16[12,16,256]{2,1,0:T(8,128)(2,1)S(1)}, bf16[12,16,256]{2,1,0:T(8,128)(2,1)S(1)}, u32[]{:S(2)}, u32[]{:S(2)}) collective-permute-start(bf16[12,16,256]{2,1,0:T(8,128)(2,1)S(1)} %bitcast.20), channel_id=1, source_target_pairs={{0,2},{2,0},{1,3},{3,1},{4,6},{6,4},{5,7},{7,5},{8,10},{10,8},{9,1... | collective-permute-start | bytes 294920 | tf_op jit(solution)/shard_map/ppermute | solution.py:27
  19.7 7.9 %copy-start = (bf16[3,3,3,256,256]{4,3,2,1,0:T(8,128)(2,1)S(1)}, bf16[3,3,3,256,256]{4,3,2,1,0:T(8,128)(2,1)}, u32[]{:S(2)}) copy-start(bf16[3,3,3,256,256]{4,3,2,1,0:T(8,128)(2,1)} %param.16) | copy-start | bytes 10616836
  19.7 7.9 %copy-start.4 = (bf16[2,2,2,256,128]{4,3,2,1,0:T(8,128)(2,1)S(1)}, bf16[2,2,2,256,128]{4,3,2,1,0:T(8,128)(2,1)}, u32[]{:S(2)}) copy-start(bf16[2,2,2,256,128]{4,3,2,1,0:T(8,128)(2,1)} %param.18) | copy-start | bytes 1572868
  19.7 7.9 %copy-start.7 = (f32[256]{0:T(256)S(1)}, f32[256]{0:T(256)}, u32[]{:S(2)}) copy-start(f32[256]{0:T(256)} %param.17) | copy-start | bytes 3076
  19.7 7.9 %copy-start.9 = (f32[128]{0:T(128)S(1)}, f32[128]{0:T(128)}, u32[]{:S(2)}) copy-start(f32[128]{0:T(128)} %param.19) | copy-start | bytes 1540
  19.7 6.2 %collective-permute-start.9 = (bf16[10,16,256]{2,1,0:T(8,128)(2,1)S(1)}, bf16[10,16,256]{2,1,0:T(8,128)(2,1)S(1)}, u32[]{:S(2)}, u32[]{:S(2)}) collective-permute-start(bf16[10,16,256]{2,1,0:T(8,128)(2,1)S(1)} %bitcast.21), channel_id=1, source_target_pairs={{0,6},{2,4},{4,10},{6,8},{8,14},{10,12},{12,30},{14,28},{28,26},{3... | collective-permute-start | bytes 245768 | tf_op jit(solution)/shard_map/ppermute | solution.py:65
  26.1 1.5 %collective-permute-start.10 = (bf16[21,16,256]{2,1,0:T(8,128)(2,1)S(1)}, bf16[21,16,256]{2,1,0:T(8,128)(2,1)S(1)}, u32[]{:S(2)}, u32[]{:S(2)}) collective-permute-start(bf16[21,16,256]{2,1,0:T(8,128)(2,1)S(1)} %get-tuple-element.34), channel_id=1, source_target_pairs={{0,1},{1,0},{2,3},{3,2},{4,5},{5,4},{6,7},{7,6},{8,9},{9,8},{10,11... | collective-permute-start | bytes 516104 | tf_op jit(solution)/shard_map/ppermute | solution.py:575
  26.2 1.4 %collective-permute-start.11 = (bf16[7,8,256]{2,1,0:T(8,128)(2,1)S(1)}, bf16[7,8,256]{2,1,0:T(8,128)(2,1)S(1)}, u32[]{:S(2)}, u32[]{:S(2)}) collective-permute-start(bf16[7,8,256]{2,1,0:T(8,128)(2,1)S(1)} %get-tuple-element.35), channel_id=1, source_target_pairs={{0,1},{1,0},{2,3},{3,2},{4,5},{5,4},{6,7},{7,6},{8,9},{9,8},{10,11... | collective-permute-start | bytes 86024 | tf_op jit(solution)/shard_map/ppermute | solution.py:576
  27.6 3.4 %copy-start.1 = (bf16[3,3,3,256,128]{4,3,2,1,0:T(8,128)(2,1)S(1)}, bf16[3,3,3,256,128]{4,3,2,1,0:T(8,128)(2,1)}, u32[]{:S(2)}) copy-start(bf16[3,3,3,256,128]{4,3,2,1,0:T(8,128)(2,1)} %param.20) | copy-start | bytes 5308420
  30.7 1.3 %collective-permute-start.12 = (bf16[8,10,256]{2,1,0:T(8,128)(2,1)S(1)}, bf16[8,10,256]{2,1,0:T(8,128)(2,1)S(1)}, u32[]{:S(2)}, u32[]{:S(2)}) collective-permute-start(bf16[8,10,256]{2,1,0:T(8,128)(2,1)S(1)} %get-tuple-element.38), channel_id=1, source_target_pairs={{0,1},{1,0},{2,3},{3,2},{4,5},{5,4},{6,7},{7,6},{8,9},{9,8},{10,11... | collective-permute-start | bytes 122888 | tf_op jit(solution)/shard_map/ppermute | solution.py:642
  31.0 1.0 %copy-start.10 = (f32[128]{0:T(128)S(1)}, f32[128]{0:T(128)}, u32[]{:S(2)}) copy-start(f32[128]{0:T(128)} %param.21) | copy-start | bytes 1540

commit v6 on v5

--- a/solution.py
+++ b/solution.py
@@ -70,10 +70,10 @@
     return move(sent[1], moves), move(sent[0], [(d, c) for c, d in moves])
 
 
-def call(kernel, outs, scratch=(), megabytes=24):
+def call(kernel, outs, scratch=(), megabytes=24, dtype=bf16):
     return pl.pallas_call(
         kernel,
-        out_shape=[jax.ShapeDtypeStruct(shape, bf16) for shape in outs],
+        out_shape=[jax.ShapeDtypeStruct(shape, dtype) for shape in outs],
         scratch_shapes=list(scratch),
         cost_estimate=pl.CostEstimate(flops=4 * 10**9, transcendentals=0, bytes_accessed=10**6),
         compiler_params=pltpu.CompilerParams(vmem_limit_bytes=megabytes << 20),
@@ -171,7 +171,7 @@
         rows_at(corner_low, corner_at, deep, tall),
         rows_at(corner_high, corner_at, deep, tall),
     )
-    last = passed.shape[0] - count
+    last = split + (sides_of("narrow") - 1) * count
     far = (
         rows_at(passed, plane_at, deep, height),
         rows_at(passed, split + corner_at, deep, tall),
@@ -190,10 +190,13 @@
     return put
 
 
-def fill_columns(columns, got, frame, planes, corner_low, corner_high, spot, height, deep, tall, half):
+def fill_columns(columns, passed, frame, planes, corner_low, corner_high, spot, height, deep, tall, half):
     plane_at, corner_at = spot
     count, corners = planes.shape[0] // 2, corner_low.shape[0] // 2
-    columns[...] = got[...]
+    total, rows, lanes = columns.shape
+    start = passed.shape[0] - total
+    for plane in range(total):
+        columns[plane] = passed[start + plane, :rows, :lanes]
     fill_planes(
         frame,
         0,
@@ -213,7 +216,6 @@
         frame[:, tall + height :] = blank
 
     at_low = lax.axis_index("pair") == 0
-    total = columns.shape[0]
     at_edge = edges("wide")
 
     def put(low_side):
@@ -227,9 +229,9 @@
     either(sends_high(), put)
 
 
-def write_columns(columns, plane, low, high, lanes):
-    at_low = lax.axis_index("pair") == 0
-    columns[plane, :, lanes] = jnp.where(at_low, high, low)
+def inner_column(block, half):
+    low, high = column_values(block, half)
+    return jnp.where(lax.axis_index("pair") == 0, high, low)
 
 
 def column_values(block, half):
@@ -276,15 +278,60 @@
         packed[tap, at : at + rows, outs:] = taken[cell - 1] if cell > 0 else blank
 
 
-def conv_rows(taps, packed, depth, height):
+def conv_sum(taps, packed, base, select):
     lanes = taps.shape[-1]
     summed = None
     for a in range(3):
         for b in range(3):
-            rows = taps[a : a + depth, b : b + height].reshape(-1, lanes)
-            part = jnp.dot(rows, packed[3 * a + b], preferred_element_type=f32)
+            rows = [taps[part].reshape(-1, lanes) for part in select(a, b)]
+            rows = rows[0] if len(rows) == 1 else jnp.concatenate(rows, axis=0)
+            part = jnp.dot(
+                rows, packed[3 * a + b, base : base + lanes], preferred_element_type=f32
+            )
             summed = part if summed is None else summed + part
     return summed
+
+
+def conv_rows(taps, packed, depth, height, base=0):
+    return conv_sum(
+        taps, packed, base, lambda a, b: [(slice(a, a + depth), slice(b, b + height))]
+    )
+
+
+def conv_border(taps, packed, depth, height, base=0):
+    def select(a, b):
+        planes = slice(a + 1, a + depth - 1)
+        rows = slice(b, b + height)
+        return [(a, rows), (a + depth - 1, rows), (planes, b), (planes, b + height - 1)]
+
+    summed = conv_sum(taps, packed, base, select)
+    columns, lanes = taps.shape[2], summed.shape[-1]
+    inner = slice(1, depth - 1)
+    at = 0
+    pieces = []
+    for where, count in (
+        ((0,), height),
+        ((depth - 1,), height),
+        ((inner, 0), depth - 2),
+        ((inner, height - 1), depth - 2),
+    ):
+        block = summed[at : at + count * columns].reshape(count, columns, lanes)
+        pieces.append((where, block))
+        at += count * columns
+    return pieces
+
+
+def inner_kernel(base, final, field, handed, packed, bias, out, taps):
+    depth, height, _, lanes = field.shape
+    start = handed.shape[0] - depth
+    columns_in = handed.at[start:, :height, : lanes // 2]
+    for plane in range(depth):
+        before, after = pair_columns(columns_in, plane, slice(None))
+        spread_pairs(taps.at[plane], 0, field[plane], before, after)
+    summed = conv_rows(taps, packed, depth - 2, height - 2, base)
+    if final:
+        summed = leaky_relu(summed + jnp.tile(bias[...], (1, 2))).astype(bf16)
+    out[...] = summed.reshape(out.shape)
 
 
 def choose_side(axis, sent, put):
@@ -315,6 +362,11 @@
 def pack_kernel(volume, packed, spread):
     for plane in range(volume.shape[0]):
         pack_pairs(packed.at[plane], volume[plane], spread.at[plane])
+
+
+def put_column(ref, at, column):
+    ref[at] = jnp.zeros(ref.shape[1:], bf16)
+    ref[at, : column.shape[0], : column.shape[1]] = column
 
 
 def edge_kernel(sizes, *refs):
@@ -331,6 +383,9 @@
 
     choose_side("narrow", edge_rows, put_rows)
     either(sends_high(), lambda high: put_boundary(handed, fields, sizes, not high))
+    field, start = fields[-1], layout(sizes)[1]
+    for plane in range(field.shape[0]):
+        put_column(handed, start + plane, inner_column(field[plane], True))
 
 
 def put_boundary(out, fields, sizes, high):
@@ -345,7 +400,7 @@
 def plane_kernel(sizes, *refs):
     fields, (handed, planes, corners) = refs[: len(sizes)], refs[len(sizes) :]
     spots, count, few = layout(sizes)
-    planes[count:] = handed[...]
+    planes[count:] = handed[:count]
     either(sends_high(), lambda high: put_boundary(planes, fields, sizes, high))
 
     def put(slot, high):
@@ -362,12 +417,13 @@
 
 
 def pass_kernel(sizes, half, *refs):
-    own, low, high, planes, corner_low, corner_high, passed, columns, ext = refs
+    own, low, high, planes, corner_low, corner_high, passed, ext = refs
     (shape, deep, tall), (_, count, few) = sizes[0], layout(sizes)
     depth, height = shape[:2]
     passed[:count] = planes[count:]
     passed[count : count + few] = corner_low[few:]
-    passed[passed.shape[0] - few :] = corner_high[few:]
+    start = passed.shape[0] - ext.shape[0]
+    passed[start - few : start] = corner_high[few:]
     fill_block(ext, own, low, high, 0, deep, tall)
     near = (
         rows_at(planes, 0, deep, height),
@@ -378,8 +434,7 @@
     either(sends_high(), put_sides(ext, depth, deep, near, blank))
     clear_edges(ext, deep, tall)
     for plane in range(ext.shape[0]):
-        left, right = column_values(ext[plane], half)
-        write_columns(columns, plane, left, right, slice(None))
+        put_column(passed, start + plane, inner_column(ext[plane], half))
 
 
 def weight_kernel(weight, packed):
@@ -398,8 +453,8 @@
     corner_low,
     corner_high,
     passed,
-    got,
     packed,
+    inner,
     bias,
     down,
     down_bias,
@@ -414,17 +469,18 @@
     spot = (0, 0)
     fill_frame(ext, own, low, high, planes, corner_low, corner_high, passed, spot, 0, 1, 1)
     fill_columns(
-        columns_in, got, frame, planes, corner_low, corner_high, spot, own.shape[1], 1, 1, True
+        columns_in, passed, frame, planes, corner_low, corner_high, spot, own.shape[1], 1, 1, True
     )
     for plane in range(ext.shape[0]):
         before, after = pair_columns(columns_in, plane, slice(None))
         spread_pairs(taps.at[plane], 0, ext[plane], before, after)
     depth, height, columns, _ = encoded.shape
     deep, tall = coarse.shape[:2]
-    summed = conv_rows(taps, packed, depth, height)
-    fine = leaky_relu(summed + jnp.tile(bias[...], (1, 2))).astype(bf16)
-    fine = fine.reshape(deep, 2, tall, 2, columns, lanes)
-    encoded[...] = fine.reshape(encoded.shape)
+    both = jnp.tile(bias[...], (1, 2))
+    encoded[1 : depth - 1, 1 : height - 1] = inner[...]
+    for where, block in conv_border(taps, packed, depth, height):
+        encoded[where] = leaky_relu(block + both).astype(bf16)
+    fine = encoded[...].reshape(deep, 2, tall, 2, columns, lanes)
     lifted = None
     for a in range(2):
         for b in range(2):
@@ -445,7 +501,6 @@
     corner_low,
     corner_high,
     passed,
-    got,
     weight,
     bias,
     up,
@@ -470,7 +525,7 @@
         at += shape[0] * tall
     (shape, deep, tall), spot = sizes[0], spots[0]
     fill_columns(
-        columns_in, got, frame, planes, corner_low, corner_high, spot, shape[1], deep, tall, False
+        columns_in, passed, frame, planes, corner_low, corner_high, spot, shape[1], deep, tall, False
     )
     for plane in range(coarse_ext.shape[0]):
         before, after = pair_columns(columns_in, plane, slice(None))
@@ -515,40 +570,52 @@
     for plane in range(planes):
         z, a = (plane + 1) // 2, (plane + 1) % 2
         whole = raised[z, a].reshape(2 * tall, count, lanes)[1 : 1 + height]
-        low, high = column_values(whole, True)
-        write_columns(columns, plane, low, high, slice(0, half))
-        low, high = column_values(encoded_ext[plane], True)
-        write_columns(columns, plane, low, high, slice(half, lanes))
+        columns[plane, :, :half] = inner_column(whole, True)
+        columns[plane, :, half:] = inner_column(encoded_ext[plane], True)
 
 
 def decode_kernel(
-    raised, encoded_ext, columns_in, packed, bias, decoded, taps, spread
+    raised,
+    encoded_ext,
+    columns_in,
+    packed,
+    inner,
+    bias,
+    decoded,
+    raised_taps,
+    encoded_taps,
+    sums,
+    spread,
 ):
     planes, height, columns, lanes = encoded_ext.shape
     half = lanes // 2
     for plane in range(planes):
         low, high = pair_columns(columns_in, plane, slice(0, half))
-        spread_pairs(taps.at[plane], 0, raised[plane + 1, 1 : 1 + height], low, high)
+        spread_pairs(raised_taps.at[plane], 0, raised[plane + 1, 1 : 1 + height], low, high)
         low, high = pair_columns(columns_in, plane, slice(half, lanes))
-        spread_pairs(taps.at[plane], 2 * lanes, encoded_ext[plane], low, high)
+        spread_pairs(encoded_taps.at[plane], 0, encoded_ext[plane], low, high)
     depth, rows, _, outs = decoded.shape
-    summed = conv_rows(taps, packed, depth, rows)
-    summed = leaky_relu(summed + jnp.tile(bias[...], (1, 2)))
+    sums[...] = conv_rows(raised_taps, packed, depth, rows).reshape(sums.shape)
+    sums[1 : depth - 1, 1 : rows - 1] += inner[...]
+    for where, block in conv_border(encoded_taps, packed, depth, rows, 2 * lanes):
+        sums[where] += block
+    summed = leaky_relu(sums[...] + jnp.tile(bias[...], (1, 2)))
     for odd in range(2):
-        half = summed[:, odd * outs : (odd + 1) * outs].reshape(depth, rows, columns, outs)
+        half = summed[:, :, :, odd * outs : (odd + 1) * outs]
         spread[:, :, pl.ds(odd, columns, stride=2), :] = half
     decoded[...] = spread[...].astype(bf16)
 
 
-def exchange(fields, halos, half, weight):
+def exchange(fields, halos, half, weight, bias):
     sizes = [(field.shape, deep, tall) for field, (deep, tall) in zip(fields, halos)]
     _, planes, corners = layout(sizes)
-    cells = fields[0].shape[2:]
+    depth, height = fields[-1].shape[:2]
+    cells = fields[-1].shape[2:]
     sides = sides_of("narrow")
     swap = [(0, 1), (1, 0)]
     rows = sum(shape[0] * tall for shape, _, tall in sizes)
     edge_rows, handed = call(
-        functools.partial(edge_kernel, sizes), [(sides, rows) + cells, (planes,) + cells], (), 8
+        functools.partial(edge_kernel, sizes), [(sides, rows) + cells, (planes + depth,) + cells], (), 8
     )(*fields)
     handed = lax.ppermute(handed, "pair", swap)
     low, high = line_exchange("narrow", edge_rows)
@@ -562,19 +629,24 @@
     corner_low, corner_high = corner_exchange(corner)
     outs = weight.shape[-1]
     (weights,) = call(weight_kernel, [(9, 4 * weight.shape[2], 2 * outs)], (), 8)(weight)
+    lanes = 2 * cells[1]
+    (inner,) = call(
+        functools.partial(inner_kernel, weights.shape[1] - lanes, half),
+        [(depth - 2, height - 2) + cells],
+        [pltpu.VMEM((depth, height, cells[0], lanes), bf16)],
+        dtype=bf16 if half else f32,
+    )(fields[-1], handed, weights, bias)
     received = (low, high, ring, corner_low, corner_high)
     shape, deep, tall = sizes[0]
     framed = (shape[0] + 2 * deep, shape[1] + 2 * tall)
-    lanes = cells[1] // 2 if half else cells[1]
-    passed, columns = call(
+    (passed,) = call(
         functools.partial(pass_kernel, sizes, half),
-        [(planes + sides * corners,) + cells, framed + (lanes,)],
+        [(planes + sides * corners + framed[0],) + cells],
         [pltpu.VMEM(framed + cells, bf16)],
         8,
     )(fields[0], *received)
     passed = lax.ppermute(passed, "pair", swap)
-    columns = lax.ppermute(columns, "pair", swap)
-    return sizes, weights, received + (passed, columns)
+    return sizes, weights, inner, received + (passed,)
 
 
 def body(
@@ -593,8 +665,9 @@
         [pltpu.VMEM((depth, height, width, skip), f32)],
         8,
     )(volume)
-    _, encode_weights, received = exchange(
-        [packed], [(1, 1)], True, w_encode.reshape(9, 3, skip, skip)
+    encode_bias, decode_bias = b_encode.reshape(1, skip), b_decode.reshape(1, skip)
+    _, encode_weights, inner, received = exchange(
+        [packed], [(1, 1)], True, w_encode.reshape(9, 3, skip, skip), encode_bias
     )
     encoded, coarse = call(
         encode_kernel,
@@ -609,13 +682,14 @@
         packed,
         *received,
         encode_weights,
-        b_encode.reshape(1, skip),
+        inner,
+        encode_bias,
         w_down.reshape(4, lanes, deep_width),
         b_down.reshape(1, deep_width),
     )
 
-    sizes, decode_weights, received = exchange(
-        [coarse, encoded], [(2, 2), (1, 1)], False, w_decode.reshape(9, 3, lanes, skip)
+    sizes, decode_weights, inner, received = exchange(
+        [coarse, encoded], [(2, 2), (1, 1)], False, w_decode.reshape(9, 3, lanes, skip), decode_bias
     )
     raised, encoded_ext, columns = call(
         functools.partial(bottom_kernel, sizes),
@@ -645,7 +719,9 @@
         decode_kernel,
         [(depth, height, width, skip)],
         [
-            pltpu.VMEM(framed + (pairs, 4 * lanes), bf16),
+            pltpu.VMEM(framed + (pairs, 2 * lanes), bf16),
+            pltpu.VMEM(framed + (pairs, 2 * lanes), bf16),
+            pltpu.VMEM((depth, height, pairs, lanes), f32),
             pltpu.VMEM((depth, height, width, skip), f32),
         ],
     )(
@@ -653,7 +729,8 @@
         encoded_ext,
         columns,
         decode_weights,
-        b_decode.reshape(1, skip),
+        inner,
+        decode_bias,
     )
     return decoded
 

time: 37 us -> 36.1 us (0.976)
  waiting for transfers between devices: 10.7 us -> 9.06 us
  local copies, waits for them, and re-layouts: 1.16 us -> 1.69 us
  Pallas kernels: 11.9 us -> 12.3 us
    ppermute x2, waiting for transfers between devices: 0.01 us -> 2.56 us  [ring_exchange(): return lax.ppermute(sent, ('groups', 'wide', 'pair'), pairs)]
    pallas_call x0 -> x2, Pallas kernels: none -> 2.2 us  [exchange(): call(functools.partial(inner_kernel, weights.shape[1] - lanes, half), [(d...]
    ppermute x2, waiting for transfers between devices: 3.3 us -> 1.62 us  [move(): return lax.ppermute(array, ('groups', 'wide', 'narrow', 'pair'), pairs)]
    ppermute x2, starting transfers between devices: 2.02 us -> 3.37 us  [line_exchange(): got = lax.ppermute(sent[0], axis, [(0, 1), (1, 0)])]
    ppermute x2, starting transfers between devices: 4.53 us -> 3.2 us  [ring_exchange(): return lax.ppermute(sent, ('groups', 'wide', 'pair'), pairs)]
    ppermute x2 -> x0, waiting for transfers between devices: 1.31 us -> none  [exchange(): columns = lax.ppermute(columns, 'pair', swap)]
    pallas_call x1, Pallas kernels: 4.83 us -> 3.78 us  [body(): call(decode_kernel, [(depth, height, width, skip)], [pltpu.VMEM(framed +...]
    ppermute x2, waiting for transfers between devices: 2.01 us -> 1.12 us  [exchange(): handed = lax.ppermute(handed, 'pair', swap)]
  transfers between devices with their start and end apart: 13 -> 11, of which waited for: 10 -> 7; matrix products, arithmetic and copies ran while one was open for 0% -> 0% of each run, Pallas kernels for 2% -> 9%
where the time goes in v6:
time: 36.1 us; the launch traced here: 36 us
  starting transfers between devices  12.7 us (35%)
  Pallas kernels  12.3 us (34%)
  waiting for transfers between devices  9.06 us (25%)
  local copies, waits for them, and re-layouts  1.69 us (5%)
    ppermute x2, starting transfers between devices, move(): return lax.ppermute(array, ('groups', 'wide', 'narrow', 'pair'), pairs)  4.52 us
    pallas_call x1, Pallas kernels, body(): call(decode_kernel, [(depth, height, width, skip)], [pltpu.VMEM(framed +...  3.78 us
    ppermute x2, starting transfers between devices, line_exchange(): got = lax.ppermute(sent[0], axis, [(0, 1), (1, 0)])  3.37 us
    ppermute x2, starting transfers between devices, ring_exchange(): return lax.ppermute(sent, ('groups', 'wide', 'pair'), pairs)  3.2 us
    pallas_call x1, Pallas kernels, body(): call(functools.partial(bottom_kernel, sizes), [(half_depth + 2, 2, half_h...  3.04 us
    ppermute x2, waiting for transfers between devices, line_exchange(): got = lax.ppermute(sent[0], axis, [(0, 1), (1, 0)])  2.75 us
    ppermute x2, waiting for transfers between devices, ring_exchange(): return lax.ppermute(sent, ('groups', 'wide', 'pair'), pairs)  2.56 us
    pallas_call x2, Pallas kernels, exchange(): call(functools.partial(inner_kernel, weights.shape[1] - lanes, half), [(d...  2.2 us
  transfers between devices with their start and end apart: 11, of which 7 were waited for; matrix products, arithmetic and copies ran while one was open for 0% of the time, Pallas kernels for 9%

profile of v6, /device:TPU:0, one launch (start us, length us, event | category | flops | bytes accessed | tf_op | source)
XLA Modules:
  0.0 36.0 jit_solution(10783621782389907368)
XLA Ops:
  0.0 1.0 %copy-done.5 = bf16[6,8,32,128]{3,2,1,0:T(8,128)(2,1)S(1)} copy-done((bf16[6,8,32,128]{3,2,1,0:T(8,128)(2,1)S(1)}, bf16[6,8,32,128]{3,2,1,0:T(8,128)(2,1)}, u32[]{:S(2)}) %copy-start.5) | copy-done | bytes 393240
  1.0 0.1 shard_map.109.refs_0_.field.own
  1.1 0.1 shard_map.110
  1.2 0.6 %collective-permute-start.1 = (bf16[14,16,256]{2,1,0:T(8,128)(2,1)S(1)}, bf16[14,16,256]{2,1,0:T(8,128)(2,1)S(1)}, u32[]{:S(2)}, u32[]{:S(2)}) collective-permute-start(bf16[14,16,256]{2,1,0:T(8,128)(2,1)S(1)} %get-tuple-element.19), channel_id=1, source_target_pairs={{0,1},{1,0},{2,3},{3,2},{4,5},{5,4},{6,7},{7,6},{8,9},{9,8},{10,11... | collective-permute-start | bytes 344072 | tf_op jit(solution)/shard_map/ppermute | solution.py:620
  1.8 2.6 %collective-permute-start = (bf16[6,16,256]{2,1,0:T(8,128)(2,1)S(1)}, bf16[6,16,256]{2,1,0:T(8,128)(2,1)S(1)}, u32[]{:S(2)}, u32[]{:S(2)}) collective-permute-start(bf16[6,16,256]{2,1,0:T(8,128)(2,1)S(1)} %bitcast.22), channel_id=1, source_target_pairs={{0,2},{2,0},{1,3},{3,1},{4,6},{6,4},{5,7},{7,5},{8,10},{10,8},{9,1... | collective-permute-start | bytes 147464 | tf_op jit(solution)/shard_map/ppermute | solution.py:27
  4.4 0.0 collective-permute-done.1.refs_1_.handed
  4.4 2.3 %collective-permute-start.3 = (bf16[2,16,256]{2,1,0:T(8,128)(2,1)S(1)}, bf16[2,16,256]{2,1,0:T(8,128)(2,1)S(1)}, u32[]{:S(2)}, u32[]{:S(2)}) collective-permute-start(bf16[2,16,256]{2,1,0:T(8,128)(2,1)S(1)} %bitcast.23), channel_id=1, source_target_pairs={{0,6},{2,4},{4,10},{6,8},{8,14},{10,12},{12,30},{14,28},{28,26},{3... | collective-permute-start | bytes 49160 | tf_op jit(solution)/shard_map/ppermute | solution.py:65
  6.7 1.6 %collective-permute-start.2 = (bf16[16,16,256]{2,1,0:T(8,128)(2,1)S(1)}, bf16[16,16,256]{2,1,0:T(8,128)(2,1)S(1)}, u32[]{:S(2)}, u32[]{:S(2)}) collective-permute-start(bf16[16,16,256]{2,1,0:T(8,128)(2,1)S(1)} %get-tuple-element.20), channel_id=1, source_target_pairs={{0,4},{4,8},{8,12},{12,28},{28,24},{24,20},{20,16},{16,0},{1,17},{... | collective-permute-start | bytes 393224 | tf_op jit(solution)/shard_map/ppermute | solution.py:51
  8.3 0.0 copy-done.2
  8.3 0.3 shard_map.113.packed
  8.6 0.0 copy-start.8
  8.6 0.0 collective-permute-done.refs_1_.refs_2_.low.high
  8.6 0.5 %collective-permute-done.3.refs_4_.refs_5_.corner_low.corner_high = bf16[2,16,256]{2,1,0:T(8,128)(2,1)S(1)} collective-permute-done((bf16[2,16,256]{2,1,0:T(8,128)(2,1)S(1)}, bf16[2,16,256]{2,1,0:T(8,128)(2,1)S(1)}, u32[]{:S(2)}, u32[]{:S(2)}) %collective-permute-start.3) | collective-permute-done | bytes 16416 | tf_op jit(solution)/shard_map/ppermute | solution.py:65
  9.1 2.6 %collective-permute-done.2.refs_3_.planes = bf16[16,16,256]{2,1,0:T(8,128)(2,1)S(1)} collective-permute-done((bf16[16,16,256]{2,1,0:T(8,128)(2,1)S(1)}, bf16[16,16,256]{2,1,0:T(8,128)(2,1)S(1)}, u32[]{:S(2)}, u32[]{:S(2)}) %collective-permute-start.2) | collective-permute-done | bytes 131104 | tf_op jit(solution)/shard_map/ppermute | solution.py:51
  11.6 0.1 shard_map.112
  11.8 0.1 collective-permute-start.4
  11.9 0.0 copy-done.8
  11.9 0.0 copy-start.3
  11.9 0.0 copy-start.6
  11.9 1.1 %shard_map.114.inner = bf16[4,6,16,256]{3,2,1,0:T(8,128)(2,1)S(1)} custom-call(bf16[6,8,16,256]{3,2,1,0:T(8,128)(2,1)S(1)} %shard_map.109.refs_0_.field.own, bf16[14,16,256]{2,1,0:T(8,128)(2,1)S(1)} %collective-permute-done.1.refs_1_.handed, bf16[9,512,256]{2,1,0:T(8,128)(2,1)S(1)} %shard_map.113.packed, f32[1,128]{1,0:T(1,128)S(1)} %bitcast.26), custom_call_target="tpu_custom_call" | custom-call | flops 4000000000 | bytes 1000000 | tf_op jit(solution)/shard_map/pallas_call | solution.py:633
  13.0 0.2 collective-permute-done.4.passed
  13.2 0.0 copy-done.3
  13.2 1.6 %shard_map.115 = (bf16[6,8,16,256]{3,2,1,0:T(8,128)(2,1)S(1)}, bf16[3,4,16,256]{3,2,1,0:T(8,128)(2,1)S(1)}) custom-call(bf16[6,8,16,256]{3,2,1,0:T(8,128)(2,1)S(1)} %shard_map.109.refs_0_.field.own, bf16[6,16,256]{2,1,0:T(8,128)(2,1)S(1)} %collective-permute-done.refs_1_.refs_2_.low.high, ...), custom_call_target="tpu_custom_call" | custom-call | flops 4000000000 | bytes 1000000 | tf_op jit(solution)/shard_map/pallas_call | solution.py:672
  14.9 0.1 shard_map.116
  15.0 0.4 %collective-permute-start.6 = (bf16[22,16,256]{2,1,0:T(8,128)(2,1)S(1)}, bf16[22,16,256]{2,1,0:T(8,128)(2,1)S(1)}, u32[]{:S(2)}, u32[]{:S(2)}) collective-permute-start(bf16[22,16,256]{2,1,0:T(8,128)(2,1)S(1)} %get-tuple-element.25), channel_id=1, source_target_pairs={{0,1},{1,0},{2,3},{3,2},{4,5},{5,4},{6,7},{7,6},{8,9},{9,8},{10,11... | collective-permute-start | bytes 540680 | tf_op jit(solution)/shard_map/ppermute | solution.py:620
  15.3 1.1 %collective-permute-done.6.refs_2_.handed = bf16[22,16,256]{2,1,0:T(8,128)(2,1)S(1)} collective-permute-done((bf16[22,16,256]{2,1,0:T(8,128)(2,1)S(1)}, bf16[22,16,256]{2,1,0:T(8,128)(2,1)S(1)}, u32[]{:S(2)}, u32[]{:S(2)}) %collective-permute-start.6) | collective-permute-done | bytes 180256 | tf_op jit(solution)/shard_map/ppermute | solution.py:620
  16.5 1.6 %collective-permute-start.7 = (bf16[32,16,256]{2,1,0:T(8,128)(2,1)S(1)}, bf16[32,16,256]{2,1,0:T(8,128)(2,1)S(1)}, u32[]{:S(2)}, u32[]{:S(2)}) collective-permute-start(bf16[32,16,256]{2,1,0:T(8,128)(2,1)S(1)} %get-tuple-element.26), channel_id=1, source_target_pairs={{0,4},{4,8},{8,12},{12,28},{28,24},{24,20},{20,16},{16,0},{1,17},{... | collective-permute-start | bytes 786440 | tf_op jit(solution)/shard_map/ppermute | solution.py:51
  18.1 0.8 %collective-permute-start.5 = (bf16[12,16,256]{2,1,0:T(8,128)(2,1)S(1)}, bf16[12,16,256]{2,1,0:T(8,128)(2,1)S(1)}, u32[]{:S(2)}, u32[]{:S(2)}) collective-permute-start(bf16[12,16,256]{2,1,0:T(8,128)(2,1)S(1)} %bitcast.20), channel_id=1, source_target_pairs={{0,2},{2,0},{1,3},{3,1},{4,6},{6,4},{5,7},{7,5},{8,10},{10,8},{9,1... | collective-permute-start | bytes 294920 | tf_op jit(solution)/shard_map/ppermute | solution.py:27
  18.9 2.2 %collective-permute-start.8 = (bf16[10,16,256]{2,1,0:T(8,128)(2,1)S(1)}, bf16[10,16,256]{2,1,0:T(8,128)(2,1)S(1)}, u32[]{:S(2)}, u32[]{:S(2)}) collective-permute-start(bf16[10,16,256]{2,1,0:T(8,128)(2,1)S(1)} %bitcast.21), channel_id=1, source_target_pairs={{0,6},{2,4},{4,10},{6,8},{8,14},{10,12},{12,30},{14,28},{28,26},{3... | collective-permute-start | bytes 245768 | tf_op jit(solution)/shard_map/ppermute | solution.py:65
  21.2 2.7 %collective-permute-done.5.refs_1_.refs_2_.low.high = bf16[12,16,256]{2,1,0:T(8,128)(2,1)S(1)} collective-permute-done((bf16[12,16,256]{2,1,0:T(8,128)(2,1)S(1)}, bf16[12,16,256]{2,1,0:T(8,128)(2,1)S(1)}, u32[]{:S(2)}, u32[]{:S(2)}) %collective-permute-start.5) | collective-permute-done | bytes 98336 | tf_op jit(solution)/shard_map/ppermute | solution.py:27
  23.9 1.1 %collective-permute-done.8.refs_4_.refs_5_.corner_low.corner_high = bf16[10,16,256]{2,1,0:T(8,128)(2,1)S(1)} collective-permute-done((bf16[10,16,256]{2,1,0:T(8,128)(2,1)S(1)}, bf16[10,16,256]{2,1,0:T(8,128)(2,1)S(1)}, u32[]{:S(2)}, u32[]{:S(2)}) %collective-permute-start.8) | collective-permute-done | bytes 81952 | tf_op jit(solution)/shard_map/ppermute | solution.py:65
  25.1 0.0 collective-permute-done.7.refs_3_.planes
  25.1 0.2 shard_map.118
  25.3 0.1 collective-permute-start.9
  25.3 0.0 copy-done.1
  25.4 0.0 copy-start
  25.4 0.0 copy-start.4
  25.4 0.0 copy-start.7
  25.4 0.0 copy-start.9
  25.4 0.6 %shard_map.120.packed = bf16[9,1024,256]{2,1,0:T(8,128)(2,1)S(1)} custom-call(bf16[9,3,256,128]{3,2,1,0:T(8,128)(2,1)S(1)} %bitcast.16), custom_call_target="tpu_custom_call" | custom-call | flops 4000000000 | bytes 1000000 | tf_op jit(solution)/shard_map/pallas_call | solution.py:631
  26.0 0.8 %collective-permute-done.9.passed = bf16[28,16,256]{2,1,0:T(8,128)(2,1)S(1)} collective-permute-done((bf16[28,16,256]{2,1,0:T(8,128)(2,1)S(1)}, bf16[28,16,256]{2,1,0:T(8,128)(2,1)S(1)}, u32[]{:S(2)}, u32[]{:S(2)}) %collective-permute-start.9) | collective-permute-done | bytes 229408 | tf_op jit(solution)/shard_map/ppermute | solution.py:648
  26.8 0.5 %copy-done = bf16[3,3,3,256,256]{4,3,2,1,0:T(8,128)(2,1)S(1)} copy-done((bf16[3,3,3,256,256]{4,3,2,1,0:T(8,128)(2,1)S(1)}, bf16[3,3,3,256,256]{4,3,2,1,0:T(8,128)(2,1)}, u32[]{:S(2)}) %copy-start) | copy-done | bytes 3538968
  27.4 0.1 copy-done.4
  27.5 3.0 %shard_map.119 = (bf16[5,2,6,2,16,256]{5,4,3,2,1,0:T(8,128)(2,1)S(1)}, bf16[8,10,16,256]{3,2,1,0:T(8,128)(2,1)S(1)}, bf16[8,10,256]{2,1,0:T(8,128)(2,1)S(1)}) custom-call(bf16[3,4,16,256]{3,2,1,0:T(8,128)(2,1)S(1)} %get-tuple-element.22.refs_0_.coarse, bf16[6,8,16,256]{3,2,1,0:T(8,128)(2,1)S(1)} %get-tuple-element.23.refs_1_.encoded.field, ...), custom_call_target="tpu_custom_call" | custom-call | flops 4000000000 | bytes 1000000 | tf_op jit(solution)/shard_map/pallas_call | solution.py:694
  30.5 0.6 %collective-permute-start.10 = (bf16[8,10,256]{2,1,0:T(8,128)(2,1)S(1)}, bf16[8,10,256]{2,1,0:T(8,128)(2,1)S(1)}, u32[]{:S(2)}, u32[]{:S(2)}) collective-permute-start(bf16[8,10,256]{2,1,0:T(8,128)(2,1)S(1)} %get-tuple-element.30), channel_id=1, source_target_pairs={{0,1},{1,0},{2,3},{3,2},{4,5},{5,4},{6,7},{7,6},{8,9},{9,8},{10,11... | collective-permute-start | bytes 122888 | tf_op jit(solution)/shard_map/ppermute | solution.py:716
  31.1 1.1 %shard_map.121.inner = f32[4,6,16,256]{3,2,1,0:T(8,128)S(1)} custom-call(bf16[6,8,16,256]{3,2,1,0:T(8,128)(2,1)S(1)} %get-tuple-element.23.refs_1_.encoded.field, bf16[22,16,256]{2,1,0:T(8,128)(2,1)S(1)} %collective-permute-done.6.refs_2_.handed, bf16[9,1024,256]{2,1,0:T(8,128)(2,1)S(1)} %shard_map.120.packed, f32[1,128]{1,0:T(1,128)S(1)} %bitcast.29), custom_call_target="tpu_custom_call" | custom-call | flops 4000000000 | bytes 1000000 | tf_op jit(solution)/shard_map/pallas_call | solution.py:633
  32.2 0.0 collective-permute-done.10.columns_in
  32.2 3.8 %shard_map.122 = bf16[6,8,32,128]{3,2,1,0:T(8,128)(2,1)} custom-call(bf16[10,12,16,256]{3,2,1,0:T(8,128)(2,1)S(1)} %bitcast.31, bf16[8,10,16,256]{3,2,1,0:T(8,128)(2,1)S(1)} %get-tuple-element.29.encoded_ext, bf16[8,10,256]{2,1,0:T(8,128)(2,1)S(1)} %collective-permute-done.10.columns_in, bf16[9,1024,256]{2,1,0:T(8,128)(2,1)S(1)} %shard_map.120.packed, ...), custom_call_target="tpu_custom_call" | custom-call | flops 4000000000 | bytes 1000000 | tf_op jit(solution)/shard_map/pallas_call | solution.py:718
  (10 shorter events, 0.1 us)
Async XLA Ops:
  0.0 1.0 %copy-start.5 = (bf16[6,8,32,128]{3,2,1,0:T(8,128)(2,1)S(1)}, bf16[6,8,32,128]{3,2,1,0:T(8,128)(2,1)}, u32[]{:S(2)}) copy-start(bf16[6,8,32,128]{3,2,1,0:T(8,128)(2,1)} %volume.1) | copy-start | bytes 1179652
  1.2 3.1 %collective-permute-start.1 = (bf16[14,16,256]{2,1,0:T(8,128)(2,1)S(1)}, bf16[14,16,256]{2,1,0:T(8,128)(2,1)S(1)}, u32[]{:S(2)}, u32[]{:S(2)}) collective-permute-start(bf16[14,16,256]{2,1,0:T(8,128)(2,1)S(1)} %get-tuple-element.19), channel_id=1, source_target_pairs={{0,1},{1,0},{2,3},{3,2},{4,5},{5,4},{6,7},{7,6},{8,9},{9,8},{10,11... | collective-permute-start | bytes 344072 | tf_op jit(solution)/shard_map/ppermute | solution.py:620
  1.8 6.5 %copy-start.2 = (bf16[3,3,3,128,128]{4,3,2,1,0:T(8,128)(2,1)S(1)}, bf16[3,3,3,128,128]{4,3,2,1,0:T(8,128)(2,1)}, u32[]{:S(2)}) copy-start(bf16[3,3,3,128,128]{4,3,2,1,0:T(8,128)(2,1)} %param.12) | copy-start | bytes 2654212
  1.8 6.8 %collective-permute-start = (bf16[6,16,256]{2,1,0:T(8,128)(2,1)S(1)}, bf16[6,16,256]{2,1,0:T(8,128)(2,1)S(1)}, u32[]{:S(2)}, u32[]{:S(2)}) collective-permute-start(bf16[6,16,256]{2,1,0:T(8,128)(2,1)S(1)} %bitcast.22), channel_id=1, source_target_pairs={{0,2},{2,0},{1,3},{3,1},{4,6},{6,4},{5,7},{7,5},{8,10},{10,8},{9,1... | collective-permute-start | bytes 147464 | tf_op jit(solution)/shard_map/ppermute | solution.py:27
  4.4 4.7 %collective-permute-start.3 = (bf16[2,16,256]{2,1,0:T(8,128)(2,1)S(1)}, bf16[2,16,256]{2,1,0:T(8,128)(2,1)S(1)}, u32[]{:S(2)}, u32[]{:S(2)}) collective-permute-start(bf16[2,16,256]{2,1,0:T(8,128)(2,1)S(1)} %bitcast.23), channel_id=1, source_target_pairs={{0,6},{2,4},{4,10},{6,8},{8,14},{10,12},{12,30},{14,28},{28,26},{3... | collective-permute-start | bytes 49160 | tf_op jit(solution)/shard_map/ppermute | solution.py:65
  6.7 5.0 %collective-permute-start.2 = (bf16[16,16,256]{2,1,0:T(8,128)(2,1)S(1)}, bf16[16,16,256]{2,1,0:T(8,128)(2,1)S(1)}, u32[]{:S(2)}, u32[]{:S(2)}) collective-permute-start(bf16[16,16,256]{2,1,0:T(8,128)(2,1)S(1)} %get-tuple-element.20), channel_id=1, source_target_pairs={{0,4},{4,8},{8,12},{12,28},{28,24},{24,20},{20,16},{16,0},{1,17},{... | collective-permute-start | bytes 393224 | tf_op jit(solution)/shard_map/ppermute | solution.py:51
  8.6 3.3 %copy-start.8 = (f32[128]{0:T(128)S(1)}, f32[128]{0:T(128)}, u32[]{:S(2)}) copy-start(f32[128]{0:T(128)} %param.13) | copy-start | bytes 1540
  11.8 1.4 %collective-permute-start.4 = (bf16[17,16,256]{2,1,0:T(8,128)(2,1)S(1)}, bf16[17,16,256]{2,1,0:T(8,128)(2,1)S(1)}, u32[]{:S(2)}, u32[]{:S(2)}) collective-permute-start(bf16[17,16,256]{2,1,0:T(8,128)(2,1)S(1)} %shard_map.112), channel_id=1, source_target_pairs={{0,1},{1,0},{2,3},{3,2},{4,5},{5,4},{6,7},{7,6},{8,9},{9,8},{10,11... | collective-permute-start | bytes 417800 | tf_op jit(solution)/shard_map/ppermute | solution.py:648
  11.9 1.3 %copy-start.3 = (bf16[2,2,2,128,256]{4,3,2,1,0:T(8,128)(2,1)S(1)}, bf16[2,2,2,128,256]{4,3,2,1,0:T(8,128)(2,1)}, u32[]{:S(2)}) copy-start(bf16[2,2,2,128,256]{4,3,2,1,0:T(8,128)(2,1)} %param.14) | copy-start | bytes 1572868
  11.9 1.3 %copy-start.6 = (f32[256]{0:T(256)S(1)}, f32[256]{0:T(256)}, u32[]{:S(2)}) copy-start(f32[256]{0:T(256)} %param.15) | copy-start | bytes 3076
  15.0 1.5 %collective-permute-start.6 = (bf16[22,16,256]{2,1,0:T(8,128)(2,1)S(1)}, bf16[22,16,256]{2,1,0:T(8,128)(2,1)S(1)}, u32[]{:S(2)}, u32[]{:S(2)}) collective-permute-start(bf16[22,16,256]{2,1,0:T(8,128)(2,1)S(1)} %get-tuple-element.25), channel_id=1, source_target_pairs={{0,1},{1,0},{2,3},{3,2},{4,5},{5,4},{6,7},{7,6},{8,9},{9,8},{10,11... | collective-permute-start | bytes 540680 | tf_op jit(solution)/shard_map/ppermute | solution.py:620
  16.5 8.5 %collective-permute-start.7 = (bf16[32,16,256]{2,1,0:T(8,128)(2,1)S(1)}, bf16[32,16,256]{2,1,0:T(8,128)(2,1)S(1)}, u32[]{:S(2)}, u32[]{:S(2)}) collective-permute-start(bf16[32,16,256]{2,1,0:T(8,128)(2,1)S(1)} %get-tuple-element.26), channel_id=1, source_target_pairs={{0,4},{4,8},{8,12},{12,28},{28,24},{24,20},{20,16},{16,0},{1,17},{... | collective-permute-start | bytes 786440 | tf_op jit(solution)/shard_map/ppermute | solution.py:51
  18.1 5.8 %collective-permute-start.5 = (bf16[12,16,256]{2,1,0:T(8,128)(2,1)S(1)}, bf16[12,16,256]{2,1,0:T(8,128)(2,1)S(1)}, u32[]{:S(2)}, u32[]{:S(2)}) collective-permute-start(bf16[12,16,256]{2,1,0:T(8,128)(2,1)S(1)} %bitcast.20), channel_id=1, source_target_pairs={{0,2},{2,0},{1,3},{3,1},{4,6},{6,4},{5,7},{7,5},{8,10},{10,8},{9,1... | collective-permute-start | bytes 294920 | tf_op jit(solution)/shard_map/ppermute | solution.py:27
  18.9 6.4 %copy-start.1 = (bf16[3,3,3,256,128]{4,3,2,1,0:T(8,128)(2,1)S(1)}, bf16[3,3,3,256,128]{4,3,2,1,0:T(8,128)(2,1)}, u32[]{:S(2)}) copy-start(bf16[3,3,3,256,128]{4,3,2,1,0:T(8,128)(2,1)} %param.20) | copy-start | bytes 5308420
  18.9 6.1 %collective-permute-start.8 = (bf16[10,16,256]{2,1,0:T(8,128)(2,1)S(1)}, bf16[10,16,256]{2,1,0:T(8,128)(2,1)S(1)}, u32[]{:S(2)}, u32[]{:S(2)}) collective-permute-start(bf16[10,16,256]{2,1,0:T(8,128)(2,1)S(1)} %bitcast.21), channel_id=1, source_target_pairs={{0,6},{2,4},{4,10},{6,8},{8,14},{10,12},{12,30},{14,28},{28,26},{3... | collective-permute-start | bytes 245768 | tf_op jit(solution)/shard_map/ppermute | solution.py:65
  25.3 1.6 %collective-permute-start.9 = (bf16[28,16,256]{2,1,0:T(8,128)(2,1)S(1)}, bf16[28,16,256]{2,1,0:T(8,128)(2,1)S(1)}, u32[]{:S(2)}, u32[]{:S(2)}) collective-permute-start(bf16[28,16,256]{2,1,0:T(8,128)(2,1)S(1)} %shard_map.118), channel_id=1, source_target_pairs={{0,1},{1,0},{2,3},{3,2},{4,5},{5,4},{6,7},{7,6},{8,9},{9,8},{10,11... | collective-permute-start | bytes 688136 | tf_op jit(solution)/shard_map/ppermute | solution.py:648
  25.4 2.0 %copy-start = (bf16[3,3,3,256,256]{4,3,2,1,0:T(8,128)(2,1)S(1)}, bf16[3,3,3,256,256]{4,3,2,1,0:T(8,128)(2,1)}, u32[]{:S(2)}) copy-start(bf16[3,3,3,256,256]{4,3,2,1,0:T(8,128)(2,1)} %param.16) | copy-start | bytes 10616836
  25.4 2.1 %copy-start.4 = (bf16[2,2,2,256,128]{4,3,2,1,0:T(8,128)(2,1)S(1)}, bf16[2,2,2,256,128]{4,3,2,1,0:T(8,128)(2,1)}, u32[]{:S(2)}) copy-start(bf16[2,2,2,256,128]{4,3,2,1,0:T(8,128)(2,1)} %param.18) | copy-start | bytes 1572868
  25.4 2.1 %copy-start.7 = (f32[256]{0:T(256)S(1)}, f32[256]{0:T(256)}, u32[]{:S(2)}) copy-start(f32[256]{0:T(256)} %param.17) | copy-start | bytes 3076
  25.4 2.1 %copy-start.9 = (f32[128]{0:T(128)S(1)}, f32[128]{0:T(128)}, u32[]{:S(2)}) copy-start(f32[128]{0:T(128)} %param.19) | copy-start | bytes 1540
  27.5 3.6 %copy-start.10 = (f32[128]{0:T(128)S(1)}, f32[128]{0:T(128)}, u32[]{:S(2)}) copy-start(f32[128]{0:T(128)} %param.21) | copy-start | bytes 1540
  30.5 1.7 %collective-permute-start.10 = (bf16[8,10,256]{2,1,0:T(8,128)(2,1)S(1)}, bf16[8,10,256]{2,1,0:T(8,128)(2,1)S(1)}, u32[]{:S(2)}, u32[]{:S(2)}) collective-permute-start(bf16[8,10,256]{2,1,0:T(8,128)(2,1)S(1)} %get-tuple-element.30), channel_id=1, source_target_pairs={{0,1},{1,0},{2,3},{3,2},{4,5},{5,4},{6,7},{7,6},{8,9},{9,8},{10,11... | collective-permute-start | bytes 122888 | tf_op jit(solution)/shard_map/ppermute | solution.py:716

commit v7 on v6

--- a/solution.py
+++ b/solution.py
@@ -190,11 +190,12 @@
     return put
 
 
-def fill_columns(columns, passed, frame, planes, corner_low, corner_high, spot, height, deep, tall, half):
+def fill_columns(
+    columns, passed, start, frame, planes, corner_low, corner_high, spot, height, deep, tall, half
+):
     plane_at, corner_at = spot
     count, corners = planes.shape[0] // 2, corner_low.shape[0] // 2
     total, rows, lanes = columns.shape
-    start = passed.shape[0] - total
     for plane in range(total):
         columns[plane] = passed[start + plane, :rows, :lanes]
     fill_planes(
@@ -416,25 +417,32 @@
     choose_side("narrow", corners, put)
 
 
-def pass_kernel(sizes, half, *refs):
-    own, low, high, planes, corner_low, corner_high, passed, ext = refs
-    (shape, deep, tall), (_, count, few) = sizes[0], layout(sizes)
-    depth, height = shape[:2]
+def pass_kernel(sizes, halves, *refs):
+    fields, (low, high, planes, corner_low, corner_high) = refs[: len(sizes)], refs[len(sizes) :][:5]
+    passed, frames = refs[len(sizes) + 5], refs[len(sizes) + 6 :]
+    spots, count, few = layout(sizes)
+    start = count + sides_of("narrow") * few
     passed[:count] = planes[count:]
     passed[count : count + few] = corner_low[few:]
-    start = passed.shape[0] - ext.shape[0]
     passed[start - few : start] = corner_high[few:]
-    fill_block(ext, own, low, high, 0, deep, tall)
-    near = (
-        rows_at(planes, 0, deep, height),
-        rows_at(corner_low, 0, deep, tall),
-        rows_at(corner_high, 0, deep, tall),
-    )
-    blank = tuple(jnp.zeros_like(part) for part in near)
-    either(sends_high(), put_sides(ext, depth, deep, near, blank))
-    clear_edges(ext, deep, tall)
-    for plane in range(ext.shape[0]):
-        put_column(passed, start + plane, inner_column(ext[plane], half))
+    at = 0
+    for own, ext, half, (shape, deep, tall), (plane_at, corner_at) in zip(
+        fields, frames, halves, sizes, spots
+    ):
+        depth, height = shape[:2]
+        fill_block(ext, own, low, high, at, deep, tall)
+        at += depth * tall
+        near = (
+            rows_at(planes, plane_at, deep, height),
+            rows_at(corner_low, corner_at, deep, tall),
+            rows_at(corner_high, corner_at, deep, tall),
+        )
+        blank = tuple(jnp.zeros_like(part) for part in near)
+        either(sends_high(), put_sides(ext, depth, deep, near, blank))
+        clear_edges(ext, deep, tall)
+        for plane in range(ext.shape[0]):
+            put_column(passed, start + plane, inner_column(ext[plane], half))
+        start += ext.shape[0]
 
 
 def weight_kernel(weight, packed):
@@ -468,8 +476,20 @@
     lanes = ext.shape[-1]
     spot = (0, 0)
     fill_frame(ext, own, low, high, planes, corner_low, corner_high, passed, spot, 0, 1, 1)
+    start = passed.shape[0] - ext.shape[0]
     fill_columns(
-        columns_in, passed, frame, planes, corner_low, corner_high, spot, own.shape[1], 1, 1, True
+        columns_in,
+        passed,
+        start,
+        frame,
+        planes,
+        corner_low,
+        corner_high,
+        spot,
+        own.shape[1],
+        1,
+        1,
+        True,
     )
     for plane in range(ext.shape[0]):
         before, after = pair_columns(columns_in, plane, slice(None))
@@ -508,25 +528,44 @@
     raised,
     encoded_ext,
     columns,
+    encoded_columns,
     coarse_ext,
     columns_in,
     frame,
+    encoded_frame,
     taps,
 ):
     lanes = coarse_ext.shape[-1]
     spots = layout(sizes)[0]
-    at = 0
-    for ext, own, spot, (shape, deep, tall) in zip(
-        (coarse_ext, encoded_ext), (coarse, encoded), spots, sizes
+    at, start = 0, passed.shape[0] - coarse_ext.shape[0] - encoded_ext.shape[0]
+    for ext, own, side, edge, half, spot, (shape, deep, tall) in zip(
+        (coarse_ext, encoded_ext),
+        (coarse, encoded),
+        (columns_in, encoded_columns),
+        (frame, encoded_frame),
+        (False, True),
+        spots,
+        sizes,
     ):
         fill_frame(
             ext, own, low, high, planes, corner_low, corner_high, passed, spot, at, deep, tall
         )
+        fill_columns(
+            side,
+            passed,
+            start,
+            edge,
+            planes,
+            corner_low,
+            corner_high,
+            spot,
+            shape[1],
+            deep,
+            tall,
+            half,
+        )
         at += shape[0] * tall
-    (shape, deep, tall), spot = sizes[0], spots[0]
-    fill_columns(
-        columns_in, passed, frame, planes, corner_low, corner_high, spot, shape[1], deep, tall, False
-    )
+        start += ext.shape[0]
     for plane in range(coarse_ext.shape[0]):
         before, after = pair_columns(columns_in, plane, slice(None))
         block = coarse_ext[plane]
@@ -535,14 +574,20 @@
         taps[plane, :, :, lanes : 2 * lanes] = block
         taps[plane, :, :, 2 * lanes :] = shifted(wide, after, -1).astype(bf16)
     deep, _, tall, _, count, _ = raised.shape
-    summed = conv_rows(taps, weight, deep, tall)
+    start, span = 0, tall
+    if sides_of("narrow") == 1:
+        start, span = jnp.where(lax.axis_index("narrow") == 0, 1, 0), tall - 1
+    summed = conv_sum(
+        taps, weight, 0, lambda a, b: [(slice(a, a + deep), pl.ds(b + start, span))]
+    )
     bottom = leaky_relu(summed + bias[...]).astype(bf16)
     both = jnp.tile(up_bias[...], (1, 2))
     for a in range(2):
         for b in range(2):
             matrix = jnp.concatenate([up[2 * a + b, 0], up[2 * a + b, 1]], axis=-1)
             lifted = jnp.dot(bottom, matrix, preferred_element_type=f32) + both
-            raised[:, a, :, b] = lifted.astype(bf16).reshape(deep, tall, count, lanes)
+            lifted = lifted.astype(bf16).reshape(deep, span, count, lanes)
+            raised[:, a, pl.ds(start, span), b] = lifted
     blank_plane = jnp.zeros(raised.shape[1:], bf16)
     blank_row = jnp.zeros((deep, 2, 2, count, lanes), bf16)
     first, last = edges("narrow")
@@ -566,47 +611,38 @@
         raised[deep - 1] = blank_plane
 
     planes, height = encoded_ext.shape[:2]
-    half = lanes // 2
     for plane in range(planes):
         z, a = (plane + 1) // 2, (plane + 1) % 2
         whole = raised[z, a].reshape(2 * tall, count, lanes)[1 : 1 + height]
-        columns[plane, :, :half] = inner_column(whole, True)
-        columns[plane, :, half:] = inner_column(encoded_ext[plane], True)
-
-
-def decode_kernel(
-    raised,
-    encoded_ext,
-    columns_in,
-    packed,
-    inner,
-    bias,
-    decoded,
-    raised_taps,
-    encoded_taps,
-    sums,
-    spread,
-):
-    planes, height, columns, lanes = encoded_ext.shape
-    half = lanes // 2
+        columns[plane] = inner_column(whole, True)
+
+
+def border_kernel(encoded_ext, columns_in, packed, inner, sums, taps):
+    lanes = taps.shape[-1]
+    for plane in range(encoded_ext.shape[0]):
+        low, high = pair_columns(columns_in, plane, slice(None))
+        spread_pairs(taps.at[plane], 0, encoded_ext[plane], low, high)
+    depth, height = sums.shape[:2]
+    sums[1 : depth - 1, 1 : height - 1] = inner[...]
+    for where, block in conv_border(taps, packed, depth, height, packed.shape[1] - lanes):
+        sums[where] = block
+
+
+def decode_kernel(raised, columns_in, packed, partial, bias, decoded, taps, spread):
+    planes, height, columns, _ = taps.shape
     for plane in range(planes):
-        low, high = pair_columns(columns_in, plane, slice(0, half))
-        spread_pairs(raised_taps.at[plane], 0, raised[plane + 1, 1 : 1 + height], low, high)
-        low, high = pair_columns(columns_in, plane, slice(half, lanes))
-        spread_pairs(encoded_taps.at[plane], 0, encoded_ext[plane], low, high)
+        low, high = pair_columns(columns_in, plane, slice(None))
+        spread_pairs(taps.at[plane], 0, raised[plane + 1, 1 : 1 + height], low, high)
     depth, rows, _, outs = decoded.shape
-    sums[...] = conv_rows(raised_taps, packed, depth, rows).reshape(sums.shape)
-    sums[1 : depth - 1, 1 : rows - 1] += inner[...]
-    for where, block in conv_border(encoded_taps, packed, depth, rows, 2 * lanes):
-        sums[where] += block
-    summed = leaky_relu(sums[...] + jnp.tile(bias[...], (1, 2)))
+    summed = conv_rows(taps, packed, depth, rows).reshape(partial.shape) + partial[...]
+    summed = leaky_relu(summed + jnp.tile(bias[...], (1, 2)))
     for odd in range(2):
         half = summed[:, :, :, odd * outs : (odd + 1) * outs]
         spread[:, :, pl.ds(odd, columns, stride=2), :] = half
     decoded[...] = spread[...].astype(bf16)
 
 
-def exchange(fields, halos, half, weight, bias):
+def exchange(turn, fields, halos, halves, weight, bias):
     sizes = [(field.shape, deep, tall) for field, (deep, tall) in zip(fields, halos)]
     _, planes, corners = layout(sizes)
     depth, height = fields[-1].shape[:2]
@@ -631,20 +667,21 @@
     (weights,) = call(weight_kernel, [(9, 4 * weight.shape[2], 2 * outs)], (), 8)(weight)
     lanes = 2 * cells[1]
     (inner,) = call(
-        functools.partial(inner_kernel, weights.shape[1] - lanes, half),
+        functools.partial(inner_kernel, weights.shape[1] - lanes, turn == 0),
         [(depth - 2, height - 2) + cells],
         [pltpu.VMEM((depth, height, cells[0], lanes), bf16)],
-        dtype=bf16 if half else f32,
+        dtype=bf16 if turn == 0 else f32,
     )(fields[-1], handed, weights, bias)
     received = (low, high, ring, corner_low, corner_high)
-    shape, deep, tall = sizes[0]
-    framed = (shape[0] + 2 * deep, shape[1] + 2 * tall)
+    frames = [
+        (shape[0] + 2 * deep, shape[1] + 2 * tall) + cells for shape, deep, tall in sizes
+    ]
     (passed,) = call(
-        functools.partial(pass_kernel, sizes, half),
-        [(planes + sides * corners + framed[0],) + cells],
-        [pltpu.VMEM(framed + cells, bf16)],
+        functools.partial(pass_kernel, sizes, halves),
+        [(planes + sides * corners + sum(frame[0] for frame in frames),) + cells],
+        [pltpu.VMEM(frame, bf16) for frame in frames],
         8,
-    )(fields[0], *received)
+    )(*fields, *received)
     passed = lax.ppermute(passed, "pair", swap)
     return sizes, weights, inner, received + (passed,)
 
@@ -667,7 +704,7 @@
     )(volume)
     encode_bias, decode_bias = b_encode.reshape(1, skip), b_decode.reshape(1, skip)
     _, encode_weights, inner, received = exchange(
-        [packed], [(1, 1)], True, w_encode.reshape(9, 3, skip, skip), encode_bias
+        0, [packed], [(1, 1)], [True], w_encode.reshape(9, 3, skip, skip), encode_bias
     )
     encoded, coarse = call(
         encode_kernel,
@@ -689,19 +726,26 @@
     )
 
     sizes, decode_weights, inner, received = exchange(
-        [coarse, encoded], [(2, 2), (1, 1)], False, w_decode.reshape(9, 3, lanes, skip), decode_bias
-    )
-    raised, encoded_ext, columns = call(
+        1,
+        [coarse, encoded],
+        [(2, 2), (1, 1)],
+        [False, True],
+        w_decode.reshape(9, 3, lanes, skip),
+        decode_bias,
+    )
+    raised, encoded_ext, columns, encoded_columns = call(
         functools.partial(bottom_kernel, sizes),
         [
             (half_depth + 2, 2, half_height + 2, 2, pairs, lanes),
             framed + (pairs, lanes),
-            framed + (lanes,),
+            framed + (skip,),
+            framed + (skip,),
         ],
         [
             pltpu.VMEM(coarse_framed + (pairs, deep_width), bf16),
             pltpu.VMEM(coarse_framed + (deep_width,), bf16),
             pltpu.VMEM((2, half_height + 4, pairs, deep_width), bf16),
+            pltpu.VMEM((1, height + 2, pairs, lanes), bf16),
             pltpu.VMEM(coarse_framed + (pairs, 3 * deep_width), bf16),
         ],
     )(
@@ -713,23 +757,21 @@
         w_up.reshape(4, 2, deep_width, skip),
         b_up.reshape(1, skip),
     )
+    taps = pltpu.VMEM(framed + (pairs, 2 * lanes), bf16)
     columns = lax.ppermute(columns, "pair", [(0, 1), (1, 0)])
+    (partial,) = call(
+        border_kernel, [(depth, height, pairs, lanes)], [taps], dtype=f32
+    )(encoded_ext, encoded_columns, decode_weights, inner)
 
     (decoded,) = call(
         decode_kernel,
         [(depth, height, width, skip)],
-        [
-            pltpu.VMEM(framed + (pairs, 2 * lanes), bf16),
-            pltpu.VMEM(framed + (pairs, 2 * lanes), bf16),
-            pltpu.VMEM((depth, height, pairs, lanes), f32),
-            pltpu.VMEM((depth, height, width, skip), f32),
-        ],
+        [taps, pltpu.VMEM((depth, height, width, skip), f32)],
     )(
         raised.reshape(depth + 4, height + 4, pairs, lanes),
-        encoded_ext,
         columns,
         decode_weights,
-        inner,
+        partial,
         decode_bias,
     )
     return decoded

time: 36.1 us -> 35.4 us (0.981)
    ppermute x2, waiting for transfers between devices: 2.56 us -> 5.3 us  [ring_exchange(): return lax.ppermute(sent, ('groups', 'wide', 'pair'), pairs)]
    ppermute x2, waiting for transfers between devices: 2.75 us -> 1.2 us  [line_exchange(): got = lax.ppermute(sent[0], axis, [(0, 1), (1, 0)])]
    ppermute x2, waiting for transfers between devices: 1.12 us -> 0.31 us  [exchange(): handed = lax.ppermute(handed, 'pair', swap)]
    ppermute x2, waiting for transfers between devices: 1 us -> 0.59 us  [exchange(): passed = lax.ppermute(passed, 'pair', swap)]
    pallas_call x5 -> x6, Pallas kernels: 6.34 us -> 6.65 us  [the longest x1 2.85 us: body(): call(decode_kernel, [(depth, height, width, skip)], [taps, pltpu.VMEM((de...]
  transfers between devices with their start and end apart: 11 -> 11, of which waited for: 7 -> 8; matrix products, arithmetic and copies ran while one was open for 0% -> 0% of each run, Pallas kernels for 9% -> 12%
where the time goes in v7:
time: 35.4 us; the launch traced here: 35.3 us
  starting transfers between devices  12.4 us (35%)
  Pallas kernels  12.3 us (35%)
  waiting for transfers between devices  8.75 us (25%)
  local copies, waits for them, and re-layouts  1.6 us (5%)
    ppermute x2, waiting for transfers between devices, ring_exchange(): return lax.ppermute(sent, ('groups', 'wide', 'pair'), pairs)  5.3 us
    ppermute x2, starting transfers between devices, move(): return lax.ppermute(array, ('groups', 'wide', 'narrow', 'pair'), pairs)  4.26 us
    ppermute x2, starting transfers between devices, line_exchange(): got = lax.ppermute(sent[0], axis, [(0, 1), (1, 0)])  3.37 us
    ppermute x2, starting transfers between devices, ring_exchange(): return lax.ppermute(sent, ('groups', 'wide', 'pair'), pairs)  3.15 us
    pallas_call x1, Pallas kernels, body(): call(decode_kernel, [(depth, height, width, skip)], [taps, pltpu.VMEM((de...  2.85 us
    pallas_call x1, Pallas kernels, body(): call(functools.partial(bottom_kernel, sizes), [(half_depth + 2, 2, half_h...  2.74 us
    pallas_call x2, Pallas kernels, exchange(): call(functools.partial(inner_kernel, weights.shape[1] - lanes, turn == 0)...  2.22 us
    pallas_call x1, Pallas kernels, body(): call(encode_kernel, [(depth, height, pairs, lanes), (half_depth, half_hei...  1.64 us
  transfers between devices with their start and end apart: 11, of which 8 were waited for; matrix products, arithmetic and copies ran while one was open for 0% of the time, Pallas kernels for 12%

profile of v7, /device:TPU:0, one launch (start us, length us, event | category | flops | bytes accessed | tf_op | source)
XLA Modules:
  0.0 35.3 jit_solution(11911055017970047632)
XLA Ops:
  0.0 1.0 %copy-done.5 = bf16[6,8,32,128]{3,2,1,0:T(8,128)(2,1)S(1)} copy-done((bf16[6,8,32,128]{3,2,1,0:T(8,128)(2,1)S(1)}, bf16[6,8,32,128]{3,2,1,0:T(8,128)(2,1)}, u32[]{:S(2)}) %copy-start.5) | copy-done | bytes 393240
  1.0 0.1 shard_map.109.refs_0_.field.own
  1.1 0.1 shard_map.110
  1.2 0.6 %collective-permute-start.1 = (bf16[14,16,256]{2,1,0:T(8,128)(2,1)S(1)}, bf16[14,16,256]{2,1,0:T(8,128)(2,1)S(1)}, u32[]{:S(2)}, u32[]{:S(2)}) collective-permute-start(bf16[14,16,256]{2,1,0:T(8,128)(2,1)S(1)} %get-tuple-element.20), channel_id=1, source_target_pairs={{0,1},{1,0},{2,3},{3,2},{4,5},{5,4},{6,7},{7,6},{8,9},{9,8},{10,11... | collective-permute-start | bytes 344072 | tf_op jit(solution)/shard_map/ppermute | solution.py:656
  1.8 2.6 %collective-permute-start = (bf16[6,16,256]{2,1,0:T(8,128)(2,1)S(1)}, bf16[6,16,256]{2,1,0:T(8,128)(2,1)S(1)}, u32[]{:S(2)}, u32[]{:S(2)}) collective-permute-start(bf16[6,16,256]{2,1,0:T(8,128)(2,1)S(1)} %bitcast.22), channel_id=1, source_target_pairs={{0,2},{2,0},{1,3},{3,1},{4,6},{6,4},{5,7},{7,5},{8,10},{10,8},{9,1... | collective-permute-start | bytes 147464 | tf_op jit(solution)/shard_map/ppermute | solution.py:27
  4.4 0.0 collective-permute-done.1.refs_1_.handed
  4.4 2.3 %collective-permute-start.3 = (bf16[2,16,256]{2,1,0:T(8,128)(2,1)S(1)}, bf16[2,16,256]{2,1,0:T(8,128)(2,1)S(1)}, u32[]{:S(2)}, u32[]{:S(2)}) collective-permute-start(bf16[2,16,256]{2,1,0:T(8,128)(2,1)S(1)} %bitcast.23), channel_id=1, source_target_pairs={{0,6},{2,4},{4,10},{6,8},{8,14},{10,12},{12,30},{14,28},{28,26},{3... | collective-permute-start | bytes 49160 | tf_op jit(solution)/shard_map/ppermute | solution.py:65
  6.7 1.6 %collective-permute-start.2 = (bf16[16,16,256]{2,1,0:T(8,128)(2,1)S(1)}, bf16[16,16,256]{2,1,0:T(8,128)(2,1)S(1)}, u32[]{:S(2)}, u32[]{:S(2)}) collective-permute-start(bf16[16,16,256]{2,1,0:T(8,128)(2,1)S(1)} %get-tuple-element.21), channel_id=1, source_target_pairs={{0,4},{4,8},{8,12},{12,28},{28,24},{24,20},{20,16},{16,0},{1,17},{... | collective-permute-start | bytes 393224 | tf_op jit(solution)/shard_map/ppermute | solution.py:51
  8.3 0.0 copy-done.2
  8.3 0.3 shard_map.113.packed
  8.6 0.0 copy-start.8
  8.6 0.0 collective-permute-done.refs_1_.refs_2_.low.high
  8.6 0.5 %collective-permute-done.3.refs_4_.refs_5_.corner_low.corner_high = bf16[2,16,256]{2,1,0:T(8,128)(2,1)S(1)} collective-permute-done((bf16[2,16,256]{2,1,0:T(8,128)(2,1)S(1)}, bf16[2,16,256]{2,1,0:T(8,128)(2,1)S(1)}, u32[]{:S(2)}, u32[]{:S(2)}) %collective-permute-start.3) | collective-permute-done | bytes 16416 | tf_op jit(solution)/shard_map/ppermute | solution.py:65
  9.1 2.6 %collective-permute-done.2.refs_3_.planes = bf16[16,16,256]{2,1,0:T(8,128)(2,1)S(1)} collective-permute-done((bf16[16,16,256]{2,1,0:T(8,128)(2,1)S(1)}, bf16[16,16,256]{2,1,0:T(8,128)(2,1)S(1)}, u32[]{:S(2)}, u32[]{:S(2)}) %collective-permute-start.2) | collective-permute-done | bytes 131104 | tf_op jit(solution)/shard_map/ppermute | solution.py:51
  11.6 0.1 shard_map.112
  11.8 0.1 collective-permute-start.4
  11.9 0.0 copy-start.3
  11.9 0.0 copy-start.6
  11.9 1.1 %shard_map.114.inner = bf16[4,6,16,256]{3,2,1,0:T(8,128)(2,1)S(1)} custom-call(bf16[6,8,16,256]{3,2,1,0:T(8,128)(2,1)S(1)} %shard_map.109.refs_0_.field.own, bf16[14,16,256]{2,1,0:T(8,128)(2,1)S(1)} %collective-permute-done.1.refs_1_.handed, bf16[9,512,256]{2,1,0:T(8,128)(2,1)S(1)} %shard_map.113.packed, f32[1,128]{1,0:T(1,128)S(1)} %bitcast.26), custom_call_target="tpu_custom_call" | custom-call | flops 4000000000 | bytes 1000000 | tf_op jit(solution)/shard_map/pallas_call | solution.py:669
  13.0 0.2 collective-permute-done.4.passed
  13.2 1.6 %shard_map.115 = (bf16[6,8,16,256]{3,2,1,0:T(8,128)(2,1)S(1)}, bf16[3,4,16,256]{3,2,1,0:T(8,128)(2,1)S(1)}) custom-call(bf16[6,8,16,256]{3,2,1,0:T(8,128)(2,1)S(1)} %shard_map.109.refs_0_.field.own, bf16[6,16,256]{2,1,0:T(8,128)(2,1)S(1)} %collective-permute-done.refs_1_.refs_2_.low.high, ...), custom_call_target="tpu_custom_call" | custom-call | flops 4000000000 | bytes 1000000 | tf_op jit(solution)/shard_map/pallas_call | solution.py:709
  14.9 0.1 shard_map.116
  15.0 0.4 %collective-permute-start.6 = (bf16[22,16,256]{2,1,0:T(8,128)(2,1)S(1)}, bf16[22,16,256]{2,1,0:T(8,128)(2,1)S(1)}, u32[]{:S(2)}, u32[]{:S(2)}) collective-permute-start(bf16[22,16,256]{2,1,0:T(8,128)(2,1)S(1)} %get-tuple-element.26), channel_id=1, source_target_pairs={{0,1},{1,0},{2,3},{3,2},{4,5},{5,4},{6,7},{7,6},{8,9},{9,8},{10,11... | collective-permute-start | bytes 540680 | tf_op jit(solution)/shard_map/ppermute | solution.py:656
  15.3 0.8 %collective-permute-start.5 = (bf16[12,16,256]{2,1,0:T(8,128)(2,1)S(1)}, bf16[12,16,256]{2,1,0:T(8,128)(2,1)S(1)}, u32[]{:S(2)}, u32[]{:S(2)}) collective-permute-start(bf16[12,16,256]{2,1,0:T(8,128)(2,1)S(1)} %bitcast.20), channel_id=1, source_target_pairs={{0,2},{2,0},{1,3},{3,1},{4,6},{6,4},{5,7},{7,5},{8,10},{10,8},{9,1... | collective-permute-start | bytes 294920 | tf_op jit(solution)/shard_map/ppermute | solution.py:27
  16.2 0.3 collective-permute-done.6.refs_2_.handed
  16.5 2.0 %collective-permute-start.8 = (bf16[10,16,256]{2,1,0:T(8,128)(2,1)S(1)}, bf16[10,16,256]{2,1,0:T(8,128)(2,1)S(1)}, u32[]{:S(2)}, u32[]{:S(2)}) collective-permute-start(bf16[10,16,256]{2,1,0:T(8,128)(2,1)S(1)} %bitcast.21), channel_id=1, source_target_pairs={{0,6},{2,4},{4,10},{6,8},{8,14},{10,12},{12,30},{14,28},{28,26},{3... | collective-permute-start | bytes 245768 | tf_op jit(solution)/shard_map/ppermute | solution.py:65
  18.5 1.6 %collective-permute-start.7 = (bf16[32,16,256]{2,1,0:T(8,128)(2,1)S(1)}, bf16[32,16,256]{2,1,0:T(8,128)(2,1)S(1)}, u32[]{:S(2)}, u32[]{:S(2)}) collective-permute-start(bf16[32,16,256]{2,1,0:T(8,128)(2,1)S(1)} %get-tuple-element.27), channel_id=1, source_target_pairs={{0,4},{4,8},{8,12},{12,28},{28,24},{24,20},{20,16},{16,0},{1,17},{... | collective-permute-start | bytes 786440 | tf_op jit(solution)/shard_map/ppermute | solution.py:51
  20.1 0.6 %shard_map.120.packed = bf16[9,1024,256]{2,1,0:T(8,128)(2,1)S(1)} custom-call(bf16[9,3,256,128]{3,2,1,0:T(8,128)(2,1)S(1)} %bitcast.16), custom_call_target="tpu_custom_call" | custom-call | flops 4000000000 | bytes 1000000 | tf_op jit(solution)/shard_map/pallas_call | solution.py:667
  20.7 0.0 copy-start.10
  20.7 1.2 %collective-permute-done.5.refs_2_.refs_3_.low.high = bf16[12,16,256]{2,1,0:T(8,128)(2,1)S(1)} collective-permute-done((bf16[12,16,256]{2,1,0:T(8,128)(2,1)S(1)}, bf16[12,16,256]{2,1,0:T(8,128)(2,1)S(1)}, u32[]{:S(2)}, u32[]{:S(2)}) %collective-permute-start.5) | collective-permute-done | bytes 98336 | tf_op jit(solution)/shard_map/ppermute | solution.py:27
  21.9 0.8 %collective-permute-done.8.refs_5_.refs_6_.corner_low.corner_high = bf16[10,16,256]{2,1,0:T(8,128)(2,1)S(1)} collective-permute-done((bf16[10,16,256]{2,1,0:T(8,128)(2,1)S(1)}, bf16[10,16,256]{2,1,0:T(8,128)(2,1)S(1)}, u32[]{:S(2)}, u32[]{:S(2)}) %collective-permute-start.8) | collective-permute-done | bytes 81952 | tf_op jit(solution)/shard_map/ppermute | solution.py:65
  22.7 2.7 %collective-permute-done.7.refs_4_.planes = bf16[32,16,256]{2,1,0:T(8,128)(2,1)S(1)} collective-permute-done((bf16[32,16,256]{2,1,0:T(8,128)(2,1)S(1)}, bf16[32,16,256]{2,1,0:T(8,128)(2,1)S(1)}, u32[]{:S(2)}, u32[]{:S(2)}) %collective-permute-start.7) | collective-permute-done | bytes 262176 | tf_op jit(solution)/shard_map/ppermute | solution.py:51
  25.5 0.3 shard_map.118
  25.8 0.1 collective-permute-start.9
  25.9 0.0 copy-start
  25.9 0.0 copy-start.4
  25.9 0.0 copy-start.7
  25.9 0.0 copy-start.9
  25.9 1.1 %shard_map.121.inner = f32[4,6,16,256]{3,2,1,0:T(8,128)S(1)} custom-call(bf16[6,8,16,256]{3,2,1,0:T(8,128)(2,1)S(1)} %get-tuple-element.24.refs_1_.encoded.field, bf16[22,16,256]{2,1,0:T(8,128)(2,1)S(1)} %collective-permute-done.6.refs_2_.handed, bf16[9,1024,256]{2,1,0:T(8,128)(2,1)S(1)} %shard_map.120.packed, f32[1,128]{1,0:T(1,128)S(1)} %bitcast.29), custom_call_target="tpu_custom_call" | custom-call | flops 4000000000 | bytes 1000000 | tf_op jit(solution)/shard_map/pallas_call | solution.py:669
  27.0 0.4 %collective-permute-done.9.passed = bf16[36,16,256]{2,1,0:T(8,128)(2,1)S(1)} collective-permute-done((bf16[36,16,256]{2,1,0:T(8,128)(2,1)S(1)}, bf16[36,16,256]{2,1,0:T(8,128)(2,1)S(1)}, u32[]{:S(2)}, u32[]{:S(2)}) %collective-permute-start.9) | collective-permute-done | bytes 294944 | tf_op jit(solution)/shard_map/ppermute | solution.py:685
  27.4 0.4 %copy-done = bf16[3,3,3,256,256]{4,3,2,1,0:T(8,128)(2,1)S(1)} copy-done((bf16[3,3,3,256,256]{4,3,2,1,0:T(8,128)(2,1)S(1)}, bf16[3,3,3,256,256]{4,3,2,1,0:T(8,128)(2,1)}, u32[]{:S(2)}) %copy-start) | copy-done | bytes 3538968
  27.9 0.1 copy-done.4
  28.0 0.0 copy-done.9
  28.0 2.7 %shard_map.119 = (bf16[5,2,6,2,16,256]{5,4,3,2,1,0:T(8,128)(2,1)S(1)}, bf16[8,10,16,256]{3,2,1,0:T(8,128)(2,1)S(1)}, bf16[8,10,128]{2,1,0:T(8,128)(2,1)S(1)}, bf16[8,10,128]{2,1,0:T(8,128)(2,1)S(1)}) custom-call(bf16[3,4,16,256]{3,2,1,0:T(8,128)(2,1)S(1)} %get-tuple-element.23.refs_0_.coarse, ...), custom_call_target="tpu_custom_call" | custom-call | flops 4000000000 | bytes 1000000 | tf_op jit(solution)/shard_map/pallas_call | solution.py:736
  30.7 0.6 %collective-permute-start.10 = (bf16[8,10,128]{2,1,0:T(8,128)(2,1)S(1)}, bf16[8,10,128]{2,1,0:T(8,128)(2,1)S(1)}, u32[]{:S(2)}, u32[]{:S(2)}) collective-permute-start(bf16[8,10,128]{2,1,0:T(8,128)(2,1)S(1)} %get-tuple-element.30), channel_id=1, source_target_pairs={{0,1},{1,0},{2,3},{3,2},{4,5},{5,4},{6,7},{7,6},{8,9},{9,8},{10,11... | collective-permute-start | bytes 61448 | tf_op jit(solution)/shard_map/ppermute | solution.py:761
  31.3 1.1 %shard_map.122.partial = f32[6,8,16,256]{3,2,1,0:T(8,128)S(1)} custom-call(bf16[8,10,16,256]{3,2,1,0:T(8,128)(2,1)S(1)} %get-tuple-element.31.encoded_ext, bf16[8,10,128]{2,1,0:T(8,128)(2,1)S(1)} %get-tuple-element.32.columns_in, bf16[9,1024,256]{2,1,0:T(8,128)(2,1)S(1)} %shard_map.120.packed, f32[4,6,16,256]{3,2,1,0:T(8,128)S(1)} %shard_map.121.inner), custom_call_target="tpu_custom_call" | custom-call | flops 4000000000 | bytes 1000000 | tf_op jit(solution)/shard_map/pallas_call | solution.py:762
  32.4 0.0 collective-permute-done.10.columns_in
  32.4 2.9 %shard_map.123 = bf16[6,8,32,128]{3,2,1,0:T(8,128)(2,1)} custom-call(bf16[10,12,16,256]{3,2,1,0:T(8,128)(2,1)S(1)} %bitcast.31, bf16[8,10,128]{2,1,0:T(8,128)(2,1)S(1)} %collective-permute-done.10.columns_in, bf16[9,1024,256]{2,1,0:T(8,128)(2,1)S(1)} %shard_map.120.packed, f32[6,8,16,256]{3,2,1,0:T(8,128)S(1)} %shard_map.122.partial, f32[1,128]{1,0:T(1,128)S(1)} %bitcast.30), custom_call_target="tpu_custom_call" | custom-call | flops 4000000000 | bytes 1000000 | tf_op jit(solution)/shard_map/pallas_call | solution.py:766
  (11 shorter events, 0.1 us)
Async XLA Ops:
  0.0 1.0 %copy-start.5 = (bf16[6,8,32,128]{3,2,1,0:T(8,128)(2,1)S(1)}, bf16[6,8,32,128]{3,2,1,0:T(8,128)(2,1)}, u32[]{:S(2)}) copy-start(bf16[6,8,32,128]{3,2,1,0:T(8,128)(2,1)} %volume.1) | copy-start | bytes 1179652
  1.2 3.1 %collective-permute-start.1 = (bf16[14,16,256]{2,1,0:T(8,128)(2,1)S(1)}, bf16[14,16,256]{2,1,0:T(8,128)(2,1)S(1)}, u32[]{:S(2)}, u32[]{:S(2)}) collective-permute-start(bf16[14,16,256]{2,1,0:T(8,128)(2,1)S(1)} %get-tuple-element.20), channel_id=1, source_target_pairs={{0,1},{1,0},{2,3},{3,2},{4,5},{5,4},{6,7},{7,6},{8,9},{9,8},{10,11... | collective-permute-start | bytes 344072 | tf_op jit(solution)/shard_map/ppermute | solution.py:656
  1.8 6.5 %copy-start.2 = (bf16[3,3,3,128,128]{4,3,2,1,0:T(8,128)(2,1)S(1)}, bf16[3,3,3,128,128]{4,3,2,1,0:T(8,128)(2,1)}, u32[]{:S(2)}) copy-start(bf16[3,3,3,128,128]{4,3,2,1,0:T(8,128)(2,1)} %param.12) | copy-start | bytes 2654212
  1.8 6.8 %collective-permute-start = (bf16[6,16,256]{2,1,0:T(8,128)(2,1)S(1)}, bf16[6,16,256]{2,1,0:T(8,128)(2,1)S(1)}, u32[]{:S(2)}, u32[]{:S(2)}) collective-permute-start(bf16[6,16,256]{2,1,0:T(8,128)(2,1)S(1)} %bitcast.22), channel_id=1, source_target_pairs={{0,2},{2,0},{1,3},{3,1},{4,6},{6,4},{5,7},{7,5},{8,10},{10,8},{9,1... | collective-permute-start | bytes 147464 | tf_op jit(solution)/shard_map/ppermute | solution.py:27
  4.4 4.7 %collective-permute-start.3 = (bf16[2,16,256]{2,1,0:T(8,128)(2,1)S(1)}, bf16[2,16,256]{2,1,0:T(8,128)(2,1)S(1)}, u32[]{:S(2)}, u32[]{:S(2)}) collective-permute-start(bf16[2,16,256]{2,1,0:T(8,128)(2,1)S(1)} %bitcast.23), channel_id=1, source_target_pairs={{0,6},{2,4},{4,10},{6,8},{8,14},{10,12},{12,30},{14,28},{28,26},{3... | collective-permute-start | bytes 49160 | tf_op jit(solution)/shard_map/ppermute | solution.py:65
  6.7 5.0 %collective-permute-start.2 = (bf16[16,16,256]{2,1,0:T(8,128)(2,1)S(1)}, bf16[16,16,256]{2,1,0:T(8,128)(2,1)S(1)}, u32[]{:S(2)}, u32[]{:S(2)}) collective-permute-start(bf16[16,16,256]{2,1,0:T(8,128)(2,1)S(1)} %get-tuple-element.21), channel_id=1, source_target_pairs={{0,4},{4,8},{8,12},{12,28},{28,24},{24,20},{20,16},{16,0},{1,17},{... | collective-permute-start | bytes 393224 | tf_op jit(solution)/shard_map/ppermute | solution.py:51
  8.6 3.3 %copy-start.8 = (f32[128]{0:T(128)S(1)}, f32[128]{0:T(128)}, u32[]{:S(2)}) copy-start(f32[128]{0:T(128)} %param.13) | copy-start | bytes 1540
  11.8 1.4 %collective-permute-start.4 = (bf16[17,16,256]{2,1,0:T(8,128)(2,1)S(1)}, bf16[17,16,256]{2,1,0:T(8,128)(2,1)S(1)}, u32[]{:S(2)}, u32[]{:S(2)}) collective-permute-start(bf16[17,16,256]{2,1,0:T(8,128)(2,1)S(1)} %shard_map.112), channel_id=1, source_target_pairs={{0,1},{1,0},{2,3},{3,2},{4,5},{5,4},{6,7},{7,6},{8,9},{9,8},{10,11... | collective-permute-start | bytes 417800 | tf_op jit(solution)/shard_map/ppermute | solution.py:685
  11.9 1.3 %copy-start.3 = (bf16[2,2,2,128,256]{4,3,2,1,0:T(8,128)(2,1)S(1)}, bf16[2,2,2,128,256]{4,3,2,1,0:T(8,128)(2,1)}, u32[]{:S(2)}) copy-start(bf16[2,2,2,128,256]{4,3,2,1,0:T(8,128)(2,1)} %param.14) | copy-start | bytes 1572868
  11.9 1.3 %copy-start.6 = (f32[256]{0:T(256)S(1)}, f32[256]{0:T(256)}, u32[]{:S(2)}) copy-start(f32[256]{0:T(256)} %param.15) | copy-start | bytes 3076
  15.0 1.5 %collective-permute-start.6 = (bf16[22,16,256]{2,1,0:T(8,128)(2,1)S(1)}, bf16[22,16,256]{2,1,0:T(8,128)(2,1)S(1)}, u32[]{:S(2)}, u32[]{:S(2)}) collective-permute-start(bf16[22,16,256]{2,1,0:T(8,128)(2,1)S(1)} %get-tuple-element.26), channel_id=1, source_target_pairs={{0,1},{1,0},{2,3},{3,2},{4,5},{5,4},{6,7},{7,6},{8,9},{9,8},{10,11... | collective-permute-start | bytes 540680 | tf_op jit(solution)/shard_map/ppermute | solution.py:656
  15.3 4.7 %copy-start.1 = (bf16[3,3,3,256,128]{4,3,2,1,0:T(8,128)(2,1)S(1)}, bf16[3,3,3,256,128]{4,3,2,1,0:T(8,128)(2,1)}, u32[]{:S(2)}) copy-start(bf16[3,3,3,256,128]{4,3,2,1,0:T(8,128)(2,1)} %param.20) | copy-start | bytes 5308420
  15.3 6.5 %collective-permute-start.5 = (bf16[12,16,256]{2,1,0:T(8,128)(2,1)S(1)}, bf16[12,16,256]{2,1,0:T(8,128)(2,1)S(1)}, u32[]{:S(2)}, u32[]{:S(2)}) collective-permute-start(bf16[12,16,256]{2,1,0:T(8,128)(2,1)S(1)} %bitcast.20), channel_id=1, source_target_pairs={{0,2},{2,0},{1,3},{3,1},{4,6},{6,4},{5,7},{7,5},{8,10},{10,8},{9,1... | collective-permute-start | bytes 294920 | tf_op jit(solution)/shard_map/ppermute | solution.py:27
  16.5 6.2 %collective-permute-start.8 = (bf16[10,16,256]{2,1,0:T(8,128)(2,1)S(1)}, bf16[10,16,256]{2,1,0:T(8,128)(2,1)S(1)}, u32[]{:S(2)}, u32[]{:S(2)}) collective-permute-start(bf16[10,16,256]{2,1,0:T(8,128)(2,1)S(1)} %bitcast.21), channel_id=1, source_target_pairs={{0,6},{2,4},{4,10},{6,8},{8,14},{10,12},{12,30},{14,28},{28,26},{3... | collective-permute-start | bytes 245768 | tf_op jit(solution)/shard_map/ppermute | solution.py:65
  18.5 7.0 %collective-permute-start.7 = (bf16[32,16,256]{2,1,0:T(8,128)(2,1)S(1)}, bf16[32,16,256]{2,1,0:T(8,128)(2,1)S(1)}, u32[]{:S(2)}, u32[]{:S(2)}) collective-permute-start(bf16[32,16,256]{2,1,0:T(8,128)(2,1)S(1)} %get-tuple-element.27), channel_id=1, source_target_pairs={{0,4},{4,8},{8,12},{12,28},{28,24},{24,20},{20,16},{16,0},{1,17},{... | collective-permute-start | bytes 786440 | tf_op jit(solution)/shard_map/ppermute | solution.py:51
  20.7 5.2 %copy-start.10 = (f32[128]{0:T(128)S(1)}, f32[128]{0:T(128)}, u32[]{:S(2)}) copy-start(f32[128]{0:T(128)} %param.21) | copy-start | bytes 1540
  25.8 1.6 %collective-permute-start.9 = (bf16[36,16,256]{2,1,0:T(8,128)(2,1)S(1)}, bf16[36,16,256]{2,1,0:T(8,128)(2,1)S(1)}, u32[]{:S(2)}, u32[]{:S(2)}) collective-permute-start(bf16[36,16,256]{2,1,0:T(8,128)(2,1)S(1)} %shard_map.118), channel_id=1, source_target_pairs={{0,1},{1,0},{2,3},{3,2},{4,5},{5,4},{6,7},{7,6},{8,9},{9,8},{10,11... | collective-permute-start | bytes 884744 | tf_op jit(solution)/shard_map/ppermute | solution.py:685
  25.9 2.0 %copy-start = (bf16[3,3,3,256,256]{4,3,2,1,0:T(8,128)(2,1)S(1)}, bf16[3,3,3,256,256]{4,3,2,1,0:T(8,128)(2,1)}, u32[]{:S(2)}) copy-start(bf16[3,3,3,256,256]{4,3,2,1,0:T(8,128)(2,1)} %param.16) | copy-start | bytes 10616836
  25.9 2.1 %copy-start.4 = (bf16[2,2,2,256,128]{4,3,2,1,0:T(8,128)(2,1)S(1)}, bf16[2,2,2,256,128]{4,3,2,1,0:T(8,128)(2,1)}, u32[]{:S(2)}) copy-start(bf16[2,2,2,256,128]{4,3,2,1,0:T(8,128)(2,1)} %param.18) | copy-start | bytes 1572868
  25.9 2.1 %copy-start.7 = (f32[256]{0:T(256)S(1)}, f32[256]{0:T(256)}, u32[]{:S(2)}) copy-start(f32[256]{0:T(256)} %param.17) | copy-start | bytes 3076
  25.9 2.1 %copy-start.9 = (f32[128]{0:T(128)S(1)}, f32[128]{0:T(128)}, u32[]{:S(2)}) copy-start(f32[128]{0:T(128)} %param.19) | copy-start | bytes 1540
  30.7 1.7 %collective-permute-start.10 = (bf16[8,10,128]{2,1,0:T(8,128)(2,1)S(1)}, bf16[8,10,128]{2,1,0:T(8,128)(2,1)S(1)}, u32[]{:S(2)}, u32[]{:S(2)}) collective-permute-start(bf16[8,10,128]{2,1,0:T(8,128)(2,1)S(1)} %get-tuple-element.30), channel_id=1, source_target_pairs={{0,1},{1,0},{2,3},{3,2},{4,5},{5,4},{6,7},{7,6},{8,9},{9,8},{10,11... | collective-permute-start | bytes 61448 | tf_op jit(solution)/shard_map/ppermute | solution.py:761

commit v8 on v7

--- a/solution.py
+++ b/solution.py
@@ -70,9 +70,10 @@
     return move(sent[1], moves), move(sent[0], [(d, c) for c, d in moves])
 
 
-def call(kernel, outs, scratch=(), megabytes=24, dtype=bf16):
+def call(kernel, outs, scratch=(), megabytes=24, dtype=bf16, **specs):
     return pl.pallas_call(
         kernel,
+        **specs,
         out_shape=[jax.ShapeDtypeStruct(shape, dtype) for shape in outs],
         scratch_shapes=list(scratch),
         cost_estimate=pl.CostEstimate(flops=4 * 10**9, transcendentals=0, bytes_accessed=10**6),
@@ -197,7 +198,7 @@
     count, corners = planes.shape[0] // 2, corner_low.shape[0] // 2
     total, rows, lanes = columns.shape
     for plane in range(total):
-        columns[plane] = passed[start + plane, :rows, :lanes]
+        columns[plane] = passed[column_place(passed, start, plane, rows, lanes)]
     fill_planes(
         frame,
         0,
@@ -253,9 +254,9 @@
     )
 
 
-def pair_columns(got, plane, lanes):
+def pair_columns(column):
     first, last = edges("pair")
-    column = got[plane, :, lanes].astype(f32)
+    column = column.astype(f32)
     blank = jnp.zeros_like(column)
     return jnp.where(first, blank, column), jnp.where(last, blank, column)
 
@@ -324,10 +325,11 @@
 
 def inner_kernel(base, final, field, handed, packed, bias, out, taps):
     depth, height, _, lanes = field.shape
-    start = handed.shape[0] - depth
-    columns_in = handed.at[start:, :height, : lanes // 2]
+    start = handed.shape[0] - field_slabs(field.shape, True)
     for plane in range(depth):
-        before, after = pair_columns(columns_in, plane, slice(None))
+        before, after = pair_columns(
+            handed[column_place(handed, start, plane, height, lanes // 2)]
+        )
         spread_pairs(taps.at[plane], 0, field[plane], before, after)
     summed = conv_rows(taps, packed, depth - 2, height - 2, base)
     if final:
@@ -360,14 +362,41 @@
         out[:, :, odd * lanes : (odd + 1) * lanes] = half.astype(bf16)
 
 
-def pack_kernel(volume, packed, spread):
-    for plane in range(volume.shape[0]):
-        pack_pairs(packed.at[plane], volume[plane], spread.at[plane])
-
-
-def put_column(ref, at, column):
-    ref[at] = jnp.zeros(ref.shape[1:], bf16)
-    ref[at, : column.shape[0], : column.shape[1]] = column
+def pack_kernel(volume, packed, here, spread, arrived):
+    copies = [
+        pltpu.make_async_copy(volume.at[plane], here.at[plane], arrived.at[plane])
+        for plane in range(volume.shape[0])
+    ]
+    for copy in copies:
+        copy.start()
+    for plane, copy in enumerate(copies):
+        copy.wait()
+        pack_pairs(packed.at[plane], here[plane], spread.at[plane])
+
+
+def per_tile(cells, rows, lanes):
+    return max(cells[0] // (-(-rows // 8) * 8), 1), cells[1] // lanes
+
+
+def slabs(cells, planes, rows, lanes):
+    down, across = per_tile(cells, rows, lanes)
+    return -(-planes // (down * across))
+
+
+def column_place(ref, start, plane, rows, lanes):
+    down, across = per_tile(ref.shape[1:], rows, lanes)
+    slab, spot = divmod(plane, down * across)
+    row, lane = spot // across * (-(-rows // 8) * 8), spot % across * lanes
+    return start + slab, slice(row, row + rows), slice(lane, lane + lanes)
+
+
+def put_column(ref, start, plane, column):
+    place = column_place(ref, start, plane, *column.shape)
+    ref[place] = column
+
+
+def field_slabs(shape, half):
+    return slabs(shape[2:], shape[0], shape[1], shape[3] // 2 if half else shape[3])
 
 
 def edge_kernel(sizes, *refs):
@@ -385,8 +414,9 @@
     choose_side("narrow", edge_rows, put_rows)
     either(sends_high(), lambda high: put_boundary(handed, fields, sizes, not high))
     field, start = fields[-1], layout(sizes)[1]
+    handed[start:] = jnp.zeros((handed.shape[0] - start,) + handed.shape[1:], bf16)
     for plane in range(field.shape[0]):
-        put_column(handed, start + plane, inner_column(field[plane], True))
+        put_column(handed, start, plane, inner_column(field[plane], True))
 
 
 def put_boundary(out, fields, sizes, high):
@@ -425,6 +455,7 @@
     passed[:count] = planes[count:]
     passed[count : count + few] = corner_low[few:]
     passed[start - few : start] = corner_high[few:]
+    passed[start:] = jnp.zeros((passed.shape[0] - start,) + passed.shape[1:], bf16)
     at = 0
     for own, ext, half, (shape, deep, tall), (plane_at, corner_at) in zip(
         fields, frames, halves, sizes, spots
@@ -441,8 +472,8 @@
         either(sends_high(), put_sides(ext, depth, deep, near, blank))
         clear_edges(ext, deep, tall)
         for plane in range(ext.shape[0]):
-            put_column(passed, start + plane, inner_column(ext[plane], half))
-        start += ext.shape[0]
+            put_column(passed, start, plane, inner_column(ext[plane], half))
+        start += field_slabs(ext.shape, half)
 
 
 def weight_kernel(weight, packed):
@@ -476,7 +507,7 @@
     lanes = ext.shape[-1]
     spot = (0, 0)
     fill_frame(ext, own, low, high, planes, corner_low, corner_high, passed, spot, 0, 1, 1)
-    start = passed.shape[0] - ext.shape[0]
+    start = passed.shape[0] - field_slabs(ext.shape, True)
     fill_columns(
         columns_in,
         passed,
@@ -492,7 +523,7 @@
         True,
     )
     for plane in range(ext.shape[0]):
-        before, after = pair_columns(columns_in, plane, slice(None))
+        before, after = pair_columns(columns_in[plane])
         spread_pairs(taps.at[plane], 0, ext[plane], before, after)
     depth, height, columns, _ = encoded.shape
     deep, tall = coarse.shape[:2]
@@ -537,7 +568,8 @@
 ):
     lanes = coarse_ext.shape[-1]
     spots = layout(sizes)[0]
-    at, start = 0, passed.shape[0] - coarse_ext.shape[0] - encoded_ext.shape[0]
+    at, start = 0, passed.shape[0]
+    start -= field_slabs(coarse_ext.shape, False) + field_slabs(encoded_ext.shape, True)
     for ext, own, side, edge, half, spot, (shape, deep, tall) in zip(
         (coarse_ext, encoded_ext),
         (coarse, encoded),
@@ -565,9 +597,9 @@
             half,
         )
         at += shape[0] * tall
-        start += ext.shape[0]
+        start += field_slabs(ext.shape, half)
     for plane in range(coarse_ext.shape[0]):
-        before, after = pair_columns(columns_in, plane, slice(None))
+        before, after = pair_columns(columns_in[plane])
         block = coarse_ext[plane]
         wide = block.astype(f32)
         taps[plane, :, :, :lanes] = shifted(wide, before, 1).astype(bf16)
@@ -620,7 +652,7 @@
 def border_kernel(encoded_ext, columns_in, packed, inner, sums, taps):
     lanes = taps.shape[-1]
     for plane in range(encoded_ext.shape[0]):
-        low, high = pair_columns(columns_in, plane, slice(None))
+        low, high = pair_columns(columns_in[plane])
         spread_pairs(taps.at[plane], 0, encoded_ext[plane], low, high)
     depth, height = sums.shape[:2]
     sums[1 : depth - 1, 1 : height - 1] = inner[...]
@@ -631,7 +663,7 @@
 def decode_kernel(raised, columns_in, packed, partial, bias, decoded, taps, spread):
     planes, height, columns, _ = taps.shape
     for plane in range(planes):
-        low, high = pair_columns(columns_in, plane, slice(None))
+        low, high = pair_columns(columns_in[plane])
         spread_pairs(taps.at[plane], 0, raised[plane + 1, 1 : 1 + height], low, high)
     depth, rows, _, outs = decoded.shape
     summed = conv_rows(taps, packed, depth, rows).reshape(partial.shape) + partial[...]
@@ -651,7 +683,7 @@
     swap = [(0, 1), (1, 0)]
     rows = sum(shape[0] * tall for shape, _, tall in sizes)
     edge_rows, handed = call(
-        functools.partial(edge_kernel, sizes), [(sides, rows) + cells, (planes + depth,) + cells], (), 8
+        functools.partial(edge_kernel, sizes), [(sides, rows) + cells, (planes + field_slabs(fields[-1].shape, True),) + cells], (), 8
     )(*fields)
     handed = lax.ppermute(handed, "pair", swap)
     low, high = line_exchange("narrow", edge_rows)
@@ -676,9 +708,10 @@
     frames = [
         (shape[0] + 2 * deep, shape[1] + 2 * tall) + cells for shape, deep, tall in sizes
     ]
+    tail = sum(field_slabs(frame, half) for frame, half in zip(frames, halves))
     (passed,) = call(
         functools.partial(pass_kernel, sizes, halves),
-        [(planes + sides * corners + sum(frame[0] for frame in frames),) + cells],
+        [(planes + sides * corners + tail,) + cells],
         [pltpu.VMEM(frame, bf16) for frame in frames],
         8,
     )(*fields, *received)
@@ -699,9 +732,14 @@
     (packed,) = call(
         pack_kernel,
         [(depth, height, pairs, lanes)],
-        [pltpu.VMEM((depth, height, width, skip), f32)],
+        [
+            pltpu.VMEM((depth, height, width, skip), bf16),
+            pltpu.VMEM((depth, height, width, skip), f32),
+            pltpu.SemaphoreType.DMA((depth,)),
+        ],
         8,
-    )(volume)
+        in_specs=[pl.BlockSpec(memory_space=pltpu.HBM)],
+    )(pltpu.with_memory_space_constraint(volume, pltpu.HBM))
     encode_bias, decode_bias = b_encode.reshape(1, skip), b_decode.reshape(1, skip)
     _, encode_weights, inner, received = exchange(
         0, [packed], [(1, 1)], [True], w_encode.reshape(9, 3, skip, skip), encode_bias

time: 35.4 us -> 35.2 us (level)
  local copies, waits for them, and re-layouts: 1.6 us -> 0.68 us
  Pallas kernels: 12.3 us -> 13.2 us
  waiting for transfers between devices: 8.75 us -> 8.39 us
    pallas_call x1, Pallas kernels: 0.13 us -> 1.07 us  [body(): call(pack_kernel, [(depth, height, pairs, lanes)], [pltpu.VMEM((depth, he...]
    unnamed x22 -> x20, local copies, waits for them, and re-layouts: 1.6 us -> 0.68 us
where the time goes in v8:
time: 35.2 us; the launch traced here: 35.1 us
  Pallas kernels  13.2 us (38%)
  starting transfers between devices  12.5 us (36%)
  waiting for transfers between devices  8.39 us (24%)
  local copies, waits for them, and re-layouts  0.68 us (2%)
    ppermute x2, waiting for transfers between devices, ring_exchange(): return lax.ppermute(sent, ('groups', 'wide', 'pair'), pairs)  5.27 us
    ppermute x2, starting transfers between devices, move(): return lax.ppermute(array, ('groups', 'wide', 'narrow', 'pair'), pairs)  4.31 us
    ppermute x2, starting transfers between devices, line_exchange(): got = lax.ppermute(sent[0], axis, [(0, 1), (1, 0)])  3.41 us
    ppermute x2, starting transfers between devices, ring_exchange(): return lax.ppermute(sent, ('groups', 'wide', 'pair'), pairs)  3.15 us
    pallas_call x1, Pallas kernels, body(): call(decode_kernel, [(depth, height, width, skip)], [taps, pltpu.VMEM((de...  2.85 us
    pallas_call x1, Pallas kernels, body(): call(functools.partial(bottom_kernel, sizes), [(half_depth + 2, 2, half_h...  2.72 us
    pallas_call x2, Pallas kernels, exchange(): call(functools.partial(inner_kernel, weights.shape[1] - lanes, turn == 0)...  2.21 us
    pallas_call x1, Pallas kernels, body(): call(encode_kernel, [(depth, height, pairs, lanes), (half_depth, half_hei...  1.64 us
  transfers between devices with their start and end apart: 11, of which 8 were waited for; matrix products, arithmetic and copies ran while one was open for 0% of the time, Pallas kernels for 12%

profile of v8, /device:TPU:0, one launch (start us, length us, event | category | flops | bytes accessed | tf_op | source)
XLA Modules:
  0.0 35.1 jit_solution(9971753979757582427)
XLA Ops:
  0.0 1.1 %shard_map.109.refs_0_.field.own = bf16[6,8,16,256]{3,2,1,0:T(8,128)(2,1)S(1)} custom-call(bf16[6,8,32,128]{3,2,1,0:T(8,128)(2,1)} %volume.1), custom_call_target="tpu_custom_call" | custom-call | flops 4000000000 | bytes 1000000 | tf_op jit(solution)/shard_map/pallas_call | solution.py:732
  1.1 0.1 shard_map.110
  1.2 0.6 %collective-permute-start.1 = (bf16[10,16,256]{2,1,0:T(8,128)(2,1)S(1)}, bf16[10,16,256]{2,1,0:T(8,128)(2,1)S(1)}, u32[]{:S(2)}, u32[]{:S(2)}) collective-permute-start(bf16[10,16,256]{2,1,0:T(8,128)(2,1)S(1)} %get-tuple-element.20), channel_id=1, source_target_pairs={{0,1},{1,0},{2,3},{3,2},{4,5},{5,4},{6,7},{7,6},{8,9},{9,8},{10,11... | collective-permute-start | bytes 245768 | tf_op jit(solution)/shard_map/ppermute | solution.py:688
  1.7 2.6 %collective-permute-start = (bf16[6,16,256]{2,1,0:T(8,128)(2,1)S(1)}, bf16[6,16,256]{2,1,0:T(8,128)(2,1)S(1)}, u32[]{:S(2)}, u32[]{:S(2)}) collective-permute-start(bf16[6,16,256]{2,1,0:T(8,128)(2,1)S(1)} %bitcast.22), channel_id=1, source_target_pairs={{0,2},{2,0},{1,3},{3,1},{4,6},{6,4},{5,7},{7,5},{8,10},{10,8},{9,1... | collective-permute-start | bytes 147464 | tf_op jit(solution)/shard_map/ppermute | solution.py:27
  4.3 0.0 collective-permute-done.1.refs_1_.handed
  4.3 2.2 %collective-permute-start.3 = (bf16[2,16,256]{2,1,0:T(8,128)(2,1)S(1)}, bf16[2,16,256]{2,1,0:T(8,128)(2,1)S(1)}, u32[]{:S(2)}, u32[]{:S(2)}) collective-permute-start(bf16[2,16,256]{2,1,0:T(8,128)(2,1)S(1)} %bitcast.23), channel_id=1, source_target_pairs={{0,6},{2,4},{4,10},{6,8},{8,14},{10,12},{12,30},{14,28},{28,26},{3... | collective-permute-start | bytes 49160 | tf_op jit(solution)/shard_map/ppermute | solution.py:65
  6.6 1.6 %collective-permute-start.2 = (bf16[16,16,256]{2,1,0:T(8,128)(2,1)S(1)}, bf16[16,16,256]{2,1,0:T(8,128)(2,1)S(1)}, u32[]{:S(2)}, u32[]{:S(2)}) collective-permute-start(bf16[16,16,256]{2,1,0:T(8,128)(2,1)S(1)} %get-tuple-element.21), channel_id=1, source_target_pairs={{0,4},{4,8},{8,12},{12,28},{28,24},{24,20},{20,16},{16,0},{1,17},{... | collective-permute-start | bytes 393224 | tf_op jit(solution)/shard_map/ppermute | solution.py:51
  8.2 0.0 copy-done.2
  8.2 0.3 shard_map.113.packed
  8.5 0.0 copy-start.7
  8.5 0.0 collective-permute-done.refs_1_.refs_2_.low.high
  8.5 0.5 %collective-permute-done.3.refs_4_.refs_5_.corner_low.corner_high = bf16[2,16,256]{2,1,0:T(8,128)(2,1)S(1)} collective-permute-done((bf16[2,16,256]{2,1,0:T(8,128)(2,1)S(1)}, bf16[2,16,256]{2,1,0:T(8,128)(2,1)S(1)}, u32[]{:S(2)}, u32[]{:S(2)}) %collective-permute-start.3) | collective-permute-done | bytes 16416 | tf_op jit(solution)/shard_map/ppermute | solution.py:65
  9.0 2.5 %collective-permute-done.2.refs_3_.planes = bf16[16,16,256]{2,1,0:T(8,128)(2,1)S(1)} collective-permute-done((bf16[16,16,256]{2,1,0:T(8,128)(2,1)S(1)}, bf16[16,16,256]{2,1,0:T(8,128)(2,1)S(1)}, u32[]{:S(2)}, u32[]{:S(2)}) %collective-permute-start.2) | collective-permute-done | bytes 131104 | tf_op jit(solution)/shard_map/ppermute | solution.py:51
  11.5 0.1 shard_map.112
  11.7 0.1 collective-permute-start.4
  11.8 0.0 copy-done.7
  11.8 0.0 copy-start.3
  11.8 0.0 copy-start.5
  11.8 1.1 %shard_map.114.inner = bf16[4,6,16,256]{3,2,1,0:T(8,128)(2,1)S(1)} custom-call(bf16[6,8,16,256]{3,2,1,0:T(8,128)(2,1)S(1)} %shard_map.109.refs_0_.field.own, bf16[10,16,256]{2,1,0:T(8,128)(2,1)S(1)} %collective-permute-done.1.refs_1_.handed, bf16[9,512,256]{2,1,0:T(8,128)(2,1)S(1)} %shard_map.113.packed, f32[1,128]{1,0:T(1,128)S(1)} %bitcast.26), custom_call_target="tpu_custom_call" | custom-call | flops 4000000000 | bytes 1000000 | tf_op jit(solution)/shard_map/pallas_call | solution.py:701
  12.9 0.1 collective-permute-done.4.passed
  13.1 0.0 copy-done.3
  13.1 1.6 %shard_map.115 = (bf16[6,8,16,256]{3,2,1,0:T(8,128)(2,1)S(1)}, bf16[3,4,16,256]{3,2,1,0:T(8,128)(2,1)S(1)}) custom-call(bf16[6,8,16,256]{3,2,1,0:T(8,128)(2,1)S(1)} %shard_map.109.refs_0_.field.own, bf16[6,16,256]{2,1,0:T(8,128)(2,1)S(1)} %collective-permute-done.refs_1_.refs_2_.low.high, ...), custom_call_target="tpu_custom_call" | custom-call | flops 4000000000 | bytes 1000000 | tf_op jit(solution)/shard_map/pallas_call | solution.py:747
  14.7 0.1 shard_map.116
  14.8 0.4 %collective-permute-start.6 = (bf16[18,16,256]{2,1,0:T(8,128)(2,1)S(1)}, bf16[18,16,256]{2,1,0:T(8,128)(2,1)S(1)}, u32[]{:S(2)}, u32[]{:S(2)}) collective-permute-start(bf16[18,16,256]{2,1,0:T(8,128)(2,1)S(1)} %get-tuple-element.26), channel_id=1, source_target_pairs={{0,1},{1,0},{2,3},{3,2},{4,5},{5,4},{6,7},{7,6},{8,9},{9,8},{10,11... | collective-permute-start | bytes 442376 | tf_op jit(solution)/shard_map/ppermute | solution.py:688
  15.2 0.9 %collective-permute-start.5 = (bf16[12,16,256]{2,1,0:T(8,128)(2,1)S(1)}, bf16[12,16,256]{2,1,0:T(8,128)(2,1)S(1)}, u32[]{:S(2)}, u32[]{:S(2)}) collective-permute-start(bf16[12,16,256]{2,1,0:T(8,128)(2,1)S(1)} %bitcast.20), channel_id=1, source_target_pairs={{0,2},{2,0},{1,3},{3,1},{4,6},{6,4},{5,7},{7,5},{8,10},{10,8},{9,1... | collective-permute-start | bytes 294920 | tf_op jit(solution)/shard_map/ppermute | solution.py:27
  16.1 0.2 collective-permute-done.6.refs_2_.handed
  16.3 2.1 %collective-permute-start.8 = (bf16[10,16,256]{2,1,0:T(8,128)(2,1)S(1)}, bf16[10,16,256]{2,1,0:T(8,128)(2,1)S(1)}, u32[]{:S(2)}, u32[]{:S(2)}) collective-permute-start(bf16[10,16,256]{2,1,0:T(8,128)(2,1)S(1)} %bitcast.21), channel_id=1, source_target_pairs={{0,6},{2,4},{4,10},{6,8},{8,14},{10,12},{12,30},{14,28},{28,26},{3... | collective-permute-start | bytes 245768 | tf_op jit(solution)/shard_map/ppermute | solution.py:65
  18.4 1.6 %collective-permute-start.7 = (bf16[32,16,256]{2,1,0:T(8,128)(2,1)S(1)}, bf16[32,16,256]{2,1,0:T(8,128)(2,1)S(1)}, u32[]{:S(2)}, u32[]{:S(2)}) collective-permute-start(bf16[32,16,256]{2,1,0:T(8,128)(2,1)S(1)} %get-tuple-element.27), channel_id=1, source_target_pairs={{0,4},{4,8},{8,12},{12,28},{28,24},{24,20},{20,16},{16,0},{1,17},{... | collective-permute-start | bytes 786440 | tf_op jit(solution)/shard_map/ppermute | solution.py:51
  20.0 0.6 %shard_map.120.packed = bf16[9,1024,256]{2,1,0:T(8,128)(2,1)S(1)} custom-call(bf16[9,3,256,128]{3,2,1,0:T(8,128)(2,1)S(1)} %bitcast.16), custom_call_target="tpu_custom_call" | custom-call | flops 4000000000 | bytes 1000000 | tf_op jit(solution)/shard_map/pallas_call | solution.py:699
  20.6 0.0 copy-start.9
  20.6 1.2 %collective-permute-done.5.refs_2_.refs_3_.low.high = bf16[12,16,256]{2,1,0:T(8,128)(2,1)S(1)} collective-permute-done((bf16[12,16,256]{2,1,0:T(8,128)(2,1)S(1)}, bf16[12,16,256]{2,1,0:T(8,128)(2,1)S(1)}, u32[]{:S(2)}, u32[]{:S(2)}) %collective-permute-start.5) | collective-permute-done | bytes 98336 | tf_op jit(solution)/shard_map/ppermute | solution.py:27
  21.8 0.7 %collective-permute-done.8.refs_5_.refs_6_.corner_low.corner_high = bf16[10,16,256]{2,1,0:T(8,128)(2,1)S(1)} collective-permute-done((bf16[10,16,256]{2,1,0:T(8,128)(2,1)S(1)}, bf16[10,16,256]{2,1,0:T(8,128)(2,1)S(1)}, u32[]{:S(2)}, u32[]{:S(2)}) %collective-permute-start.8) | collective-permute-done | bytes 81952 | tf_op jit(solution)/shard_map/ppermute | solution.py:65
  22.5 2.8 %collective-permute-done.7.refs_4_.planes = bf16[32,16,256]{2,1,0:T(8,128)(2,1)S(1)} collective-permute-done((bf16[32,16,256]{2,1,0:T(8,128)(2,1)S(1)}, bf16[32,16,256]{2,1,0:T(8,128)(2,1)S(1)}, u32[]{:S(2)}, u32[]{:S(2)}) %collective-permute-start.7) | collective-permute-done | bytes 262176 | tf_op jit(solution)/shard_map/ppermute | solution.py:51
  25.3 0.3 shard_map.118
  25.6 0.1 collective-permute-start.9
  25.7 0.0 copy-start
  25.7 0.0 copy-start.4
  25.7 0.0 copy-start.6
  25.7 0.0 copy-start.8
  25.7 1.1 %shard_map.121.inner = f32[4,6,16,256]{3,2,1,0:T(8,128)S(1)} custom-call(bf16[6,8,16,256]{3,2,1,0:T(8,128)(2,1)S(1)} %get-tuple-element.24.refs_1_.encoded.field, bf16[18,16,256]{2,1,0:T(8,128)(2,1)S(1)} %collective-permute-done.6.refs_2_.handed, bf16[9,1024,256]{2,1,0:T(8,128)(2,1)S(1)} %shard_map.120.packed, f32[1,128]{1,0:T(1,128)S(1)} %bitcast.29), custom_call_target="tpu_custom_call" | custom-call | flops 4000000000 | bytes 1000000 | tf_op jit(solution)/shard_map/pallas_call | solution.py:701
  26.8 0.3 collective-permute-done.9.passed
  27.2 0.5 %copy-done = bf16[3,3,3,256,256]{4,3,2,1,0:T(8,128)(2,1)S(1)} copy-done((bf16[3,3,3,256,256]{4,3,2,1,0:T(8,128)(2,1)S(1)}, bf16[3,3,3,256,256]{4,3,2,1,0:T(8,128)(2,1)}, u32[]{:S(2)}) %copy-start) | copy-done | bytes 3538968
  27.7 0.1 copy-done.4
  27.8 2.7 %shard_map.119 = (bf16[5,2,6,2,16,256]{5,4,3,2,1,0:T(8,128)(2,1)S(1)}, bf16[8,10,16,256]{3,2,1,0:T(8,128)(2,1)S(1)}, bf16[8,10,128]{2,1,0:T(8,128)(2,1)S(1)}, bf16[8,10,128]{2,1,0:T(8,128)(2,1)S(1)}) custom-call(bf16[3,4,16,256]{3,2,1,0:T(8,128)(2,1)S(1)} %get-tuple-element.23.refs_0_.coarse, ...), custom_call_target="tpu_custom_call" | custom-call | flops 4000000000 | bytes 1000000 | tf_op jit(solution)/shard_map/pallas_call | solution.py:774
  30.5 0.6 %collective-permute-start.10 = (bf16[8,10,128]{2,1,0:T(8,128)(2,1)S(1)}, bf16[8,10,128]{2,1,0:T(8,128)(2,1)S(1)}, u32[]{:S(2)}, u32[]{:S(2)}) collective-permute-start(bf16[8,10,128]{2,1,0:T(8,128)(2,1)S(1)} %get-tuple-element.30), channel_id=1, source_target_pairs={{0,1},{1,0},{2,3},{3,2},{4,5},{5,4},{6,7},{7,6},{8,9},{9,8},{10,11... | collective-permute-start | bytes 61448 | tf_op jit(solution)/shard_map/ppermute | solution.py:799
  31.1 1.1 %shard_map.122.partial = f32[6,8,16,256]{3,2,1,0:T(8,128)S(1)} custom-call(bf16[8,10,16,256]{3,2,1,0:T(8,128)(2,1)S(1)} %get-tuple-element.31.encoded_ext, bf16[8,10,128]{2,1,0:T(8,128)(2,1)S(1)} %get-tuple-element.32.columns_in, bf16[9,1024,256]{2,1,0:T(8,128)(2,1)S(1)} %shard_map.120.packed, f32[4,6,16,256]{3,2,1,0:T(8,128)S(1)} %shard_map.121.inner), custom_call_target="tpu_custom_call" | custom-call | flops 4000000000 | bytes 1000000 | tf_op jit(solution)/shard_map/pallas_call | solution.py:800
  32.2 0.0 collective-permute-done.10.columns_in
  32.2 2.9 %shard_map.123 = bf16[6,8,32,128]{3,2,1,0:T(8,128)(2,1)} custom-call(bf16[10,12,16,256]{3,2,1,0:T(8,128)(2,1)S(1)} %bitcast.31, bf16[8,10,128]{2,1,0:T(8,128)(2,1)S(1)} %collective-permute-done.10.columns_in, bf16[9,1024,256]{2,1,0:T(8,128)(2,1)S(1)} %shard_map.120.packed, f32[6,8,16,256]{3,2,1,0:T(8,128)S(1)} %shard_map.122.partial, f32[1,128]{1,0:T(1,128)S(1)} %bitcast.30), custom_call_target="tpu_custom_call" | custom-call | flops 4000000000 | bytes 1000000 | tf_op jit(solution)/shard_map/pallas_call | solution.py:804
  (9 shorter events, 0.1 us)
Async XLA Ops:
  1.2 3.1 %collective-permute-start.1 = (bf16[10,16,256]{2,1,0:T(8,128)(2,1)S(1)}, bf16[10,16,256]{2,1,0:T(8,128)(2,1)S(1)}, u32[]{:S(2)}, u32[]{:S(2)}) collective-permute-start(bf16[10,16,256]{2,1,0:T(8,128)(2,1)S(1)} %get-tuple-element.20), channel_id=1, source_target_pairs={{0,1},{1,0},{2,3},{3,2},{4,5},{5,4},{6,7},{7,6},{8,9},{9,8},{10,11... | collective-permute-start | bytes 245768 | tf_op jit(solution)/shard_map/ppermute | solution.py:688
  1.7 6.4 %copy-start.2 = (bf16[3,3,3,128,128]{4,3,2,1,0:T(8,128)(2,1)S(1)}, bf16[3,3,3,128,128]{4,3,2,1,0:T(8,128)(2,1)}, u32[]{:S(2)}) copy-start(bf16[3,3,3,128,128]{4,3,2,1,0:T(8,128)(2,1)} %param.12) | copy-start | bytes 2654212
  1.7 6.7 %collective-permute-start = (bf16[6,16,256]{2,1,0:T(8,128)(2,1)S(1)}, bf16[6,16,256]{2,1,0:T(8,128)(2,1)S(1)}, u32[]{:S(2)}, u32[]{:S(2)}) collective-permute-start(bf16[6,16,256]{2,1,0:T(8,128)(2,1)S(1)} %bitcast.22), channel_id=1, source_target_pairs={{0,2},{2,0},{1,3},{3,1},{4,6},{6,4},{5,7},{7,5},{8,10},{10,8},{9,1... | collective-permute-start | bytes 147464 | tf_op jit(solution)/shard_map/ppermute | solution.py:27
  4.3 4.7 %collective-permute-start.3 = (bf16[2,16,256]{2,1,0:T(8,128)(2,1)S(1)}, bf16[2,16,256]{2,1,0:T(8,128)(2,1)S(1)}, u32[]{:S(2)}, u32[]{:S(2)}) collective-permute-start(bf16[2,16,256]{2,1,0:T(8,128)(2,1)S(1)} %bitcast.23), channel_id=1, source_target_pairs={{0,6},{2,4},{4,10},{6,8},{8,14},{10,12},{12,30},{14,28},{28,26},{3... | collective-permute-start | bytes 49160 | tf_op jit(solution)/shard_map/ppermute | solution.py:65
  6.6 5.0 %collective-permute-start.2 = (bf16[16,16,256]{2,1,0:T(8,128)(2,1)S(1)}, bf16[16,16,256]{2,1,0:T(8,128)(2,1)S(1)}, u32[]{:S(2)}, u32[]{:S(2)}) collective-permute-start(bf16[16,16,256]{2,1,0:T(8,128)(2,1)S(1)} %get-tuple-element.21), channel_id=1, source_target_pairs={{0,4},{4,8},{8,12},{12,28},{28,24},{24,20},{20,16},{16,0},{1,17},{... | collective-permute-start | bytes 393224 | tf_op jit(solution)/shard_map/ppermute | solution.py:51
  8.5 3.3 %copy-start.7 = (f32[128]{0:T(128)S(1)}, f32[128]{0:T(128)}, u32[]{:S(2)}) copy-start(f32[128]{0:T(128)} %param.13) | copy-start | bytes 1540
  11.7 1.4 %collective-permute-start.4 = (bf16[13,16,256]{2,1,0:T(8,128)(2,1)S(1)}, bf16[13,16,256]{2,1,0:T(8,128)(2,1)S(1)}, u32[]{:S(2)}, u32[]{:S(2)}) collective-permute-start(bf16[13,16,256]{2,1,0:T(8,128)(2,1)S(1)} %shard_map.112), channel_id=1, source_target_pairs={{0,1},{1,0},{2,3},{3,2},{4,5},{5,4},{6,7},{7,6},{8,9},{9,8},{10,11... | collective-permute-start | bytes 319496 | tf_op jit(solution)/shard_map/ppermute | solution.py:718
  11.8 1.3 %copy-start.3 = (bf16[2,2,2,128,256]{4,3,2,1,0:T(8,128)(2,1)S(1)}, bf16[2,2,2,128,256]{4,3,2,1,0:T(8,128)(2,1)}, u32[]{:S(2)}) copy-start(bf16[2,2,2,128,256]{4,3,2,1,0:T(8,128)(2,1)} %param.14) | copy-start | bytes 1572868
  11.8 1.3 %copy-start.5 = (f32[256]{0:T(256)S(1)}, f32[256]{0:T(256)}, u32[]{:S(2)}) copy-start(f32[256]{0:T(256)} %param.15) | copy-start | bytes 3076
  14.8 1.4 %collective-permute-start.6 = (bf16[18,16,256]{2,1,0:T(8,128)(2,1)S(1)}, bf16[18,16,256]{2,1,0:T(8,128)(2,1)S(1)}, u32[]{:S(2)}, u32[]{:S(2)}) collective-permute-start(bf16[18,16,256]{2,1,0:T(8,128)(2,1)S(1)} %get-tuple-element.26), channel_id=1, source_target_pairs={{0,1},{1,0},{2,3},{3,2},{4,5},{5,4},{6,7},{7,6},{8,9},{9,8},{10,11... | collective-permute-start | bytes 442376 | tf_op jit(solution)/shard_map/ppermute | solution.py:688
  15.2 4.7 %copy-start.1 = (bf16[3,3,3,256,128]{4,3,2,1,0:T(8,128)(2,1)S(1)}, bf16[3,3,3,256,128]{4,3,2,1,0:T(8,128)(2,1)}, u32[]{:S(2)}) copy-start(bf16[3,3,3,256,128]{4,3,2,1,0:T(8,128)(2,1)} %param.20) | copy-start | bytes 5308420
  15.2 6.5 %collective-permute-start.5 = (bf16[12,16,256]{2,1,0:T(8,128)(2,1)S(1)}, bf16[12,16,256]{2,1,0:T(8,128)(2,1)S(1)}, u32[]{:S(2)}, u32[]{:S(2)}) collective-permute-start(bf16[12,16,256]{2,1,0:T(8,128)(2,1)S(1)} %bitcast.20), channel_id=1, source_target_pairs={{0,2},{2,0},{1,3},{3,1},{4,6},{6,4},{5,7},{7,5},{8,10},{10,8},{9,1... | collective-permute-start | bytes 294920 | tf_op jit(solution)/shard_map/ppermute | solution.py:27
  16.3 6.2 %collective-permute-start.8 = (bf16[10,16,256]{2,1,0:T(8,128)(2,1)S(1)}, bf16[10,16,256]{2,1,0:T(8,128)(2,1)S(1)}, u32[]{:S(2)}, u32[]{:S(2)}) collective-permute-start(bf16[10,16,256]{2,1,0:T(8,128)(2,1)S(1)} %bitcast.21), channel_id=1, source_target_pairs={{0,6},{2,4},{4,10},{6,8},{8,14},{10,12},{12,30},{14,28},{28,26},{3... | collective-permute-start | bytes 245768 | tf_op jit(solution)/shard_map/ppermute | solution.py:65
  18.4 6.9 %collective-permute-start.7 = (bf16[32,16,256]{2,1,0:T(8,128)(2,1)S(1)}, bf16[32,16,256]{2,1,0:T(8,128)(2,1)S(1)}, u32[]{:S(2)}, u32[]{:S(2)}) collective-permute-start(bf16[32,16,256]{2,1,0:T(8,128)(2,1)S(1)} %get-tuple-element.27), channel_id=1, source_target_pairs={{0,4},{4,8},{8,12},{12,28},{28,24},{24,20},{20,16},{16,0},{1,17},{... | collective-permute-start | bytes 786440 | tf_op jit(solution)/shard_map/ppermute | solution.py:51
  20.6 5.1 %copy-start.9 = (f32[128]{0:T(128)S(1)}, f32[128]{0:T(128)}, u32[]{:S(2)}) copy-start(f32[128]{0:T(128)} %param.21) | copy-start | bytes 1540
  25.6 1.6 %collective-permute-start.9 = (bf16[29,16,256]{2,1,0:T(8,128)(2,1)S(1)}, bf16[29,16,256]{2,1,0:T(8,128)(2,1)S(1)}, u32[]{:S(2)}, u32[]{:S(2)}) collective-permute-start(bf16[29,16,256]{2,1,0:T(8,128)(2,1)S(1)} %shard_map.118), channel_id=1, source_target_pairs={{0,1},{1,0},{2,3},{3,2},{4,5},{5,4},{6,7},{7,6},{8,9},{9,8},{10,11... | collective-permute-start | bytes 712712 | tf_op jit(solution)/shard_map/ppermute | solution.py:718
  25.7 2.0 %copy-start = (bf16[3,3,3,256,256]{4,3,2,1,0:T(8,128)(2,1)S(1)}, bf16[3,3,3,256,256]{4,3,2,1,0:T(8,128)(2,1)}, u32[]{:S(2)}) copy-start(bf16[3,3,3,256,256]{4,3,2,1,0:T(8,128)(2,1)} %param.16) | copy-start | bytes 10616836
  25.7 2.1 %copy-start.4 = (bf16[2,2,2,256,128]{4,3,2,1,0:T(8,128)(2,1)S(1)}, bf16[2,2,2,256,128]{4,3,2,1,0:T(8,128)(2,1)}, u32[]{:S(2)}) copy-start(bf16[2,2,2,256,128]{4,3,2,1,0:T(8,128)(2,1)} %param.18) | copy-start | bytes 1572868
  25.7 2.1 %copy-start.6 = (f32[256]{0:T(256)S(1)}, f32[256]{0:T(256)}, u32[]{:S(2)}) copy-start(f32[256]{0:T(256)} %param.17) | copy-start | bytes 3076
  25.7 2.1 %copy-start.8 = (f32[128]{0:T(128)S(1)}, f32[128]{0:T(128)}, u32[]{:S(2)}) copy-start(f32[128]{0:T(128)} %param.19) | copy-start | bytes 1540
  30.5 1.7 %collective-permute-start.10 = (bf16[8,10,128]{2,1,0:T(8,128)(2,1)S(1)}, bf16[8,10,128]{2,1,0:T(8,128)(2,1)S(1)}, u32[]{:S(2)}, u32[]{:S(2)}) collective-permute-start(bf16[8,10,128]{2,1,0:T(8,128)(2,1)S(1)} %get-tuple-element.30), channel_id=1, source_target_pairs={{0,1},{1,0},{2,3},{3,2},{4,5},{5,4},{6,7},{7,6},{8,9},{9,8},{10,11... | collective-permute-start | bytes 61448 | tf_op jit(solution)/shard_map/ppermute | solution.py:799

commit v9 on v8

--- a/solution.py
+++ b/solution.py
@@ -614,12 +614,14 @@
     )
     bottom = leaky_relu(summed + bias[...]).astype(bf16)
     both = jnp.tile(up_bias[...], (1, 2))
+    size = span * count
     for a in range(2):
         for b in range(2):
             matrix = jnp.concatenate([up[2 * a + b, 0], up[2 * a + b, 1]], axis=-1)
-            lifted = jnp.dot(bottom, matrix, preferred_element_type=f32) + both
-            lifted = lifted.astype(bf16).reshape(deep, span, count, lanes)
-            raised[:, a, pl.ds(start, span), b] = lifted
+            used = bottom[size : deep * size] if a == 0 else bottom[: (deep - 1) * size]
+            lifted = jnp.dot(used, matrix, preferred_element_type=f32) + both
+            lifted = lifted.astype(bf16).reshape(deep - 1, span, count, lanes)
+            raised[1 - a : deep - a, a, pl.ds(start, span), b] = lifted
     blank_plane = jnp.zeros(raised.shape[1:], bf16)
     blank_row = jnp.zeros((deep, 2, 2, count, lanes), bf16)
     first, last = edges("narrow")

time: 35.2 us -> 35.2 us (level)
  no operation moved by 1% of the time
where the time goes in v9:
time: 35.2 us; the launch traced here: 35 us
  Pallas kernels  13.2 us (38%)
  starting transfers between devices  12.5 us (36%)
  waiting for transfers between devices  8.39 us (24%)
  local copies, waits for them, and re-layouts  0.68 us (2%)
    ppermute x2, waiting for transfers between devices, ring_exchange(): return lax.ppermute(sent, ('groups', 'wide', 'pair'), pairs)  5.27 us
    ppermute x2, starting transfers between devices, move(): return lax.ppermute(array, ('groups', 'wide', 'narrow', 'pair'), pairs)  4.31 us
    ppermute x2, starting transfers between devices, line_exchange(): got = lax.ppermute(sent[0], axis, [(0, 1), (1, 0)])  3.41 us
    ppermute x2, starting transfers between devices, ring_exchange(): return lax.ppermute(sent, ('groups', 'wide', 'pair'), pairs)  3.15 us
    pallas_call x1, Pallas kernels, body(): call(decode_kernel, [(depth, height, width, skip)], [taps, pltpu.VMEM((de...  2.85 us
    pallas_call x1, Pallas kernels, body(): call(functools.partial(bottom_kernel, sizes), [(half_depth + 2, 2, half_h...  2.65 us
    pallas_call x2, Pallas kernels, exchange(): call(functools.partial(inner_kernel, weights.shape[1] - lanes, turn == 0)...  2.21 us
    pallas_call x1, Pallas kernels, body(): call(encode_kernel, [(depth, height, pairs, lanes), (half_depth, half_hei...  1.64 us
  transfers between devices with their start and end apart: 11, of which 8 were waited for; matrix products, arithmetic and copies ran while one was open for 0% of the time, Pallas kernels for 12%

profile of v9, /device:TPU:0, one launch (start us, length us, event | category | flops | bytes accessed | tf_op | source)
XLA Modules:
  0.0 35.0 jit_solution(13916142967017804976)
XLA Ops:
  0.0 1.1 %shard_map.109.refs_0_.field.own = bf16[6,8,16,256]{3,2,1,0:T(8,128)(2,1)S(1)} custom-call(bf16[6,8,32,128]{3,2,1,0:T(8,128)(2,1)} %volume.1), custom_call_target="tpu_custom_call" | custom-call | flops 4000000000 | bytes 1000000 | tf_op jit(solution)/shard_map/pallas_call | solution.py:734
  1.1 0.1 shard_map.110
  1.2 0.6 %collective-permute-start.1 = (bf16[10,16,256]{2,1,0:T(8,128)(2,1)S(1)}, bf16[10,16,256]{2,1,0:T(8,128)(2,1)S(1)}, u32[]{:S(2)}, u32[]{:S(2)}) collective-permute-start(bf16[10,16,256]{2,1,0:T(8,128)(2,1)S(1)} %get-tuple-element.20), channel_id=1, source_target_pairs={{0,1},{1,0},{2,3},{3,2},{4,5},{5,4},{6,7},{7,6},{8,9},{9,8},{10,11... | collective-permute-start | bytes 245768 | tf_op jit(solution)/shard_map/ppermute | solution.py:690
  1.7 2.6 %collective-permute-start = (bf16[6,16,256]{2,1,0:T(8,128)(2,1)S(1)}, bf16[6,16,256]{2,1,0:T(8,128)(2,1)S(1)}, u32[]{:S(2)}, u32[]{:S(2)}) collective-permute-start(bf16[6,16,256]{2,1,0:T(8,128)(2,1)S(1)} %bitcast.22), channel_id=1, source_target_pairs={{0,2},{2,0},{1,3},{3,1},{4,6},{6,4},{5,7},{7,5},{8,10},{10,8},{9,1... | collective-permute-start | bytes 147464 | tf_op jit(solution)/shard_map/ppermute | solution.py:27
  4.3 0.0 collective-permute-done.1.refs_1_.handed
  4.3 2.2 %collective-permute-start.3 = (bf16[2,16,256]{2,1,0:T(8,128)(2,1)S(1)}, bf16[2,16,256]{2,1,0:T(8,128)(2,1)S(1)}, u32[]{:S(2)}, u32[]{:S(2)}) collective-permute-start(bf16[2,16,256]{2,1,0:T(8,128)(2,1)S(1)} %bitcast.23), channel_id=1, source_target_pairs={{0,6},{2,4},{4,10},{6,8},{8,14},{10,12},{12,30},{14,28},{28,26},{3... | collective-permute-start | bytes 49160 | tf_op jit(solution)/shard_map/ppermute | solution.py:65
  6.6 1.6 %collective-permute-start.2 = (bf16[16,16,256]{2,1,0:T(8,128)(2,1)S(1)}, bf16[16,16,256]{2,1,0:T(8,128)(2,1)S(1)}, u32[]{:S(2)}, u32[]{:S(2)}) collective-permute-start(bf16[16,16,256]{2,1,0:T(8,128)(2,1)S(1)} %get-tuple-element.21), channel_id=1, source_target_pairs={{0,4},{4,8},{8,12},{12,28},{28,24},{24,20},{20,16},{16,0},{1,17},{... | collective-permute-start | bytes 393224 | tf_op jit(solution)/shard_map/ppermute | solution.py:51
  8.2 0.0 copy-done.2
  8.2 0.3 shard_map.113.packed
  8.5 0.0 copy-start.7
  8.5 0.0 collective-permute-done.refs_1_.refs_2_.low.high
  8.5 0.5 %collective-permute-done.3.refs_4_.refs_5_.corner_low.corner_high = bf16[2,16,256]{2,1,0:T(8,128)(2,1)S(1)} collective-permute-done((bf16[2,16,256]{2,1,0:T(8,128)(2,1)S(1)}, bf16[2,16,256]{2,1,0:T(8,128)(2,1)S(1)}, u32[]{:S(2)}, u32[]{:S(2)}) %collective-permute-start.3) | collective-permute-done | bytes 16416 | tf_op jit(solution)/shard_map/ppermute | solution.py:65
  9.0 2.5 %collective-permute-done.2.refs_3_.planes = bf16[16,16,256]{2,1,0:T(8,128)(2,1)S(1)} collective-permute-done((bf16[16,16,256]{2,1,0:T(8,128)(2,1)S(1)}, bf16[16,16,256]{2,1,0:T(8,128)(2,1)S(1)}, u32[]{:S(2)}, u32[]{:S(2)}) %collective-permute-start.2) | collective-permute-done | bytes 131104 | tf_op jit(solution)/shard_map/ppermute | solution.py:51
  11.5 0.1 shard_map.112
  11.7 0.1 collective-permute-start.4
  11.8 0.0 copy-done.7
  11.8 0.0 copy-start.3
  11.8 0.0 copy-start.5
  11.8 1.1 %shard_map.114.inner = bf16[4,6,16,256]{3,2,1,0:T(8,128)(2,1)S(1)} custom-call(bf16[6,8,16,256]{3,2,1,0:T(8,128)(2,1)S(1)} %shard_map.109.refs_0_.field.own, bf16[10,16,256]{2,1,0:T(8,128)(2,1)S(1)} %collective-permute-done.1.refs_1_.handed, bf16[9,512,256]{2,1,0:T(8,128)(2,1)S(1)} %shard_map.113.packed, f32[1,128]{1,0:T(1,128)S(1)} %bitcast.26), custom_call_target="tpu_custom_call" | custom-call | flops 4000000000 | bytes 1000000 | tf_op jit(solution)/shard_map/pallas_call | solution.py:703
  12.9 0.1 collective-permute-done.4.passed
  13.1 0.0 copy-done.3
  13.1 1.6 %shard_map.115 = (bf16[6,8,16,256]{3,2,1,0:T(8,128)(2,1)S(1)}, bf16[3,4,16,256]{3,2,1,0:T(8,128)(2,1)S(1)}) custom-call(bf16[6,8,16,256]{3,2,1,0:T(8,128)(2,1)S(1)} %shard_map.109.refs_0_.field.own, bf16[6,16,256]{2,1,0:T(8,128)(2,1)S(1)} %collective-permute-done.refs_1_.refs_2_.low.high, ...), custom_call_target="tpu_custom_call" | custom-call | flops 4000000000 | bytes 1000000 | tf_op jit(solution)/shard_map/pallas_call | solution.py:749
  14.7 0.1 shard_map.116
  14.8 0.4 %collective-permute-start.6 = (bf16[18,16,256]{2,1,0:T(8,128)(2,1)S(1)}, bf16[18,16,256]{2,1,0:T(8,128)(2,1)S(1)}, u32[]{:S(2)}, u32[]{:S(2)}) collective-permute-start(bf16[18,16,256]{2,1,0:T(8,128)(2,1)S(1)} %get-tuple-element.26), channel_id=1, source_target_pairs={{0,1},{1,0},{2,3},{3,2},{4,5},{5,4},{6,7},{7,6},{8,9},{9,8},{10,11... | collective-permute-start | bytes 442376 | tf_op jit(solution)/shard_map/ppermute | solution.py:690
  15.2 0.9 %collective-permute-start.5 = (bf16[12,16,256]{2,1,0:T(8,128)(2,1)S(1)}, bf16[12,16,256]{2,1,0:T(8,128)(2,1)S(1)}, u32[]{:S(2)}, u32[]{:S(2)}) collective-permute-start(bf16[12,16,256]{2,1,0:T(8,128)(2,1)S(1)} %bitcast.20), channel_id=1, source_target_pairs={{0,2},{2,0},{1,3},{3,1},{4,6},{6,4},{5,7},{7,5},{8,10},{10,8},{9,1... | collective-permute-start | bytes 294920 | tf_op jit(solution)/shard_map/ppermute | solution.py:27
  16.1 0.2 collective-permute-done.6.refs_2_.handed
  16.3 2.1 %collective-permute-start.8 = (bf16[10,16,256]{2,1,0:T(8,128)(2,1)S(1)}, bf16[10,16,256]{2,1,0:T(8,128)(2,1)S(1)}, u32[]{:S(2)}, u32[]{:S(2)}) collective-permute-start(bf16[10,16,256]{2,1,0:T(8,128)(2,1)S(1)} %bitcast.21), channel_id=1, source_target_pairs={{0,6},{2,4},{4,10},{6,8},{8,14},{10,12},{12,30},{14,28},{28,26},{3... | collective-permute-start | bytes 245768 | tf_op jit(solution)/shard_map/ppermute | solution.py:65
  18.4 1.6 %collective-permute-start.7 = (bf16[32,16,256]{2,1,0:T(8,128)(2,1)S(1)}, bf16[32,16,256]{2,1,0:T(8,128)(2,1)S(1)}, u32[]{:S(2)}, u32[]{:S(2)}) collective-permute-start(bf16[32,16,256]{2,1,0:T(8,128)(2,1)S(1)} %get-tuple-element.27), channel_id=1, source_target_pairs={{0,4},{4,8},{8,12},{12,28},{28,24},{24,20},{20,16},{16,0},{1,17},{... | collective-permute-start | bytes 786440 | tf_op jit(solution)/shard_map/ppermute | solution.py:51
  20.0 0.6 %shard_map.120.packed = bf16[9,1024,256]{2,1,0:T(8,128)(2,1)S(1)} custom-call(bf16[9,3,256,128]{3,2,1,0:T(8,128)(2,1)S(1)} %bitcast.16), custom_call_target="tpu_custom_call" | custom-call | flops 4000000000 | bytes 1000000 | tf_op jit(solution)/shard_map/pallas_call | solution.py:701
  20.6 0.0 copy-start.9
  20.6 1.2 %collective-permute-done.5.refs_2_.refs_3_.low.high = bf16[12,16,256]{2,1,0:T(8,128)(2,1)S(1)} collective-permute-done((bf16[12,16,256]{2,1,0:T(8,128)(2,1)S(1)}, bf16[12,16,256]{2,1,0:T(8,128)(2,1)S(1)}, u32[]{:S(2)}, u32[]{:S(2)}) %collective-permute-start.5) | collective-permute-done | bytes 98336 | tf_op jit(solution)/shard_map/ppermute | solution.py:27
  21.8 0.7 %collective-permute-done.8.refs_5_.refs_6_.corner_low.corner_high = bf16[10,16,256]{2,1,0:T(8,128)(2,1)S(1)} collective-permute-done((bf16[10,16,256]{2,1,0:T(8,128)(2,1)S(1)}, bf16[10,16,256]{2,1,0:T(8,128)(2,1)S(1)}, u32[]{:S(2)}, u32[]{:S(2)}) %collective-permute-start.8) | collective-permute-done | bytes 81952 | tf_op jit(solution)/shard_map/ppermute | solution.py:65
  22.5 2.8 %collective-permute-done.7.refs_4_.planes = bf16[32,16,256]{2,1,0:T(8,128)(2,1)S(1)} collective-permute-done((bf16[32,16,256]{2,1,0:T(8,128)(2,1)S(1)}, bf16[32,16,256]{2,1,0:T(8,128)(2,1)S(1)}, u32[]{:S(2)}, u32[]{:S(2)}) %collective-permute-start.7) | collective-permute-done | bytes 262176 | tf_op jit(solution)/shard_map/ppermute | solution.py:51
  25.3 0.3 shard_map.118
  25.6 0.1 collective-permute-start.9
  25.7 0.0 copy-start
  25.7 0.0 copy-start.4
  25.7 0.0 copy-start.6
  25.7 0.0 copy-start.8
  25.7 1.1 %shard_map.121.inner = f32[4,6,16,256]{3,2,1,0:T(8,128)S(1)} custom-call(bf16[6,8,16,256]{3,2,1,0:T(8,128)(2,1)S(1)} %get-tuple-element.24.refs_1_.encoded.field, bf16[18,16,256]{2,1,0:T(8,128)(2,1)S(1)} %collective-permute-done.6.refs_2_.handed, bf16[9,1024,256]{2,1,0:T(8,128)(2,1)S(1)} %shard_map.120.packed, f32[1,128]{1,0:T(1,128)S(1)} %bitcast.29), custom_call_target="tpu_custom_call" | custom-call | flops 4000000000 | bytes 1000000 | tf_op jit(solution)/shard_map/pallas_call | solution.py:703
  26.8 0.3 collective-permute-done.9.passed
  27.2 0.5 %copy-done = bf16[3,3,3,256,256]{4,3,2,1,0:T(8,128)(2,1)S(1)} copy-done((bf16[3,3,3,256,256]{4,3,2,1,0:T(8,128)(2,1)S(1)}, bf16[3,3,3,256,256]{4,3,2,1,0:T(8,128)(2,1)}, u32[]{:S(2)}) %copy-start) | copy-done | bytes 3538968
  27.7 0.1 copy-done.4
  27.8 2.6 %shard_map.119 = (bf16[5,2,6,2,16,256]{5,4,3,2,1,0:T(8,128)(2,1)S(1)}, bf16[8,10,16,256]{3,2,1,0:T(8,128)(2,1)S(1)}, bf16[8,10,128]{2,1,0:T(8,128)(2,1)S(1)}, bf16[8,10,128]{2,1,0:T(8,128)(2,1)S(1)}) custom-call(bf16[3,4,16,256]{3,2,1,0:T(8,128)(2,1)S(1)} %get-tuple-element.23.refs_0_.coarse, ...), custom_call_target="tpu_custom_call" | custom-call | flops 4000000000 | bytes 1000000 | tf_op jit(solution)/shard_map/pallas_call | solution.py:776
  30.4 0.6 %collective-permute-start.10 = (bf16[8,10,128]{2,1,0:T(8,128)(2,1)S(1)}, bf16[8,10,128]{2,1,0:T(8,128)(2,1)S(1)}, u32[]{:S(2)}, u32[]{:S(2)}) collective-permute-start(bf16[8,10,128]{2,1,0:T(8,128)(2,1)S(1)} %get-tuple-element.30), channel_id=1, source_target_pairs={{0,1},{1,0},{2,3},{3,2},{4,5},{5,4},{6,7},{7,6},{8,9},{9,8},{10,11... | collective-permute-start | bytes 61448 | tf_op jit(solution)/shard_map/ppermute | solution.py:801
  31.0 1.1 %shard_map.122.partial = f32[6,8,16,256]{3,2,1,0:T(8,128)S(1)} custom-call(bf16[8,10,16,256]{3,2,1,0:T(8,128)(2,1)S(1)} %get-tuple-element.31.encoded_ext, bf16[8,10,128]{2,1,0:T(8,128)(2,1)S(1)} %get-tuple-element.32.columns_in, bf16[9,1024,256]{2,1,0:T(8,128)(2,1)S(1)} %shard_map.120.packed, f32[4,6,16,256]{3,2,1,0:T(8,128)S(1)} %shard_map.121.inner), custom_call_target="tpu_custom_call" | custom-call | flops 4000000000 | bytes 1000000 | tf_op jit(solution)/shard_map/pallas_call | solution.py:802
  32.1 0.0 collective-permute-done.10.columns_in
  32.1 2.9 %shard_map.123 = bf16[6,8,32,128]{3,2,1,0:T(8,128)(2,1)} custom-call(bf16[10,12,16,256]{3,2,1,0:T(8,128)(2,1)S(1)} %bitcast.31, bf16[8,10,128]{2,1,0:T(8,128)(2,1)S(1)} %collective-permute-done.10.columns_in, bf16[9,1024,256]{2,1,0:T(8,128)(2,1)S(1)} %shard_map.120.packed, f32[6,8,16,256]{3,2,1,0:T(8,128)S(1)} %shard_map.122.partial, f32[1,128]{1,0:T(1,128)S(1)} %bitcast.30), custom_call_target="tpu_custom_call" | custom-call | flops 4000000000 | bytes 1000000 | tf_op jit(solution)/shard_map/pallas_call | solution.py:806
  (9 shorter events, 0.1 us)
Async XLA Ops:
  1.2 3.1 %collective-permute-start.1 = (bf16[10,16,256]{2,1,0:T(8,128)(2,1)S(1)}, bf16[10,16,256]{2,1,0:T(8,128)(2,1)S(1)}, u32[]{:S(2)}, u32[]{:S(2)}) collective-permute-start(bf16[10,16,256]{2,1,0:T(8,128)(2,1)S(1)} %get-tuple-element.20), channel_id=1, source_target_pairs={{0,1},{1,0},{2,3},{3,2},{4,5},{5,4},{6,7},{7,6},{8,9},{9,8},{10,11... | collective-permute-start | bytes 245768 | tf_op jit(solution)/shard_map/ppermute | solution.py:690
  1.7 6.4 %copy-start.2 = (bf16[3,3,3,128,128]{4,3,2,1,0:T(8,128)(2,1)S(1)}, bf16[3,3,3,128,128]{4,3,2,1,0:T(8,128)(2,1)}, u32[]{:S(2)}) copy-start(bf16[3,3,3,128,128]{4,3,2,1,0:T(8,128)(2,1)} %param.12) | copy-start | bytes 2654212
  1.7 6.7 %collective-permute-start = (bf16[6,16,256]{2,1,0:T(8,128)(2,1)S(1)}, bf16[6,16,256]{2,1,0:T(8,128)(2,1)S(1)}, u32[]{:S(2)}, u32[]{:S(2)}) collective-permute-start(bf16[6,16,256]{2,1,0:T(8,128)(2,1)S(1)} %bitcast.22), channel_id=1, source_target_pairs={{0,2},{2,0},{1,3},{3,1},{4,6},{6,4},{5,7},{7,5},{8,10},{10,8},{9,1... | collective-permute-start | bytes 147464 | tf_op jit(solution)/shard_map/ppermute | solution.py:27
  4.3 4.7 %collective-permute-start.3 = (bf16[2,16,256]{2,1,0:T(8,128)(2,1)S(1)}, bf16[2,16,256]{2,1,0:T(8,128)(2,1)S(1)}, u32[]{:S(2)}, u32[]{:S(2)}) collective-permute-start(bf16[2,16,256]{2,1,0:T(8,128)(2,1)S(1)} %bitcast.23), channel_id=1, source_target_pairs={{0,6},{2,4},{4,10},{6,8},{8,14},{10,12},{12,30},{14,28},{28,26},{3... | collective-permute-start | bytes 49160 | tf_op jit(solution)/shard_map/ppermute | solution.py:65
  6.6 5.0 %collective-permute-start.2 = (bf16[16,16,256]{2,1,0:T(8,128)(2,1)S(1)}, bf16[16,16,256]{2,1,0:T(8,128)(2,1)S(1)}, u32[]{:S(2)}, u32[]{:S(2)}) collective-permute-start(bf16[16,16,256]{2,1,0:T(8,128)(2,1)S(1)} %get-tuple-element.21), channel_id=1, source_target_pairs={{0,4},{4,8},{8,12},{12,28},{28,24},{24,20},{20,16},{16,0},{1,17},{... | collective-permute-start | bytes 393224 | tf_op jit(solution)/shard_map/ppermute | solution.py:51
  8.5 3.3 %copy-start.7 = (f32[128]{0:T(128)S(1)}, f32[128]{0:T(128)}, u32[]{:S(2)}) copy-start(f32[128]{0:T(128)} %param.13) | copy-start | bytes 1540
  11.7 1.4 %collective-permute-start.4 = (bf16[13,16,256]{2,1,0:T(8,128)(2,1)S(1)}, bf16[13,16,256]{2,1,0:T(8,128)(2,1)S(1)}, u32[]{:S(2)}, u32[]{:S(2)}) collective-permute-start(bf16[13,16,256]{2,1,0:T(8,128)(2,1)S(1)} %shard_map.112), channel_id=1, source_target_pairs={{0,1},{1,0},{2,3},{3,2},{4,5},{5,4},{6,7},{7,6},{8,9},{9,8},{10,11... | collective-permute-start | bytes 319496 | tf_op jit(solution)/shard_map/ppermute | solution.py:720
  11.8 1.3 %copy-start.3 = (bf16[2,2,2,128,256]{4,3,2,1,0:T(8,128)(2,1)S(1)}, bf16[2,2,2,128,256]{4,3,2,1,0:T(8,128)(2,1)}, u32[]{:S(2)}) copy-start(bf16[2,2,2,128,256]{4,3,2,1,0:T(8,128)(2,1)} %param.14) | copy-start | bytes 1572868
  11.8 1.3 %copy-start.5 = (f32[256]{0:T(256)S(1)}, f32[256]{0:T(256)}, u32[]{:S(2)}) copy-start(f32[256]{0:T(256)} %param.15) | copy-start | bytes 3076
  14.8 1.4 %collective-permute-start.6 = (bf16[18,16,256]{2,1,0:T(8,128)(2,1)S(1)}, bf16[18,16,256]{2,1,0:T(8,128)(2,1)S(1)}, u32[]{:S(2)}, u32[]{:S(2)}) collective-permute-start(bf16[18,16,256]{2,1,0:T(8,128)(2,1)S(1)} %get-tuple-element.26), channel_id=1, source_target_pairs={{0,1},{1,0},{2,3},{3,2},{4,5},{5,4},{6,7},{7,6},{8,9},{9,8},{10,11... | collective-permute-start | bytes 442376 | tf_op jit(solution)/shard_map/ppermute | solution.py:690
  15.2 4.7 %copy-start.1 = (bf16[3,3,3,256,128]{4,3,2,1,0:T(8,128)(2,1)S(1)}, bf16[3,3,3,256,128]{4,3,2,1,0:T(8,128)(2,1)}, u32[]{:S(2)}) copy-start(bf16[3,3,3,256,128]{4,3,2,1,0:T(8,128)(2,1)} %param.20) | copy-start | bytes 5308420
  15.2 6.5 %collective-permute-start.5 = (bf16[12,16,256]{2,1,0:T(8,128)(2,1)S(1)}, bf16[12,16,256]{2,1,0:T(8,128)(2,1)S(1)}, u32[]{:S(2)}, u32[]{:S(2)}) collective-permute-start(bf16[12,16,256]{2,1,0:T(8,128)(2,1)S(1)} %bitcast.20), channel_id=1, source_target_pairs={{0,2},{2,0},{1,3},{3,1},{4,6},{6,4},{5,7},{7,5},{8,10},{10,8},{9,1... | collective-permute-start | bytes 294920 | tf_op jit(solution)/shard_map/ppermute | solution.py:27
  16.3 6.2 %collective-permute-start.8 = (bf16[10,16,256]{2,1,0:T(8,128)(2,1)S(1)}, bf16[10,16,256]{2,1,0:T(8,128)(2,1)S(1)}, u32[]{:S(2)}, u32[]{:S(2)}) collective-permute-start(bf16[10,16,256]{2,1,0:T(8,128)(2,1)S(1)} %bitcast.21), channel_id=1, source_target_pairs={{0,6},{2,4},{4,10},{6,8},{8,14},{10,12},{12,30},{14,28},{28,26},{3... | collective-permute-start | bytes 245768 | tf_op jit(solution)/shard_map/ppermute | solution.py:65
  18.4 6.9 %collective-permute-start.7 = (bf16[32,16,256]{2,1,0:T(8,128)(2,1)S(1)}, bf16[32,16,256]{2,1,0:T(8,128)(2,1)S(1)}, u32[]{:S(2)}, u32[]{:S(2)}) collective-permute-start(bf16[32,16,256]{2,1,0:T(8,128)(2,1)S(1)} %get-tuple-element.27), channel_id=1, source_target_pairs={{0,4},{4,8},{8,12},{12,28},{28,24},{24,20},{20,16},{16,0},{1,17},{... | collective-permute-start | bytes 786440 | tf_op jit(solution)/shard_map/ppermute | solution.py:51
  20.6 5.1 %copy-start.9 = (f32[128]{0:T(128)S(1)}, f32[128]{0:T(128)}, u32[]{:S(2)}) copy-start(f32[128]{0:T(128)} %param.21) | copy-start | bytes 1540
  25.6 1.6 %collective-permute-start.9 = (bf16[29,16,256]{2,1,0:T(8,128)(2,1)S(1)}, bf16[29,16,256]{2,1,0:T(8,128)(2,1)S(1)}, u32[]{:S(2)}, u32[]{:S(2)}) collective-permute-start(bf16[29,16,256]{2,1,0:T(8,128)(2,1)S(1)} %shard_map.118), channel_id=1, source_target_pairs={{0,1},{1,0},{2,3},{3,2},{4,5},{5,4},{6,7},{7,6},{8,9},{9,8},{10,11... | collective-permute-start | bytes 712712 | tf_op jit(solution)/shard_map/ppermute | solution.py:720
  25.7 2.0 %copy-start = (bf16[3,3,3,256,256]{4,3,2,1,0:T(8,128)(2,1)S(1)}, bf16[3,3,3,256,256]{4,3,2,1,0:T(8,128)(2,1)}, u32[]{:S(2)}) copy-start(bf16[3,3,3,256,256]{4,3,2,1,0:T(8,128)(2,1)} %param.16) | copy-start | bytes 10616836
  25.7 2.1 %copy-start.4 = (bf16[2,2,2,256,128]{4,3,2,1,0:T(8,128)(2,1)S(1)}, bf16[2,2,2,256,128]{4,3,2,1,0:T(8,128)(2,1)}, u32[]{:S(2)}) copy-start(bf16[2,2,2,256,128]{4,3,2,1,0:T(8,128)(2,1)} %param.18) | copy-start | bytes 1572868
  25.7 2.1 %copy-start.6 = (f32[256]{0:T(256)S(1)}, f32[256]{0:T(256)}, u32[]{:S(2)}) copy-start(f32[256]{0:T(256)} %param.17) | copy-start | bytes 3076
  25.7 2.1 %copy-start.8 = (f32[128]{0:T(128)S(1)}, f32[128]{0:T(128)}, u32[]{:S(2)}) copy-start(f32[128]{0:T(128)} %param.19) | copy-start | bytes 1540
  30.4 1.7 %collective-permute-start.10 = (bf16[8,10,128]{2,1,0:T(8,128)(2,1)S(1)}, bf16[8,10,128]{2,1,0:T(8,128)(2,1)S(1)}, u32[]{:S(2)}, u32[]{:S(2)}) collective-permute-start(bf16[8,10,128]{2,1,0:T(8,128)(2,1)S(1)} %get-tuple-element.30), channel_id=1, source_target_pairs={{0,1},{1,0},{2,3},{3,2},{4,5},{5,4},{6,7},{7,6},{8,9},{9,8},{10,11... | collective-permute-start | bytes 61448 | tf_op jit(solution)/shard_map/ppermute | solution.py:801

commit v10 on v9

--- a/solution.py
+++ b/solution.py
@@ -362,7 +362,7 @@
         out[:, :, odd * lanes : (odd + 1) * lanes] = half.astype(bf16)
 
 
-def pack_kernel(volume, packed, here, spread, arrived):
+def pack_kernel(sizes, volume, packed, edge_rows, handed, here, spread, arrived):
     copies = [
         pltpu.make_async_copy(volume.at[plane], here.at[plane], arrived.at[plane])
         for plane in range(volume.shape[0])
@@ -372,6 +372,7 @@
     for plane, copy in enumerate(copies):
         copy.wait()
         pack_pairs(packed.at[plane], here[plane], spread.at[plane])
+    edge_kernel(sizes, packed, edge_rows, handed)
 
 
 def per_tile(cells, rows, lanes):
@@ -485,6 +486,7 @@
 
 
 def encode_kernel(
+    sizes,
     own,
     low,
     high,
@@ -499,6 +501,8 @@
     down_bias,
     encoded,
     coarse,
+    edge_rows,
+    handed,
     ext,
     columns_in,
     frame,
@@ -540,6 +544,7 @@
             )
             lifted = part if lifted is None else lifted + part
     coarse[...] = leaky_relu(lifted + down_bias[...]).astype(bf16).reshape(coarse.shape)
+    edge_kernel(sizes, coarse, encoded, edge_rows, handed)
 
 
 def bottom_kernel(
@@ -676,17 +681,23 @@
     decoded[...] = spread[...].astype(bf16)
 
 
-def exchange(turn, fields, halos, halves, weight, bias):
-    sizes = [(field.shape, deep, tall) for field, (deep, tall) in zip(fields, halos)]
+def sizes_of(shapes, halos):
+    return [(shape, deep, tall) for shape, (deep, tall) in zip(shapes, halos)]
+
+
+def edge_shapes(sizes):
+    last = sizes[-1][0]
+    rows = sum(shape[0] * tall for shape, _, tall in sizes)
+    planes = layout(sizes)[1] + field_slabs(last, True)
+    return [(sides_of("narrow"), rows) + last[2:], (planes,) + last[2:]]
+
+
+def exchange(turn, fields, edge_rows, handed, sizes, halves, weight, bias):
     _, planes, corners = layout(sizes)
     depth, height = fields[-1].shape[:2]
     cells = fields[-1].shape[2:]
     sides = sides_of("narrow")
     swap = [(0, 1), (1, 0)]
-    rows = sum(shape[0] * tall for shape, _, tall in sizes)
-    edge_rows, handed = call(
-        functools.partial(edge_kernel, sizes), [(sides, rows) + cells, (planes + field_slabs(fields[-1].shape, True),) + cells], (), 8
-    )(*fields)
     handed = lax.ppermute(handed, "pair", swap)
     low, high = line_exchange("narrow", edge_rows)
     ring, corner = call(
@@ -718,7 +729,7 @@
         8,
     )(*fields, *received)
     passed = lax.ppermute(passed, "pair", swap)
-    return sizes, weights, inner, received + (passed,)
+    return weights, inner, received + (passed,)
 
 
 def body(
@@ -731,9 +742,11 @@
     framed = (depth + 2, height + 2)
     coarse_framed = (half_depth + 4, half_height + 4)
 
-    (packed,) = call(
-        pack_kernel,
-        [(depth, height, pairs, lanes)],
+    fine, half = (depth, height, pairs, lanes), (half_depth, half_height, pairs, deep_width)
+    sizes = sizes_of([fine], [(1, 1)])
+    packed, edge_rows, handed = call(
+        functools.partial(pack_kernel, sizes),
+        [fine] + edge_shapes(sizes),
         [
             pltpu.VMEM((depth, height, width, skip), bf16),
             pltpu.VMEM((depth, height, width, skip), f32),
@@ -743,12 +756,20 @@
         in_specs=[pl.BlockSpec(memory_space=pltpu.HBM)],
     )(pltpu.with_memory_space_constraint(volume, pltpu.HBM))
     encode_bias, decode_bias = b_encode.reshape(1, skip), b_decode.reshape(1, skip)
-    _, encode_weights, inner, received = exchange(
-        0, [packed], [(1, 1)], [True], w_encode.reshape(9, 3, skip, skip), encode_bias
-    )
-    encoded, coarse = call(
-        encode_kernel,
-        [(depth, height, pairs, lanes), (half_depth, half_height, pairs, deep_width)],
+    encode_weights, inner, received = exchange(
+        0,
+        [packed],
+        edge_rows,
+        handed,
+        sizes,
+        [True],
+        w_encode.reshape(9, 3, skip, skip),
+        encode_bias,
+    )
+    sizes = sizes_of([half, fine], [(2, 2), (1, 1)])
+    encoded, coarse, edge_rows, handed = call(
+        functools.partial(encode_kernel, sizes),
+        [fine, half] + edge_shapes(sizes),
         [
             pltpu.VMEM(framed + (pairs, lanes), bf16),
             pltpu.VMEM(framed + (skip,), bf16),
@@ -765,10 +786,12 @@
         b_down.reshape(1, deep_width),
     )
 
-    sizes, decode_weights, inner, received = exchange(
+    decode_weights, inner, received = exchange(
         1,
         [coarse, encoded],
-        [(2, 2), (1, 1)],
+        edge_rows,
+        handed,
+        sizes,
         [False, True],
         w_decode.reshape(9, 3, lanes, skip),
         decode_bias,

time: 35.2 us -> 35.1 us (level)
    pallas_call x4 -> x2, Pallas kernels: 2.88 us -> 2.84 us  [the longest x1 1.7 us: body(): call(functools.partial(encode_kernel, sizes), [fine, half] + edge_shapes(...]
where the time goes in v10:
time: 35.1 us; the launch traced here: 34.9 us
  Pallas kernels  13.1 us (37%)
  starting transfers between devices  12.5 us (36%)
  waiting for transfers between devices  8.4 us (24%)
  local copies, waits for them, and re-layouts  0.68 us (2%)
    ppermute x2, waiting for transfers between devices, ring_exchange(): return lax.ppermute(sent, ('groups', 'wide', 'pair'), pairs)  5.28 us
    ppermute x2, starting transfers between devices, move(): return lax.ppermute(array, ('groups', 'wide', 'narrow', 'pair'), pairs)  4.32 us
    ppermute x2, starting transfers between devices, line_exchange(): got = lax.ppermute(sent[0], axis, [(0, 1), (1, 0)])  3.39 us
    ppermute x2, starting transfers between devices, ring_exchange(): return lax.ppermute(sent, ('groups', 'wide', 'pair'), pairs)  3.16 us
    pallas_call x1, Pallas kernels, body(): call(decode_kernel, [(depth, height, width, skip)], [taps, pltpu.VMEM((de...  2.85 us
    pallas_call x1, Pallas kernels, body(): call(functools.partial(bottom_kernel, sizes), [(half_depth + 2, 2, half_h...  2.65 us
    pallas_call x2, Pallas kernels, exchange(): call(functools.partial(inner_kernel, weights.shape[1] - lanes, turn == 0)...  2.21 us
    pallas_call x1, Pallas kernels, body(): call(functools.partial(encode_kernel, sizes), [fine, half] + edge_shapes(...  1.7 us
  transfers between devices with their start and end apart: 11, of which 8 were waited for; matrix products, arithmetic and copies ran while one was open for 0% of the time, Pallas kernels for 12%

profile of v10, /device:TPU:0, one launch (start us, length us, event | category | flops | bytes accessed | tf_op | source)
XLA Modules:
  0.0 34.9 jit_solution(9795845928230912919)
XLA Ops:
  0.0 1.1 %shard_map.109 = (bf16[6,8,16,256]{3,2,1,0:T(8,128)(2,1)S(1)}, bf16[1,6,16,256]{3,2,1,0:T(8,128)(2,1)S(1)}, bf16[10,16,256]{2,1,0:T(8,128)(2,1)S(1)}) custom-call(bf16[6,8,32,128]{3,2,1,0:T(8,128)(2,1)} %volume.1), custom_call_target="tpu_custom_call" | custom-call | flops 4000000000 | bytes 1000000 | tf_op jit(solution)/shard_map/pallas_call | solution.py:747
  1.1 0.6 %collective-permute-start.1 = (bf16[10,16,256]{2,1,0:T(8,128)(2,1)S(1)}, bf16[10,16,256]{2,1,0:T(8,128)(2,1)S(1)}, u32[]{:S(2)}, u32[]{:S(2)}) collective-permute-start(bf16[10,16,256]{2,1,0:T(8,128)(2,1)S(1)} %get-tuple-element.22), channel_id=1, source_target_pairs={{0,1},{1,0},{2,3},{3,2},{4,5},{5,4},{6,7},{7,6},{8,9},{9,8},{10,11... | collective-permute-start | bytes 245768 | tf_op jit(solution)/shard_map/ppermute | solution.py:701
  1.7 2.6 %collective-permute-start = (bf16[6,16,256]{2,1,0:T(8,128)(2,1)S(1)}, bf16[6,16,256]{2,1,0:T(8,128)(2,1)S(1)}, u32[]{:S(2)}, u32[]{:S(2)}) collective-permute-start(bf16[6,16,256]{2,1,0:T(8,128)(2,1)S(1)} %bitcast.22), channel_id=1, source_target_pairs={{0,2},{2,0},{1,3},{3,1},{4,6},{6,4},{5,7},{7,5},{8,10},{10,8},{9,1... | collective-permute-start | bytes 147464 | tf_op jit(solution)/shard_map/ppermute | solution.py:27
  4.3 0.0 collective-permute-done.1.refs_1_.handed
  4.3 2.2 %collective-permute-start.3 = (bf16[2,16,256]{2,1,0:T(8,128)(2,1)S(1)}, bf16[2,16,256]{2,1,0:T(8,128)(2,1)S(1)}, u32[]{:S(2)}, u32[]{:S(2)}) collective-permute-start(bf16[2,16,256]{2,1,0:T(8,128)(2,1)S(1)} %bitcast.23), channel_id=1, source_target_pairs={{0,6},{2,4},{4,10},{6,8},{8,14},{10,12},{12,30},{14,28},{28,26},{3... | collective-permute-start | bytes 49160 | tf_op jit(solution)/shard_map/ppermute | solution.py:65
  6.6 1.6 %collective-permute-start.2 = (bf16[16,16,256]{2,1,0:T(8,128)(2,1)S(1)}, bf16[16,16,256]{2,1,0:T(8,128)(2,1)S(1)}, u32[]{:S(2)}, u32[]{:S(2)}) collective-permute-start(bf16[16,16,256]{2,1,0:T(8,128)(2,1)S(1)} %get-tuple-element.23), channel_id=1, source_target_pairs={{0,4},{4,8},{8,12},{12,28},{28,24},{24,20},{20,16},{16,0},{1,17},{... | collective-permute-start | bytes 393224 | tf_op jit(solution)/shard_map/ppermute | solution.py:51
  8.1 0.0 copy-done.2
  8.1 0.3 shard_map.112.packed
  8.4 0.0 copy-start.7
  8.5 0.0 collective-permute-done.refs_1_.refs_2_.low.high
  8.5 0.5 %collective-permute-done.3.refs_4_.refs_5_.corner_low.corner_high = bf16[2,16,256]{2,1,0:T(8,128)(2,1)S(1)} collective-permute-done((bf16[2,16,256]{2,1,0:T(8,128)(2,1)S(1)}, bf16[2,16,256]{2,1,0:T(8,128)(2,1)S(1)}, u32[]{:S(2)}, u32[]{:S(2)}) %collective-permute-start.3) | collective-permute-done | bytes 16416 | tf_op jit(solution)/shard_map/ppermute | solution.py:65
  9.0 2.5 %collective-permute-done.2.refs_3_.planes = bf16[16,16,256]{2,1,0:T(8,128)(2,1)S(1)} collective-permute-done((bf16[16,16,256]{2,1,0:T(8,128)(2,1)S(1)}, bf16[16,16,256]{2,1,0:T(8,128)(2,1)S(1)}, u32[]{:S(2)}, u32[]{:S(2)}) %collective-permute-start.2) | collective-permute-done | bytes 131104 | tf_op jit(solution)/shard_map/ppermute | solution.py:51
  11.5 0.1 shard_map.111
  11.7 0.1 collective-permute-start.4
  11.8 0.0 copy-done.7
  11.8 0.0 copy-start.3
  11.8 0.0 copy-start.5
  11.8 1.1 %shard_map.113.inner = bf16[4,6,16,256]{3,2,1,0:T(8,128)(2,1)S(1)} custom-call(bf16[6,8,16,256]{3,2,1,0:T(8,128)(2,1)S(1)} %get-tuple-element.20.refs_0_.field.own, bf16[10,16,256]{2,1,0:T(8,128)(2,1)S(1)} %collective-permute-done.1.refs_1_.handed, bf16[9,512,256]{2,1,0:T(8,128)(2,1)S(1)} %shard_map.112.packed, f32[1,128]{1,0:T(1,128)S(1)} %bitcast.26), custom_call_target="tpu_custom_call" | custom-call | flops 4000000000 | bytes 1000000 | tf_op jit(solution)/shard_map/pallas_call | solution.py:714
  12.9 0.1 collective-permute-done.4.passed
  13.1 0.0 copy-done.5
  13.1 1.7 %shard_map.114 = (bf16[6,8,16,256]{3,2,1,0:T(8,128)(2,1)S(1)}, bf16[3,4,16,256]{3,2,1,0:T(8,128)(2,1)S(1)}, bf16[1,12,16,256]{3,2,1,0:T(8,128)(2,1)S(1)}, bf16[18,16,256]{2,1,0:T(8,128)(2,1)S(1)}) custom-call(bf16[6,8,16,256]{3,2,1,0:T(8,128)(2,1)S(1)} %get-tuple-element.20.refs_0_.field.own, ...), custom_call_target="tpu_custom_call" | custom-call | flops 4000000000 | bytes 1000000 | tf_op jit(solution)/shard_map/pallas_call | solution.py:770
  14.8 0.4 %collective-permute-start.6 = (bf16[18,16,256]{2,1,0:T(8,128)(2,1)S(1)}, bf16[18,16,256]{2,1,0:T(8,128)(2,1)S(1)}, u32[]{:S(2)}, u32[]{:S(2)}) collective-permute-start(bf16[18,16,256]{2,1,0:T(8,128)(2,1)S(1)} %get-tuple-element.28), channel_id=1, source_target_pairs={{0,1},{1,0},{2,3},{3,2},{4,5},{5,4},{6,7},{7,6},{8,9},{9,8},{10,11... | collective-permute-start | bytes 442376 | tf_op jit(solution)/shard_map/ppermute | solution.py:701
  15.2 0.8 %collective-permute-start.5 = (bf16[12,16,256]{2,1,0:T(8,128)(2,1)S(1)}, bf16[12,16,256]{2,1,0:T(8,128)(2,1)S(1)}, u32[]{:S(2)}, u32[]{:S(2)}) collective-permute-start(bf16[12,16,256]{2,1,0:T(8,128)(2,1)S(1)} %bitcast.20), channel_id=1, source_target_pairs={{0,2},{2,0},{1,3},{3,1},{4,6},{6,4},{5,7},{7,5},{8,10},{10,8},{9,1... | collective-permute-start | bytes 294920 | tf_op jit(solution)/shard_map/ppermute | solution.py:27
  16.0 0.2 collective-permute-done.6.refs_2_.handed
  16.3 2.1 %collective-permute-start.8 = (bf16[10,16,256]{2,1,0:T(8,128)(2,1)S(1)}, bf16[10,16,256]{2,1,0:T(8,128)(2,1)S(1)}, u32[]{:S(2)}, u32[]{:S(2)}) collective-permute-start(bf16[10,16,256]{2,1,0:T(8,128)(2,1)S(1)} %bitcast.21), channel_id=1, source_target_pairs={{0,6},{2,4},{4,10},{6,8},{8,14},{10,12},{12,30},{14,28},{28,26},{3... | collective-permute-start | bytes 245768 | tf_op jit(solution)/shard_map/ppermute | solution.py:65
  18.3 1.6 %collective-permute-start.7 = (bf16[32,16,256]{2,1,0:T(8,128)(2,1)S(1)}, bf16[32,16,256]{2,1,0:T(8,128)(2,1)S(1)}, u32[]{:S(2)}, u32[]{:S(2)}) collective-permute-start(bf16[32,16,256]{2,1,0:T(8,128)(2,1)S(1)} %get-tuple-element.29), channel_id=1, source_target_pairs={{0,4},{4,8},{8,12},{12,28},{28,24},{24,20},{20,16},{16,0},{1,17},{... | collective-permute-start | bytes 786440 | tf_op jit(solution)/shard_map/ppermute | solution.py:51
  19.9 0.0 copy-done.1
  19.9 0.6 %shard_map.118.packed = bf16[9,1024,256]{2,1,0:T(8,128)(2,1)S(1)} custom-call(bf16[9,3,256,128]{3,2,1,0:T(8,128)(2,1)S(1)} %bitcast.16), custom_call_target="tpu_custom_call" | custom-call | flops 4000000000 | bytes 1000000 | tf_op jit(solution)/shard_map/pallas_call | solution.py:712
  20.5 0.0 copy-start.9
  20.5 1.2 %collective-permute-done.5.refs_2_.refs_3_.low.high = bf16[12,16,256]{2,1,0:T(8,128)(2,1)S(1)} collective-permute-done((bf16[12,16,256]{2,1,0:T(8,128)(2,1)S(1)}, bf16[12,16,256]{2,1,0:T(8,128)(2,1)S(1)}, u32[]{:S(2)}, u32[]{:S(2)}) %collective-permute-start.5) | collective-permute-done | bytes 98336 | tf_op jit(solution)/shard_map/ppermute | solution.py:27
  21.7 0.7 %collective-permute-done.8.refs_5_.refs_6_.corner_low.corner_high = bf16[10,16,256]{2,1,0:T(8,128)(2,1)S(1)} collective-permute-done((bf16[10,16,256]{2,1,0:T(8,128)(2,1)S(1)}, bf16[10,16,256]{2,1,0:T(8,128)(2,1)S(1)}, u32[]{:S(2)}, u32[]{:S(2)}) %collective-permute-start.8) | collective-permute-done | bytes 81952 | tf_op jit(solution)/shard_map/ppermute | solution.py:65
  22.5 2.8 %collective-permute-done.7.refs_4_.planes = bf16[32,16,256]{2,1,0:T(8,128)(2,1)S(1)} collective-permute-done((bf16[32,16,256]{2,1,0:T(8,128)(2,1)S(1)}, bf16[32,16,256]{2,1,0:T(8,128)(2,1)S(1)}, u32[]{:S(2)}, u32[]{:S(2)}) %collective-permute-start.7) | collective-permute-done | bytes 262176 | tf_op jit(solution)/shard_map/ppermute | solution.py:51
  25.2 0.3 shard_map.116
  25.5 0.1 collective-permute-start.9
  25.6 0.0 copy-start
  25.6 0.0 copy-start.4
  25.7 0.0 copy-start.6
  25.7 0.0 copy-start.8
  25.7 1.1 %shard_map.119.inner = f32[4,6,16,256]{3,2,1,0:T(8,128)S(1)} custom-call(bf16[6,8,16,256]{3,2,1,0:T(8,128)(2,1)S(1)} %get-tuple-element.26.refs_1_.encoded.field, bf16[18,16,256]{2,1,0:T(8,128)(2,1)S(1)} %collective-permute-done.6.refs_2_.handed, bf16[9,1024,256]{2,1,0:T(8,128)(2,1)S(1)} %shard_map.118.packed, f32[1,128]{1,0:T(1,128)S(1)} %bitcast.29), custom_call_target="tpu_custom_call" | custom-call | flops 4000000000 | bytes 1000000 | tf_op jit(solution)/shard_map/pallas_call | solution.py:714
  26.8 0.3 collective-permute-done.9.passed
  27.1 0.5 %copy-done = bf16[3,3,3,256,256]{4,3,2,1,0:T(8,128)(2,1)S(1)} copy-done((bf16[3,3,3,256,256]{4,3,2,1,0:T(8,128)(2,1)S(1)}, bf16[3,3,3,256,256]{4,3,2,1,0:T(8,128)(2,1)}, u32[]{:S(2)}) %copy-start) | copy-done | bytes 3538968
  27.6 0.1 copy-done.4
  27.7 0.0 copy-done.8
  27.7 2.6 %shard_map.117 = (bf16[5,2,6,2,16,256]{5,4,3,2,1,0:T(8,128)(2,1)S(1)}, bf16[8,10,16,256]{3,2,1,0:T(8,128)(2,1)S(1)}, bf16[8,10,128]{2,1,0:T(8,128)(2,1)S(1)}, bf16[8,10,128]{2,1,0:T(8,128)(2,1)S(1)}) custom-call(bf16[3,4,16,256]{3,2,1,0:T(8,128)(2,1)S(1)} %get-tuple-element.25.refs_0_.coarse, ...), custom_call_target="tpu_custom_call" | custom-call | flops 4000000000 | bytes 1000000 | tf_op jit(solution)/shard_map/pallas_call | solution.py:799
  30.4 0.6 %collective-permute-start.10 = (bf16[8,10,128]{2,1,0:T(8,128)(2,1)S(1)}, bf16[8,10,128]{2,1,0:T(8,128)(2,1)S(1)}, u32[]{:S(2)}, u32[]{:S(2)}) collective-permute-start(bf16[8,10,128]{2,1,0:T(8,128)(2,1)S(1)} %get-tuple-element.32), channel_id=1, source_target_pairs={{0,1},{1,0},{2,3},{3,2},{4,5},{5,4},{6,7},{7,6},{8,9},{9,8},{10,11... | collective-permute-start | bytes 61448 | tf_op jit(solution)/shard_map/ppermute | solution.py:824
  31.0 1.1 %shard_map.120.partial = f32[6,8,16,256]{3,2,1,0:T(8,128)S(1)} custom-call(bf16[8,10,16,256]{3,2,1,0:T(8,128)(2,1)S(1)} %get-tuple-element.33.encoded_ext, bf16[8,10,128]{2,1,0:T(8,128)(2,1)S(1)} %get-tuple-element.34.columns_in, bf16[9,1024,256]{2,1,0:T(8,128)(2,1)S(1)} %shard_map.118.packed, f32[4,6,16,256]{3,2,1,0:T(8,128)S(1)} %shard_map.119.inner), custom_call_target="tpu_custom_call" | custom-call | flops 4000000000 | bytes 1000000 | tf_op jit(solution)/shard_map/pallas_call | solution.py:825
  32.1 0.0 collective-permute-done.10.columns_in
  32.1 2.9 %shard_map.121 = bf16[6,8,32,128]{3,2,1,0:T(8,128)(2,1)} custom-call(bf16[10,12,16,256]{3,2,1,0:T(8,128)(2,1)S(1)} %bitcast.31, bf16[8,10,128]{2,1,0:T(8,128)(2,1)S(1)} %collective-permute-done.10.columns_in, bf16[9,1024,256]{2,1,0:T(8,128)(2,1)S(1)} %shard_map.118.packed, f32[6,8,16,256]{3,2,1,0:T(8,128)S(1)} %shard_map.120.partial, f32[1,128]{1,0:T(1,128)S(1)} %bitcast.30), custom_call_target="tpu_custom_call" | custom-call | flops 4000000000 | bytes 1000000 | tf_op jit(solution)/shard_map/pallas_call | solution.py:829
  (7 shorter events, 0.1 us)
Async XLA Ops:
  1.1 3.1 %collective-permute-start.1 = (bf16[10,16,256]{2,1,0:T(8,128)(2,1)S(1)}, bf16[10,16,256]{2,1,0:T(8,128)(2,1)S(1)}, u32[]{:S(2)}, u32[]{:S(2)}) collective-permute-start(bf16[10,16,256]{2,1,0:T(8,128)(2,1)S(1)} %get-tuple-element.22), channel_id=1, source_target_pairs={{0,1},{1,0},{2,3},{3,2},{4,5},{5,4},{6,7},{7,6},{8,9},{9,8},{10,11... | collective-permute-start | bytes 245768 | tf_op jit(solution)/shard_map/ppermute | solution.py:701
  1.7 6.7 %collective-permute-start = (bf16[6,16,256]{2,1,0:T(8,128)(2,1)S(1)}, bf16[6,16,256]{2,1,0:T(8,128)(2,1)S(1)}, u32[]{:S(2)}, u32[]{:S(2)}) collective-permute-start(bf16[6,16,256]{2,1,0:T(8,128)(2,1)S(1)} %bitcast.22), channel_id=1, source_target_pairs={{0,2},{2,0},{1,3},{3,1},{4,6},{6,4},{5,7},{7,5},{8,10},{10,8},{9,1... | collective-permute-start | bytes 147464 | tf_op jit(solution)/shard_map/ppermute | solution.py:27
  4.3 3.9 %copy-start.2 = (bf16[3,3,3,128,128]{4,3,2,1,0:T(8,128)(2,1)S(1)}, bf16[3,3,3,128,128]{4,3,2,1,0:T(8,128)(2,1)}, u32[]{:S(2)}) copy-start(bf16[3,3,3,128,128]{4,3,2,1,0:T(8,128)(2,1)} %param.12) | copy-start | bytes 2654212
  4.3 4.7 %collective-permute-start.3 = (bf16[2,16,256]{2,1,0:T(8,128)(2,1)S(1)}, bf16[2,16,256]{2,1,0:T(8,128)(2,1)S(1)}, u32[]{:S(2)}, u32[]{:S(2)}) collective-permute-start(bf16[2,16,256]{2,1,0:T(8,128)(2,1)S(1)} %bitcast.23), channel_id=1, source_target_pairs={{0,6},{2,4},{4,10},{6,8},{8,14},{10,12},{12,30},{14,28},{28,26},{3... | collective-permute-start | bytes 49160 | tf_op jit(solution)/shard_map/ppermute | solution.py:65
  6.6 5.0 %collective-permute-start.2 = (bf16[16,16,256]{2,1,0:T(8,128)(2,1)S(1)}, bf16[16,16,256]{2,1,0:T(8,128)(2,1)S(1)}, u32[]{:S(2)}, u32[]{:S(2)}) collective-permute-start(bf16[16,16,256]{2,1,0:T(8,128)(2,1)S(1)} %get-tuple-element.23), channel_id=1, source_target_pairs={{0,4},{4,8},{8,12},{12,28},{28,24},{24,20},{20,16},{16,0},{1,17},{... | collective-permute-start | bytes 393224 | tf_op jit(solution)/shard_map/ppermute | solution.py:51
  8.4 3.3 %copy-start.7 = (f32[128]{0:T(128)S(1)}, f32[128]{0:T(128)}, u32[]{:S(2)}) copy-start(f32[128]{0:T(128)} %param.13) | copy-start | bytes 1540
  11.7 1.4 %collective-permute-start.4 = (bf16[13,16,256]{2,1,0:T(8,128)(2,1)S(1)}, bf16[13,16,256]{2,1,0:T(8,128)(2,1)S(1)}, u32[]{:S(2)}, u32[]{:S(2)}) collective-permute-start(bf16[13,16,256]{2,1,0:T(8,128)(2,1)S(1)} %shard_map.111), channel_id=1, source_target_pairs={{0,1},{1,0},{2,3},{3,2},{4,5},{5,4},{6,7},{7,6},{8,9},{9,8},{10,11... | collective-permute-start | bytes 319496 | tf_op jit(solution)/shard_map/ppermute | solution.py:731
  11.8 1.3 %copy-start.3 = (bf16[2,2,2,128,256]{4,3,2,1,0:T(8,128)(2,1)S(1)}, bf16[2,2,2,128,256]{4,3,2,1,0:T(8,128)(2,1)}, u32[]{:S(2)}) copy-start(bf16[2,2,2,128,256]{4,3,2,1,0:T(8,128)(2,1)} %param.14) | copy-start | bytes 1572868
  11.8 1.3 %copy-start.5 = (f32[256]{0:T(256)S(1)}, f32[256]{0:T(256)}, u32[]{:S(2)}) copy-start(f32[256]{0:T(256)} %param.15) | copy-start | bytes 3076
  14.8 1.4 %collective-permute-start.6 = (bf16[18,16,256]{2,1,0:T(8,128)(2,1)S(1)}, bf16[18,16,256]{2,1,0:T(8,128)(2,1)S(1)}, u32[]{:S(2)}, u32[]{:S(2)}) collective-permute-start(bf16[18,16,256]{2,1,0:T(8,128)(2,1)S(1)} %get-tuple-element.28), channel_id=1, source_target_pairs={{0,1},{1,0},{2,3},{3,2},{4,5},{5,4},{6,7},{7,6},{8,9},{9,8},{10,11... | collective-permute-start | bytes 442376 | tf_op jit(solution)/shard_map/ppermute | solution.py:701
  15.2 6.5 %collective-permute-start.5 = (bf16[12,16,256]{2,1,0:T(8,128)(2,1)S(1)}, bf16[12,16,256]{2,1,0:T(8,128)(2,1)S(1)}, u32[]{:S(2)}, u32[]{:S(2)}) collective-permute-start(bf16[12,16,256]{2,1,0:T(8,128)(2,1)S(1)} %bitcast.20), channel_id=1, source_target_pairs={{0,2},{2,0},{1,3},{3,1},{4,6},{6,4},{5,7},{7,5},{8,10},{10,8},{9,1... | collective-permute-start | bytes 294920 | tf_op jit(solution)/shard_map/ppermute | solution.py:27
  16.2 3.7 %copy-start.1 = (bf16[3,3,3,256,128]{4,3,2,1,0:T(8,128)(2,1)S(1)}, bf16[3,3,3,256,128]{4,3,2,1,0:T(8,128)(2,1)}, u32[]{:S(2)}) copy-start(bf16[3,3,3,256,128]{4,3,2,1,0:T(8,128)(2,1)} %param.20) | copy-start | bytes 5308420
  16.3 6.2 %collective-permute-start.8 = (bf16[10,16,256]{2,1,0:T(8,128)(2,1)S(1)}, bf16[10,16,256]{2,1,0:T(8,128)(2,1)S(1)}, u32[]{:S(2)}, u32[]{:S(2)}) collective-permute-start(bf16[10,16,256]{2,1,0:T(8,128)(2,1)S(1)} %bitcast.21), channel_id=1, source_target_pairs={{0,6},{2,4},{4,10},{6,8},{8,14},{10,12},{12,30},{14,28},{28,26},{3... | collective-permute-start | bytes 245768 | tf_op jit(solution)/shard_map/ppermute | solution.py:65
  18.3 6.9 %collective-permute-start.7 = (bf16[32,16,256]{2,1,0:T(8,128)(2,1)S(1)}, bf16[32,16,256]{2,1,0:T(8,128)(2,1)S(1)}, u32[]{:S(2)}, u32[]{:S(2)}) collective-permute-start(bf16[32,16,256]{2,1,0:T(8,128)(2,1)S(1)} %get-tuple-element.29), channel_id=1, source_target_pairs={{0,4},{4,8},{8,12},{12,28},{28,24},{24,20},{20,16},{16,0},{1,17},{... | collective-permute-start | bytes 786440 | tf_op jit(solution)/shard_map/ppermute | solution.py:51
  20.5 5.1 %copy-start.9 = (f32[128]{0:T(128)S(1)}, f32[128]{0:T(128)}, u32[]{:S(2)}) copy-start(f32[128]{0:T(128)} %param.21) | copy-start | bytes 1540
  25.5 1.6 %collective-permute-start.9 = (bf16[29,16,256]{2,1,0:T(8,128)(2,1)S(1)}, bf16[29,16,256]{2,1,0:T(8,128)(2,1)S(1)}, u32[]{:S(2)}, u32[]{:S(2)}) collective-permute-start(bf16[29,16,256]{2,1,0:T(8,128)(2,1)S(1)} %shard_map.116), channel_id=1, source_target_pairs={{0,1},{1,0},{2,3},{3,2},{4,5},{5,4},{6,7},{7,6},{8,9},{9,8},{10,11... | collective-permute-start | bytes 712712 | tf_op jit(solution)/shard_map/ppermute | solution.py:731
  25.6 2.0 %copy-start = (bf16[3,3,3,256,256]{4,3,2,1,0:T(8,128)(2,1)S(1)}, bf16[3,3,3,256,256]{4,3,2,1,0:T(8,128)(2,1)}, u32[]{:S(2)}) copy-start(bf16[3,3,3,256,256]{4,3,2,1,0:T(8,128)(2,1)} %param.16) | copy-start | bytes 10616836
  25.6 2.1 %copy-start.4 = (bf16[2,2,2,256,128]{4,3,2,1,0:T(8,128)(2,1)S(1)}, bf16[2,2,2,256,128]{4,3,2,1,0:T(8,128)(2,1)}, u32[]{:S(2)}) copy-start(bf16[2,2,2,256,128]{4,3,2,1,0:T(8,128)(2,1)} %param.18) | copy-start | bytes 1572868
  25.7 2.1 %copy-start.6 = (f32[256]{0:T(256)S(1)}, f32[256]{0:T(256)}, u32[]{:S(2)}) copy-start(f32[256]{0:T(256)} %param.17) | copy-start | bytes 3076
  25.7 2.1 %copy-start.8 = (f32[128]{0:T(128)S(1)}, f32[128]{0:T(128)}, u32[]{:S(2)}) copy-start(f32[128]{0:T(128)} %param.19) | copy-start | bytes 1540
  30.4 1.7 %collective-permute-start.10 = (bf16[8,10,128]{2,1,0:T(8,128)(2,1)S(1)}, bf16[8,10,128]{2,1,0:T(8,128)(2,1)S(1)}, u32[]{:S(2)}, u32[]{:S(2)}) collective-permute-start(bf16[8,10,128]{2,1,0:T(8,128)(2,1)S(1)} %get-tuple-element.32), channel_id=1, source_target_pairs={{0,1},{1,0},{2,3},{3,2},{4,5},{5,4},{6,7},{7,6},{8,9},{9,8},{10,11... | collective-permute-start | bytes 61448 | tf_op jit(solution)/shard_map/ppermute | solution.py:824
